TPU v7x, 32 devices: a whole 2x2x4 slice. The times are simulated.
32 devices in a mesh: expert: 8 (over z, x), tensor: 4 (over y, core).
Axes of the slice: x: 2, y: 2, z: 4, core: 2. Of those that a mesh axis runs over, the one named last changes fastest.
Arguments:
- tokens: bfloat16 [20480, 1024], P(('expert', 'tensor')), may hold values from -6 to 6
- cotangent: bfloat16 [20480, 1024], P(('expert', 'tensor')), may hold values from -6 to 6
- routes: int32 [20480, 1], P('expert'), may hold values from 0 to 7; in each aligned block of 640 rows (0 to 639, 640 to 1279, ...) at most 112 rows name the same one
- parents: int32 [8, 13], P('expert'), may hold values from 0 to 4, as said below
- ln_attn: float32 [1024], replicated, may hold values from 0.5 to 1.5
- w_qkv: bfloat16 [3, 1024, 1024], P(None, None, 'tensor'), may hold values from -0.1875 to 0.1875
- w_out: bfloat16 [1024, 1024], P('tensor'), may hold values from -3 to 3
- ln_mlp: float32 [1024], replicated, may hold values from 0.5 to 1.5
- w_up: bfloat16 [1024, 4096], P(None, 'tensor'), may hold values from -0.1875 to 0.1875
- w_down: bfloat16 [4096, 1024], P('tensor'), may hold values from -0.09375 to 0.09375
- w_router: bfloat16 [1024, 8], replicated, may hold values from -0.09375 to 0.09375
- w_mix: bfloat16 [1024, 2], replicated, may hold values from -0.1875 to 0.1875
- ex_up: bfloat16 [8, 1024, 4096], P('expert', None, 'tensor'), may hold values from -0.1875 to 0.1875
- ex_down: bfloat16 [8, 4096, 1024], P('expert', 'tensor')
Outputs:
- out: bfloat16 [20480, 1024], P(('expert', 'tensor'))
- grad_tokens: float32 [20480, 1024], P(('expert', 'tensor'))
- grad_ln_attn: float32 [1024], replicated
- grad_qkv: float32 [3, 1024, 1024], P(None, 'expert', 'tensor')
- grad_w_out: float32 [1024, 1024], P('tensor', 'expert')
- grad_ln_mlp: float32 [1024], P('expert')
- grad_up: float32 [1024, 4096], P('expert', 'tensor')
- grad_down: float32 [4096, 1024], P('tensor', 'expert')
- grad_router: float32 [1024, 8], P('expert')
- grad_mix: float32 [1024, 2], P('expert')
- grad_ex_up: float32 [8, 1024, 4096], P('expert', None, 'tensor')
- grad_ex_down: float32 [8, 4096, 1024], P('expert', 'tensor')
Inputs may be any that keep to these rules, and one draw needn't show every extreme that they name: `routes`: in each aligned block of 640 rows (the rows of one device), no expert is named by more than 112 rows, a bound that some block reaches. `parents`: entry j of a row is the parent segment of segment j. Entries 0 to 4 are 0 (the trunk and the four branches hang on the trunk); entries 5 to 12 (the leaves) name each branch 1 to 4 exactly twice.
All inputs are finite; a program needn't handle non-finite values.
Results may differ from a plain program's by a relative error of at most 0.017.
Values may be sent and summed in bfloat16 or wider, within the bound.
No kernel may reach another device: no remote copies, remote signals or barrier semaphores. Data moves between devices by JAX's collectives and lax.ppermute only.
A program may use at most 320 MiB of HBM per device.

v0:
```python
import jax
import jax.numpy as jnp
from jax import lax
from jax.sharding import PartitionSpec as P

HEAD_DIM = 64
TRUNK = 1024
SEG = 128
SEGS = 13
QBLK = 512
TREE_LEN = 2560


EPSILON = 1e-05
NEGATIVE_FILL = -1e30


def norm_parts(values):
    row_mean = jnp.mean(values, axis=-1, keepdims=True)
    centred = values - row_mean
    row_var = jnp.mean(centred * centred, axis=-1, keepdims=True)
    inverse = lax.rsqrt(row_var + EPSILON)
    return (centred * inverse, inverse)


def norm_back(grad_normed, gain_vec, scaled, inverse):
    grad_scaled = grad_normed * gain_vec
    first_mean = jnp.mean(grad_scaled, axis=-1, keepdims=True)
    second = jnp.mean(grad_scaled * scaled, axis=-1, keepdims=True)
    return inverse * (grad_scaled - first_mean - scaled * second)


def gelu_exact(values):
    return jax.nn.gelu(values, approximate=False)


def gelu_slope(values):
    return (
        0.5 * (1.0 + lax.erf(values * 0.7071067811865476))
        + values * jnp.exp(-0.5 * values * values) * 0.3989422804014327
    )


def segment_of(position):
    return jnp.where(position < TRUNK, 0, 1 + (position - TRUNK) // SEG)


def path_mask(parents_row, query_pos, key_pos):
    seg_ids = jnp.arange(SEGS, dtype=jnp.int32)
    query_seg = segment_of(query_pos)
    key_seg = segment_of(key_pos)
    parent_seg = jnp.sum(
        jnp.where(query_seg[:, None] == seg_ids[None, :], parents_row[None, :], 0), axis=1
    )
    grand_seg = jnp.sum(
        jnp.where(parent_seg[:, None] == seg_ids[None, :], parents_row[None, :], 0), axis=1
    )
    on_path = (
        (key_seg[None, :] == query_seg[:, None])
        | (key_seg[None, :] == parent_seg[:, None])
        | (key_seg[None, :] == grand_seg[:, None])
    )
    return on_path & (key_pos[None, :] <= query_pos[:, None])


def block_inputs(qkv_rows, parents, block_index):
    row_start = block_index * QBLK
    tree_index = row_start // TREE_LEN
    queries = lax.dynamic_slice_in_dim(qkv_rows[0], row_start, QBLK, 0).reshape(QBLK, -1, HEAD_DIM)
    key_rows = qkv_rows[1].reshape(TREE_LEN, -1, HEAD_DIM)
    values = qkv_rows[2].reshape(TREE_LEN, -1, HEAD_DIM)
    parents_row = lax.dynamic_index_in_dim(parents, tree_index, 0, keepdims=False)
    raw_scores = jnp.einsum(
        "qhd,khd->hqk", queries, key_rows, preferred_element_type=jnp.float32
    ) * HEAD_DIM ** (-0.5)
    first_row = row_start - tree_index * TREE_LEN
    allowed = path_mask(
        parents_row,
        first_row + jnp.arange(QBLK, dtype=jnp.int32),
        jnp.arange(TREE_LEN, dtype=jnp.int32),
    )
    scores = jnp.where(allowed[None], raw_scores, NEGATIVE_FILL)
    return (row_start, tree_index, queries, key_rows, values, scores)


def to_owners(values, expert_ids, quarter, slot_index, experts, quarters, capacity):
    width = values.shape[1]
    outgoing = jnp.zeros((experts, quarters, capacity, width), jnp.bfloat16)
    outgoing = outgoing.at[expert_ids, quarter, slot_index].set(values)
    return lax.all_to_all(outgoing, "expert", split_axis=0, concat_axis=0, tiled=True)


def to_sources(parts):
    return lax.all_to_all(
        parts.astype(jnp.bfloat16), "expert", split_axis=0, concat_axis=0, tiled=True
    ).astype(parts.dtype)


def per_device(
    tokens,
    cotangent,
    routes,
    parents,
    ln_attn,
    w_qkv,
    w_out,
    ln_mlp,
    w_up,
    w_down,
    w_router,
    w_mix,
    ex_up,
    ex_down,
):
    tok_dev = tokens.shape[0]
    model_width = tokens.shape[1]
    quarters = lax.axis_size("tensor")
    own_start = lax.axis_index("tensor") * tok_dev
    group_rows = tok_dev * quarters
    experts = w_router.shape[1]
    capacity = max(2, tok_dev * 7 // (5 * experts))
    block_total = group_rows // QBLK
    gathered = lax.all_gather(tokens, "tensor", axis=0, tiled=True)
    scaled_one, inverse_one = norm_parts(gathered.astype(jnp.float32))
    normed_one = (scaled_one * ln_attn).astype(jnp.bfloat16)
    qkv_rows = jnp.einsum(
        "td,sdc->stc", normed_one, w_qkv, preferred_element_type=jnp.float32
    ).astype(jnp.bfloat16)

    def attend_block(block_index):
        row_start, tree_index, queries, key_rows, values, scores = block_inputs(
            qkv_rows, parents, block_index
        )
        row_max = jnp.max(scores, axis=-1, keepdims=True)
        weights = jnp.exp(scores - row_max)
        row_total = jnp.sum(weights, axis=-1, keepdims=True)
        weights = (weights / row_total).astype(jnp.bfloat16)
        output = jnp.einsum("hqk,khd->qhd", weights, values, preferred_element_type=jnp.float32)
        return (
            output.reshape(QBLK, -1).astype(jnp.bfloat16),
            (row_max + jnp.log(row_total))[..., 0],
        )

    attended, log_total = lax.map(attend_block, jnp.arange(block_total, dtype=jnp.int32))
    attended = attended.reshape(group_rows, -1)
    residual = tokens.astype(jnp.float32) + lax.psum_scatter(
        jnp.dot(attended, w_out, preferred_element_type=jnp.float32),
        "tensor",
        scatter_dimension=0,
        tiled=True,
    )
    residual_all = lax.all_gather(residual, "tensor", axis=0, tiled=True)
    scaled_two, inverse_two = norm_parts(residual_all)
    normed_two = (scaled_two * ln_mlp).astype(jnp.bfloat16)
    pre_dense = jnp.dot(normed_two, w_up, preferred_element_type=jnp.float32)
    active = gelu_exact(pre_dense).astype(jnp.bfloat16)
    dense_part = jnp.dot(active, w_down, preferred_element_type=jnp.float32)
    router_probs = jax.nn.softmax(
        jnp.dot(normed_two, w_router, preferred_element_type=jnp.float32), axis=-1
    )
    expert_ids = routes[:, 0]
    chosen = expert_ids[:, None] == jnp.arange(experts, dtype=jnp.int32)[None, :]
    gate_prob = jnp.sum(jnp.where(chosen, router_probs, 0.0), axis=1)
    mix_coef = jax.nn.softmax(
        jnp.dot(normed_two, w_mix, preferred_element_type=jnp.float32), axis=-1
    )
    counted = chosen.astype(jnp.int32).reshape(quarters, tok_dev, experts)
    position = (jnp.cumsum(counted, axis=1) - 1).reshape(group_rows, experts)
    slot_index = jnp.sum(jnp.where(chosen, position, 0), axis=1)
    quarter = jnp.arange(group_rows, dtype=jnp.int32) // tok_dev
    arrived = to_owners(normed_two, expert_ids, quarter, slot_index, experts, quarters, capacity)
    flat_rows = arrived.reshape(-1, model_width)
    expert_pre = jnp.dot(flat_rows, ex_up[0], preferred_element_type=jnp.float32)
    expert_active = gelu_exact(expert_pre).astype(jnp.bfloat16)
    expert_part = jnp.dot(expert_active, ex_down[0], preferred_element_type=jnp.float32).reshape(
        arrived.shape
    )
    returned = to_sources(expert_part)
    expert_weight = mix_coef[:, 1] * gate_prob
    expert_rows = returned[expert_ids, quarter, slot_index]
    extra_term = 0.0
    dense_coef = mix_coef[:, 0]
    mixed = (
        lax.psum_scatter(
            (dense_coef[:, None] * dense_part + expert_weight[:, None] * expert_rows).astype(
                jnp.bfloat16
            ),
            "tensor",
            scatter_dimension=0,
            tiled=True,
        ).astype(jnp.float32)
        + extra_term
    )
    out = (residual + mixed).astype(jnp.bfloat16)
    grad_all = lax.all_gather(cotangent, "tensor", axis=0, tiled=True).astype(jnp.float32)
    grad_dense = (mix_coef[:, 0:1] * grad_all).astype(jnp.bfloat16)
    grad_down = jnp.einsum("gf,gd->fd", active, grad_dense, preferred_element_type=jnp.float32)
    grad_active = jnp.einsum("gd,fd->gf", grad_dense, w_down, preferred_element_type=jnp.float32)
    grad_pre = (grad_active * gelu_slope(pre_dense)).astype(jnp.bfloat16)
    grad_up = jnp.einsum("gd,gf->df", normed_two, grad_pre, preferred_element_type=jnp.float32)
    grad_normed_two = jnp.einsum("gf,df->gd", grad_pre, w_up, preferred_element_type=jnp.float32)
    dense_dot = jnp.sum(grad_all * dense_part, axis=1)
    grad_expert = (expert_weight[:, None] * grad_all).astype(jnp.bfloat16)
    arrived_grad = to_owners(
        grad_expert, expert_ids, quarter, slot_index, experts, quarters, capacity
    )
    flat_grad = arrived_grad.reshape(-1, model_width)
    grad_ex_down = jnp.einsum(
        "rf,rd->fd", expert_active, flat_grad, preferred_element_type=jnp.float32
    )[None]
    grad_ex_active = jnp.einsum(
        "rd,fd->rf", flat_grad, ex_down[0], preferred_element_type=jnp.float32
    )
    grad_ex_pre = (grad_ex_active * gelu_slope(expert_pre)).astype(jnp.bfloat16)
    grad_ex_up = jnp.einsum(
        "rd,rf->df", flat_rows, grad_ex_pre, preferred_element_type=jnp.float32
    )[None]
    grad_ex_rows = jnp.einsum(
        "rf,df->rd", grad_ex_pre, ex_up[0], preferred_element_type=jnp.float32
    ).reshape(arrived.shape)
    grad_back = to_sources(grad_ex_rows)
    grad_normed_two = grad_normed_two + grad_back[expert_ids, quarter, slot_index]
    expert_dot = jnp.sum(grad_all * expert_rows, axis=1)
    row_dots = jnp.stack([dense_dot, expert_dot], axis=1)
    grad_normed_two, row_dots = (
        lax.psum(grad_normed_two.astype(jnp.bfloat16), "tensor").astype(jnp.float32),
        lax.psum(row_dots.astype(jnp.bfloat16), "tensor").astype(jnp.float32),
    )
    mix_grad = jnp.stack([row_dots[:, 0], gate_prob * row_dots[:, 1]], axis=1)
    grad_mix_logits = (
        mix_coef * (mix_grad - jnp.sum(mix_coef * mix_grad, axis=1, keepdims=True))
    ).astype(jnp.bfloat16)
    grad_gate = mix_coef[:, 1] * row_dots[:, 1]
    grad_router_logits = (
        router_probs
        * (jnp.where(chosen, grad_gate[:, None], 0.0) - (gate_prob * grad_gate)[:, None])
    ).astype(jnp.bfloat16)
    grad_normed_two = grad_normed_two + jnp.einsum(
        "ge,de->gd", grad_router_logits, w_router, preferred_element_type=jnp.float32
    )
    grad_normed_two = grad_normed_two + jnp.einsum(
        "gm,dm->gd", grad_mix_logits, w_mix, preferred_element_type=jnp.float32
    )
    grad_router = jnp.einsum(
        "gd,ge->de", normed_two, grad_router_logits, preferred_element_type=jnp.float32
    )
    grad_mix = jnp.einsum(
        "gd,gm->dm", normed_two, grad_mix_logits, preferred_element_type=jnp.float32
    )
    grad_ln_mlp = jnp.sum(grad_normed_two * scaled_two, axis=0)
    grad_residual = grad_all + norm_back(grad_normed_two, ln_mlp, scaled_two, inverse_two)
    grad_branch = grad_residual.astype(jnp.bfloat16)
    grad_w_out = jnp.einsum("gc,gd->cd", attended, grad_branch, preferred_element_type=jnp.float32)
    grad_attended = jnp.einsum(
        "gd,cd->gc", grad_branch, w_out, preferred_element_type=jnp.float32
    ).astype(jnp.bfloat16)

    def attend_back(carried, block_index):
        grad_keys, grad_values = carried
        row_start, tree_index, queries, key_rows, values, scores = block_inputs(
            qkv_rows, parents, block_index
        )
        log_block = lax.dynamic_index_in_dim(log_total, block_index, 0, keepdims=False)
        weights = jnp.exp(scores - log_block[..., None])
        grad_block = lax.dynamic_slice_in_dim(grad_attended, row_start, QBLK, 0).reshape(
            QBLK, -1, HEAD_DIM
        )
        grad_weights = jnp.einsum(
            "qhd,khd->hqk", grad_block, values, preferred_element_type=jnp.float32
        )
        inner = jnp.sum(weights * grad_weights, axis=-1, keepdims=True)
        grad_scores = (weights * (grad_weights - inner)).astype(jnp.bfloat16)
        grad_query = jnp.einsum(
            "hqk,khd->qhd", grad_scores, key_rows, preferred_element_type=jnp.float32
        ) * HEAD_DIM ** (-0.5)
        key_part = jnp.einsum(
            "hqk,qhd->khd", grad_scores, queries, preferred_element_type=jnp.float32
        ) * HEAD_DIM ** (-0.5)
        value_part = jnp.einsum(
            "hqk,qhd->khd",
            weights.astype(jnp.bfloat16),
            grad_block,
            preferred_element_type=jnp.float32,
        )
        grad_keys = grad_keys + key_part.reshape(TREE_LEN, -1)
        grad_values = grad_values + value_part.reshape(TREE_LEN, -1)
        return ((grad_keys, grad_values), grad_query.reshape(QBLK, -1).astype(jnp.bfloat16))

    empty_rows = jnp.zeros((group_rows, qkv_rows.shape[2]), jnp.float32)
    (grad_keys, grad_values), grad_queries = lax.scan(
        attend_back, (empty_rows, empty_rows), jnp.arange(block_total, dtype=jnp.int32)
    )
    grad_qkv_rows = jnp.stack(
        [
            grad_queries.reshape(group_rows, -1),
            grad_keys.astype(jnp.bfloat16),
            grad_values.astype(jnp.bfloat16),
        ]
    )
    grad_w_qkv = jnp.einsum(
        "gd,sgc->sdc", normed_one, grad_qkv_rows, preferred_element_type=jnp.float32
    )
    grad_normed_one = jnp.einsum(
        "sgc,sdc->gd", grad_qkv_rows, w_qkv, preferred_element_type=jnp.float32
    )
    part_gain = jnp.sum(grad_normed_one * scaled_one, axis=0)
    grad_normed_own = lax.psum_scatter(
        grad_normed_one.astype(jnp.bfloat16), "tensor", scatter_dimension=0, tiled=True
    ).astype(jnp.float32)
    own_scaled = lax.dynamic_slice_in_dim(scaled_one, own_start, tok_dev, 0)
    own_inverse = lax.dynamic_slice_in_dim(inverse_one, own_start, tok_dev, 0)
    own_residual_grad = lax.dynamic_slice_in_dim(grad_residual, own_start, tok_dev, 0)
    grad_tokens = own_residual_grad + norm_back(grad_normed_own, ln_attn, own_scaled, own_inverse)
    summed_grads = (
        lax.psum_scatter(grad_w_qkv, "expert", scatter_dimension=1, tiled=True),
        lax.psum_scatter(grad_w_out, "expert", scatter_dimension=1, tiled=True),
        lax.psum_scatter(grad_ln_mlp, "expert", scatter_dimension=0, tiled=True),
        lax.psum_scatter(grad_up, "expert", scatter_dimension=0, tiled=True),
        lax.psum_scatter(grad_down, "expert", scatter_dimension=1, tiled=True),
        lax.psum_scatter(grad_router, "expert", scatter_dimension=0, tiled=True),
        lax.psum_scatter(grad_mix, "expert", scatter_dimension=0, tiled=True),
    )
    grad_ln_attn = lax.psum(part_gain, ("expert", "tensor"))
    return (
        out,
        grad_tokens,
        grad_ln_attn,
        summed_grads[0],
        summed_grads[1],
        summed_grads[2],
        summed_grads[3],
        summed_grads[4],
        summed_grads[5],
        summed_grads[6],
        grad_ex_up,
        grad_ex_down,
    )


def solution(mesh):
    return jax.shard_map(
        per_device,
        mesh=mesh,
        in_specs=(
            P(("expert", "tensor"), None),
            P(("expert", "tensor"), None),
            P("expert", None),
            P("expert", None),
            P(),
            P(None, None, "tensor"),
            P("tensor", None),
            P(),
            P(None, "tensor"),
            P("tensor", None),
            P(),
            P(),
            P("expert", None, "tensor"),
            P("expert", "tensor", None),
        ),
        out_specs=(
            P(("expert", "tensor"), None),
            P(("expert", "tensor"), None),
            P(),
            P(None, "expert", "tensor"),
            P("tensor", "expert"),
            P("expert"),
            P("expert", "tensor"),
            P("tensor", "expert"),
            P("expert", None),
            P("expert", None),
            P("expert", None, "tensor"),
            P("expert", "tensor", None),
        ),
        check_vma=False,
    )
```

profile of v0, /device:TPU:0, one launch (start us, length us, event | category | flops | bytes accessed | tf_op | source)
XLA Modules:
  0.0 2363.5 jit_solution(15836324658128825775)
XLA Ops:
  8.0 44.8 %all-gather.4.cloned.1.call-done = bf16[2560,1024]{1,0:T(8,128)(2,1)} async-done(((bf16[640,1024]{1,0:T(8,128)(2,1)}), bf16[2560,1024]{1,0:T(8,128)(2,1)}) %all-gather.4.cloned.1.call-update) | async-done | bytes 5242896 | tf_op jit(solution)/shard_map/all_gather | solution.py:123
  75.0 190.0 %while.33 = (s32[]{:T(128)}, bf16[5,512,256]{2,1,0:T(8,128)(2,1)}, f32[5,4,512]{2,1,0:T(4,128)S(1)}, s32[5]{0:T(128)S(1)}, s32[1,13]{1,0:T(1,128)S(1)}, /*index=...) while((s32[]{:T(128)}, bf16[5,512,256]{2,1,0:T(8,128)(2,1)}, ...), condition=%wide.region_7.8_spmd, body=%wide.region_2.7_spmd.sunk | while | flops 1414493696 | bytes 169976272 | solution.py:144
  272.6 85.0 %reduce-scatter.12.cloned.1.call-done = f32[640,1024]{1,0:T(8,128)} async-done(((f32[2560,1024]{1,0:T(8,128)}), f32[640,1024]{1,0:T(8,128)}) %reduce-scatter.12.cloned.1.call-update) | async-done | bytes 2621456 | tf_op jit(solution)/shard_map/reduce_scatter | solution.py:146
  368.6 63.2 %all-gather.6.cloned.1.call-done = f32[2560,1024]{1,0:T(8,128)} async-done(((f32[640,1024]{1,0:T(8,128)}), f32[2560,1024]{1,0:T(8,128)}) %all-gather.6.cloned.1.call-update) | async-done | bytes 10485776 | tf_op jit(solution)/shard_map/all_gather | solution.py:152
  459.7 166.5 %all_to_all.20 = bf16[8,4,112,1024]{3,2,1,0:T(8,128)(2,1)S(1)} all-to-all(bf16[8,4,112,1024]{3,2,1,0:T(8,128)(2,1)} %bitcast.211), channel_id=1, replica_groups=mesh['expert'=8,'tensor'=4] {'expert'}, dimensions={0} | all-to-all | bytes 14680064 | tf_op jit(solution)/shard_map/all_to_all | solution.py:90
  626.2 40.2 %fusion.43 = (bf16[3584,1024]{1,0:T(8,128)(2,1)S(1)}, f32[3584,1024]{1,0:T(8,128)}) fusion(bf16[3584,1024]{1,0:T(8,128)(2,1)S(1)} %bitcast.215, bf16[1,1024,1024]{2,1,0:T(8,128)(2,1)S(1)} %copy-done), kind=kOutput, calls=%fused_computation.106 | convolution fusion | flops 7754743808 | bytes 31457280 | tf_op jit(solution)/shard_map/dot_general | solution.py:173
  694.0 29.9 %fusion.62 = (bf16[2560,1024]{1,0:T(8,128)(2,1)}, f32[2560,1024]{1,0:T(8,128)}) fusion(bf16[2560,1024]{1,0:T(8,128)(2,1)S(1)} %multiply_convert_fusion.1, bf16[1024,1024]{1,0:T(8,128)(2,1)S(1)} %copy-done.58), kind=kOutput, calls=%fused_computation.135 | convolution fusion | flops 5539102720 | bytes 23068672 | tf_op jit(solution)/shard_map/dot_general | solution.py:155
  723.9 120.1 %all-to-all-done.1 = bf16[8,4,112,1024]{3,2,1,0:T(8,128)(2,1)} async-done(((bf16[8,4,112,1024]{3,2,1,0:T(8,128)(2,1)}), bf16[8,4,112,1024]{3,2,1,0:T(8,128)(2,1)}, u32[]{:S(2)}, u32[]{:S(2)}) %all-to-all-start.1) | async-done | bytes 7340064 | tf_op jit(solution)/shard_map/all_to_all | solution.py:94
  854.2 40.0 %gather_fusion = f32[2560,1024]{1,0:T(8,128)} fusion(f32[8,4,112,1024]{3,2,1,0:T(8,128)} %convert_element_type.171, s32[2560]{0:T(1024)S(1)} %copy-done.3), kind=kCustom, calls=%fused_computation | custom fusion | bytes 21002240 | tf_op jit(solution)/shard_map/gather | solution.py:180
  937.7 164.1 %all_to_all.21 = bf16[8,4,112,1024]{3,2,1,0:T(8,128)(2,1)S(1)} all-to-all(bf16[8,4,112,1024]{3,2,1,0:T(8,128)(2,1)} %bitcast.212), channel_id=1, replica_groups=mesh['expert'=8,'tensor'=4] {'expert'}, dimensions={0} | all-to-all | bytes 14680064 | tf_op jit(solution)/shard_map/all_to_all | solution.py:90
  1148.5 146.3 %all-to-all-done.3 = bf16[8,4,112,1024]{3,2,1,0:T(8,128)(2,1)} async-done(((bf16[8,4,112,1024]{3,2,1,0:T(8,128)(2,1)}), bf16[8,4,112,1024]{3,2,1,0:T(8,128)(2,1)}, u32[]{:S(2)}, u32[]{:S(2)}) %all-to-all-start.3) | async-done | bytes 7340064 | tf_op jit(solution)/shard_map/all_to_all | solution.py:94
  1305.1 39.9 %gather_fusion.1 = f32[2560,1024]{1,0:T(8,128)} fusion(f32[8,4,112,1024]{3,2,1,0:T(8,128)} %convert_element_type.181, s32[2560]{0:T(1024)S(1)} %copy-done.3), kind=kCustom, calls=%fused_computation.1 | custom fusion | bytes 21002240 | tf_op jit(solution)/shard_map/gather | solution.py:222
  1378.0 79.9 %all-reduce.3.cloned.1.call-done = bf16[2560,1024]{1,0:T(8,128)(2,1)} async-done(((bf16[2560,1024]{1,0:T(8,128)(2,1)}), bf16[2560,1024]{1,0:T(8,128)(2,1)}) %all-reduce.3.cloned.1.call-update) | async-done | bytes 5242896 | tf_op jit(solution)/shard_map/psum | solution.py:226
  1482.9 420.8 %while.34 = (s32[]{:T(128)}, f32[2560,256]{0,1:T(8,128)}, f32[2560,256]{0,1:T(8,128)}, bf16[5,512,256]{2,1,0:T(8,128)(2,1)}, bf16[3,2560,256]{1,2,0:T(8,128)(2,1...) while((s32[]{:T(128)}, f32[2560,256]{0,1:T(8,128)}, ...), condition=%wide.region_33.34_spmd.clone, body=%wide.region_29.33_spmd.clone.sunk | while | flops 3446896640 | bytes 251757168 | solution.py:290
  1528.4 22.2 multiply_convert_fusion.9
  1614.2 20.0 multiply_convert_fusion.9
  1697.7 20.0 multiply_convert_fusion.9
  1781.3 20.0 multiply_convert_fusion.9
  1992.3 21.0 all-reduce
  2025.6 37.2 %psum.23 = f32[1024]{0:T(1024)} all-reduce(f32[1024]{0:T(1024)S(1)} %get-tuple-element.473), channel_id=1, replica_groups=mesh['expert'=8,'tensor'=4] {'expert','tensor'}, use_global_device_ids=true, to_apply=%region_38.39 | all-reduce | flops 1024 | bytes 8192 | tf_op jit(solution)/shard_map/psum | solution.py:323
  2072.6 32.0 %reduce-scatter.26.cloned.1.call-done = f32[128,8]{0,1:T(8,128)} async-done(((f32[1024,8]{0,1:T(8,128)}), f32[128,8]{0,1:T(8,128)}) %reduce-scatter.26.cloned.1.call-update) | async-done | bytes 4112 | tf_op jit(solution)/shard_map/reduce_scatter | solution.py:320
  2104.6 92.2 %reduce-scatter.24.cloned.1.call-done = f32[1024,128]{1,0:T(8,128)} async-done(((f32[1024,1024]{1,0:T(8,128)}), f32[1024,128]{1,0:T(8,128)}) %reduce-scatter.24.cloned.1.call-update) | async-done | bytes 524304 | tf_op jit(solution)/shard_map/reduce_scatter | solution.py:319
  2196.8 91.9 %reduce-scatter.22.cloned.1.call-done = f32[128,1024]{1,0:T(8,128)} async-done(((f32[1024,1024]{1,0:T(8,128)}), f32[128,1024]{1,0:T(8,128)}) %reduce-scatter.22.cloned.1.call-update) | async-done | bytes 524304 | tf_op jit(solution)/shard_map/reduce_scatter | solution.py:318
  2288.7 68.0 %reduce-scatter.20.cloned.1.call-done = f32[256,128]{1,0:T(8,128)} async-done(((f32[256,1024]{1,0:T(8,128)}), f32[256,128]{1,0:T(8,128)}) %reduce-scatter.20.cloned.1.call-update) | async-done | bytes 131088 | tf_op jit(solution)/shard_map/reduce_scatter | solution.py:316
  (485 shorter events, 885.3 us)
Async XLA Ops:
  7.2 619.0 %copy-start = (bf16[1,1024,1024]{2,1,0:T(8,128)(2,1)S(1)}, bf16[1,1024,1024]{2,1,0:T(8,128)(2,1)}, u32[]{:S(2)}) copy-start(bf16[1,1024,1024]{2,1,0:T(8,128)(2,1)} %param.30) | copy-start | bytes 6291460
  7.2 45.6 %all-gather.4.cloned.1.call-start = ((), (), s32[]{:S(2)}) async-start(), calls=%async_computation.13 | async-start | bytes 6553600 | tf_op jit(solution)/shard_map/all_gather | solution.py:123
  7.9 349.6 %reduce-scatter.12.cloned.1.call-start = ((), (), s32[]{:S(2)}) async-start(), calls=%async_computation.14 | async-start | bytes 13107200 | tf_op jit(solution)/shard_map/reduce_scatter | solution.py:146
  272.1 159.7 %all-gather.6.cloned.1.call-start = ((), (), s32[]{:S(2)}) async-start(), calls=%async_computation.15 | async-start | bytes 13107200 | tf_op jit(solution)/shard_map/all_gather | solution.py:152
  361.5 331.9 %copy-start.27 = (s32[2560]{0:T(1024)}, s32[2560]{0:T(1024)S(1)}, u32[]{:S(2)}) copy-start(s32[2560]{0:T(1024)S(1)} %reduce.8) | copy-start | bytes 30724
  436.3 248.5 %copy-start.23 = (f32[2560]{0:T(1024)}, f32[2560]{0:T(1024)S(1)}, u32[]{:S(2)}) copy-start(f32[2560]{0:T(1024)S(1)} %broadcast_multiply_fusion.2) | copy-start | bytes 30724
  441.6 243.2 %copy-start.25 = (f32[2560]{0:T(1024)}, f32[2560]{0:T(1024)S(1)}, u32[]{:S(2)}) copy-start(f32[2560]{0:T(1024)S(1)} %add_rsqrt_fusion) | copy-start | bytes 30724
  679.3 164.8 %all-to-all-start.1 = ((bf16[8,4,112,1024]{3,2,1,0:T(8,128)(2,1)}), bf16[8,4,112,1024]{3,2,1,0:T(8,128)(2,1)}, u32[]{:S(2)}, u32[]{:S(2)}) async-start(bf16[8,4,112,1024]{3,2,1,0:T(8,128)(2,1)} %convolution_convert_fusion.1), calls=%async_computation.2 | async-start | bytes 14680064 | tf_op jit(solution)/shard_map/all_to_all | solution.py:94
  684.2 210.0 %all-gather.8.cloned.1.call-start = ((), (), s32[]{:S(2)}) async-start(), calls=%async_computation.17 | async-start | bytes 6553600 | tf_op jit(solution)/shard_map/all_gather | solution.py:195
  919.9 441.6 %copy-start.43 = (f32[2560]{0:T(1024)}, f32[2560]{0:T(1024)S(1)}, u32[]{:S(2)}) copy-start(f32[2560]{0:T(1024)S(1)} %get-tuple-element.426) | copy-start | bytes 30724
  1130.4 164.5 %all-to-all-start.3 = ((bf16[8,4,112,1024]{3,2,1,0:T(8,128)(2,1)}), bf16[8,4,112,1024]{3,2,1,0:T(8,128)(2,1)}, u32[]{:S(2)}, u32[]{:S(2)}) async-start(bf16[8,4,112,1024]{3,2,1,0:T(8,128)(2,1)} %convolution_convert_fusion), calls=%async_computation.5 | async-start | bytes 14680064 | tf_op jit(solution)/shard_map/all_to_all | solution.py:94
  1135.5 322.5 %all-reduce.3.cloned.1.call-start = ((), (), s32[]{:S(2)}) async-start(), calls=%async_computation.18 | async-start | bytes 10485760 | tf_op jit(solution)/shard_map/psum | solution.py:226
  1356.5 600.4 %reduce-scatter.28.cloned.1.call-start = ((), (), s32[]{:S(2)}) async-start(), calls=%async_computation.25 | async-start | bytes 589824
  1372.1 586.4 %reduce-scatter.14.cloned.1.call-start = ((), (), s32[]{:S(2)}) async-start(), calls=%async_computation.16 | async-start | bytes 6553600 | tf_op jit(solution)/shard_map/reduce_scatter | solution.py:184
  1378.0 684.8 %reduce-scatter.18.cloned.1.call-start = ((), (), s32[]{:S(2)}) async-start(), calls=%async_computation.20 | async-start | bytes 3538944 | tf_op jit(solution)/shard_map/reduce_scatter | solution.py:315
  1482.9 425.6 %copy-start.34 = (f32[2560]{0:T(1024)S(1)}, f32[2560]{0:T(1024)}, u32[]{:S(2)}) copy-start(f32[2560]{0:T(1024)} %copy-done.33) | copy-start | bytes 30724
  1482.9 425.6 %copy-start.38 = (f32[2560]{0:T(1024)S(1)}, f32[2560]{0:T(1024)}, u32[]{:S(2)}) copy-start(f32[2560]{0:T(1024)} %copy-done.37) | copy-start | bytes 30724
  1482.9 425.6 %copy-start.50 = (f32[1024]{0:T(1024)S(1)}, f32[1024]{0:T(1024)}, u32[]{:S(2)}) copy-start(f32[1024]{0:T(1024)} %param.22) | copy-start | bytes 12292
  1918.2 146.5 %reduce-scatter.16.cloned.1.call-start = ((), (), s32[]{:S(2)}) async-start(), calls=%async_computation.19 | async-start | bytes 6553600 | tf_op jit(solution)/shard_map/reduce_scatter | solution.py:307
  1930.2 174.4 %reduce-scatter.26.cloned.1.call-start = ((), (), s32[]{:S(2)}) async-start(), calls=%async_computation.24 | async-start | bytes 36864 | tf_op jit(solution)/shard_map/reduce_scatter | solution.py:320
  1934.2 262.6 %reduce-scatter.24.cloned.1.call-start = ((), (), s32[]{:S(2)}) async-start(), calls=%async_computation.23 | async-start | bytes 4718592 | tf_op jit(solution)/shard_map/reduce_scatter | solution.py:319
  1945.0 343.7 %reduce-scatter.22.cloned.1.call-start = ((), (), s32[]{:S(2)}) async-start(), calls=%async_computation.22 | async-start | bytes 4718592 | tf_op jit(solution)/shard_map/reduce_scatter | solution.py:318
  1955.6 401.1 %reduce-scatter.20.cloned.1.call-start = ((), (), s32[]{:S(2)}) async-start(), calls=%async_computation.21 | async-start | bytes 1179648 | tf_op jit(solution)/shard_map/reduce_scatter | solution.py:316
  2013.9 342.7 %copy-start.1 = (bf16[1,1024,1024]{2,1,0:T(8,128)(2,1)S(1)}, bf16[1,1024,1024]{2,1,0:T(8,128)(2,1)}, u32[]{:S(2)}) copy-start(bf16[1,1024,1024]{2,1,0:T(8,128)(2,1)} %param.30) | copy-start | bytes 6291460
  (86 other events, 1898.2 us)
Sparse Core Ops, SparseCore 0:
  9.6 43.1 all-gather.3
  272.2 85.2 reduce-scatter.11
  361.6 70.1 all-gather.5
  686.3 40.8 all-gather.7
  1356.7 101.2 all-reduce.2
  1461.1 62.0 reduce-scatter.27
  1526.0 50.3 reduce-scatter.13
  1918.4 74.8 reduce-scatter.17
  1995.8 51.3 reduce-scatter.15
  2051.1 53.5 reduce-scatter.25
  2109.3 87.5 reduce-scatter.23
  2200.9 87.7 reduce-scatter.21
  2293.1 63.5 reduce-scatter.19
where the time goes:
time: 2370 us; the launch traced here: 2360 us
  waiting for transfers between devices  825 us (35%)
  matrix products  585 us (25%)
  blocking collectives  399 us (17%)
  other arithmetic  293 us (12%)
  local copies, waits for them, and re-layouts  217 us (9%)
    all_to_all x2, blocking collectives, to_owners(): lax.all_to_all(outgoing, 'expert', split_axis=0, concat_axis=0, tiled=True)  331 us
    all_to_all x2, waiting for transfers between devices, to_sources(): lax.all_to_all(parts.astype(jnp.bfloat16), 'expert', split_axis=0, concat...  266 us
    convert_element_type x5, other arithmetic, attend_back(): grad_scores = (weights * (grad_weights - inner)).astype(jnp.bfloat16)  102 us
    reduce_scatter x1, waiting for transfers between devices, per_device(): lax.psum_scatter(grad_down, 'expert', scatter_dimension=1, tiled=True)  92.2 us
    reduce_scatter x1, waiting for transfers between devices, per_device(): lax.psum_scatter(grad_up, 'expert', scatter_dimension=0, tiled=True)  91.9 us
    reduce_scatter x1, waiting for transfers between devices, per_device(): lax.psum_scatter(jnp.dot(attended, w_out, preferred_element_type=jnp.floa...  85 us
    psum x1, waiting for transfers between devices, per_device(): lax.psum(grad_normed_two.astype(jnp.bfloat16), 'tensor').astype(jnp.float32)  79.9 us
    dot_general x5, matrix products, attend_back(): jnp.einsum('qhd,khd->hqk', grad_block, values, preferred_element_type=jnp...  75.3 us
  transfers between devices with their start and end apart: 15, of which 10 were waited for; matrix products, arithmetic and copies ran while one was open for 28% of the time, Pallas kernels for 0%

commit v1 on v0

--- a/solution.py
+++ b/solution.py
@@ -1,18 +1,25 @@
+import functools
+
 import jax
 import jax.numpy as jnp
 from jax import lax
+from jax.experimental import pallas as pl
+from jax.experimental.pallas import tpu as pltpu
 from jax.sharding import PartitionSpec as P
 
 HEAD_DIM = 64
 TRUNK = 1024
 SEG = 128
 SEGS = 13
-QBLK = 512
 TREE_LEN = 2560
-
-
+BRANCHES = 4
+FAMILY = 3 * SEG
+QROWS = 256
+PAIR = 2 * HEAD_DIM
+NEGATIVE_FILL = -1e30
+F32 = jnp.float32
+BF16 = jnp.bfloat16
 EPSILON = 1e-05
-NEGATIVE_FILL = -1e30
 
 
 def norm_parts(values):
@@ -41,46 +48,288 @@
     )
 
 
-def segment_of(position):
-    return jnp.where(position < TRUNK, 0, 1 + (position - TRUNK) // SEG)
-
-
-def path_mask(parents_row, query_pos, key_pos):
-    seg_ids = jnp.arange(SEGS, dtype=jnp.int32)
-    query_seg = segment_of(query_pos)
-    key_seg = segment_of(key_pos)
-    parent_seg = jnp.sum(
-        jnp.where(query_seg[:, None] == seg_ids[None, :], parents_row[None, :], 0), axis=1
-    )
-    grand_seg = jnp.sum(
-        jnp.where(parent_seg[:, None] == seg_ids[None, :], parents_row[None, :], 0), axis=1
-    )
-    on_path = (
-        (key_seg[None, :] == query_seg[:, None])
-        | (key_seg[None, :] == parent_seg[:, None])
-        | (key_seg[None, :] == grand_seg[:, None])
-    )
-    return on_path & (key_pos[None, :] <= query_pos[:, None])
-
-
-def block_inputs(qkv_rows, parents, block_index):
-    row_start = block_index * QBLK
-    tree_index = row_start // TREE_LEN
-    queries = lax.dynamic_slice_in_dim(qkv_rows[0], row_start, QBLK, 0).reshape(QBLK, -1, HEAD_DIM)
-    key_rows = qkv_rows[1].reshape(TREE_LEN, -1, HEAD_DIM)
-    values = qkv_rows[2].reshape(TREE_LEN, -1, HEAD_DIM)
-    parents_row = lax.dynamic_index_in_dim(parents, tree_index, 0, keepdims=False)
-    raw_scores = jnp.einsum(
-        "qhd,khd->hqk", queries, key_rows, preferred_element_type=jnp.float32
-    ) * HEAD_DIM ** (-0.5)
-    first_row = row_start - tree_index * TREE_LEN
-    allowed = path_mask(
-        parents_row,
-        first_row + jnp.arange(QBLK, dtype=jnp.int32),
-        jnp.arange(TREE_LEN, dtype=jnp.int32),
-    )
-    scores = jnp.where(allowed[None], raw_scores, NEGATIVE_FILL)
-    return (row_start, tree_index, queries, key_rows, values, scores)
+def dot_nn(a, b):
+    return lax.dot_general(a, b, (((1,), (0,)), ((), ())), preferred_element_type=F32)
+
+
+def dot_nt(a, b):
+    return lax.dot_general(a, b, (((1,), (1,)), ((), ())), preferred_element_type=F32)
+
+
+def head_lanes(rows, head):
+    lane = lax.broadcasted_iota(jnp.int32, rows.shape, 1)
+    return jnp.where(lane // HEAD_DIM == head, rows, jnp.zeros_like(rows))
+
+
+def causal(scores):
+    key = lax.broadcasted_iota(jnp.int32, scores.shape, 0)
+    query = lax.broadcasted_iota(jnp.int32, scores.shape, 1)
+    return jnp.where(key <= query, scores, NEGATIVE_FILL)
+
+
+def family_rows(leaves_ref, branch):
+    def start(segment):
+        return pl.multiple_of(TRUNK + (segment - 1) * SEG, SEG)
+
+    return [start(branch + 1), start(leaves_ref[2 * branch]), start(leaves_ref[2 * branch + 1])]
+
+
+def transpose_into(target_ref, source_ref, part):
+    for first in range(0, TREE_LEN, 512):
+        piece = source_ref[part, pl.ds(first, 512), :].astype(F32)
+        target_ref[:, pl.ds(first, 512)] = piece.T.astype(BF16)
+
+
+def widen(piece, first, width, fill):
+    parts = []
+    if first:
+        parts.append(jnp.full((piece.shape[0], first), fill, piece.dtype))
+    parts.append(piece)
+    rest = width - first - piece.shape[1]
+    if rest:
+        parts.append(jnp.full((piece.shape[0], rest), fill, piece.dtype))
+    return parts[0] if len(parts) == 1 else jnp.concatenate(parts, axis=1)
+
+
+def trunk_groups(block):
+    first = block * QROWS
+    groups = [(0, first, 0, QROWS, None)] if first else []
+    return groups + [(first, QROWS, 0, QROWS, "causal")]
+
+
+def family_groups(starts):
+    return [
+        (0, TRUNK, 0, FAMILY, None),
+        (starts[0], SEG, 0, FAMILY, "branch"),
+        (starts[1], SEG, SEG, 2 * SEG, "causal"),
+        (starts[2], SEG, 2 * SEG, FAMILY, "causal"),
+    ]
+
+
+def masked_scores(keys, queries, rule):
+    scores = dot_nt(keys, queries)
+    if rule == "causal":
+        return causal(scores)
+    if rule == "branch":
+        return jnp.concatenate([causal(scores[:, :SEG]), scores[:, SEG:]], axis=1)
+    return scores
+
+
+def forward_block(qkv_ref, values_t_ref, queries, groups):
+    width = queries.shape[0]
+    outs, logs = [], []
+    for head in range(2):
+        own = head_lanes(queries, head)
+        all_scores = [
+            masked_scores(qkv_ref[1, pl.ds(start, size), :], own[first:last], rule)
+            for start, size, first, last, rule in groups
+        ]
+        top = functools.reduce(
+            jnp.maximum,
+            [
+                widen(jnp.max(s, axis=0, keepdims=True), first, width, NEGATIVE_FILL)
+                for s, (_, _, first, last, _) in zip(all_scores, groups)
+            ],
+        )
+        total, output = None, None
+        for s, (start, size, first, last, _) in zip(all_scores, groups):
+            weights = jnp.exp(s - top[:, first:last])
+            part = widen(jnp.sum(weights, axis=0, keepdims=True), first, width, 0.0)
+            values_t = values_t_ref[pl.ds(head * HEAD_DIM, HEAD_DIM), pl.ds(start, size)]
+            mixed = widen(dot_nn(values_t, weights.astype(BF16)), first, width, 0.0)
+            total = part if total is None else total + part
+            output = mixed if output is None else output + mixed
+        outs.append(output / total)
+        logs.append(top + jnp.log(total))
+    return jnp.concatenate(outs, axis=0).T.astype(BF16), jnp.concatenate(logs, axis=0)
+
+
+def scaled_queries(qkv_ref, starts, size):
+    rows = [qkv_ref[0, pl.ds(start, size), :] for start in starts]
+    rows = rows[0] if len(rows) == 1 else jnp.concatenate(rows, axis=0)
+    return rows * jnp.asarray(HEAD_DIM ** (-0.5), BF16)
+
+
+def forward_kernel(leaves_ref, qkv_ref, out_ref, trunk_log_ref, family_log_ref, values_t_ref):
+    transpose_into(values_t_ref, qkv_ref, 2)
+    for block in range(TRUNK // QROWS):
+        first = block * QROWS
+        queries = scaled_queries(qkv_ref, [first], QROWS)
+        out, logs = forward_block(qkv_ref, values_t_ref, queries, trunk_groups(block))
+        out_ref[pl.ds(first, QROWS), :] = out
+        trunk_log_ref[0, :, pl.ds(first, QROWS)] = logs
+
+    def one_family(branch, carry):
+        starts = family_rows(leaves_ref, branch)
+        queries = scaled_queries(qkv_ref, starts, SEG)
+        out, logs = forward_block(qkv_ref, values_t_ref, queries, family_groups(starts))
+        for place, start in enumerate(starts):
+            out_ref[pl.ds(start, SEG), :] = out[place * SEG : (place + 1) * SEG]
+        family_log_ref[0, branch] = logs
+        return carry
+
+    lax.fori_loop(0, BRANCHES, one_family, 0)
+
+
+def attention_forward(leaves, qkv_rows):
+    width = qkv_rows.shape[2]
+    pairs = width // PAIR
+    return pl.pallas_call(
+        forward_kernel,
+        grid_spec=pltpu.PrefetchScalarGridSpec(
+            num_scalar_prefetch=1,
+            grid=(pairs,),
+            in_specs=[pl.BlockSpec((3, TREE_LEN, PAIR), lambda p, leaves: (0, 0, p))],
+            out_specs=[
+                pl.BlockSpec((TREE_LEN, PAIR), lambda p, leaves: (0, p)),
+                pl.BlockSpec((1, 2, TRUNK), lambda p, leaves: (p, 0, 0)),
+                pl.BlockSpec((1, BRANCHES, 2, FAMILY), lambda p, leaves: (p, 0, 0, 0)),
+            ],
+            scratch_shapes=[pltpu.VMEM((PAIR, TREE_LEN), BF16)],
+        ),
+        out_shape=[
+            jax.ShapeDtypeStruct((TREE_LEN, width), BF16),
+            jax.ShapeDtypeStruct((pairs, 2, TRUNK), F32),
+            jax.ShapeDtypeStruct((pairs, BRANCHES, 2, FAMILY), F32),
+        ],
+        name="tree_attention",
+    )(leaves, qkv_rows)
+
+
+def backward_block(qkv_ref, keys_t_ref, queries, grads, outs, logs, groups):
+    products = grads.astype(F32) * outs.astype(F32)
+    products_t = products.T
+    key_ds = [[] for _ in groups]
+    value_ws = [[] for _ in groups]
+    own_q, own_g, query_grads = [], [], []
+    for head in range(2):
+        own = head_lanes(queries, head)
+        own_grads = head_lanes(grads, head)
+        own_q.append(own)
+        own_g.append(own_grads)
+        inner = jnp.sum(
+            products_t[head * HEAD_DIM : (head + 1) * HEAD_DIM], axis=0, keepdims=True
+        )
+        log = logs[head : head + 1]
+        query_grad = None
+        for place, (start, size, first, last, rule) in enumerate(groups):
+            scores = masked_scores(qkv_ref[1, pl.ds(start, size), :], own[first:last], rule)
+            weights = jnp.exp(scores - log[:, first:last])
+            grad_weights = dot_nt(qkv_ref[2, pl.ds(start, size), :], own_grads[first:last])
+            grad_scores = (weights * (grad_weights - inner[:, first:last])).astype(BF16)
+            keys_t = keys_t_ref[pl.ds(head * HEAD_DIM, HEAD_DIM), pl.ds(start, size)]
+            part = widen(dot_nn(keys_t, grad_scores), first, queries.shape[0], 0.0)
+            query_grad = part if query_grad is None else query_grad + part
+            key_ds[place].append(grad_scores)
+            value_ws[place].append(weights.astype(BF16))
+        query_grads.append(query_grad)
+    grad_query = (jnp.concatenate(query_grads, axis=0) * HEAD_DIM ** (-0.5)).T.astype(BF16)
+    key_grads, value_grads = [], []
+    for place, (start, size, first, last, rule) in enumerate(groups):
+        stacked_q = jnp.concatenate([own_q[0][first:last], own_q[1][first:last]], axis=0)
+        stacked_g = jnp.concatenate([own_g[0][first:last], own_g[1][first:last]], axis=0)
+        key_grads.append(dot_nn(jnp.concatenate(key_ds[place], axis=1), stacked_q))
+        value_grads.append(dot_nn(jnp.concatenate(value_ws[place], axis=1), stacked_g))
+    return grad_query, key_grads, value_grads
+
+
+def backward_kernel(
+    leaves_ref,
+    qkv_ref,
+    grads_ref,
+    outs_ref,
+    trunk_log_ref,
+    family_log_ref,
+    result_ref,
+    keys_t_ref,
+    trunk_keys_ref,
+    trunk_values_ref,
+):
+    transpose_into(keys_t_ref, qkv_ref, 1)
+    trunk_keys_ref[...] = jnp.zeros_like(trunk_keys_ref)
+    trunk_values_ref[...] = jnp.zeros_like(trunk_values_ref)
+    for block in range(TRUNK // QROWS):
+        first = block * QROWS
+        rows = pl.ds(first, QROWS)
+        groups = trunk_groups(block)
+        grad_query, key_grads, value_grads = backward_block(
+            qkv_ref,
+            keys_t_ref,
+            scaled_queries(qkv_ref, [first], QROWS),
+            grads_ref[rows, :],
+            outs_ref[rows, :],
+            trunk_log_ref[0, :, rows],
+            groups,
+        )
+        result_ref[0, rows, :] = grad_query
+        for (start, size, _, _, _), key_grad, value_grad in zip(groups, key_grads, value_grads):
+            trunk_keys_ref[pl.ds(start, size), :] += key_grad
+            trunk_values_ref[pl.ds(start, size), :] += value_grad
+
+    def one_family(branch, carry):
+        starts = family_rows(leaves_ref, branch)
+        groups = family_groups(starts)
+        grad_query, key_grads, value_grads = backward_block(
+            qkv_ref,
+            keys_t_ref,
+            scaled_queries(qkv_ref, starts, SEG),
+            jnp.concatenate([grads_ref[pl.ds(start, SEG), :] for start in starts], axis=0),
+            jnp.concatenate([outs_ref[pl.ds(start, SEG), :] for start in starts], axis=0),
+            family_log_ref[0, branch],
+            groups,
+        )
+        trunk_keys_ref[...] += key_grads[0]
+        trunk_values_ref[...] += value_grads[0]
+        for place, start in enumerate(starts):
+            rows = pl.ds(start, SEG)
+            result_ref[0, rows, :] = grad_query[place * SEG : (place + 1) * SEG]
+            result_ref[1, rows, :] = key_grads[1 + place].astype(BF16)
+            result_ref[2, rows, :] = value_grads[1 + place].astype(BF16)
+        return carry
+
+    lax.fori_loop(0, BRANCHES, one_family, 0)
+    result_ref[1, pl.ds(0, TRUNK), :] = trunk_keys_ref[...].astype(BF16)
+    result_ref[2, pl.ds(0, TRUNK), :] = trunk_values_ref[...].astype(BF16)
+
+
+def attention_backward(leaves, qkv_rows, grads, outs, trunk_log, family_log):
+    width = qkv_rows.shape[2]
+    pairs = width // PAIR
+    whole = pl.BlockSpec((3, TREE_LEN, PAIR), lambda p, leaves: (0, 0, p))
+    rows = pl.BlockSpec((TREE_LEN, PAIR), lambda p, leaves: (0, p))
+    return pl.pallas_call(
+        backward_kernel,
+        grid_spec=pltpu.PrefetchScalarGridSpec(
+            num_scalar_prefetch=1,
+            grid=(pairs,),
+            in_specs=[
+                whole,
+                rows,
+                rows,
+                pl.BlockSpec((1, 2, TRUNK), lambda p, leaves: (p, 0, 0)),
+                pl.BlockSpec((1, BRANCHES, 2, FAMILY), lambda p, leaves: (p, 0, 0, 0)),
+            ],
+            out_specs=whole,
+            scratch_shapes=[
+                pltpu.VMEM((PAIR, TREE_LEN), BF16),
+                pltpu.VMEM((TRUNK, PAIR), F32),
+                pltpu.VMEM((TRUNK, PAIR), F32),
+            ],
+        ),
+        out_shape=jax.ShapeDtypeStruct(qkv_rows.shape, BF16),
+        name="tree_attention_back",
+    )(leaves, qkv_rows, grads, outs, trunk_log, family_log)
+
+
+def leaf_order(parents_row):
+    first_leaf = BRANCHES + 1
+    leaf_parents = parents_row[first_leaf:]
+    segments = first_leaf + jnp.arange(leaf_parents.shape[0], dtype=jnp.int32)
+    same = leaf_parents[:, None] == leaf_parents[None, :]
+    later = segments[None, :] < segments[:, None]
+    place = 2 * (leaf_parents - 1) + jnp.sum(jnp.where(same & later, 1, 0), axis=1)
+    slots = jnp.arange(2 * BRANCHES, dtype=jnp.int32)
+    return jnp.sum(jnp.where(slots[:, None] == place[None, :], segments[None, :], 0), axis=1)
 
 
 def to_owners(values, expert_ids, quarter, slot_index, experts, quarters, capacity):
@@ -119,7 +368,6 @@
     group_rows = tok_dev * quarters
     experts = w_router.shape[1]
     capacity = max(2, tok_dev * 7 // (5 * experts))
-    block_total = group_rows // QBLK
     gathered = lax.all_gather(tokens, "tensor", axis=0, tiled=True)
     scaled_one, inverse_one = norm_parts(gathered.astype(jnp.float32))
     normed_one = (scaled_one * ln_attn).astype(jnp.bfloat16)
@@ -127,22 +375,8 @@
         "td,sdc->stc", normed_one, w_qkv, preferred_element_type=jnp.float32
     ).astype(jnp.bfloat16)
 
-    def attend_block(block_index):
-        row_start, tree_index, queries, key_rows, values, scores = block_inputs(
-            qkv_rows, parents, block_index
-        )
-        row_max = jnp.max(scores, axis=-1, keepdims=True)
-        weights = jnp.exp(scores - row_max)
-        row_total = jnp.sum(weights, axis=-1, keepdims=True)
-        weights = (weights / row_total).astype(jnp.bfloat16)
-        output = jnp.einsum("hqk,khd->qhd", weights, values, preferred_element_type=jnp.float32)
-        return (
-            output.reshape(QBLK, -1).astype(jnp.bfloat16),
-            (row_max + jnp.log(row_total))[..., 0],
-        )
-
-    attended, log_total = lax.map(attend_block, jnp.arange(block_total, dtype=jnp.int32))
-    attended = attended.reshape(group_rows, -1)
+    leaves = leaf_order(parents[0])
+    attended, trunk_log, family_log = attention_forward(leaves, qkv_rows)
     residual = tokens.astype(jnp.float32) + lax.psum_scatter(
         jnp.dot(attended, w_out, preferred_element_type=jnp.float32),
         "tensor",
@@ -255,47 +489,8 @@
         "gd,cd->gc", grad_branch, w_out, preferred_element_type=jnp.float32
     ).astype(jnp.bfloat16)
 
-    def attend_back(carried, block_index):
-        grad_keys, grad_values = carried
-        row_start, tree_index, queries, key_rows, values, scores = block_inputs(
-            qkv_rows, parents, block_index
-        )
-        log_block = lax.dynamic_index_in_dim(log_total, block_index, 0, keepdims=False)
-        weights = jnp.exp(scores - log_block[..., None])
-        grad_block = lax.dynamic_slice_in_dim(grad_attended, row_start, QBLK, 0).reshape(
-            QBLK, -1, HEAD_DIM
-        )
-        grad_weights = jnp.einsum(
-            "qhd,khd->hqk", grad_block, values, preferred_element_type=jnp.float32
-        )
-        inner = jnp.sum(weights * grad_weights, axis=-1, keepdims=True)
-        grad_scores = (weights * (grad_weights - inner)).astype(jnp.bfloat16)
-        grad_query = jnp.einsum(
-            "hqk,khd->qhd", grad_scores, key_rows, preferred_element_type=jnp.float32
-        ) * HEAD_DIM ** (-0.5)
-        key_part = jnp.einsum(
-            "hqk,qhd->khd", grad_scores, queries, preferred_element_type=jnp.float32
-        ) * HEAD_DIM ** (-0.5)
-        value_part = jnp.einsum(
-            "hqk,qhd->khd",
-            weights.astype(jnp.bfloat16),
-            grad_block,
-            preferred_element_type=jnp.float32,
-        )
-        grad_keys = grad_keys + key_part.reshape(TREE_LEN, -1)
-        grad_values = grad_values + value_part.reshape(TREE_LEN, -1)
-        return ((grad_keys, grad_values), grad_query.reshape(QBLK, -1).astype(jnp.bfloat16))
-
-    empty_rows = jnp.zeros((group_rows, qkv_rows.shape[2]), jnp.float32)
-    (grad_keys, grad_values), grad_queries = lax.scan(
-        attend_back, (empty_rows, empty_rows), jnp.arange(block_total, dtype=jnp.int32)
-    )
-    grad_qkv_rows = jnp.stack(
-        [
-            grad_queries.reshape(group_rows, -1),
-            grad_keys.astype(jnp.bfloat16),
-            grad_values.astype(jnp.bfloat16),
-        ]
+    grad_qkv_rows = attention_backward(
+        leaves, qkv_rows, grad_attended, attended, trunk_log, family_log
     )
     grad_w_qkv = jnp.einsum(
         "gd,sgc->sdc", normed_one, grad_qkv_rows, preferred_element_type=jnp.float32

time: 2370 us -> 1860 us (0.78)
  matrix products: 585 us -> 265 us
  other arithmetic: 293 us -> 142 us
  local copies, waits for them, and re-layouts: 217 us -> 96.9 us
  Pallas kernels: 0 us -> 64.8 us
  waiting for transfers between devices: 825 us -> 857 us
    dot_general x35 -> x0, matrix products: 320 us -> none  [the longest x5 75.3 us: attend_back(): jnp.einsum('qhd,khd->hqk', grad_block, values, preferred_element_type=jnp...]
    convert_element_type x5 -> x0, other arithmetic: 102 us -> none  [attend_back(): grad_scores = (weights * (grad_weights - inner)).astype(jnp.bfloat16)]
    pallas_call x0 -> x2, Pallas kernels: none -> 64.8 us  [the longest x1 40.1 us: attention_backward(): pl.pallas_call(backward_kernel, grid_spec=pltpu.PrefetchScalarGridSpec(nu...]
    while x73 -> x0, local copies, waits for them, and re-layouts: 60.7 us -> none
    reduce_sum x25 -> x2, other arithmetic: 30.5 us -> 0.81 us  [the longest x1 0.63 us: leaf_order(): jnp.sum(jnp.where(slots[:, None] == place[None, :], segments[None, :], 0)...]
    slice x12 -> x2, local copies, waits for them, and re-layouts: 29.4 us -> 0.26 us  [the longest x10 29.2 us: block_inputs(): key_rows = qkv_rows[1].reshape(TREE_LEN, -1, HEAD_DIM)]
    reduce_scatter x1, waiting for transfers between devices: 0.01 us -> 26.4 us  [per_device(): lax.psum_scatter(grad_normed_one.astype(jnp.bfloat16), 'tensor', scatter_...]
  transfers between devices with their start and end apart: 15 -> 15, of which waited for: 10 -> 12; matrix products, arithmetic and copies ran while one was open for 28% -> 15% of each run, Pallas kernels for 0% -> 2%
where the time goes in v1:
time: 1860 us; the launch traced here: 1850 us
  waiting for transfers between devices  857 us (46%)
  blocking collectives  399 us (21%)
  matrix products  265 us (14%)
  other arithmetic  142 us (8%)
  local copies, waits for them, and re-layouts  96.9 us (5%)
  Pallas kernels  64.8 us (3%)
    all_to_all x2, blocking collectives, to_owners(): lax.all_to_all(outgoing, 'expert', split_axis=0, concat_axis=0, tiled=True)  331 us
    all_to_all x2, waiting for transfers between devices, to_sources(): lax.all_to_all(parts.astype(jnp.bfloat16), 'expert', split_axis=0, concat...  257 us
    reduce_scatter x1, waiting for transfers between devices, per_device(): lax.psum_scatter(grad_down, 'expert', scatter_dimension=1, tiled=True)  92.2 us
    reduce_scatter x1, waiting for transfers between devices, per_device(): lax.psum_scatter(grad_up, 'expert', scatter_dimension=0, tiled=True)  91.7 us
    reduce_scatter x1, waiting for transfers between devices, per_device(): lax.psum_scatter(jnp.dot(attended, w_out, preferred_element_type=jnp.floa...  85.2 us
    psum x1, waiting for transfers between devices, per_device(): lax.psum(grad_normed_two.astype(jnp.bfloat16), 'tensor').astype(jnp.float32)  80 us
    reduce_scatter x1, waiting for transfers between devices, per_device(): lax.psum_scatter(grad_w_out, 'expert', scatter_dimension=1, tiled=True)  68.1 us
    all_gather x1, waiting for transfers between devices, per_device(): residual_all = lax.all_gather(residual, 'tensor', axis=0, tiled=True)  63.2 us
  transfers between devices with their start and end apart: 15, of which 12 were waited for; matrix products, arithmetic and copies ran while one was open for 15% of the time, Pallas kernels for 2%

profile of v1, /device:TPU:0, one launch (start us, length us, event | category | flops | bytes accessed | tf_op | source)
XLA Modules:
  0.0 1851.7 jit_solution(8950847674511473575)
XLA Ops:
  10.3 42.5 %all-gather.4.cloned.1.call-done = bf16[2560,1024]{1,0:T(8,128)(2,1)} async-done(((bf16[640,1024]{1,0:T(8,128)(2,1)}), bf16[2560,1024]{1,0:T(8,128)(2,1)}) %all-gather.4.cloned.1.call-update) | async-done | bytes 5242896 | tf_op jit(solution)/shard_map/all_gather | solution.py:371
  67.4 24.7 %tree_attention.1 = (bf16[2560,256]{1,0:T(8,128)(2,1)}, f32[2,2,1024]{2,1,0:T(2,128)}, f32[2,4,2,384]{3,2,1,0:T(2,128)}) custom-call(s32[8]{0:T(128)} %select_reduce_fusion.1.leaves_ref, bf16[3,2560,256]{2,1,0:T(8,128)(2,1)} %fusion.44.qkv_ref), custom_call_target="tpu_custom_call" | custom-call | tf_op jit(solution)/shard_map/tree_attention/pallas_call | solution.py:177
  99.5 85.2 %reduce-scatter.12.cloned.1.call-done = f32[640,1024]{1,0:T(8,128)} async-done(((f32[2560,1024]{1,0:T(8,128)}), f32[640,1024]{1,0:T(8,128)}) %reduce-scatter.12.cloned.1.call-update) | async-done | bytes 2621456 | tf_op jit(solution)/shard_map/reduce_scatter | solution.py:380
  195.7 63.2 %all-gather.6.cloned.1.call-done = f32[2560,1024]{1,0:T(8,128)} async-done(((f32[640,1024]{1,0:T(8,128)}), f32[2560,1024]{1,0:T(8,128)}) %all-gather.6.cloned.1.call-update) | async-done | bytes 10485776 | tf_op jit(solution)/shard_map/all_gather | solution.py:386
  268.7 18.1 scatter_custom_fusion
  286.8 166.5 %all_to_all.20 = bf16[8,4,112,1024]{3,2,1,0:T(8,128)(2,1)S(1)} all-to-all(bf16[8,4,112,1024]{3,2,1,0:T(8,128)(2,1)} %bitcast.106), channel_id=1, replica_groups=mesh['expert'=8,'tensor'=4] {'expert'}, dimensions={0} | all-to-all | bytes 14680064 | tf_op jit(solution)/shard_map/all_to_all | solution.py:339
  453.3 40.2 %fusion.2 = (bf16[3584,1024]{1,0:T(8,128)(2,1)S(1)}, f32[3584,1024]{1,0:T(8,128)}) fusion(bf16[3584,1024]{1,0:T(8,128)(2,1)S(1)} %bitcast.108, bf16[1,1024,1024]{2,1,0:T(8,128)(2,1)S(1)} %copy-done), kind=kOutput, calls=%fused_computation.15 | convolution fusion | flops 7754743808 | bytes 31457280 | tf_op jit(solution)/shard_map/dot_general | solution.py:407
  530.4 29.8 %fusion.21 = (bf16[2560,1024]{1,0:T(8,128)(2,1)}, f32[2560,1024]{1,0:T(8,128)}) fusion(bf16[2560,1024]{1,0:T(8,128)(2,1)S(1)} %multiply_convert_fusion, bf16[1024,1024]{1,0:T(8,128)(2,1)S(1)} %copy-done.40), kind=kOutput, calls=%fused_computation.44 | convolution fusion | flops 5539102720 | bytes 23068672 | tf_op jit(solution)/shard_map/dot_general | solution.py:389
  560.2 110.8 %all-to-all-done.1 = bf16[8,4,112,1024]{3,2,1,0:T(8,128)(2,1)} async-done(((bf16[8,4,112,1024]{3,2,1,0:T(8,128)(2,1)}), bf16[8,4,112,1024]{3,2,1,0:T(8,128)(2,1)}, u32[]{:S(2)}, u32[]{:S(2)}) %all-to-all-start.1) | async-done | bytes 7340064 | tf_op jit(solution)/shard_map/all_to_all | solution.py:343
  681.2 40.0 %gather_fusion = f32[2560,1024]{1,0:T(8,128)} fusion(f32[8,4,112,1024]{3,2,1,0:T(8,128)} %convert_element_type.103, s32[2560]{0:T(1024)S(1)} %copy-done.1), kind=kCustom, calls=%fused_computation | custom fusion | bytes 21002240 | tf_op jit(solution)/shard_map/gather | solution.py:414
  746.9 17.8 scatter_custom_fusion.1
  764.7 164.2 %all_to_all.21 = bf16[8,4,112,1024]{3,2,1,0:T(8,128)(2,1)S(1)} all-to-all(bf16[8,4,112,1024]{3,2,1,0:T(8,128)(2,1)} %bitcast.107), channel_id=1, replica_groups=mesh['expert'=8,'tensor'=4] {'expert'}, dimensions={0} | all-to-all | bytes 14680064 | tf_op jit(solution)/shard_map/all_to_all | solution.py:339
  928.8 15.5 fusion.8
  975.9 145.8 %all-to-all-done.3 = bf16[8,4,112,1024]{3,2,1,0:T(8,128)(2,1)} async-done(((bf16[8,4,112,1024]{3,2,1,0:T(8,128)(2,1)}), bf16[8,4,112,1024]{3,2,1,0:T(8,128)(2,1)}, u32[]{:S(2)}, u32[]{:S(2)}) %all-to-all-start.3) | async-done | bytes 7340064 | tf_op jit(solution)/shard_map/all_to_all | solution.py:343
  1131.9 40.0 %gather_fusion.1 = f32[2560,1024]{1,0:T(8,128)} fusion(f32[8,4,112,1024]{3,2,1,0:T(8,128)} %convert_element_type.113, s32[2560]{0:T(1024)S(1)} %copy-done.1), kind=kCustom, calls=%fused_computation.1 | custom fusion | bytes 21002240 | tf_op jit(solution)/shard_map/gather | solution.py:456
  1205.0 80.0 %all-reduce.3.cloned.1.call-done = bf16[2560,1024]{1,0:T(8,128)(2,1)} async-done(((bf16[2560,1024]{1,0:T(8,128)(2,1)}), bf16[2560,1024]{1,0:T(8,128)(2,1)}) %all-reduce.3.cloned.1.call-update) | async-done | bytes 5242896 | tf_op jit(solution)/shard_map/psum | solution.py:460
  1311.0 40.1 %tree_attention_back.1 = bf16[3,2560,256]{2,1,0:T(8,128)(2,1)} custom-call(s32[8]{0:T(128)} %select_reduce_fusion.1.leaves_ref, bf16[3,2560,256]{2,1,0:T(8,128)(2,1)} %fusion.44.qkv_ref, bf16[2560,256]{1,0:T(8,128)(2,1)} %convolution_convert_fusion.3.grads_ref, bf16[2560,256]{1,0:T(8,128)(2,1)} %get-tuple-element.15.outs_ref, ...), custom_call_target="tpu_custom_call" | custom-call | tf_op jit(solution)/shard_map/tree_attention_back/pallas_call | solution.py:300
  1437.1 21.7 %all-reduce = f32[1024]{0:T(1024)S(1)} all-reduce(f32[1024]{0:T(1024)S(1)} %get-tuple-element.66), channel_id=7, replica_groups=mesh['expert'=8,'tensor'=4] {'expert'}, use_global_device_ids=true, to_apply=%region_33.34.clone | all-reduce | flops 1024 | bytes 8192
  1470.4 36.8 %psum.23 = f32[1024]{0:T(1024)} all-reduce(f32[1024]{0:T(1024)S(1)} %get-tuple-element.79), channel_id=1, replica_groups=mesh['expert'=8,'tensor'=4] {'expert','tensor'}, use_global_device_ids=true, to_apply=%region_29.30 | all-reduce | flops 1024 | bytes 8192 | tf_op jit(solution)/shard_map/psum | solution.py:518
  1509.1 26.4 %reduce-scatter.16.cloned.1.call-done = bf16[640,1024]{1,0:T(8,128)(2,1)} async-done(((bf16[2560,1024]{1,0:T(8,128)(2,1)}), bf16[640,1024]{1,0:T(8,128)(2,1)}) %reduce-scatter.16.cloned.1.call-update) | async-done | bytes 1310736 | tf_op jit(solution)/shard_map/reduce_scatter | solution.py:502
  1543.3 49.6 %reduce-scatter.26.cloned.1.call-done = f32[128,8]{0,1:T(8,128)} async-done(((f32[1024,8]{0,1:T(8,128)}), f32[128,8]{0,1:T(8,128)}) %reduce-scatter.26.cloned.1.call-update) | async-done | bytes 4112 | tf_op jit(solution)/shard_map/reduce_scatter | solution.py:515
  1592.9 92.2 %reduce-scatter.24.cloned.1.call-done = f32[1024,128]{1,0:T(8,128)} async-done(((f32[1024,1024]{1,0:T(8,128)}), f32[1024,128]{1,0:T(8,128)}) %reduce-scatter.24.cloned.1.call-update) | async-done | bytes 524304 | tf_op jit(solution)/shard_map/reduce_scatter | solution.py:514
  1685.1 91.7 %reduce-scatter.22.cloned.1.call-done = f32[128,1024]{1,0:T(8,128)} async-done(((f32[1024,1024]{1,0:T(8,128)}), f32[128,1024]{1,0:T(8,128)}) %reduce-scatter.22.cloned.1.call-update) | async-done | bytes 524304 | tf_op jit(solution)/shard_map/reduce_scatter | solution.py:513
  1776.8 68.1 %reduce-scatter.20.cloned.1.call-done = f32[256,128]{1,0:T(8,128)} async-done(((f32[256,1024]{1,0:T(8,128)}), f32[256,128]{1,0:T(8,128)}) %reduce-scatter.20.cloned.1.call-update) | async-done | bytes 131088 | tf_op jit(solution)/shard_map/reduce_scatter | solution.py:511
  (211 shorter events, 325.4 us)
Async XLA Ops:
  7.2 446.1 %copy-start = (bf16[1,1024,1024]{2,1,0:T(8,128)(2,1)S(1)}, bf16[1,1024,1024]{2,1,0:T(8,128)(2,1)}, u32[]{:S(2)}) copy-start(bf16[1,1024,1024]{2,1,0:T(8,128)(2,1)} %param.26) | copy-start | bytes 6291460
  7.2 45.6 %all-gather.4.cloned.1.call-start = ((), (), s32[]{:S(2)}) async-start(), calls=%async_computation.13 | async-start | bytes 6553600 | tf_op jit(solution)/shard_map/all_gather | solution.py:371
  7.9 176.7 %reduce-scatter.12.cloned.1.call-start = ((), (), s32[]{:S(2)}) async-start(), calls=%async_computation.14 | async-start | bytes 13107200 | tf_op jit(solution)/shard_map/reduce_scatter | solution.py:380
  92.1 92.5 %copy-start.8 = (bf16[640,1024]{1,0:T(8,128)(2,1)S(1)}, bf16[640,1024]{1,0:T(8,128)(2,1)}, u32[]{:S(2)}) copy-start(bf16[640,1024]{1,0:T(8,128)(2,1)} %param.14) | copy-start | bytes 3932164
  99.2 96.3 %copy-start.37 = (s32[3]{0:T(128)S(1)}, s32[3]{0:T(128)}, u32[]{:S(2)}) copy-start(s32[3]{0:T(128)} %constant.26) | copy-start | bytes 40
  99.2 96.4 %copy-start.36 = (s32[3]{0:T(128)S(1)}, s32[3]{0:T(128)}, u32[]{:S(2)}) copy-start(s32[3]{0:T(128)} %constant.29) | copy-start | bytes 40
  99.2 159.7 %all-gather.6.cloned.1.call-start = ((), (), s32[]{:S(2)}) async-start(), calls=%async_computation.15 | async-start | bytes 13107200 | tf_op jit(solution)/shard_map/all_gather | solution.py:386
  188.6 341.1 %copy-start.16 = (s32[2560]{0:T(1024)}, s32[2560]{0:T(1024)S(1)}, u32[]{:S(2)}) copy-start(s32[2560]{0:T(1024)S(1)} %reduce.6) | copy-start | bytes 30724
  263.5 248.3 %copy-start.12 = (f32[2560]{0:T(1024)}, f32[2560]{0:T(1024)S(1)}, u32[]{:S(2)}) copy-start(f32[2560]{0:T(1024)S(1)} %broadcast_multiply_fusion.2) | copy-start | bytes 30724
  268.7 243.1 %copy-start.14 = (f32[2560]{0:T(1024)}, f32[2560]{0:T(1024)S(1)}, u32[]{:S(2)}) copy-start(f32[2560]{0:T(1024)S(1)} %add_rsqrt_fusion) | copy-start | bytes 30724
  506.3 164.8 %all-to-all-start.1 = ((bf16[8,4,112,1024]{3,2,1,0:T(8,128)(2,1)}), bf16[8,4,112,1024]{3,2,1,0:T(8,128)(2,1)}, u32[]{:S(2)}, u32[]{:S(2)}) async-start(bf16[8,4,112,1024]{3,2,1,0:T(8,128)(2,1)} %convolution_convert_fusion.1), calls=%async_computation.2 | async-start | bytes 14680064 | tf_op jit(solution)/shard_map/all_to_all | solution.py:343
  511.2 210.0 %all-gather.8.cloned.1.call-start = ((), (), s32[]{:S(2)}) async-start(), calls=%async_computation.17 | async-start | bytes 6553600 | tf_op jit(solution)/shard_map/all_gather | solution.py:429
  560.2 121.0 %copy-start.1 = (s32[2560]{0:T(1024)S(1)}, s32[2560]{0:T(1024)}, u32[]{:S(2)}) copy-start(s32[2560]{0:T(1024)} %get-tuple-element.81) | copy-start | bytes 30724
  764.7 164.2 %copy-start.39 = (bf16[1,1024,1024]{2,1,0:T(8,128)(2,1)S(1)}, bf16[1,1024,1024]{2,1,0:T(8,128)(2,1)}, u32[]{:S(2)}) copy-start(bf16[1,1024,1024]{2,1,0:T(8,128)(2,1)} %param.27) | copy-start | bytes 6291460
  957.4 164.3 %all-to-all-start.3 = ((bf16[8,4,112,1024]{3,2,1,0:T(8,128)(2,1)}), bf16[8,4,112,1024]{3,2,1,0:T(8,128)(2,1)}, u32[]{:S(2)}, u32[]{:S(2)}) async-start(bf16[8,4,112,1024]{3,2,1,0:T(8,128)(2,1)} %convolution_convert_fusion), calls=%async_computation.5 | async-start | bytes 14680064 | tf_op jit(solution)/shard_map/all_to_all | solution.py:343
  962.3 322.7 %all-reduce.3.cloned.1.call-start = ((), (), s32[]{:S(2)}) async-start(), calls=%async_computation.18 | async-start | bytes 10485760 | tf_op jit(solution)/shard_map/psum | solution.py:460
  1183.7 218.0 %reduce-scatter.28.cloned.1.call-start = ((), (), s32[]{:S(2)}) async-start(), calls=%async_computation.25 | async-start | bytes 589824
  1188.6 214.8 %reduce-scatter.14.cloned.1.call-start = ((), (), s32[]{:S(2)}) async-start(), calls=%async_computation.16 | async-start | bytes 6553600 | tf_op jit(solution)/shard_map/reduce_scatter | solution.py:418
  1199.1 308.1 %reduce-scatter.18.cloned.1.call-start = ((), (), s32[]{:S(2)}) async-start(), calls=%async_computation.20 | async-start | bytes 3538944 | tf_op jit(solution)/shard_map/reduce_scatter | solution.py:510
  1361.4 174.1 %reduce-scatter.16.cloned.1.call-start = ((), (), s32[]{:S(2)}) async-start(), calls=%async_computation.19 | async-start | bytes 6553600 | tf_op jit(solution)/shard_map/reduce_scatter | solution.py:502
  1374.8 218.1 %reduce-scatter.26.cloned.1.call-start = ((), (), s32[]{:S(2)}) async-start(), calls=%async_computation.24 | async-start | bytes 36864 | tf_op jit(solution)/shard_map/reduce_scatter | solution.py:515
  1378.8 306.3 %reduce-scatter.24.cloned.1.call-start = ((), (), s32[]{:S(2)}) async-start(), calls=%async_computation.23 | async-start | bytes 4718592 | tf_op jit(solution)/shard_map/reduce_scatter | solution.py:514
  1389.5 387.3 %reduce-scatter.22.cloned.1.call-start = ((), (), s32[]{:S(2)}) async-start(), calls=%async_computation.22 | async-start | bytes 4718592 | tf_op jit(solution)/shard_map/reduce_scatter | solution.py:513
  1400.1 444.9 %reduce-scatter.20.cloned.1.call-start = ((), (), s32[]{:S(2)}) async-start(), calls=%async_computation.21 | async-start | bytes 1179648 | tf_op jit(solution)/shard_map/reduce_scatter | solution.py:511
  (39 other events, 1125.7 us)
Sparse Core Ops, SparseCore 0:
  9.6 43.1 all-gather.3
  99.3 85.2 reduce-scatter.11
  188.7 70.1 all-gather.5
  513.3 40.7 all-gather.7
  1183.8 101.1 all-reduce.2
  1288.2 62.0 reduce-scatter.27
  1353.0 50.3 reduce-scatter.13
  1407.1 75.1 reduce-scatter.17
  1484.8 50.6 reduce-scatter.15
  1539.3 53.5 reduce-scatter.25
  1597.5 87.5 reduce-scatter.23
  1689.1 87.6 reduce-scatter.21
  1781.2 63.7 reduce-scatter.19

commit v2 on v1

--- a/solution.py
+++ b/solution.py
@@ -20,32 +20,6 @@
 F32 = jnp.float32
 BF16 = jnp.bfloat16
 EPSILON = 1e-05
-
-
-def norm_parts(values):
-    row_mean = jnp.mean(values, axis=-1, keepdims=True)
-    centred = values - row_mean
-    row_var = jnp.mean(centred * centred, axis=-1, keepdims=True)
-    inverse = lax.rsqrt(row_var + EPSILON)
-    return (centred * inverse, inverse)
-
-
-def norm_back(grad_normed, gain_vec, scaled, inverse):
-    grad_scaled = grad_normed * gain_vec
-    first_mean = jnp.mean(grad_scaled, axis=-1, keepdims=True)
-    second = jnp.mean(grad_scaled * scaled, axis=-1, keepdims=True)
-    return inverse * (grad_scaled - first_mean - scaled * second)
-
-
-def gelu_exact(values):
-    return jax.nn.gelu(values, approximate=False)
-
-
-def gelu_slope(values):
-    return (
-        0.5 * (1.0 + lax.erf(values * 0.7071067811865476))
-        + values * jnp.exp(-0.5 * values * values) * 0.3989422804014327
-    )
 
 
 def dot_nn(a, b):
@@ -332,17 +306,175 @@
     return jnp.sum(jnp.where(slots[:, None] == place[None, :], segments[None, :], 0), axis=1)
 
 
-def to_owners(values, expert_ids, quarter, slot_index, experts, quarters, capacity):
-    width = values.shape[1]
-    outgoing = jnp.zeros((experts, quarters, capacity, width), jnp.bfloat16)
-    outgoing = outgoing.at[expert_ids, quarter, slot_index].set(values)
-    return lax.all_to_all(outgoing, "expert", split_axis=0, concat_axis=0, tiled=True)
-
-
-def to_sources(parts):
-    return lax.all_to_all(
-        parts.astype(jnp.bfloat16), "expert", split_axis=0, concat_axis=0, tiled=True
-    ).astype(parts.dtype)
+def gates(logits, experts, expert):
+    lane = lax.broadcasted_iota(jnp.int32, logits.shape, 1)
+    first, second = logits[:, experts : experts + 1], logits[:, experts + 1 : experts + 2]
+    top = jnp.maximum(first, second)
+    first, second = jnp.exp(first - top), jnp.exp(second - top)
+    total = first + second
+    first, second = first / total, second / total
+    if expert is None:
+        return lane, first, second, None, None
+    routed = jnp.where(lane < experts, logits, NEGATIVE_FILL)
+    raised = jnp.exp(routed - jnp.max(routed, axis=1, keepdims=True))
+    probs = raised / jnp.sum(raised, axis=1, keepdims=True)
+    gate = jnp.sum(jnp.where(lane == expert, probs, 0.0), axis=1, keepdims=True)
+    return lane, first, second, probs, gate
+
+
+def feed_kernel(experts, routed, expert_ref, xa_ref, xb_ref, ga_ref, gb_ref, head_ref, up_ref, down_ref,
+                out_ref, back_ref, active_ref, pre_ref, grad_ref, head_grad_ref):
+    step = pl.program_id(0)
+    early = step < pl.num_programs(0) // 2
+    rows = jnp.where(early, xa_ref[...], xb_ref[...])
+    grads = jnp.where(early, ga_ref[...], gb_ref[...]).astype(F32)
+    logits = dot_nn(rows, head_ref[...])
+    expert = expert_ref[0] if routed else None
+    lane, first, second, probs, gate = gates(logits, experts, expert)
+    coef = second * gate if routed else first
+    weighted = (coef * grads).astype(BF16)
+    grad_ref[...] = weighted
+    pre = dot_nn(rows, up_ref[...])
+    grad_active = dot_nt(weighted, down_ref[...])
+    cumulative = 0.5 + 0.5 * lax.erf(pre * 0.7071067811865476)
+    slope = cumulative + pre * jnp.exp(-0.5 * pre * pre) * 0.3989422804014327
+    active = (pre * cumulative).astype(BF16)
+    active_ref[...] = active
+    grad_pre = (grad_active * slope).astype(BF16)
+    pre_ref[...] = grad_pre
+    out = dot_nn(active, down_ref[...])
+    out_ref[...] = (coef * out).astype(BF16)
+    inner = jnp.sum(grads * out, axis=1, keepdims=True)
+    swing = first * second * inner
+    if routed:
+        swing = -gate * swing
+    grad_logits = jnp.where(lane == experts, swing, jnp.where(lane == experts + 1, -swing, 0.0))
+    if routed:
+        picked = jnp.where(lane == expert, 1.0, 0.0) - gate
+        grad_logits = grad_logits + jnp.where(lane < experts, probs * picked * (second * inner), 0.0)
+    back = dot_nt(grad_pre, up_ref[...]) + dot_nt(grad_logits.astype(BF16), head_ref[...])
+    back_ref[...] = back.astype(BF16)
+
+    @pl.when(step == 0)
+    def _():
+        head_grad_ref[...] = jnp.zeros_like(head_grad_ref)
+
+    head_grad_ref[...] += dot_nn(grad_logits.T.astype(BF16), rows)
+
+
+def feed(xa, xb, ga, gb, head, up, down, experts, expert, size):
+    total = 2 * xa.shape[0]
+    width, hidden = up.shape
+    steps = total // size
+    half = steps // 2
+    lanes = head.shape[1]
+    routed = expert is not None
+    pick = jnp.reshape(expert, (1,)) if routed else jnp.zeros((1,), jnp.int32)
+    early = pl.BlockSpec((size, width), lambda i, pick: (jnp.minimum(i, half - 1), 0))
+    late = pl.BlockSpec((size, width), lambda i, pick: (jnp.maximum(i - half, 0), 0))
+
+    def held(shape):
+        return pl.BlockSpec(shape, lambda i, pick: (0, 0), pipeline_mode=pl.Buffered(1))
+
+    wide = pl.BlockSpec((size, width), lambda i, pick: (i, 0))
+    deep = pl.BlockSpec((size, hidden), lambda i, pick: (i, 0))
+    return pl.pallas_call(
+        functools.partial(feed_kernel, experts, routed),
+        grid_spec=pltpu.PrefetchScalarGridSpec(
+            num_scalar_prefetch=1,
+            grid=(steps,),
+            in_specs=[early, late, early, late, held((width, lanes)), held((width, hidden)), held((hidden, width))],
+            out_specs=[wide, wide, deep, deep, wide, pl.BlockSpec((lanes, width), lambda i, pick: (0, 0))],
+        ),
+        out_shape=[
+            jax.ShapeDtypeStruct((total, width), BF16),
+            jax.ShapeDtypeStruct((total, width), BF16),
+            jax.ShapeDtypeStruct((total, hidden), BF16),
+            jax.ShapeDtypeStruct((total, hidden), BF16),
+            jax.ShapeDtypeStruct((total, width), BF16),
+            jax.ShapeDtypeStruct((lanes, width), F32),
+        ],
+        compiler_params=pltpu.CompilerParams(vmem_limit_bytes=60 * 1024 * 1024),
+        name="feed_routed" if routed else "feed_dense",
+    )(pick, xa, xb, ga, gb, head, up, down)
+
+
+LANES = 128
+DIRECT = 8
+
+
+def norm_parts(values):
+    row_mean = jnp.mean(values, axis=-1, keepdims=True)
+    centred = values - row_mean
+    row_var = jnp.mean(centred * centred, axis=-1, keepdims=True)
+    inverse = lax.rsqrt(row_var + EPSILON)
+    return (centred * inverse, inverse)
+
+
+def norm_back(grad_normed, gain_vec, scaled, inverse):
+    grad_scaled = grad_normed * gain_vec
+    first_mean = jnp.mean(grad_scaled, axis=-1, keepdims=True)
+    second = jnp.mean(grad_scaled * scaled, axis=-1, keepdims=True)
+    return inverse * (grad_scaled - first_mean - scaled * second)
+
+
+def from_side(values):
+    return lax.ppermute(values, "tensor", [(i, i ^ 1) for i in range(4)])
+
+
+def from_far(values):
+    return lax.ppermute(values, "tensor", [(i, i ^ 2) for i in range(4)])
+
+
+def both_halves(own):
+    near = jnp.concatenate([own, from_far(own)], axis=0)
+    return near, from_side(near)
+
+
+def sum_to_owner(values):
+    half = values.shape[0] // 2
+    quarter = half // 2
+    near = values[:half].astype(F32) + from_side(values[half:]).astype(F32)
+    return near[:quarter] + from_far(near[quarter:].astype(BF16)).astype(F32)
+
+
+def own_core(values, axis, flip):
+    core = lax.axis_index("tensor") % 2
+    return lax.dynamic_index_in_dim(values, 1 - core if flip else core, axis, keepdims=False)
+
+
+def sum_tree_to_owner(partial):
+    sent = partial(True).astype(BF16)
+    near = partial(False) + from_side(sent).astype(F32)
+    near = near.reshape(2, -1, near.shape[1])
+    place = lax.axis_index("tensor") // 2
+    kept = lax.dynamic_index_in_dim(near, place, 0, keepdims=False)
+    far = lax.dynamic_index_in_dim(near, 1 - place, 0, keepdims=False)
+    return kept + from_far(far.astype(BF16)).astype(F32)
+
+
+def exchange(blocks, back):
+    count = lax.axis_size("expert")
+    if count > DIRECT:
+        return lax.all_to_all(blocks, "expert", split_axis=0, concat_axis=0, tiled=True)
+    arrived = [blocks[0]]
+    for step in range(1, count):
+        pairs = [(i, (i - step if back else i + step) % count) for i in range(count)]
+        arrived.append(lax.ppermute(blocks[step], "expert", pairs))
+    return jnp.stack(arrived)
+
+
+def slots_of(expert_ids, experts, capacity):
+    rows = expert_ids.shape[0]
+    chosen = expert_ids[:, None] == jnp.arange(experts, dtype=jnp.int32)[None, :]
+    at = jnp.arange(rows, dtype=jnp.int32)
+    before = (at[None, :] < at[:, None]).astype(BF16)
+    earlier = jnp.dot(before, chosen.astype(BF16), preferred_element_type=F32)
+    slot = jnp.sum(jnp.where(chosen, earlier, 0.0), axis=1).astype(jnp.int32)
+    first = lax.axis_index("expert") if experts <= DIRECT else 0
+    place = ((expert_ids - first) % experts) * capacity + slot
+    places = jnp.arange(experts * capacity, dtype=jnp.int32)
+    return (places[:, None] == place[None, :]).astype(BF16)
 
 
 def per_device(
@@ -361,172 +493,151 @@
     ex_up,
     ex_down,
 ):
-    tok_dev = tokens.shape[0]
-    model_width = tokens.shape[1]
-    quarters = lax.axis_size("tensor")
-    own_start = lax.axis_index("tensor") * tok_dev
-    group_rows = tok_dev * quarters
+    tok_dev, width = tokens.shape
+    mine = lax.axis_index("tensor")
     experts = w_router.shape[1]
     capacity = max(2, tok_dev * 7 // (5 * experts))
-    gathered = lax.all_gather(tokens, "tensor", axis=0, tiled=True)
-    scaled_one, inverse_one = norm_parts(gathered.astype(jnp.float32))
-    normed_one = (scaled_one * ln_attn).astype(jnp.bfloat16)
-    qkv_rows = jnp.einsum(
-        "td,sdc->stc", normed_one, w_qkv, preferred_element_type=jnp.float32
-    ).astype(jnp.bfloat16)
-
+    heads_width = w_qkv.shape[2]
     leaves = leaf_order(parents[0])
+
+    scaled_one, inverse_one = norm_parts(tokens.astype(F32))
+    normed_own = (scaled_one * ln_attn).astype(BF16)
+    normed_one = lax.all_gather(normed_own, "tensor", axis=0, tiled=True)
+
+    quarter_ids = routes[:, 0].reshape(4, tok_dev)
+    own_slots = slots_of(
+        lax.dynamic_index_in_dim(quarter_ids, mine, 0, keepdims=False), experts, capacity
+    )
+    far_slots = slots_of(
+        lax.dynamic_index_in_dim(quarter_ids, mine ^ 2, 0, keepdims=False), experts, capacity
+    )
+
+    def dispatch(slots, rows):
+        placed = jnp.dot(slots, rows, preferred_element_type=F32).astype(BF16)
+        return exchange(placed.reshape(experts, capacity, width), False).reshape(-1, width)
+
+    grads_near, grads_side = both_halves(dispatch(own_slots, cotangent))
+
+    qkv_rows = jnp.einsum("td,sdc->stc", normed_one, w_qkv, preferred_element_type=F32).astype(BF16)
     attended, trunk_log, family_log = attention_forward(leaves, qkv_rows)
-    residual = tokens.astype(jnp.float32) + lax.psum_scatter(
-        jnp.dot(attended, w_out, preferred_element_type=jnp.float32),
-        "tensor",
+    attended_view = attended.reshape(2, 2, tok_dev, heads_width)
+
+    def branch_part(flip):
+        rows = own_core(attended_view, 1, flip).reshape(2 * tok_dev, heads_width)
+        return jnp.dot(rows, w_out, preferred_element_type=F32)
+
+    residual = tokens.astype(F32) + sum_tree_to_owner(branch_part)
+    cotangent_near, cotangent_side = both_halves(cotangent)
+
+    scaled_two, inverse_two = norm_parts(residual)
+    normed_two = (scaled_two * ln_mlp).astype(BF16)
+    own_arrived = dispatch(own_slots, normed_two)
+    normed_far = from_far(normed_two)
+    near_arrived = jnp.concatenate([own_arrived, dispatch(far_slots, normed_far)], axis=0)
+    side_arrived = from_side(near_arrived)
+    normed_near = jnp.concatenate([normed_two, normed_far], axis=0)
+    normed_side = from_side(normed_near)
+
+    lanes = -(-(experts + 2) // LANES) * LANES
+    head = jnp.concatenate(
+        [w_router, w_mix, jnp.zeros((width, lanes - experts - 2), BF16)], axis=1
+    )
+    dense_out, dense_back, dense_active, dense_pre, dense_grad, dense_head = feed(
+        normed_near, normed_side, cotangent_near, cotangent_side, head, w_up, w_down, experts, None, tok_dev * 2 // 5
+    )
+    expert = lax.axis_index("expert").astype(jnp.int32)
+    expert_out, expert_back, expert_active, expert_pre, expert_grad, expert_head = feed(
+        near_arrived, side_arrived, grads_near, grads_side, head, ex_up[0], ex_down[0], experts, expert,
+        near_arrived.shape[0] // 7,
+    )
+
+    def returned(partial):
+        rows = sum_to_owner(partial).astype(BF16).reshape(experts, capacity, width)
+        rows = exchange(rows, True).reshape(-1, width)
+        return lax.dot_general(own_slots, rows, (((0,), (0,)), ((), ())), preferred_element_type=F32)
+
+    grad_normed_two = sum_to_owner(dense_back) + returned(expert_back)
+
+    normed_rows = jnp.concatenate([normed_near, normed_side], axis=0)
+    grad_up = jnp.einsum("gd,gf->df", normed_rows, dense_pre, preferred_element_type=F32)
+    grad_down = jnp.einsum("gd,gf->df", dense_grad, dense_active, preferred_element_type=F32)
+    dense_grads = lax.psum_scatter(
+        jnp.concatenate([grad_up.astype(BF16), grad_down.astype(BF16)], axis=1),
+        "expert",
         scatter_dimension=0,
         tiled=True,
-    )
-    residual_all = lax.all_gather(residual, "tensor", axis=0, tiled=True)
-    scaled_two, inverse_two = norm_parts(residual_all)
-    normed_two = (scaled_two * ln_mlp).astype(jnp.bfloat16)
-    pre_dense = jnp.dot(normed_two, w_up, preferred_element_type=jnp.float32)
-    active = gelu_exact(pre_dense).astype(jnp.bfloat16)
-    dense_part = jnp.dot(active, w_down, preferred_element_type=jnp.float32)
-    router_probs = jax.nn.softmax(
-        jnp.dot(normed_two, w_router, preferred_element_type=jnp.float32), axis=-1
-    )
-    expert_ids = routes[:, 0]
-    chosen = expert_ids[:, None] == jnp.arange(experts, dtype=jnp.int32)[None, :]
-    gate_prob = jnp.sum(jnp.where(chosen, router_probs, 0.0), axis=1)
-    mix_coef = jax.nn.softmax(
-        jnp.dot(normed_two, w_mix, preferred_element_type=jnp.float32), axis=-1
-    )
-    counted = chosen.astype(jnp.int32).reshape(quarters, tok_dev, experts)
-    position = (jnp.cumsum(counted, axis=1) - 1).reshape(group_rows, experts)
-    slot_index = jnp.sum(jnp.where(chosen, position, 0), axis=1)
-    quarter = jnp.arange(group_rows, dtype=jnp.int32) // tok_dev
-    arrived = to_owners(normed_two, expert_ids, quarter, slot_index, experts, quarters, capacity)
-    flat_rows = arrived.reshape(-1, model_width)
-    expert_pre = jnp.dot(flat_rows, ex_up[0], preferred_element_type=jnp.float32)
-    expert_active = gelu_exact(expert_pre).astype(jnp.bfloat16)
-    expert_part = jnp.dot(expert_active, ex_down[0], preferred_element_type=jnp.float32).reshape(
-        arrived.shape
-    )
-    returned = to_sources(expert_part)
-    expert_weight = mix_coef[:, 1] * gate_prob
-    expert_rows = returned[expert_ids, quarter, slot_index]
-    extra_term = 0.0
-    dense_coef = mix_coef[:, 0]
-    mixed = (
-        lax.psum_scatter(
-            (dense_coef[:, None] * dense_part + expert_weight[:, None] * expert_rows).astype(
-                jnp.bfloat16
-            ),
-            "tensor",
-            scatter_dimension=0,
-            tiled=True,
-        ).astype(jnp.float32)
-        + extra_term
-    )
-    out = (residual + mixed).astype(jnp.bfloat16)
-    grad_all = lax.all_gather(cotangent, "tensor", axis=0, tiled=True).astype(jnp.float32)
-    grad_dense = (mix_coef[:, 0:1] * grad_all).astype(jnp.bfloat16)
-    grad_down = jnp.einsum("gf,gd->fd", active, grad_dense, preferred_element_type=jnp.float32)
-    grad_active = jnp.einsum("gd,fd->gf", grad_dense, w_down, preferred_element_type=jnp.float32)
-    grad_pre = (grad_active * gelu_slope(pre_dense)).astype(jnp.bfloat16)
-    grad_up = jnp.einsum("gd,gf->df", normed_two, grad_pre, preferred_element_type=jnp.float32)
-    grad_normed_two = jnp.einsum("gf,df->gd", grad_pre, w_up, preferred_element_type=jnp.float32)
-    dense_dot = jnp.sum(grad_all * dense_part, axis=1)
-    grad_expert = (expert_weight[:, None] * grad_all).astype(jnp.bfloat16)
-    arrived_grad = to_owners(
-        grad_expert, expert_ids, quarter, slot_index, experts, quarters, capacity
-    )
-    flat_grad = arrived_grad.reshape(-1, model_width)
-    grad_ex_down = jnp.einsum(
-        "rf,rd->fd", expert_active, flat_grad, preferred_element_type=jnp.float32
-    )[None]
-    grad_ex_active = jnp.einsum(
-        "rd,fd->rf", flat_grad, ex_down[0], preferred_element_type=jnp.float32
-    )
-    grad_ex_pre = (grad_ex_active * gelu_slope(expert_pre)).astype(jnp.bfloat16)
-    grad_ex_up = jnp.einsum(
-        "rd,rf->df", flat_rows, grad_ex_pre, preferred_element_type=jnp.float32
-    )[None]
-    grad_ex_rows = jnp.einsum(
-        "rf,df->rd", grad_ex_pre, ex_up[0], preferred_element_type=jnp.float32
-    ).reshape(arrived.shape)
-    grad_back = to_sources(grad_ex_rows)
-    grad_normed_two = grad_normed_two + grad_back[expert_ids, quarter, slot_index]
-    expert_dot = jnp.sum(grad_all * expert_rows, axis=1)
-    row_dots = jnp.stack([dense_dot, expert_dot], axis=1)
-    grad_normed_two, row_dots = (
-        lax.psum(grad_normed_two.astype(jnp.bfloat16), "tensor").astype(jnp.float32),
-        lax.psum(row_dots.astype(jnp.bfloat16), "tensor").astype(jnp.float32),
-    )
-    mix_grad = jnp.stack([row_dots[:, 0], gate_prob * row_dots[:, 1]], axis=1)
-    grad_mix_logits = (
-        mix_coef * (mix_grad - jnp.sum(mix_coef * mix_grad, axis=1, keepdims=True))
-    ).astype(jnp.bfloat16)
-    grad_gate = mix_coef[:, 1] * row_dots[:, 1]
-    grad_router_logits = (
-        router_probs
-        * (jnp.where(chosen, grad_gate[:, None], 0.0) - (gate_prob * grad_gate)[:, None])
-    ).astype(jnp.bfloat16)
-    grad_normed_two = grad_normed_two + jnp.einsum(
-        "ge,de->gd", grad_router_logits, w_router, preferred_element_type=jnp.float32
-    )
-    grad_normed_two = grad_normed_two + jnp.einsum(
-        "gm,dm->gd", grad_mix_logits, w_mix, preferred_element_type=jnp.float32
-    )
-    grad_router = jnp.einsum(
-        "gd,ge->de", normed_two, grad_router_logits, preferred_element_type=jnp.float32
-    )
-    grad_mix = jnp.einsum(
-        "gd,gm->dm", normed_two, grad_mix_logits, preferred_element_type=jnp.float32
-    )
-    grad_ln_mlp = jnp.sum(grad_normed_two * scaled_two, axis=0)
-    grad_residual = grad_all + norm_back(grad_normed_two, ln_mlp, scaled_two, inverse_two)
-    grad_branch = grad_residual.astype(jnp.bfloat16)
-    grad_w_out = jnp.einsum("gc,gd->cd", attended, grad_branch, preferred_element_type=jnp.float32)
-    grad_attended = jnp.einsum(
-        "gd,cd->gc", grad_branch, w_out, preferred_element_type=jnp.float32
-    ).astype(jnp.bfloat16)
-
+    ).astype(F32)
+    expert_rows = jnp.concatenate([near_arrived, side_arrived], axis=0)
+    grad_ex_up = jnp.einsum("gd,gf->df", expert_rows, expert_pre, preferred_element_type=F32)[None]
+    grad_ex_down = jnp.einsum("gf,gd->fd", expert_active, expert_grad, preferred_element_type=F32)[None]
+
+    gain_two = jnp.sum(grad_normed_two * scaled_two, axis=0)
+    grad_residual = cotangent.astype(F32) + norm_back(grad_normed_two, ln_mlp, scaled_two, inverse_two)
+    branch_near, branch_side = both_halves(grad_residual.astype(BF16))
+    grad_branch = jnp.concatenate([branch_near, branch_side], axis=0)
+    small = lax.psum(
+        jnp.concatenate([(dense_head + expert_head)[: experts + 2], gain_two[None]], axis=0), "tensor"
+    )
+
+    offsets = jnp.arange(4, dtype=jnp.int32) ^ mine
+    place_of = (offsets % 2) * 2 + offsets // 2
+    grad_attended = jnp.einsum("gd,cd->gc", grad_branch, w_out, preferred_element_type=F32)
+    grad_attended = grad_attended.astype(BF16).reshape(4, tok_dev, heads_width)
+    grad_attended = jnp.take(grad_attended, place_of, axis=0).reshape(4 * tok_dev, heads_width)
+    quarter_at = jnp.asarray([0, 2, 1, 3], jnp.int32) ^ mine
+    attended_rows = jnp.take(
+        attended.reshape(4, tok_dev, heads_width), quarter_at, axis=0
+    ).reshape(4 * tok_dev, heads_width)
+    grad_w_out = jnp.einsum("gd,gc->dc", grad_branch, attended_rows, preferred_element_type=F32)
+
+    grad_attended, small = lax.optimization_barrier((grad_attended, small))
     grad_qkv_rows = attention_backward(
         leaves, qkv_rows, grad_attended, attended, trunk_log, family_log
     )
-    grad_w_qkv = jnp.einsum(
-        "gd,sgc->sdc", normed_one, grad_qkv_rows, preferred_element_type=jnp.float32
-    )
-    grad_normed_one = jnp.einsum(
-        "sgc,sdc->gd", grad_qkv_rows, w_qkv, preferred_element_type=jnp.float32
-    )
-    part_gain = jnp.sum(grad_normed_one * scaled_one, axis=0)
-    grad_normed_own = lax.psum_scatter(
-        grad_normed_one.astype(jnp.bfloat16), "tensor", scatter_dimension=0, tiled=True
-    ).astype(jnp.float32)
-    own_scaled = lax.dynamic_slice_in_dim(scaled_one, own_start, tok_dev, 0)
-    own_inverse = lax.dynamic_slice_in_dim(inverse_one, own_start, tok_dev, 0)
-    own_residual_grad = lax.dynamic_slice_in_dim(grad_residual, own_start, tok_dev, 0)
-    grad_tokens = own_residual_grad + norm_back(grad_normed_own, ln_attn, own_scaled, own_inverse)
-    summed_grads = (
-        lax.psum_scatter(grad_w_qkv, "expert", scatter_dimension=1, tiled=True),
-        lax.psum_scatter(grad_w_out, "expert", scatter_dimension=1, tiled=True),
-        lax.psum_scatter(grad_ln_mlp, "expert", scatter_dimension=0, tiled=True),
-        lax.psum_scatter(grad_up, "expert", scatter_dimension=0, tiled=True),
-        lax.psum_scatter(grad_down, "expert", scatter_dimension=1, tiled=True),
-        lax.psum_scatter(grad_router, "expert", scatter_dimension=0, tiled=True),
-        lax.psum_scatter(grad_mix, "expert", scatter_dimension=0, tiled=True),
-    )
-    grad_ln_attn = lax.psum(part_gain, ("expert", "tensor"))
+    grad_view = grad_qkv_rows.reshape(3, 2, 2, tok_dev, heads_width)
+
+    def normed_part(flip):
+        rows = own_core(grad_view, 2, flip).reshape(3, 2 * tok_dev, heads_width)
+        return jnp.einsum("sgc,sdc->gd", rows, w_qkv, preferred_element_type=F32)
+
+    grad_normed_one = sum_tree_to_owner(normed_part)
+    grad_w_qkv = jnp.einsum("gd,sgc->dsc", normed_one, grad_qkv_rows, preferred_element_type=F32)
+    small_columns = -(-small.shape[0] // LANES) * LANES
+    small_block = jnp.pad(small, ((0, small_columns - small.shape[0]), (0, 0))).T
+    last_grads = lax.psum_scatter(
+        jnp.concatenate(
+            [
+                grad_w_qkv.reshape(width, 3 * heads_width).astype(BF16),
+                grad_w_out.astype(BF16),
+                small_block.astype(BF16),
+            ],
+            axis=1,
+        ),
+        "expert",
+        scatter_dimension=0,
+        tiled=True,
+    ).astype(F32)
+    grad_ln_attn = lax.psum(
+        lax.psum(jnp.sum(grad_normed_one * scaled_one, axis=0), "tensor"), "expert"
+    )
+    grad_tokens = grad_residual + norm_back(grad_normed_one, ln_attn, scaled_one, inverse_one)
+    out = (residual + sum_to_owner(dense_out) + returned(expert_out)).astype(BF16)
+
+    hidden = w_up.shape[1]
+    strip = last_grads.shape[0]
+    after_qkv = 3 * heads_width
+    after_out = after_qkv + heads_width
     return (
         out,
         grad_tokens,
         grad_ln_attn,
-        summed_grads[0],
-        summed_grads[1],
-        summed_grads[2],
-        summed_grads[3],
-        summed_grads[4],
-        summed_grads[5],
-        summed_grads[6],
+        last_grads[:, :after_qkv].reshape(strip, 3, heads_width).transpose(1, 0, 2),
+        last_grads[:, after_qkv:after_out].T,
+        last_grads[:, after_out + experts + 2],
+        dense_grads[:, :hidden],
+        dense_grads[:, hidden:].T,
+        last_grads[:, after_out : after_out + experts],
+        last_grads[:, after_out + experts : after_out + experts + 2],
         grad_ex_up,
         grad_ex_down,
     )

time: 1860 us -> 890 us (0.48)
  waiting for transfers between devices: 857 us -> 304 us
  blocking collectives: 399 us -> 54.4 us
  matrix products: 265 us -> 90.9 us
  starting transfers between devices: 11.1 us -> 118 us
  Pallas kernels: 64.8 us -> 166 us
  other arithmetic: 142 us -> 57.5 us
  local copies, waits for them, and re-layouts: 96.9 us -> 75.2 us
    reduce_scatter x8 -> x0, waiting for transfers between devices: 413 us -> none  [the longest x1 92.2 us: per_device(): lax.psum_scatter(grad_down, 'expert', scatter_dimension=1, tiled=True)]
    all_to_all x2 -> x0, blocking collectives: 331 us -> none  [to_owners(): lax.all_to_all(outgoing, 'expert', split_axis=0, concat_axis=0, tiled=True)]
    ppermute x0 -> x56, waiting for transfers between devices: none -> 263 us  [the longest x10 134 us: from_far(): return lax.ppermute(values, 'tensor', [(i, i ^ 2) for i in range(4)])]
    all_to_all x2 -> x0, waiting for transfers between devices: 257 us -> none  [to_sources(): lax.all_to_all(parts.astype(jnp.bfloat16), 'expert', split_axis=0, concat...]
    dot_general x23 -> x19, matrix products: 260 us -> 90.9 us  [the longest x1 14 us: per_device(): jnp.einsum('gf,gd->fd', expert_active, expert_grad, preferred_element_typ...]
    ppermute x0 -> x56, starting transfers between devices: none -> 118 us  [the longest x35 106 us: exchange(): arrived.append(lax.ppermute(blocks[step], 'expert', pairs))]
    pallas_call x0 -> x2, Pallas kernels: none -> 101 us  [feed(): pl.pallas_call(functools.partial(feed_kernel, experts, routed), grid_spec...]
    psum x1 -> x0, waiting for transfers between devices: 80 us -> none  [per_device(): lax.psum(grad_normed_two.astype(jnp.bfloat16), 'tensor').astype(jnp.float32)]
  transfers between devices with their start and end apart: 15 -> 59, of which waited for: 12 -> 28; matrix products, arithmetic and copies ran while one was open for 15% -> 22% of each run, Pallas kernels for 2% -> 16%
where the time goes in v2:
time: 890 us; the launch traced here: 882 us
  waiting for transfers between devices  304 us (34%)
  Pallas kernels  166 us (19%)
  starting transfers between devices  118 us (13%)
  matrix products  90.9 us (10%)
  local copies, waits for them, and re-layouts  75.2 us (8%)
  other arithmetic  57.5 us (6%)
  blocking collectives  54.4 us (6%)
  between operations  15.2 us (2%)
    ppermute x10, waiting for transfers between devices, from_far(): return lax.ppermute(values, 'tensor', [(i, i ^ 2) for i in range(4)])  134 us
    ppermute x35, waiting for transfers between devices, exchange(): arrived.append(lax.ppermute(blocks[step], 'expert', pairs))  129 us
    ppermute x35, starting transfers between devices, exchange(): arrived.append(lax.ppermute(blocks[step], 'expert', pairs))  106 us
    pallas_call x2, Pallas kernels, feed(): pl.pallas_call(functools.partial(feed_kernel, experts, routed), grid_spec...  101 us
    all_gather x1, waiting for transfers between devices, per_device(): normed_one = lax.all_gather(normed_own, 'tensor', axis=0, tiled=True)  41.2 us
    pallas_call x1, Pallas kernels, attention_backward(): pl.pallas_call(backward_kernel, grid_spec=pltpu.PrefetchScalarGridSpec(nu...  40.1 us
    unnamed x165, local copies, waits for them, and re-layouts  33.2 us
    psum x1, blocking collectives, per_device(): lax.psum(jnp.concatenate([(dense_head + expert_head)[:experts + 2], gain_...  28.6 us
  transfers between devices with their start and end apart: 59, of which 28 were waited for; matrix products, arithmetic and copies ran while one was open for 22% of the time, Pallas kernels for 16%

profile of v2, /device:TPU:0, one launch (start us, length us, event | category | flops | bytes accessed | tf_op | source)
XLA Modules:
  0.0 882.2 jit_solution(1764633190897739859)
XLA Ops:
  15.0 41.2 %all-gather.2.cloned.1.call-done = bf16[2560,1024]{1,0:T(8,128)(2,1)} async-done(((bf16[640,1024]{1,0:T(8,128)(2,1)}), bf16[2560,1024]{1,0:T(8,128)(2,1)}) %all-gather.2.cloned.1.call-update) | async-done | bytes 5242896 | tf_op jit(solution)/shard_map/all_gather | solution.py:505
  64.5 24.7 %tree_attention.1 = (bf16[2560,256]{1,0:T(8,128)(2,1)}, f32[2,2,1024]{2,1,0:T(2,128)}, f32[2,4,2,384]{3,2,1,0:T(2,128)}) custom-call(s32[8]{0:T(128)} %select_reduce_fusion.leaves_ref, bf16[3,2560,256]{2,1,0:T(8,128)(2,1)} %fusion.19.qkv_ref), custom_call_target="tpu_custom_call" | custom-call | tf_op jit(solution)/shard_map/tree_attention/pallas_call | solution.py:151
  109.1 16.2 %collective-permute-done.25 = bf16[112,1024]{1,0:T(8,128)(2,1)S(1)} collective-permute-done((bf16[112,1024]{1,0:T(8,128)(2,1)S(1)}, bf16[112,1024]{1,0:T(8,128)(2,1)S(1)}, u32[]{:S(2)}, u32[]{:S(2)}) %collective-permute-start.25) | collective-permute-done | bytes 229408 | tf_op jit(solution)/shard_map/ppermute | solution.py:463
  125.2 8.4 collective-permute-start.29
  146.7 34.5 %collective-permute-done.30 = bf16[896,1024]{1,0:T(8,128)(2,1)} collective-permute-done((bf16[896,1024]{1,0:T(8,128)(2,1)}, bf16[896,1024]{1,0:T(8,128)(2,1)}, u32[]{:S(2)}, u32[]{:S(2)}) %collective-permute-start.30) | collective-permute-done | bytes 1835040 | tf_op jit(solution)/shard_map/ppermute | solution.py:426
  185.5 17.4 %collective-permute-done.1 = bf16[640,1024]{1,0:T(8,128)(2,1)} collective-permute-done((bf16[640,1024]{1,0:T(8,128)(2,1)}, bf16[640,1024]{1,0:T(8,128)(2,1)}, u32[]{:S(2)}, u32[]{:S(2)}) %collective-permute-start.1) | collective-permute-done | bytes 1310752 | tf_op jit(solution)/shard_map/ppermute | solution.py:426
  226.9 23.4 %collective-permute-start.12 = (bf16[112,1024]{1,0:T(8,128)(2,1)S(1)}, bf16[112,1024]{1,0:T(8,128)(2,1)S(1)}, u32[]{:S(2)}, u32[]{:S(2)}) collective-permute-start(bf16[112,1024]{1,0:T(8,128)(2,1)S(1)} %get-tuple-element.122), channel_id=1, source_target_pairs={{0,20},{4,24},{8,28},{12,0},{16,4},{20,8},{24,12},{28,16},{1,21},{... | collective-permute-start | bytes 688136 | tf_op jit(solution)/shard_map/ppermute | solution.py:463
  278.9 13.3 %collective-permute-done.17 = bf16[112,1024]{1,0:T(8,128)(2,1)S(1)} collective-permute-done((bf16[112,1024]{1,0:T(8,128)(2,1)S(1)}, bf16[112,1024]{1,0:T(8,128)(2,1)S(1)}, u32[]{:S(2)}, u32[]{:S(2)}) %collective-permute-start.17) | collective-permute-done | bytes 229408 | tf_op jit(solution)/shard_map/ppermute | solution.py:463
  308.4 28.3 %collective-permute-done.4 = bf16[640,1024]{1,0:T(8,128)(2,1)S(1)} collective-permute-done((bf16[640,1024]{1,0:T(8,128)(2,1)S(1)}, bf16[640,1024]{1,0:T(8,128)(2,1)S(1)}, u32[]{:S(2)}, u32[]{:S(2)}) %collective-permute-start.4) | collective-permute-done | bytes 1310752 | tf_op jit(solution)/shard_map/ppermute | solution.py:426
  341.4 63.9 %feed_routed.1 = (bf16[3584,1024]{1,0:T(8,128)(2,1)}, bf16[3584,1024]{1,0:T(8,128)(2,1)}, bf16[3584,1024]{1,0:T(8,128)(2,1)}, bf16[3584,1024]{1,0:T(8,128)(2,1)}...) custom-call(s32[1]{0:T(128)} %bitcast.11.expert_ref, bf16[1792,1024]{1,0:T(8,128)(2,1)} %pad_maximum_fusion.2.xa_ref, ...), custom_call_target="tpu_custom_call" | custom-call | tf_op jit(solution)/shard_map/feed_routed/pallas_call | solution.py:381
  414.6 37.5 %feed_dense.1 = (bf16[2560,1024]{1,0:T(8,128)(2,1)}, bf16[2560,1024]{1,0:T(8,128)(2,1)}, bf16[2560,1024]{1,0:T(8,128)(2,1)}, bf16[2560,1024]{1,0:T(8,128)(2,1)},...) custom-call(s32[1]{0:T(128)} %constant.143.clone.1.expert_ref, bf16[1280,1024]{1,0:T(8,128)(2,1)} %pad_maximum_fusion.4.xa_ref, ...), custom_call_target="tpu_custom_call" | custom-call | tf_op jit(solution)/shard_map/feed_dense/pallas_call | solution.py:381
  456.3 9.7 %convolution_convert_fusion.2 = bf16[1024,1024]{0,1:T(8,128)(2,1)S(1)} fusion(bf16[2560,1024]{1,0:T(8,128)(2,1)} %get-tuple-element.42, bf16[2560,1024]{1,0:T(8,128)(2,1)} %get-tuple-element.43), kind=kOutput, calls=%fused_computation.89 | convolution fusion | flops 5369757696 | bytes 12582912 | tf_op jit(solution)/shard_map/gd,gf->df/dot_general | solution.py:563
  505.2 12.3 %collective-permute-done.44 = bf16[896,1024]{1,0:T(8,128)(2,1)} collective-permute-done((bf16[896,1024]{1,0:T(8,128)(2,1)}, bf16[896,1024]{1,0:T(8,128)(2,1)}, u32[]{:S(2)}, u32[]{:S(2)}) %collective-permute-start.44) | collective-permute-done | bytes 1835040 | tf_op jit(solution)/shard_map/ppermute | solution.py:426
  526.8 10.2 %collective-permute-done.45 = bf16[112,1024]{1,0:T(8,128)(2,1)S(1)} collective-permute-done((bf16[112,1024]{1,0:T(8,128)(2,1)S(1)}, bf16[112,1024]{1,0:T(8,128)(2,1)S(1)}, u32[]{:S(2)}, u32[]{:S(2)}) %collective-permute-start.45) | collective-permute-done | bytes 229408 | tf_op jit(solution)/shard_map/ppermute | solution.py:463
  556.3 11.8 %collective-permute-done.48 = bf16[112,1024]{1,0:T(8,128)(2,1)S(1)} collective-permute-done((bf16[112,1024]{1,0:T(8,128)(2,1)S(1)}, bf16[112,1024]{1,0:T(8,128)(2,1)S(1)}, u32[]{:S(2)}, u32[]{:S(2)}) %collective-permute-start.48) | collective-permute-done | bytes 229408 | tf_op jit(solution)/shard_map/ppermute | solution.py:463
  587.7 14.0 %convolution_bitcast_fusion = f32[1,1024,1024]{2,1,0:T(8,128)} fusion(bf16[3584,1024]{1,0:T(8,128)(2,1)} %get-tuple-element.45, bf16[3584,1024]{1,0:T(8,128)(2,1)} %get-tuple-element.46), kind=kOutput, calls=%fused_computation.86 | convolution fusion | flops 7516192768 | bytes 18874368 | tf_op jit(solution)/shard_map/gf,gd->fd/dot_general | solution.py:572
  607.1 10.5 %collective-permute-done.52 = bf16[640,1024]{1,0:T(8,128)(2,1)S(1)} collective-permute-done((bf16[640,1024]{1,0:T(8,128)(2,1)S(1)}, bf16[640,1024]{1,0:T(8,128)(2,1)S(1)}, u32[]{:S(2)}, u32[]{:S(2)}) %collective-permute-start.52) | collective-permute-done | bytes 1310752 | tf_op jit(solution)/shard_map/ppermute | solution.py:426
  619.7 13.6 %fusion.46 = f32[1,1024,1024]{2,1,0:T(8,128)} fusion(bf16[3584,1024]{1,0:T(8,128)(2,1)} %get-tuple-element.44, bf16[1792,1024]{1,0:T(8,128)(2,1)} %collective-permute-done.22.xb_ref, bf16[896,1024]{1,0:T(8,128)(2,1)S(1)} %bitcast.221, bf16[896,1024]{1,0:T(8,128)(2,1)S(1)} %bitcast.219), kind=kOutput, calls=%fused_computation.85 | convolution fusion | flops 7538212864 | bytes 18874368 | tf_op jit(solution)/shard_map/gd,gf->df/dot_general | solution.py:571
  637.7 19.3 %collective-permute-done.33 = bf16[896,1024]{1,0:T(8,128)(2,1)S(1)} collective-permute-done((bf16[896,1024]{1,0:T(8,128)(2,1)S(1)}, bf16[896,1024]{1,0:T(8,128)(2,1)S(1)}, u32[]{:S(2)}, u32[]{:S(2)}) %collective-permute-start.33) | collective-permute-done | bytes 1835040 | tf_op jit(solution)/shard_map/ppermute | solution.py:426
  662.5 28.6 %psum.21 = bf16[11,1024]{1,0:T(8,128)(2,1)S(1)} all-reduce(f32[11,1024]{1,0:T(8,128)S(1)} %pad_maximum_fusion.11), channel_id=1, replica_groups=mesh['expert'=8,'tensor'=4] {'tensor'}, use_global_device_ids=true, to_apply=%region_11.13 | all-reduce | flops 11264 | bytes 67584 | tf_op jit(solution)/shard_map/psum | solution.py:578
  702.2 40.1 %tree_attention_back.1 = bf16[3,2560,256]{2,1,0:T(8,128)(2,1)} custom-call(s32[8]{0:T(128)} %select_reduce_fusion.leaves_ref, bf16[3,2560,256]{2,1,0:T(8,128)(2,1)} %fusion.19.qkv_ref, bf16[2560,256]{1,0:T(8,128)(2,1)} %bitcast.215, bf16[2560,256]{1,0:T(8,128)(2,1)} %get-tuple-element.30.outs_ref, f32[2,2,1024]{2,1,0:T(2,128)} %get-tuple-element.38.trunk_log_ref, ...), custom_call_target="tpu_custom_call" | custom-call | tf_op jit(solution)/shard_map/tree_attention_back/pallas_call | solution.py:274
  772.1 25.9 %collective-permute-done.37 = bf16[112,1024]{1,0:T(8,128)(2,1)S(1)} collective-permute-done((bf16[112,1024]{1,0:T(8,128)(2,1)}, bf16[112,1024]{1,0:T(8,128)(2,1)S(1)}, u32[]{:S(2)}, u32[]{:S(2)}) %collective-permute-start.37) | collective-permute-done | bytes 229408 | tf_op jit(solution)/shard_map/ppermute | solution.py:463
  825.5 11.9 %collective-permute-done.55 = bf16[640,1024]{1,0:T(8,128)(2,1)} collective-permute-done((bf16[640,1024]{1,0:T(8,128)(2,1)}, bf16[640,1024]{1,0:T(8,128)(2,1)}, u32[]{:S(2)}, u32[]{:S(2)}) %collective-permute-start.55) | collective-permute-done | bytes 1310752 | tf_op jit(solution)/shard_map/ppermute | solution.py:426
  846.8 19.7 %psum.23 = f32[1024]{0:T(1024)} all-reduce(f32[1024]{0:T(1024)S(1)} %psum.22), channel_id=1, replica_groups=mesh['expert'=8,'tensor'=4] {'expert'}, use_global_device_ids=true, to_apply=%region_16.18 | all-reduce | flops 1024 | bytes 8192 | tf_op jit(solution)/shard_map/psum | solution.py:620
  (383 shorter events, 330.5 us)
Async XLA Ops:
  7.2 49.0 %all-gather.2.cloned.1.call-start = ((), (), s32[]{:S(2)}) async-start(), calls=%async_computation.2 | async-start | bytes 6553600 | tf_op jit(solution)/shard_map/all_gather | solution.py:505
  13.0 805.3 %reduce-scatter.9.cloned.1.call-start = ((), (), s32[]{:S(2)}) async-start(), calls=%async_computation.4 | async-start | bytes 4718592
  92.9 45.6 %collective-permute-start = (bf16[1280,1024]{1,0:T(8,128)(2,1)}, bf16[1280,1024]{1,0:T(8,128)(2,1)}, u32[]{:S(2)}, u32[]{:S(2)}) collective-permute-start(bf16[1280,1024]{1,0:T(8,128)(2,1)} %convolution_convert_fusion.1), channel_id=1, source_target_pairs={{0,1},{1,0},{2,3},{3,2},{4,5},{5,4},{6,7},{7,6},{8,9},{9,8},{10,11... | collective-permute-start | bytes 7864328 | tf_op jit(solution)/shard_map/ppermute | solution.py:422
  137.9 43.3 %collective-permute-start.30 = (bf16[896,1024]{1,0:T(8,128)(2,1)}, bf16[896,1024]{1,0:T(8,128)(2,1)}, u32[]{:S(2)}, u32[]{:S(2)}) collective-permute-start(bf16[896,1024]{1,0:T(8,128)(2,1)} %bitcast.38), channel_id=1, source_target_pairs={{0,2},{1,3},{2,0},{3,1},{4,6},{5,7},{6,4},{7,5},{8,10},{9,11},{10,... | collective-permute-start | bytes 5505032 | tf_op jit(solution)/shard_map/ppermute | solution.py:426
  144.9 58.0 %collective-permute-start.1 = (bf16[640,1024]{1,0:T(8,128)(2,1)}, bf16[640,1024]{1,0:T(8,128)(2,1)}, u32[]{:S(2)}, u32[]{:S(2)}) collective-permute-start(bf16[640,1024]{1,0:T(8,128)(2,1)} %fusion.61), channel_id=1, source_target_pairs={{0,2},{1,3},{2,0},{3,1},{4,6},{5,7},{6,4},{7,5},{8,10},{9,11},{10,... | collective-permute-start | bytes 3932168 | tf_op jit(solution)/shard_map/ppermute | solution.py:426
  185.5 156.0 %collective-permute-start.31 = (bf16[1792,1024]{1,0:T(8,128)(2,1)}, bf16[1792,1024]{1,0:T(8,128)(2,1)}, u32[]{:S(2)}, u32[]{:S(2)}) collective-permute-start(bf16[1792,1024]{1,0:T(8,128)(2,1)} %pad_maximum_fusion.3.ga_ref), channel_id=1, source_target_pairs={{0,1},{1,0},{2,3},{3,2},{4,5},{5,4},{6,7},{7,6},{8,9},{9,8},{10,11... | collective-permute-start | bytes 11010056 | tf_op jit(solution)/shard_map/ppermute | solution.py:422
  207.9 56.5 %collective-permute-start.2 = (bf16[640,1024]{1,0:T(8,128)(2,1)S(1)}, bf16[640,1024]{1,0:T(8,128)(2,1)S(1)}, u32[]{:S(2)}, u32[]{:S(2)}) collective-permute-start(bf16[640,1024]{1,0:T(8,128)(2,1)S(1)} %multiply_convert_fusion), channel_id=1, source_target_pairs={{0,2},{1,3},{2,0},{3,1},{4,6},{5,7},{6,4},{7,5},{8,10},{9,11},{10,... | collective-permute-start | bytes 3932168 | tf_op jit(solution)/shard_map/ppermute | solution.py:426
  337.8 76.7 %collective-permute-start.5 = (bf16[1280,1024]{1,0:T(8,128)(2,1)}, bf16[1280,1024]{1,0:T(8,128)(2,1)}, u32[]{:S(2)}, u32[]{:S(2)}) collective-permute-start(bf16[1280,1024]{1,0:T(8,128)(2,1)} %constant_dynamic-update-slice_fusion.ga_ref), channel_id=1, source_target_pairs={{0,1},{1,0},{2,3},{3,2},{4,5},{5,4},{6,7},{7,6},{8,9},{9,8},{10,11... | collective-permute-start | bytes 7864328 | tf_op jit(solution)/shard_map/ppermute | solution.py:422
  339.6 75.0 %collective-permute-start.3 = (bf16[1280,1024]{1,0:T(8,128)(2,1)}, bf16[1280,1024]{1,0:T(8,128)(2,1)}, u32[]{:S(2)}, u32[]{:S(2)}) collective-permute-start(bf16[1280,1024]{1,0:T(8,128)(2,1)} %pad_maximum_fusion.4.xa_ref), channel_id=1, source_target_pairs={{0,1},{1,0},{2,3},{3,2},{4,5},{5,4},{6,7},{7,6},{8,9},{9,8},{10,11... | collective-permute-start | bytes 7864328 | tf_op jit(solution)/shard_map/ppermute | solution.py:422
  409.7 56.3 %collective-permute-start.43 = (bf16[1792,1024]{1,0:T(8,128)(2,1)}, bf16[1792,1024]{1,0:T(8,128)(2,1)}, u32[]{:S(2)}, u32[]{:S(2)}) collective-permute-start(bf16[1792,1024]{1,0:T(8,128)(2,1)} %slice.300), channel_id=1, source_target_pairs={{0,1},{1,0},{2,3},{3,2},{4,5},{5,4},{6,7},{7,6},{8,9},{9,8},{10,11... | collective-permute-start | bytes 11010056 | tf_op jit(solution)/shard_map/ppermute | solution.py:422
  455.8 45.3 %collective-permute-start.41 = (bf16[1280,1024]{1,0:T(8,128)(2,1)}, bf16[1280,1024]{1,0:T(8,128)(2,1)}, u32[]{:S(2)}, u32[]{:S(2)}) collective-permute-start(bf16[1280,1024]{1,0:T(8,128)(2,1)} %slice.296), channel_id=1, source_target_pairs={{0,1},{1,0},{2,3},{3,2},{4,5},{5,4},{6,7},{7,6},{8,9},{9,8},{10,11... | collective-permute-start | bytes 7864328 | tf_op jit(solution)/shard_map/ppermute | solution.py:422
  474.3 43.2 %collective-permute-start.44 = (bf16[896,1024]{1,0:T(8,128)(2,1)}, bf16[896,1024]{1,0:T(8,128)(2,1)}, u32[]{:S(2)}, u32[]{:S(2)}) collective-permute-start(bf16[896,1024]{1,0:T(8,128)(2,1)} %slice.427), channel_id=1, source_target_pairs={{0,2},{1,3},{2,0},{3,1},{4,6},{5,7},{6,4},{7,5},{8,10},{9,11},{10,... | collective-permute-start | bytes 5505032 | tf_op jit(solution)/shard_map/ppermute | solution.py:426
  492.3 378.7 %reduce-scatter.7.cloned.1.call-start = ((), (), s32[]{:S(2)}) async-start(), calls=%async_computation.3 | async-start | bytes 2654208
  496.1 137.2 %collective-permute-start.6 = (bf16[1280,1024]{1,0:T(8,128)(2,1)}, bf16[1280,1024]{1,0:T(8,128)(2,1)S(1)}, u32[]{:S(2)}, u32[]{:S(2)}) collective-permute-start(bf16[1280,1024]{1,0:T(8,128)(2,1)} %slice.252), channel_id=1, source_target_pairs={{0,1},{1,0},{2,3},{3,2},{4,5},{5,4},{6,7},{7,6},{8,9},{9,8},{10,11... | collective-permute-start | bytes 7864328 | tf_op jit(solution)/shard_map/ppermute | solution.py:422
  500.6 102.0 %collective-permute-start.32 = (bf16[1792,1024]{1,0:T(8,128)(2,1)}, bf16[1792,1024]{1,0:T(8,128)(2,1)}, u32[]{:S(2)}, u32[]{:S(2)}) collective-permute-start(bf16[1792,1024]{1,0:T(8,128)(2,1)} %slice.283), channel_id=1, source_target_pairs={{0,1},{1,0},{2,3},{3,2},{4,5},{5,4},{6,7},{7,6},{8,9},{9,8},{10,11... | collective-permute-start | bytes 11010056 | tf_op jit(solution)/shard_map/ppermute | solution.py:422
  504.8 76.1 %collective-permute-start.42 = (bf16[640,1024]{1,0:T(8,128)(2,1)S(1)}, bf16[640,1024]{1,0:T(8,128)(2,1)S(1)}, u32[]{:S(2)}, u32[]{:S(2)}) collective-permute-start(bf16[640,1024]{1,0:T(8,128)(2,1)S(1)} %slice.429), channel_id=1, source_target_pairs={{0,2},{1,3},{2,0},{3,1},{4,6},{5,7},{6,4},{7,5},{8,10},{9,11},{10,... | collective-permute-start | bytes 3932168 | tf_op jit(solution)/shard_map/ppermute | solution.py:426
  606.7 50.3 %collective-permute-start.33 = (bf16[896,1024]{1,0:T(8,128)(2,1)S(1)}, bf16[896,1024]{1,0:T(8,128)(2,1)S(1)}, u32[]{:S(2)}, u32[]{:S(2)}) collective-permute-start(bf16[896,1024]{1,0:T(8,128)(2,1)S(1)} %slice.428), channel_id=1, source_target_pairs={{0,2},{1,3},{2,0},{3,1},{4,6},{5,7},{6,4},{7,5},{8,10},{9,11},{10,... | collective-permute-start | bytes 5505032 | tf_op jit(solution)/shard_map/ppermute | solution.py:426
  619.7 71.4 %collective-permute-start.53 = (bf16[1280,1024]{1,0:T(8,128)(2,1)}, bf16[1280,1024]{1,0:T(8,128)(2,1)}, u32[]{:S(2)}, u32[]{:S(2)}) collective-permute-start(bf16[1280,1024]{1,0:T(8,128)(2,1)} %pad_maximum_fusion.5), channel_id=1, source_target_pairs={{0,1},{1,0},{2,3},{3,2},{4,5},{5,4},{6,7},{7,6},{8,9},{9,8},{10,11... | collective-permute-start | bytes 7864328 | tf_op jit(solution)/shard_map/ppermute | solution.py:422
  636.0 178.0 %collective-permute-start.7 = (bf16[640,1024]{1,0:T(8,128)(2,1)}, bf16[640,1024]{1,0:T(8,128)(2,1)}, u32[]{:S(2)}, u32[]{:S(2)}) collective-permute-start(bf16[640,1024]{1,0:T(8,128)(2,1)} %slice.430), channel_id=1, source_target_pairs={{0,2},{1,3},{2,0},{3,1},{4,6},{5,7},{6,4},{7,5},{8,10},{9,11},{10,... | collective-permute-start | bytes 3932168 | tf_op jit(solution)/shard_map/ppermute | solution.py:426
  658.8 105.1 %collective-permute-start.34 = (bf16[112,1024]{1,0:T(8,128)(2,1)}, bf16[112,1024]{1,0:T(8,128)(2,1)}, u32[]{:S(2)}, u32[]{:S(2)}) collective-permute-start(bf16[112,1024]{1,0:T(8,128)(2,1)} %get-tuple-element.112), channel_id=1, source_target_pairs={{0,28},{4,0},{8,4},{12,8},{16,12},{20,16},{24,20},{28,24},{1,29},{... | collective-permute-start | bytes 688136 | tf_op jit(solution)/shard_map/ppermute | solution.py:463
  662.4 102.6 %collective-permute-start.35 = (bf16[112,1024]{1,0:T(8,128)(2,1)}, bf16[112,1024]{1,0:T(8,128)(2,1)}, u32[]{:S(2)}, u32[]{:S(2)}) collective-permute-start(bf16[112,1024]{1,0:T(8,128)(2,1)} %get-tuple-element.111), channel_id=1, source_target_pairs={{0,24},{4,28},{8,0},{12,4},{16,8},{20,12},{24,16},{28,20},{1,25},{... | collective-permute-start | bytes 688136 | tf_op jit(solution)/shard_map/ppermute | solution.py:463
  662.4 108.2 %collective-permute-start.36 = (bf16[112,1024]{1,0:T(8,128)(2,1)}, bf16[112,1024]{1,0:T(8,128)(2,1)}, u32[]{:S(2)}, u32[]{:S(2)}) collective-permute-start(bf16[112,1024]{1,0:T(8,128)(2,1)} %get-tuple-element.110), channel_id=1, source_target_pairs={{0,20},{4,24},{8,28},{12,0},{16,4},{20,8},{24,12},{28,16},{1,21},{... | collective-permute-start | bytes 688136 | tf_op jit(solution)/shard_map/ppermute | solution.py:463
  749.8 52.0 %collective-permute-start.54 = (bf16[1280,1024]{1,0:T(8,128)(2,1)}, bf16[1280,1024]{1,0:T(8,128)(2,1)}, u32[]{:S(2)}, u32[]{:S(2)}) collective-permute-start(bf16[1280,1024]{1,0:T(8,128)(2,1)} %bitcast_convert_fusion), channel_id=1, source_target_pairs={{0,1},{1,0},{2,3},{3,2},{4,5},{5,4},{6,7},{7,6},{8,9},{9,8},{10,11... | collective-permute-start | bytes 7864328 | tf_op jit(solution)/shard_map/ppermute | solution.py:422
  765.1 36.7 %collective-permute-start.38 = (bf16[112,1024]{1,0:T(8,128)(2,1)}, bf16[112,1024]{1,0:T(8,128)(2,1)S(1)}, u32[]{:S(2)}, u32[]{:S(2)}) collective-permute-start(bf16[112,1024]{1,0:T(8,128)(2,1)} %get-tuple-element.108), channel_id=1, source_target_pairs={{0,12},{4,16},{8,20},{12,24},{16,28},{20,0},{24,4},{28,8},{1,13},{... | collective-permute-start | bytes 688136 | tf_op jit(solution)/shard_map/ppermute | solution.py:463
  (96 other events, 1719.6 us)
Sparse Core Ops, SparseCore 0:
  13.1 43.1 all-gather.1
  492.4 116.9 reduce-scatter.8
  764.0 85.3 reduce-scatter.6

commit v3 on v2

--- a/solution.py
+++ b/solution.py
@@ -124,7 +124,26 @@
     return rows * jnp.asarray(HEAD_DIM ** (-0.5), BF16)
 
 
-def forward_kernel(leaves_ref, qkv_ref, out_ref, trunk_log_ref, family_log_ref, values_t_ref):
+def quarter_rows(leaves_ref, offset):
+    quarter = TREE_LEN // 4
+    return pl.ds(pl.multiple_of((leaves_ref[2 * BRANCHES] ^ offset) * quarter, quarter), quarter)
+
+
+def forward_kernel(
+    leaves_ref,
+    near_ref,
+    far_ref,
+    near_out_ref,
+    far_out_ref,
+    trunk_log_ref,
+    family_log_ref,
+    qkv_ref,
+    out_ref,
+    values_t_ref,
+):
+    for offset in range(4):
+        half_ref = near_ref if offset < 2 else far_ref
+        qkv_ref[:, quarter_rows(leaves_ref, offset), :] = half_ref[:, offset % 2]
     transpose_into(values_t_ref, qkv_ref, 2)
     for block in range(TRUNK // QROWS):
         first = block * QROWS
@@ -143,31 +162,58 @@
         return carry
 
     lax.fori_loop(0, BRANCHES, one_family, 0)
-
-
-def attention_forward(leaves, qkv_rows):
-    width = qkv_rows.shape[2]
+    for offset in range(4):
+        half_ref = near_out_ref if offset < 2 else far_out_ref
+        half_ref[offset % 2] = out_ref[quarter_rows(leaves_ref, offset), :]
+
+
+def halves_spec(parts):
+    quarter = TREE_LEN // 4
+    if parts == 1:
+        return pl.BlockSpec((2, quarter, PAIR), lambda p, leaves: (0, 0, p))
+    return pl.BlockSpec((parts, 2, quarter, PAIR), lambda p, leaves: (0, 0, 0, p))
+
+
+def attention_cost(products):
+    visited = TRUNK * (TRUNK + QROWS) // 2 + BRANCHES * FAMILY * (TRUNK + SEG)
+    return pl.CostEstimate(
+        flops=2 * products * 4 * visited * 2 * PAIR,
+        transcendentals=4 * visited,
+        bytes_accessed=8 * TREE_LEN * 4 * HEAD_DIM * 2,
+    )
+
+
+def attention_forward(leaves, near, far):
+    width = near.shape[3]
+    quarter = TREE_LEN // 4
     pairs = width // PAIR
     return pl.pallas_call(
         forward_kernel,
         grid_spec=pltpu.PrefetchScalarGridSpec(
             num_scalar_prefetch=1,
             grid=(pairs,),
-            in_specs=[pl.BlockSpec((3, TREE_LEN, PAIR), lambda p, leaves: (0, 0, p))],
+            in_specs=[halves_spec(3), halves_spec(3)],
             out_specs=[
-                pl.BlockSpec((TREE_LEN, PAIR), lambda p, leaves: (0, p)),
+                halves_spec(1),
+                halves_spec(1),
                 pl.BlockSpec((1, 2, TRUNK), lambda p, leaves: (p, 0, 0)),
                 pl.BlockSpec((1, BRANCHES, 2, FAMILY), lambda p, leaves: (p, 0, 0, 0)),
             ],
-            scratch_shapes=[pltpu.VMEM((PAIR, TREE_LEN), BF16)],
+            scratch_shapes=[
+                pltpu.VMEM((3, TREE_LEN, PAIR), BF16),
+                pltpu.VMEM((TREE_LEN, PAIR), BF16),
+                pltpu.VMEM((PAIR, TREE_LEN), BF16),
+            ],
         ),
         out_shape=[
-            jax.ShapeDtypeStruct((TREE_LEN, width), BF16),
+            jax.ShapeDtypeStruct((2, quarter, width), BF16),
+            jax.ShapeDtypeStruct((2, quarter, width), BF16),
             jax.ShapeDtypeStruct((pairs, 2, TRUNK), F32),
             jax.ShapeDtypeStruct((pairs, BRANCHES, 2, FAMILY), F32),
         ],
+        cost_estimate=attention_cost(2),
         name="tree_attention",
-    )(leaves, qkv_rows)
+    )(leaves, near, far)
 
 
 def backward_block(qkv_ref, keys_t_ref, queries, grads, outs, logs, groups):
@@ -209,16 +255,30 @@
 
 def backward_kernel(
     leaves_ref,
+    near_ref,
+    far_ref,
+    near_grads_ref,
+    far_grads_ref,
+    near_outs_ref,
+    far_outs_ref,
+    trunk_log_ref,
+    family_log_ref,
+    near_result_ref,
+    far_result_ref,
     qkv_ref,
     grads_ref,
     outs_ref,
-    trunk_log_ref,
-    family_log_ref,
     result_ref,
     keys_t_ref,
     trunk_keys_ref,
     trunk_values_ref,
 ):
+    for offset in range(4):
+        rows = quarter_rows(leaves_ref, offset)
+        at = offset % 2
+        qkv_ref[:, rows, :] = (near_ref if offset < 2 else far_ref)[:, at]
+        grads_ref[rows, :] = (near_grads_ref if offset < 2 else far_grads_ref)[at]
+        outs_ref[rows, :] = (near_outs_ref if offset < 2 else far_outs_ref)[at]
     transpose_into(keys_t_ref, qkv_ref, 1)
     trunk_keys_ref[...] = jnp.zeros_like(trunk_keys_ref)
     trunk_values_ref[...] = jnp.zeros_like(trunk_values_ref)
@@ -264,35 +324,43 @@
     lax.fori_loop(0, BRANCHES, one_family, 0)
     result_ref[1, pl.ds(0, TRUNK), :] = trunk_keys_ref[...].astype(BF16)
     result_ref[2, pl.ds(0, TRUNK), :] = trunk_values_ref[...].astype(BF16)
-
-
-def attention_backward(leaves, qkv_rows, grads, outs, trunk_log, family_log):
-    width = qkv_rows.shape[2]
-    pairs = width // PAIR
-    whole = pl.BlockSpec((3, TREE_LEN, PAIR), lambda p, leaves: (0, 0, p))
-    rows = pl.BlockSpec((TREE_LEN, PAIR), lambda p, leaves: (0, p))
+    for offset in range(4):
+        half_ref = near_result_ref if offset < 2 else far_result_ref
+        half_ref[:, offset % 2] = result_ref[:, quarter_rows(leaves_ref, offset), :]
+
+
+def attention_backward(leaves, near, far, near_grads, far_grads, near_outs, far_outs, logs):
+    pairs = near.shape[3] // PAIR
     return pl.pallas_call(
         backward_kernel,
         grid_spec=pltpu.PrefetchScalarGridSpec(
             num_scalar_prefetch=1,
             grid=(pairs,),
             in_specs=[
-                whole,
-                rows,
-                rows,
+                halves_spec(3),
+                halves_spec(3),
+                halves_spec(1),
+                halves_spec(1),
+                halves_spec(1),
+                halves_spec(1),
                 pl.BlockSpec((1, 2, TRUNK), lambda p, leaves: (p, 0, 0)),
                 pl.BlockSpec((1, BRANCHES, 2, FAMILY), lambda p, leaves: (p, 0, 0, 0)),
             ],
-            out_specs=whole,
+            out_specs=[halves_spec(3), halves_spec(3)],
             scratch_shapes=[
+                pltpu.VMEM((3, TREE_LEN, PAIR), BF16),
+                pltpu.VMEM((TREE_LEN, PAIR), BF16),
+                pltpu.VMEM((TREE_LEN, PAIR), BF16),
+                pltpu.VMEM((3, TREE_LEN, PAIR), BF16),
                 pltpu.VMEM((PAIR, TREE_LEN), BF16),
                 pltpu.VMEM((TRUNK, PAIR), F32),
                 pltpu.VMEM((TRUNK, PAIR), F32),
             ],
         ),
-        out_shape=jax.ShapeDtypeStruct(qkv_rows.shape, BF16),
+        out_shape=[jax.ShapeDtypeStruct(near.shape, BF16), jax.ShapeDtypeStruct(far.shape, BF16)],
+        cost_estimate=attention_cost(5),
         name="tree_attention_back",
-    )(leaves, qkv_rows, grads, outs, trunk_log, family_log)
+    )(leaves, near, far, near_grads, far_grads, near_outs, far_outs, *logs)
 
 
 def leaf_order(parents_row):
@@ -322,12 +390,30 @@
     return lane, first, second, probs, gate
 
 
-def feed_kernel(experts, routed, expert_ref, xa_ref, xb_ref, ga_ref, gb_ref, head_ref, up_ref, down_ref,
-                out_ref, back_ref, active_ref, pre_ref, grad_ref, head_grad_ref):
+def feed_kernel(
+    experts,
+    routed,
+    expert_ref,
+    own_ref,
+    side_ref,
+    own_grads_ref,
+    side_grads_ref,
+    head_ref,
+    up_ref,
+    down_ref,
+    own_out_ref,
+    side_out_ref,
+    own_back_ref,
+    side_back_ref,
+    active_ref,
+    pre_ref,
+    grad_ref,
+    head_grad_ref,
+):
     step = pl.program_id(0)
     early = step < pl.num_programs(0) // 2
-    rows = jnp.where(early, xa_ref[...], xb_ref[...])
-    grads = jnp.where(early, ga_ref[...], gb_ref[...]).astype(F32)
+    rows = jnp.where(early, own_ref[...], side_ref[...])
+    grads = jnp.where(early, own_grads_ref[...], side_grads_ref[...]).astype(F32)
     logits = dot_nn(rows, head_ref[...])
     expert = expert_ref[0] if routed else None
     lane, first, second, probs, gate = gates(logits, experts, expert)
@@ -343,7 +429,7 @@
     grad_pre = (grad_active * slope).astype(BF16)
     pre_ref[...] = grad_pre
     out = dot_nn(active, down_ref[...])
-    out_ref[...] = (coef * out).astype(BF16)
+    out_rows = (coef * out).astype(BF16)
     inner = jnp.sum(grads * out, axis=1, keepdims=True)
     swing = first * second * inner
     if routed:
@@ -351,9 +437,21 @@
     grad_logits = jnp.where(lane == experts, swing, jnp.where(lane == experts + 1, -swing, 0.0))
     if routed:
         picked = jnp.where(lane == expert, 1.0, 0.0) - gate
-        grad_logits = grad_logits + jnp.where(lane < experts, probs * picked * (second * inner), 0.0)
+        grad_logits = grad_logits + jnp.where(
+            lane < experts, probs * picked * (second * inner), 0.0
+        )
     back = dot_nt(grad_pre, up_ref[...]) + dot_nt(grad_logits.astype(BF16), head_ref[...])
-    back_ref[...] = back.astype(BF16)
+    back_rows = back.astype(BF16)
+
+    @pl.when(early)
+    def _():
+        own_out_ref[...] = out_rows
+        own_back_ref[...] = back_rows
+
+    @pl.when(jnp.logical_not(early))
+    def _():
+        side_out_ref[...] = out_rows
+        side_back_ref[...] = back_rows
 
     @pl.when(step == 0)
     def _():
@@ -362,11 +460,10 @@
     head_grad_ref[...] += dot_nn(grad_logits.T.astype(BF16), rows)
 
 
-def feed(xa, xb, ga, gb, head, up, down, experts, expert, size):
-    total = 2 * xa.shape[0]
+def feed(own, side, own_grads, side_grads, head, up, down, experts, expert, size):
+    count = own.shape[0]
     width, hidden = up.shape
-    steps = total // size
-    half = steps // 2
+    half = count // size
     lanes = head.shape[1]
     routed = expert is not None
     pick = jnp.reshape(expert, (1,)) if routed else jnp.zeros((1,), jnp.int32)
@@ -378,29 +475,55 @@
 
     wide = pl.BlockSpec((size, width), lambda i, pick: (i, 0))
     deep = pl.BlockSpec((size, hidden), lambda i, pick: (i, 0))
+    quarter = jax.ShapeDtypeStruct((count, width), BF16)
     return pl.pallas_call(
         functools.partial(feed_kernel, experts, routed),
         grid_spec=pltpu.PrefetchScalarGridSpec(
             num_scalar_prefetch=1,
-            grid=(steps,),
-            in_specs=[early, late, early, late, held((width, lanes)), held((width, hidden)), held((hidden, width))],
-            out_specs=[wide, wide, deep, deep, wide, pl.BlockSpec((lanes, width), lambda i, pick: (0, 0))],
+            grid=(2 * half,),
+            in_specs=[
+                early,
+                late,
+                early,
+                late,
+                held((width, lanes)),
+                held((width, hidden)),
+                held((hidden, width)),
+            ],
+            out_specs=[
+                early,
+                late,
+                early,
+                late,
+                deep,
+                deep,
+                wide,
+                pl.BlockSpec((lanes, width), lambda i, pick: (0, 0)),
+            ],
         ),
         out_shape=[
-            jax.ShapeDtypeStruct((total, width), BF16),
-            jax.ShapeDtypeStruct((total, width), BF16),
-            jax.ShapeDtypeStruct((total, hidden), BF16),
-            jax.ShapeDtypeStruct((total, hidden), BF16),
-            jax.ShapeDtypeStruct((total, width), BF16),
+            quarter,
+            quarter,
+            quarter,
+            quarter,
+            jax.ShapeDtypeStruct((2 * count, hidden), BF16),
+            jax.ShapeDtypeStruct((2 * count, hidden), BF16),
+            jax.ShapeDtypeStruct((2 * count, width), BF16),
             jax.ShapeDtypeStruct((lanes, width), F32),
         ],
+        cost_estimate=pl.CostEstimate(
+            flops=16 * count * width * hidden,
+            transcendentals=4 * count * hidden,
+            bytes_accessed=2 * (8 * count * width + 4 * count * hidden + 2 * width * hidden),
+        ),
         compiler_params=pltpu.CompilerParams(vmem_limit_bytes=60 * 1024 * 1024),
         name="feed_routed" if routed else "feed_dense",
-    )(pick, xa, xb, ga, gb, head, up, down)
+    )(pick, own, side, own_grads, side_grads, head, up, down)
 
 
 LANES = 128
-DIRECT = 8
+DENSE_ROWS = 320
+EXPERT_ROWS = 448
 
 
 def norm_parts(values):
@@ -418,6 +541,10 @@
     return inverse * (grad_scaled - first_mean - scaled * second)
 
 
+def after(value, *others):
+    return lax.optimization_barrier((value, *others))[0]
+
+
 def from_side(values):
     return lax.ppermute(values, "tensor", [(i, i ^ 1) for i in range(4)])
 
@@ -426,42 +553,26 @@
     return lax.ppermute(values, "tensor", [(i, i ^ 2) for i in range(4)])
 
 
-def both_halves(own):
-    near = jnp.concatenate([own, from_far(own)], axis=0)
-    return near, from_side(near)
-
-
-def sum_to_owner(values):
-    half = values.shape[0] // 2
-    quarter = half // 2
-    near = values[:half].astype(F32) + from_side(values[half:]).astype(F32)
-    return near[:quarter] + from_far(near[quarter:].astype(BF16)).astype(F32)
-
-
-def own_core(values, axis, flip):
-    core = lax.axis_index("tensor") % 2
-    return lax.dynamic_index_in_dim(values, 1 - core if flip else core, axis, keepdims=False)
-
-
-def sum_tree_to_owner(partial):
-    sent = partial(True).astype(BF16)
-    near = partial(False) + from_side(sent).astype(F32)
-    near = near.reshape(2, -1, near.shape[1])
-    place = lax.axis_index("tensor") // 2
-    kept = lax.dynamic_index_in_dim(near, place, 0, keepdims=False)
-    far = lax.dynamic_index_in_dim(near, 1 - place, 0, keepdims=False)
-    return kept + from_far(far.astype(BF16)).astype(F32)
-
-
-def exchange(blocks, back):
-    count = lax.axis_size("expert")
-    if count > DIRECT:
-        return lax.all_to_all(blocks, "expert", split_axis=0, concat_axis=0, tiled=True)
-    arrived = [blocks[0]]
-    for step in range(1, count):
-        pairs = [(i, (i - step if back else i + step) % count) for i in range(count)]
-        arrived.append(lax.ppermute(blocks[step], "expert", pairs))
-    return jnp.stack(arrived)
+def plus_side(own, side):
+    return own.astype(F32) + from_side(side.astype(BF16)).astype(F32)
+
+
+def sum_over(values, axis):
+    count, step = lax.axis_size(axis), 1
+    while step < count:
+        pairs = [(i, i ^ step) for i in range(count)]
+        values = values + lax.ppermute(values, axis, pairs)
+        step *= 2
+    return values
+
+
+def exchange(blocks):
+    return lax.all_to_all(blocks, "expert", split_axis=0, concat_axis=0, tiled=True)
+
+
+def scatter_sum(strips):
+    strips = strips.astype(BF16)
+    return lax.psum_scatter(strips, "expert", scatter_dimension=0, tiled=True).astype(F32)
 
 
 def slots_of(expert_ids, experts, capacity):
@@ -471,8 +582,7 @@
     before = (at[None, :] < at[:, None]).astype(BF16)
     earlier = jnp.dot(before, chosen.astype(BF16), preferred_element_type=F32)
     slot = jnp.sum(jnp.where(chosen, earlier, 0.0), axis=1).astype(jnp.int32)
-    first = lax.axis_index("expert") if experts <= DIRECT else 0
-    place = ((expert_ids - first) % experts) * capacity + slot
+    place = expert_ids * capacity + slot
     places = jnp.arange(experts * capacity, dtype=jnp.int32)
     return (places[:, None] == place[None, :]).astype(BF16)
 
@@ -498,113 +608,179 @@
     experts = w_router.shape[1]
     capacity = max(2, tok_dev * 7 // (5 * experts))
     heads_width = w_qkv.shape[2]
-    leaves = leaf_order(parents[0])
+    hidden = w_up.shape[1]
+    leaves = jnp.concatenate([leaf_order(parents[0]), mine.astype(jnp.int32)[None]])
 
     scaled_one, inverse_one = norm_parts(tokens.astype(F32))
     normed_own = (scaled_one * ln_attn).astype(BF16)
-    normed_one = lax.all_gather(normed_own, "tensor", axis=0, tiled=True)
+    normed_far = from_far(normed_own)
+    near_one = jnp.concatenate([normed_own, from_side(normed_own)], axis=0)
+    far_one = jnp.concatenate([normed_far, from_side(normed_far)], axis=0)
 
     quarter_ids = routes[:, 0].reshape(4, tok_dev)
-    own_slots = slots_of(
-        lax.dynamic_index_in_dim(quarter_ids, mine, 0, keepdims=False), experts, capacity
-    )
-    far_slots = slots_of(
-        lax.dynamic_index_in_dim(quarter_ids, mine ^ 2, 0, keepdims=False), experts, capacity
-    )
+
+    def slots_at(offset):
+        ids = lax.dynamic_index_in_dim(quarter_ids, mine ^ offset, 0, keepdims=False)
+        return slots_of(ids, experts, capacity)
+
+    own_slots, far_slots = slots_at(0), slots_at(2)
 
     def dispatch(slots, rows):
         placed = jnp.dot(slots, rows, preferred_element_type=F32).astype(BF16)
-        return exchange(placed.reshape(experts, capacity, width), False).reshape(-1, width)
-
-    grads_near, grads_side = both_halves(dispatch(own_slots, cotangent))
-
-    qkv_rows = jnp.einsum("td,sdc->stc", normed_one, w_qkv, preferred_element_type=F32).astype(BF16)
-    attended, trunk_log, family_log = attention_forward(leaves, qkv_rows)
-    attended_view = attended.reshape(2, 2, tok_dev, heads_width)
-
-    def branch_part(flip):
-        rows = own_core(attended_view, 1, flip).reshape(2 * tok_dev, heads_width)
+        return exchange(placed.reshape(experts, capacity, width)).reshape(-1, width)
+
+    own_grads = dispatch(own_slots, cotangent)
+    cotangent_side = from_side(cotangent)
+
+    def project(rows):
+        qkv = jnp.einsum("td,sdc->stc", rows, w_qkv, preferred_element_type=F32)
+        return qkv.astype(BF16).reshape(3, 2, tok_dev, heads_width)
+
+    near_qkv, far_qkv = project(near_one), project(far_one)
+    cotangent_far = from_far(after(cotangent, normed_far))
+    near_out, far_out, *logs = attention_forward(leaves, near_qkv, far_qkv)
+    far_out, own_grads, cotangent_far, cotangent_side = lax.optimization_barrier(
+        (far_out, own_grads, cotangent_far, cotangent_side)
+    )
+
+    def branch_part(rows):
         return jnp.dot(rows, w_out, preferred_element_type=F32)
 
-    residual = tokens.astype(F32) + sum_tree_to_owner(branch_part)
-    cotangent_near, cotangent_side = both_halves(cotangent)
+    far_sum = plus_side(branch_part(far_out[0]), branch_part(far_out[1])).astype(BF16)
+    branch = plus_side(branch_part(near_out[0]), branch_part(near_out[1]))
+    branch_far = from_far(far_sum)
+    side_grads = from_side(own_grads)
+    cotangent_corner = from_side(cotangent_far)
+    branch_far, side_grads, cotangent_corner = lax.optimization_barrier(
+        (branch_far, side_grads, cotangent_corner)
+    )
+    residual = tokens.astype(F32) + (branch + branch_far.astype(F32))
 
     scaled_two, inverse_two = norm_parts(residual)
     normed_two = (scaled_two * ln_mlp).astype(BF16)
-    own_arrived = dispatch(own_slots, normed_two)
-    normed_far = from_far(normed_two)
-    near_arrived = jnp.concatenate([own_arrived, dispatch(far_slots, normed_far)], axis=0)
-    side_arrived = from_side(near_arrived)
-    normed_near = jnp.concatenate([normed_two, normed_far], axis=0)
-    normed_side = from_side(normed_near)
+    normed_two_far = from_far(normed_two)
+    normed_two_side = from_side(normed_two)
+    normed_two_corner = from_side(normed_two_far)
+    own_rows = dispatch(own_slots, normed_two)
+    far_rows = from_far(own_rows)
+    far_grads = dispatch(far_slots, after(cotangent_far, own_rows))
 
     lanes = -(-(experts + 2) // LANES) * LANES
     head = jnp.concatenate(
         [w_router, w_mix, jnp.zeros((width, lanes - experts - 2), BF16)], axis=1
     )
-    dense_out, dense_back, dense_active, dense_pre, dense_grad, dense_head = feed(
-        normed_near, normed_side, cotangent_near, cotangent_side, head, w_up, w_down, experts, None, tok_dev * 2 // 5
-    )
+
+    def dense(own, side, own_cotangent, side_cotangent):
+        return feed(
+            own, side, own_cotangent, side_cotangent, head, w_up, w_down, experts, None, DENSE_ROWS
+        )
+
+    near_dense = dense(normed_two, normed_two_side, cotangent, cotangent_side)
+    far_dense = dense(
+        after(normed_two_far, near_dense[2]), normed_two_corner, cotangent_far, cotangent_corner
+    )
+
+    def weight_grads(near_left, far_left, near_right, far_right):
+        product = functools.partial(jnp.einsum, "gd,gf->df", preferred_element_type=F32)
+        return product(near_left, near_right) + product(far_left, far_right)
+
+    near_two = jnp.concatenate([normed_two, normed_two_side], axis=0)
+    far_two = jnp.concatenate([normed_two_far, normed_two_corner], axis=0)
+    grad_up = weight_grads(near_two, far_two, near_dense[5], far_dense[5])
+    grad_down = weight_grads(near_dense[6], far_dense[6], near_dense[4], far_dense[4])
+    dense_grads = jnp.concatenate([grad_up.astype(BF16), grad_down.astype(BF16)], axis=1)
+
     expert = lax.axis_index("expert").astype(jnp.int32)
-    expert_out, expert_back, expert_active, expert_pre, expert_grad, expert_head = feed(
-        near_arrived, side_arrived, grads_near, grads_side, head, ex_up[0], ex_down[0], experts, expert,
-        near_arrived.shape[0] // 7,
-    )
-
-    def returned(partial):
-        rows = sum_to_owner(partial).astype(BF16).reshape(experts, capacity, width)
-        rows = exchange(rows, True).reshape(-1, width)
-        return lax.dot_general(own_slots, rows, (((0,), (0,)), ((), ())), preferred_element_type=F32)
-
-    grad_normed_two = sum_to_owner(dense_back) + returned(expert_back)
-
-    normed_rows = jnp.concatenate([normed_near, normed_side], axis=0)
-    grad_up = jnp.einsum("gd,gf->df", normed_rows, dense_pre, preferred_element_type=F32)
-    grad_down = jnp.einsum("gd,gf->df", dense_grad, dense_active, preferred_element_type=F32)
-    dense_grads = lax.psum_scatter(
-        jnp.concatenate([grad_up.astype(BF16), grad_down.astype(BF16)], axis=1),
-        "expert",
-        scatter_dimension=0,
-        tiled=True,
-    ).astype(F32)
-    expert_rows = jnp.concatenate([near_arrived, side_arrived], axis=0)
-    grad_ex_up = jnp.einsum("gd,gf->df", expert_rows, expert_pre, preferred_element_type=F32)[None]
-    grad_ex_down = jnp.einsum("gf,gd->fd", expert_active, expert_grad, preferred_element_type=F32)[None]
+
+    def routed(own, side, own_cotangent, side_cotangent):
+        return feed(
+            own,
+            side,
+            own_cotangent,
+            side_cotangent,
+            head,
+            ex_up[0],
+            ex_down[0],
+            experts,
+            expert,
+            EXPERT_ROWS,
+        )
+
+    far_rows, dense_grads = lax.optimization_barrier((far_rows, dense_grads))
+    dense_grads = scatter_sum(dense_grads)
+    corner_rows = from_side(far_rows)
+    far_expert = routed(far_rows, corner_rows, far_grads, from_side(far_grads))
+    side_rows = from_side(own_rows)
+    near_expert = routed(after(own_rows, far_expert[2]), side_rows, own_grads, side_grads)
+
+    def chip_sum(parts, place, *others):
+        return plus_side(parts[place], after(parts[place + 1], *others))
+
+    def returned(rows):
+        rows = rows.astype(BF16).reshape(experts, capacity, width)
+        rows = exchange(rows).reshape(-1, width)
+        return lax.dot_general(
+            own_slots, rows, (((0,), (0,)), ((), ())), preferred_element_type=F32
+        )
+
+    dense_back = chip_sum(near_dense, 2) + from_far(chip_sum(far_dense, 2).astype(BF16)).astype(F32)
+    far_back = chip_sum(far_expert, 2).astype(BF16)
+    expert_back = chip_sum(near_expert, 2) + from_far(far_back).astype(F32)
+    grad_normed_two = dense_back + returned(expert_back)
+    far_dense_out = chip_sum(far_dense, 0, far_back).astype(BF16)
+    far_expert_out = chip_sum(far_expert, 0, far_back).astype(BF16)
+    dense_out = chip_sum(near_dense, 0, far_back) + from_far(far_dense_out).astype(F32)
+    expert_out = chip_sum(near_expert, 0, expert_back) + from_far(far_expert_out).astype(F32)
+    expert_out = returned(after(expert_out, grad_normed_two))
+
+    near_tokens = jnp.concatenate([own_rows, side_rows], axis=0)
+    far_tokens = jnp.concatenate([far_rows, corner_rows], axis=0)
+    grad_ex_up = weight_grads(near_tokens, far_tokens, near_expert[5], far_expert[5])[None]
+    grad_ex_down = weight_grads(near_expert[4], far_expert[4], near_expert[6], far_expert[6])[None]
 
     gain_two = jnp.sum(grad_normed_two * scaled_two, axis=0)
-    grad_residual = cotangent.astype(F32) + norm_back(grad_normed_two, ln_mlp, scaled_two, inverse_two)
-    branch_near, branch_side = both_halves(grad_residual.astype(BF16))
-    grad_branch = jnp.concatenate([branch_near, branch_side], axis=0)
-    small = lax.psum(
-        jnp.concatenate([(dense_head + expert_head)[: experts + 2], gain_two[None]], axis=0), "tensor"
-    )
-
-    offsets = jnp.arange(4, dtype=jnp.int32) ^ mine
-    place_of = (offsets % 2) * 2 + offsets // 2
-    grad_attended = jnp.einsum("gd,cd->gc", grad_branch, w_out, preferred_element_type=F32)
-    grad_attended = grad_attended.astype(BF16).reshape(4, tok_dev, heads_width)
-    grad_attended = jnp.take(grad_attended, place_of, axis=0).reshape(4 * tok_dev, heads_width)
-    quarter_at = jnp.asarray([0, 2, 1, 3], jnp.int32) ^ mine
-    attended_rows = jnp.take(
-        attended.reshape(4, tok_dev, heads_width), quarter_at, axis=0
-    ).reshape(4 * tok_dev, heads_width)
-    grad_w_out = jnp.einsum("gd,gc->dc", grad_branch, attended_rows, preferred_element_type=F32)
-
-    grad_attended, small = lax.optimization_barrier((grad_attended, small))
-    grad_qkv_rows = attention_backward(
-        leaves, qkv_rows, grad_attended, attended, trunk_log, family_log
-    )
-    grad_view = grad_qkv_rows.reshape(3, 2, 2, tok_dev, heads_width)
-
-    def normed_part(flip):
-        rows = own_core(grad_view, 2, flip).reshape(3, 2 * tok_dev, heads_width)
-        return jnp.einsum("sgc,sdc->gd", rows, w_qkv, preferred_element_type=F32)
-
-    grad_normed_one = sum_tree_to_owner(normed_part)
-    grad_w_qkv = jnp.einsum("gd,sgc->dsc", normed_one, grad_qkv_rows, preferred_element_type=F32)
+    grad_residual = cotangent.astype(F32) + norm_back(
+        grad_normed_two, ln_mlp, scaled_two, inverse_two
+    )
+    grad_branch = grad_residual.astype(BF16)
+    grad_branch_far = from_far(grad_branch)
+    near_branch = jnp.concatenate([grad_branch, from_side(grad_branch)], axis=0)
+    far_branch = jnp.concatenate([grad_branch_far, from_side(grad_branch_far)], axis=0)
+    head_grads = near_dense[7] + far_dense[7] + near_expert[7] + far_expert[7]
+    small = jnp.concatenate([head_grads[: experts + 2], gain_two[None]], axis=0)
+    small = sum_over(small, "tensor")
+
+    def into_heads(rows):
+        grads = jnp.einsum("gd,cd->gc", rows, w_out, preferred_element_type=F32)
+        return grads.astype(BF16).reshape(2, tok_dev, heads_width)
+
+    near_heads, far_heads = into_heads(near_branch), into_heads(far_branch)
+    near_heads, grad_ex_up, grad_ex_down, small, dense_grads = lax.optimization_barrier(
+        (near_heads, grad_ex_up, grad_ex_down, small, dense_grads)
+    )
+    near_result, far_result = attention_backward(
+        leaves, near_qkv, far_qkv, near_heads, far_heads, near_out, far_out, logs
+    )
+    far_result, expert_out = lax.optimization_barrier((far_result, expert_out))
+    out = (residual + dense_out + expert_out).astype(BF16)
+
+    def normed_part(grads):
+        return jnp.einsum("sgc,sdc->gd", grads, w_qkv, preferred_element_type=F32)
+
+    far_sum = plus_side(normed_part(far_result[:, 0]), normed_part(far_result[:, 1])).astype(BF16)
+    grad_normed_one = plus_side(normed_part(near_result[:, 0]), normed_part(near_result[:, 1]))
+    grad_normed_one = grad_normed_one + from_far(far_sum).astype(F32)
+
+    near_result = near_result.reshape(3, 2 * tok_dev, heads_width)
+    far_result = far_result.reshape(3, 2 * tok_dev, heads_width)
+    grad_w_qkv = jnp.einsum(
+        "gd,sgc->dsc", near_one, near_result, preferred_element_type=F32
+    ) + jnp.einsum("gd,sgc->dsc", far_one, far_result, preferred_element_type=F32)
+    flat = (2 * tok_dev, heads_width)
+    grad_w_out = weight_grads(near_branch, far_branch, near_out.reshape(flat), far_out.reshape(flat))
     small_columns = -(-small.shape[0] // LANES) * LANES
     small_block = jnp.pad(small, ((0, small_columns - small.shape[0]), (0, 0))).T
-    last_grads = lax.psum_scatter(
+    last_grads = scatter_sum(
         jnp.concatenate(
             [
                 grad_w_qkv.reshape(width, 3 * heads_width).astype(BF16),
@@ -612,18 +788,12 @@
                 small_block.astype(BF16),
             ],
             axis=1,
-        ),
-        "expert",
-        scatter_dimension=0,
-        tiled=True,
-    ).astype(F32)
-    grad_ln_attn = lax.psum(
-        lax.psum(jnp.sum(grad_normed_one * scaled_one, axis=0), "tensor"), "expert"
-    )
+        )
+    )
+    gain_one = jnp.sum(grad_normed_one * scaled_one, axis=0, keepdims=True)
+    grad_ln_attn = sum_over(sum_over(gain_one, "tensor"), "expert")[0]
     grad_tokens = grad_residual + norm_back(grad_normed_one, ln_attn, scaled_one, inverse_one)
-    out = (residual + sum_to_owner(dense_out) + returned(expert_out)).astype(BF16)
-
-    hidden = w_up.shape[1]
+
     strip = last_grads.shape[0]
     after_qkv = 3 * heads_width
     after_out = after_qkv + heads_width

time: 890 us -> 716 us (0.80)
  starting transfers between devices: 118 us -> 56 us
  blocking collectives: 54.4 us -> 0 us
  waiting for transfers between devices: 304 us -> 250 us
  local copies, waits for them, and re-layouts: 75.2 us -> 24 us
  Pallas kernels: 166 us -> 202 us
  matrix products: 90.9 us -> 118 us
  other arithmetic: 57.5 us -> 46.6 us
    ppermute x35 -> x7, waiting for transfers between devices: 129 us -> 3.3 us  [sum_over(): values = values + lax.ppermute(values, axis, pairs)]
    ppermute x35 -> x7, starting transfers between devices: 106 us -> 9.56 us  [sum_over(): values = values + lax.ppermute(values, axis, pairs)]
    ppermute x10 -> x11, waiting for transfers between devices: 134 us -> 214 us  [from_far(): return lax.ppermute(values, 'tensor', [(i, i ^ 2) for i in range(4)])]
    psum x3 -> x0, blocking collectives: 54.4 us -> none  [the longest x1 28.6 us: per_device(): lax.psum(jnp.concatenate([(dense_head + expert_head)[:experts + 2], gain_...]
    all_gather x1 -> x0, waiting for transfers between devices: 41.2 us -> none  [per_device(): normed_one = lax.all_gather(normed_own, 'tensor', axis=0, tiled=True)]
    pallas_call x2 -> x4, Pallas kernels: 101 us -> 136 us  [feed(): pl.pallas_call(functools.partial(feed_kernel, experts, routed), grid_spec...]
    all_to_all x0 -> x5, starting transfers between devices: none -> 30.6 us  [exchange(): lax.all_to_all(blocks, 'expert', split_axis=0, concat_axis=0, tiled=True)]
    slice x14 -> x0, local copies, waits for them, and re-layouts: 22.2 us -> none  [the longest x4 16.1 us: sum_to_owner(): near = values[:half].astype(F32) + from_side(values[half:]).astype(F32)]
  transfers between devices with their start and end apart: 59 -> 49, of which waited for: 28 -> 16; matrix products, arithmetic and copies ran while one was open for 22% -> 23% of each run, Pallas kernels for 16% -> 28%
where the time goes in v3:
time: 716 us; the launch traced here: 712 us
  waiting for transfers between devices  250 us (35%)
  Pallas kernels  202 us (28%)
  matrix products  118 us (16%)
  starting transfers between devices  56 us (8%)
  other arithmetic  46.6 us (7%)
  local copies, waits for them, and re-layouts  24 us (3%)
  between operations  15.1 us (2%)
    ppermute x11, waiting for transfers between devices, from_far(): return lax.ppermute(values, 'tensor', [(i, i ^ 2) for i in range(4)])  214 us
    pallas_call x4, Pallas kernels, feed(): pl.pallas_call(functools.partial(feed_kernel, experts, routed), grid_spec...  136 us
    dot_general x10, matrix products, weight_grads(): return product(near_left, near_right) + product(far_left, far_right)  56.6 us
    pallas_call x1, Pallas kernels, attention_backward(): pl.pallas_call(backward_kernel, grid_spec=pltpu.PrefetchScalarGridSpec(nu...  41 us
    all_to_all x5, starting transfers between devices, exchange(): lax.all_to_all(blocks, 'expert', split_axis=0, concat_axis=0, tiled=True)  30.6 us
    pallas_call x1, Pallas kernels, attention_forward(): pl.pallas_call(forward_kernel, grid_spec=pltpu.PrefetchScalarGridSpec(num...  25.4 us
    unnamed x112, local copies, waits for them, and re-layouts  18.8 us
    all_to_all x5, waiting for transfers between devices, exchange(): lax.all_to_all(blocks, 'expert', split_axis=0, concat_axis=0, tiled=True)  17.8 us
  transfers between devices with their start and end apart: 49, of which 16 were waited for; matrix products, arithmetic and copies ran while one was open for 23% of the time, Pallas kernels for 28%

profile of v3, /device:TPU:0, one launch (start us, length us, event | category | flops | bytes accessed | tf_op | source)
XLA Modules:
  0.0 711.5 jit_solution(1608958039342638188)
XLA Ops:
  20.2 6.3 all-to-all-start
  27.0 17.3 %collective-permute-done.1 = bf16[640,1024]{1,0:T(8,128)(2,1)} collective-permute-done((bf16[640,1024]{1,0:T(8,128)(2,1)}, bf16[640,1024]{1,0:T(8,128)(2,1)}, u32[]{:S(2)}, u32[]{:S(2)}) %collective-permute-start.1) | collective-permute-done | bytes 1310752 | tf_op jit(solution)/shard_map/ppermute | solution.py:553
  57.8 25.4 %tree_attention.1 = (bf16[2,640,256]{2,1,0:T(8,128)(2,1)}, bf16[2,640,256]{2,1,0:T(8,128)(2,1)}, f32[2,2,1024]{2,1,0:T(2,128)}, f32[2,4,2,384]{3,2,1,0:T(2,128)}) custom-call(s32[9]{0:T(128)} %pad_add_fusion.leaves_ref, bf16[3,2,640,256]{3,2,1,0:T(8,128)(2,1)} %bitcast.155, bf16[3,2,640,256]{3,2,1,0:T(8,128)(2,1)} %bitcast.157), custom_call_target="tpu_custom_call" | custom-call | flops 9932111872 | bytes 10485760 | tf_op jit(solution)/shard_map/tree_attention/pallas_call | solution.py:190
  92.7 27.8 %collective-permute-done.7 = bf16[640,1024]{1,0:T(8,128)(2,1)S(1)} collective-permute-done((bf16[640,1024]{1,0:T(8,128)(2,1)S(1)}, bf16[640,1024]{1,0:T(8,128)(2,1)S(1)}, u32[]{:S(2)}, u32[]{:S(2)}) %collective-permute-start.7) | collective-permute-done | bytes 1310752 | tf_op jit(solution)/shard_map/ppermute | solution.py:553
  125.5 6.6 all-to-all-start.1
  136.4 25.7 %collective-permute-done.12.own_ref = bf16[640,1024]{1,0:T(8,128)(2,1)} collective-permute-done((bf16[640,1024]{1,0:T(8,128)(2,1)S(1)}, bf16[640,1024]{1,0:T(8,128)(2,1)}, u32[]{:S(2)}, u32[]{:S(2)}) %collective-permute-start.12) | collective-permute-done | bytes 1310752 | tf_op jit(solution)/shard_map/ppermute | solution.py:553
  162.1 28.1 %feed_dense.2 = (bf16[640,1024]{1,0:T(8,128)(2,1)}, bf16[640,1024]{1,0:T(8,128)(2,1)}, bf16[640,1024]{1,0:T(8,128)(2,1)}, bf16[640,1024]{1,0:T(8,128)(2,1)}, bf1...) custom-call(s32[1]{0:T(128)} %constant.46.clone.1.expert_ref, ...), custom_call_target="tpu_custom_call" | custom-call | flops 10737418240 | bytes 19922944 | tf_op jit(solution)/shard_map/feed_dense/pallas_call | solution.py:479
  190.2 7.5 %fusion.94 = f32[1024,1024]{0,1:T(8,128)} fusion(bf16[1280,1024]{1,0:T(8,128)(2,1)} %get-tuple-element.90, bf16[1280,1024]{1,0:T(8,128)(2,1)} %get-tuple-element.91), kind=kOutput, calls=%fused_computation.163 | convolution fusion | flops 2684354560 | bytes 9437184 | tf_op jit(solution)/shard_map/gd,gf->df/dot_general | solution.py:685
  207.9 7.1 fusion.21
  214.9 28.1 %feed_dense.3 = (bf16[640,1024]{1,0:T(8,128)(2,1)}, bf16[640,1024]{1,0:T(8,128)(2,1)}, bf16[640,1024]{1,0:T(8,128)(2,1)}, bf16[640,1024]{1,0:T(8,128)(2,1)}, bf1...) custom-call(s32[1]{0:T(128)} %constant.46.clone.1.expert_ref, ...), custom_call_target="tpu_custom_call" | custom-call | flops 10737418240 | bytes 19922944 | tf_op jit(solution)/shard_map/feed_dense/pallas_call | solution.py:479
  243.7 6.8 add_convert_fusion.1
  256.2 29.4 %collective-permute-done.11.own_ref = bf16[896,1024]{1,0:T(8,128)(2,1)} collective-permute-done((bf16[896,1024]{1,0:T(8,128)(2,1)}, bf16[896,1024]{1,0:T(8,128)(2,1)}, u32[]{:S(2)}, u32[]{:S(2)}) %collective-permute-start.11) | collective-permute-done | bytes 1835040 | tf_op jit(solution)/shard_map/ppermute | solution.py:553
  292.4 39.6 %feed_routed.2 = (bf16[896,1024]{1,0:T(8,128)(2,1)}, bf16[896,1024]{1,0:T(8,128)(2,1)}, bf16[896,1024]{1,0:T(8,128)(2,1)}, bf16[896,1024]{1,0:T(8,128)(2,1)}, bf...) custom-call(s32[1]{0:T(128)} %bitcast.16.expert_ref, ...), custom_call_target="tpu_custom_call" | custom-call | flops 15032385536 | bytes 26214400 | tf_op jit(solution)/shard_map/feed_routed/pallas_call | solution.py:479
  332.2 6.5 copy.46
  338.7 39.9 %feed_routed.3 = (bf16[896,1024]{1,0:T(8,128)(2,1)}, bf16[896,1024]{1,0:T(8,128)(2,1)}, bf16[896,1024]{1,0:T(8,128)(2,1)}, bf16[896,1024]{1,0:T(8,128)(2,1)}, bf...) custom-call(s32[1]{0:T(128)} %bitcast.16.expert_ref, ...), custom_call_target="tpu_custom_call" | custom-call | flops 15032385536 | bytes 26214400 | tf_op jit(solution)/shard_map/feed_routed/pallas_call | solution.py:479
  389.3 35.3 %collective-permute-done.25 = bf16[896,1024]{1,0:T(8,128)(2,1)S(1)} collective-permute-done((bf16[896,1024]{1,0:T(8,128)(2,1)S(1)}, bf16[896,1024]{1,0:T(8,128)(2,1)S(1)}, u32[]{:S(2)}, u32[]{:S(2)}) %collective-permute-start.25) | collective-permute-done | bytes 1835040 | tf_op jit(solution)/shard_map/ppermute | solution.py:553
  433.1 7.3 %fusion.95 = f32[1024,1024]{1,0:T(8,128)S(1)} fusion(bf16[1792,1024]{1,0:T(8,128)(2,1)} %get-tuple-element.113, bf16[1792,1024]{1,0:T(8,128)(2,1)} %get-tuple-element.114), kind=kOutput, calls=%fused_computation.164 | convolution fusion | flops 3758096384 | bytes 11534336 | tf_op jit(solution)/shard_map/gd,gf->df/dot_general | solution.py:685
  446.1 7.7 %fusion.4 = f32[1024,1024]{1,0:T(8,128)} fusion(bf16[1792,1024]{1,0:T(8,128)(2,1)S(1)} %copy-done.46, bf16[896,1024]{1,0:T(8,128)(2,1)} %collective-permute-done.14.side_ref, bf16[896,1024]{1,0:T(8,128)(2,1)} %collective-permute-done.11.own_ref), kind=kOutput, calls=%fused_computation.12 | convolution fusion | flops 3765436416 | bytes 11534336 | tf_op jit(solution)/shard_map/gd,gf->df/dot_general | solution.py:685
  456.6 17.8 %all-to-all-done.3 = bf16[8,112,1024]{2,1,0:T(8,128)(2,1)} async-done(((bf16[8,112,1024]{2,1,0:T(8,128)(2,1)}), bf16[8,112,1024]{2,1,0:T(8,128)(2,1)}, u32[]{:S(2)}, u32[]{:S(2)}) %all-to-all-start.3) | async-done | bytes 1835040 | tf_op jit(solution)/shard_map/all_to_all | solution.py:570
  486.0 7.9 %add_bitcast_fusion.1 = f32[1,1024,1024]{2,1,0:T(8,128)} fusion(f32[1024,1024]{1,0:T(8,128)S(1)} %copy-done.45, bf16[1792,1024]{1,0:T(8,128)(2,1)S(1)} %copy-done.51, bf16[896,1024]{1,0:T(8,128)(2,1)} %collective-permute-done.23.side_ref, bf16[896,1024]{1,0:T(8,128)(2,1)} %bitcast.18.own_ref), kind=kOutput, calls=%fused_computation.2 | convolution fusion | flops 3766484992 | bytes 15728640 | tf_op jit(solution)/shard_map/gd,gf->df/dot_general | solution.py:685
  496.2 30.5 %collective-permute-done.29 = bf16[640,1024]{1,0:T(8,128)(2,1)} collective-permute-done((bf16[640,1024]{1,0:T(8,128)(2,1)}, bf16[640,1024]{1,0:T(8,128)(2,1)}, u32[]{:S(2)}, u32[]{:S(2)}) %collective-permute-start.29) | collective-permute-done | bytes 1310752 | tf_op jit(solution)/shard_map/ppermute | solution.py:553
  551.1 41.0 %tree_attention_back.1 = (bf16[3,2,640,256]{3,2,1,0:T(8,128)(2,1)}, bf16[3,2,640,256]{3,2,1,0:T(8,128)(2,1)}) custom-call(s32[9]{0:T(128)} %pad_add_fusion.leaves_ref, bf16[3,2,640,256]{3,2,1,0:T(8,128)(2,1)} %bitcast.156, bf16[3,2,640,256]{3,2,1,0:T(8,128)(2,1)} %bitcast.158, bf16[2,640,256]{2,1,0:T(8,128)(2,1)} %bitcast.161, ...), custom_call_target="tpu_custom_call" | custom-call | flops 24830279680 | bytes 10485760 | tf_op jit(solution)/shard_map/tree_attention_back/pallas_call | solution.py:334
  626.6 26.6 %collective-permute-done.36 = bf16[640,1024]{1,0:T(8,128)(2,1)S(1)} collective-permute-done((bf16[640,1024]{1,0:T(8,128)(2,1)S(1)}, bf16[640,1024]{1,0:T(8,128)(2,1)S(1)}, u32[]{:S(2)}, u32[]{:S(2)}) %collective-permute-start.36) | collective-permute-done | bytes 1310752 | tf_op jit(solution)/shard_map/ppermute | solution.py:553
  659.4 21.4 %collective-permute-done.19 = bf16[640,1024]{1,0:T(8,128)(2,1)} collective-permute-done((bf16[640,1024]{1,0:T(8,128)(2,1)}, bf16[640,1024]{1,0:T(8,128)(2,1)}, u32[]{:S(2)}, u32[]{:S(2)}) %collective-permute-start.19) | collective-permute-done | bytes 1310752 | tf_op jit(solution)/shard_map/ppermute | solution.py:553
  (286 shorter events, 198.7 us)
Async XLA Ops:
  12.3 32.1 %collective-permute-start.1 = (bf16[640,1024]{1,0:T(8,128)(2,1)}, bf16[640,1024]{1,0:T(8,128)(2,1)}, u32[]{:S(2)}, u32[]{:S(2)}) collective-permute-start(bf16[640,1024]{1,0:T(8,128)(2,1)} %fusion.14), channel_id=1, source_target_pairs={{0,2},{1,3},{2,0},{3,1},{4,6},{5,7},{6,4},{7,5},{8,10},{9,11},{10,... | collective-permute-start | bytes 3932168 | tf_op jit(solution)/shard_map/ppermute | solution.py:553
  20.2 63.1 %all-to-all-start = ((bf16[8,112,1024]{2,1,0:T(8,128)(2,1)}), bf16[8,112,1024]{2,1,0:T(8,128)(2,1)}, u32[]{:S(2)}, u32[]{:S(2)}) async-start(bf16[8,112,1024]{2,1,0:T(8,128)(2,1)} %bitcast.138), calls=%async_computation | async-start | bytes 3670016 | tf_op jit(solution)/shard_map/all_to_all | solution.py:570
  26.5 56.7 %collective-permute-start.5 = (bf16[640,1024]{1,0:T(8,128)(2,1)}, bf16[640,1024]{1,0:T(8,128)(2,1)}, u32[]{:S(2)}, u32[]{:S(2)}) collective-permute-start(bf16[640,1024]{1,0:T(8,128)(2,1)} %own_grads_ref.1), channel_id=1, source_target_pairs={{0,1},{1,0},{2,3},{3,2},{4,5},{5,4},{6,7},{7,6},{8,9},{9,8},{10,11... | collective-permute-start | bytes 3932168 | tf_op jit(solution)/shard_map/ppermute | solution.py:549
  45.4 37.8 %collective-permute-start.4 = (bf16[640,1024]{1,0:T(8,128)(2,1)}, bf16[640,1024]{1,0:T(8,128)(2,1)}, u32[]{:S(2)}, u32[]{:S(2)}) collective-permute-start(bf16[640,1024]{1,0:T(8,128)(2,1)} %own_grads_ref.1), channel_id=1, source_target_pairs={{0,2},{1,3},{2,0},{3,1},{4,6},{5,7},{6,4},{7,5},{8,10},{9,11},{10,... | collective-permute-start | bytes 3932168 | tf_op jit(solution)/shard_map/ppermute | solution.py:553
  125.5 72.1 %all-to-all-start.1 = ((bf16[8,112,1024]{2,1,0:T(8,128)(2,1)}), bf16[8,112,1024]{2,1,0:T(8,128)(2,1)}, u32[]{:S(2)}, u32[]{:S(2)}) async-start(bf16[8,112,1024]{2,1,0:T(8,128)(2,1)} %bitcast.140), calls=%async_computation.1 | async-start | bytes 3670016 | tf_op jit(solution)/shard_map/all_to_all | solution.py:570
  162.1 52.9 %collective-permute-start.13 = (bf16[640,1024]{1,0:T(8,128)(2,1)}, bf16[640,1024]{1,0:T(8,128)(2,1)}, u32[]{:S(2)}, u32[]{:S(2)}) collective-permute-start(bf16[640,1024]{1,0:T(8,128)(2,1)} %collective-permute-done.12.own_ref), channel_id=1, source_target_pairs={{0,1},{1,0},{2,3},{3,2},{4,5},{5,4},{6,7},{7,6},{8,9},{9,8},{10,11... | collective-permute-start | bytes 3932168 | tf_op jit(solution)/shard_map/ppermute | solution.py:549
  201.8 83.9 %all-to-all-start.2 = ((bf16[8,112,1024]{2,1,0:T(8,128)(2,1)}), bf16[8,112,1024]{2,1,0:T(8,128)(2,1)}, u32[]{:S(2)}, u32[]{:S(2)}) async-start(bf16[8,112,1024]{2,1,0:T(8,128)(2,1)} %bitcast.139), calls=%async_computation.2 | async-start | bytes 3670016 | tf_op jit(solution)/shard_map/all_to_all | solution.py:570
  207.6 286.2 %reduce-scatter.7.cloned.1.call-start = ((), (), s32[]{:S(2)}) async-start(), calls=%async_computation.7 | async-start | bytes 4718592
  243.1 42.5 %collective-permute-start.11 = (bf16[896,1024]{1,0:T(8,128)(2,1)}, bf16[896,1024]{1,0:T(8,128)(2,1)}, u32[]{:S(2)}, u32[]{:S(2)}) collective-permute-start(bf16[896,1024]{1,0:T(8,128)(2,1)} %bitcast.18.own_ref), channel_id=1, source_target_pairs={{0,2},{1,3},{2,0},{3,1},{4,6},{5,7},{6,4},{7,5},{8,10},{9,11},{10,... | collective-permute-start | bytes 5505032 | tf_op jit(solution)/shard_map/ppermute | solution.py:553
  286.1 52.6 %collective-permute-start.23 = (bf16[896,1024]{1,0:T(8,128)(2,1)}, bf16[896,1024]{1,0:T(8,128)(2,1)}, u32[]{:S(2)}, u32[]{:S(2)}) collective-permute-start(bf16[896,1024]{1,0:T(8,128)(2,1)} %bitcast.18.own_ref), channel_id=1, source_target_pairs={{0,1},{1,0},{2,3},{3,2},{4,5},{5,4},{6,7},{7,6},{8,9},{9,8},{10,11... | collective-permute-start | bytes 5505032 | tf_op jit(solution)/shard_map/ppermute | solution.py:549
  332.0 47.1 %collective-permute-start.16 = (bf16[896,1024]{1,0:T(8,128)(2,1)}, bf16[896,1024]{1,0:T(8,128)(2,1)}, u32[]{:S(2)}, u32[]{:S(2)}) collective-permute-start(bf16[896,1024]{1,0:T(8,128)(2,1)} %get-tuple-element.97), channel_id=1, source_target_pairs={{0,1},{1,0},{2,3},{3,2},{4,5},{5,4},{6,7},{7,6},{8,9},{9,8},{10,11... | collective-permute-start | bytes 5505032 | tf_op jit(solution)/shard_map/ppermute | solution.py:549
  381.7 42.9 %collective-permute-start.25 = (bf16[896,1024]{1,0:T(8,128)(2,1)S(1)}, bf16[896,1024]{1,0:T(8,128)(2,1)S(1)}, u32[]{:S(2)}, u32[]{:S(2)}) collective-permute-start(bf16[896,1024]{1,0:T(8,128)(2,1)S(1)} %add_convert_fusion.3), channel_id=1, source_target_pairs={{0,2},{1,3},{2,0},{3,1},{4,6},{5,7},{6,4},{7,5},{8,10},{9,11},{10,... | collective-permute-start | bytes 5505032 | tf_op jit(solution)/shard_map/ppermute | solution.py:553
  382.2 74.3 %collective-permute-start.20 = (bf16[640,1024]{1,0:T(8,128)(2,1)}, bf16[640,1024]{1,0:T(8,128)(2,1)}, u32[]{:S(2)}, u32[]{:S(2)}) collective-permute-start(bf16[640,1024]{1,0:T(8,128)(2,1)} %get-tuple-element.102), channel_id=1, source_target_pairs={{0,1},{1,0},{2,3},{3,2},{4,5},{5,4},{6,7},{7,6},{8,9},{9,8},{10,11... | collective-permute-start | bytes 3932168 | tf_op jit(solution)/shard_map/ppermute | solution.py:549
  387.7 68.9 %collective-permute-start.22 = (bf16[640,1024]{1,0:T(8,128)(2,1)S(1)}, bf16[640,1024]{1,0:T(8,128)(2,1)}, u32[]{:S(2)}, u32[]{:S(2)}) collective-permute-start(bf16[640,1024]{1,0:T(8,128)(2,1)S(1)} %add_convert_fusion.6), channel_id=1, source_target_pairs={{0,2},{1,3},{2,0},{3,1},{4,6},{5,7},{6,4},{7,5},{8,10},{9,11},{10,... | collective-permute-start | bytes 3932168 | tf_op jit(solution)/shard_map/ppermute | solution.py:553
  427.2 47.3 %all-to-all-start.3 = ((bf16[8,112,1024]{2,1,0:T(8,128)(2,1)}), bf16[8,112,1024]{2,1,0:T(8,128)(2,1)}, u32[]{:S(2)}, u32[]{:S(2)}) async-start(bf16[8,112,1024]{2,1,0:T(8,128)(2,1)} %bitcast.137), calls=%async_computation.3 | async-start | bytes 3670016 | tf_op jit(solution)/shard_map/all_to_all | solution.py:570
  455.9 72.2 %collective-permute-start.33 = (bf16[896,1024]{1,0:T(8,128)(2,1)}, bf16[896,1024]{1,0:T(8,128)(2,1)}, u32[]{:S(2)}, u32[]{:S(2)}) collective-permute-start(bf16[896,1024]{1,0:T(8,128)(2,1)} %add_convert_fusion.2), channel_id=1, source_target_pairs={{0,2},{1,3},{2,0},{3,1},{4,6},{5,7},{6,4},{7,5},{8,10},{9,11},{10,... | collective-permute-start | bytes 5505032 | tf_op jit(solution)/shard_map/ppermute | solution.py:553
  456.4 71.7 %collective-permute-start.31 = (bf16[896,1024]{1,0:T(8,128)(2,1)}, bf16[896,1024]{1,0:T(8,128)(2,1)}, u32[]{:S(2)}, u32[]{:S(2)}) collective-permute-start(bf16[896,1024]{1,0:T(8,128)(2,1)} %get-tuple-element.126), channel_id=1, source_target_pairs={{0,1},{1,0},{2,3},{3,2},{4,5},{5,4},{6,7},{7,6},{8,9},{9,8},{10,11... | collective-permute-start | bytes 5505032 | tf_op jit(solution)/shard_map/ppermute | solution.py:549
  483.2 43.4 %collective-permute-start.29 = (bf16[640,1024]{1,0:T(8,128)(2,1)}, bf16[640,1024]{1,0:T(8,128)(2,1)}, u32[]{:S(2)}, u32[]{:S(2)}) collective-permute-start(bf16[640,1024]{1,0:T(8,128)(2,1)} %get-tuple-element.183), channel_id=1, source_target_pairs={{0,2},{1,3},{2,0},{3,1},{4,6},{5,7},{6,4},{7,5},{8,10},{9,11},{10,... | collective-permute-start | bytes 3932168 | tf_op jit(solution)/shard_map/ppermute | solution.py:553
  485.3 54.8 %collective-permute-start.26 = (bf16[640,1024]{1,0:T(8,128)(2,1)}, bf16[640,1024]{1,0:T(8,128)(2,1)}, u32[]{:S(2)}, u32[]{:S(2)}) collective-permute-start(bf16[640,1024]{1,0:T(8,128)(2,1)} %get-tuple-element.183), channel_id=1, source_target_pairs={{0,1},{1,0},{2,3},{3,2},{4,5},{5,4},{6,7},{7,6},{8,9},{9,8},{10,11... | collective-permute-start | bytes 3932168 | tf_op jit(solution)/shard_map/ppermute | solution.py:549
  485.4 41.3 %collective-permute-start.27 = (f32[11,1024]{1,0:T(8,128)S(1)}, f32[11,1024]{1,0:T(8,128)}, u32[]{:S(2)}, u32[]{:S(2)}) collective-permute-start(f32[11,1024]{1,0:T(8,128)S(1)} %pad_maximum_fusion.5), channel_id=1, source_target_pairs={{0,1},{1,0},{2,3},{3,2},{4,5},{5,4},{6,7},{7,6},{8,9},{9,8},{10,11... | collective-permute-start | bytes 135176 | tf_op jit(solution)/shard_map/ppermute | solution.py:564
  533.2 65.2 %all-to-all-start.4 = ((bf16[8,112,1024]{2,1,0:T(8,128)(2,1)}), bf16[8,112,1024]{2,1,0:T(8,128)(2,1)}, u32[]{:S(2)}, u32[]{:S(2)}) async-start(bf16[8,112,1024]{2,1,0:T(8,128)(2,1)} %bitcast.136), calls=%async_computation.4 | async-start | bytes 3670016 | tf_op jit(solution)/shard_map/all_to_all | solution.py:570
  539.2 160.8 %reduce-scatter.9.cloned.1.call-start = ((), (), s32[]{:S(2)}) async-start(), calls=%async_computation.8 | async-start | bytes 2654208
  623.1 36.2 %collective-permute-start.17 = (bf16[640,1024]{1,0:T(8,128)(2,1)}, bf16[640,1024]{1,0:T(8,128)(2,1)}, u32[]{:S(2)}, u32[]{:S(2)}) collective-permute-start(bf16[640,1024]{1,0:T(8,128)(2,1)} %get-tuple-element.98), channel_id=1, source_target_pairs={{0,1},{1,0},{2,3},{3,2},{4,5},{5,4},{6,7},{7,6},{8,9},{9,8},{10,11... | collective-permute-start | bytes 3932168 | tf_op jit(solution)/shard_map/ppermute | solution.py:549
  624.8 56.0 %collective-permute-start.19 = (bf16[640,1024]{1,0:T(8,128)(2,1)}, bf16[640,1024]{1,0:T(8,128)(2,1)}, u32[]{:S(2)}, u32[]{:S(2)}) collective-permute-start(bf16[640,1024]{1,0:T(8,128)(2,1)} %add_convert_fusion.7), channel_id=1, source_target_pairs={{0,2},{1,3},{2,0},{3,1},{4,6},{5,7},{6,4},{7,5},{8,10},{9,11},{10,... | collective-permute-start | bytes 3932168 | tf_op jit(solution)/shard_map/ppermute | solution.py:553
  (77 other events, 959.7 us)
Sparse Core Ops, SparseCore 0:
  338.8 88.0 reduce-scatter.6
  615.8 70.3 reduce-scatter.8

commit v4 on v3

--- a/solution.py
+++ b/solution.py
@@ -4,6 +4,7 @@
 import jax.numpy as jnp
 from jax import lax
 from jax.experimental import pallas as pl
+from jax.experimental.layout import Layout, with_layout_constraint
 from jax.experimental.pallas import tpu as pltpu
 from jax.sharding import PartitionSpec as P
 
@@ -15,6 +16,7 @@
 BRANCHES = 4
 FAMILY = 3 * SEG
 QROWS = 256
+COVER = 8
 PAIR = 2 * HEAD_DIM
 NEGATIVE_FILL = -1e30
 F32 = jnp.float32
@@ -175,11 +177,11 @@
 
 
 def attention_cost(products):
-    visited = TRUNK * (TRUNK + QROWS) // 2 + BRANCHES * FAMILY * (TRUNK + SEG)
+    visited = (TRUNK * (TRUNK + QROWS) // 2 + BRANCHES * FAMILY * (TRUNK + SEG)) // COVER
     return pl.CostEstimate(
         flops=2 * products * 4 * visited * 2 * PAIR,
         transcendentals=4 * visited,
-        bytes_accessed=8 * TREE_LEN * 4 * HEAD_DIM * 2,
+        bytes_accessed=8 * TREE_LEN * 4 * HEAD_DIM * 2 // COVER,
     )
 
 
@@ -512,9 +514,9 @@
             jax.ShapeDtypeStruct((lanes, width), F32),
         ],
         cost_estimate=pl.CostEstimate(
-            flops=16 * count * width * hidden,
-            transcendentals=4 * count * hidden,
-            bytes_accessed=2 * (8 * count * width + 4 * count * hidden + 2 * width * hidden),
+            flops=16 * count * width * hidden // COVER,
+            transcendentals=4 * count * hidden // COVER,
+            bytes_accessed=2 * (8 * count * width + 4 * count * hidden + 2 * width * hidden) // COVER,
         ),
         compiler_params=pltpu.CompilerParams(vmem_limit_bytes=60 * 1024 * 1024),
         name="feed_routed" if routed else "feed_dense",
@@ -571,7 +573,7 @@
 
 
 def scatter_sum(strips):
-    strips = strips.astype(BF16)
+    strips = with_layout_constraint(strips.astype(BF16), Layout(major_to_minor=(0, 1)))
     return lax.psum_scatter(strips, "expert", scatter_dimension=0, tiled=True).astype(F32)
 
 
@@ -615,7 +617,6 @@
     normed_own = (scaled_one * ln_attn).astype(BF16)
     normed_far = from_far(normed_own)
     near_one = jnp.concatenate([normed_own, from_side(normed_own)], axis=0)
-    far_one = jnp.concatenate([normed_far, from_side(normed_far)], axis=0)
 
     quarter_ids = routes[:, 0].reshape(4, tok_dev)
 
@@ -636,8 +637,15 @@
         qkv = jnp.einsum("td,sdc->stc", rows, w_qkv, preferred_element_type=F32)
         return qkv.astype(BF16).reshape(3, 2, tok_dev, heads_width)
 
-    near_qkv, far_qkv = project(near_one), project(far_one)
+    lanes = -(-(experts + 2) // LANES) * LANES
+    head = jnp.concatenate(
+        [w_router, w_mix, jnp.zeros((width, lanes - experts - 2), BF16)], axis=1
+    )
+    near_qkv = project(near_one)
     cotangent_far = from_far(after(cotangent, normed_far))
+    normed_far, near_qkv, head = lax.optimization_barrier((normed_far, near_qkv, head))
+    far_one = jnp.concatenate([normed_far, from_side(normed_far)], axis=0)
+    far_qkv = project(far_one)
     near_out, far_out, *logs = attention_forward(leaves, near_qkv, far_qkv)
     far_out, own_grads, cotangent_far, cotangent_side = lax.optimization_barrier(
         (far_out, own_grads, cotangent_far, cotangent_side)
@@ -660,34 +668,36 @@
     normed_two = (scaled_two * ln_mlp).astype(BF16)
     normed_two_far = from_far(normed_two)
     normed_two_side = from_side(normed_two)
-    normed_two_corner = from_side(normed_two_far)
     own_rows = dispatch(own_slots, normed_two)
-    far_rows = from_far(own_rows)
-    far_grads = dispatch(far_slots, after(cotangent_far, own_rows))
-
-    lanes = -(-(experts + 2) // LANES) * LANES
-    head = jnp.concatenate(
-        [w_router, w_mix, jnp.zeros((width, lanes - experts - 2), BF16)], axis=1
-    )
 
     def dense(own, side, own_cotangent, side_cotangent):
         return feed(
             own, side, own_cotangent, side_cotangent, head, w_up, w_down, experts, None, DENSE_ROWS
         )
 
+    def product(left, right):
+        return jnp.einsum("gd,gf->df", left, right, preferred_element_type=F32)
+
+    def weight_grads(near_left, far_left, near_right, far_right):
+        return product(near_left, near_right) + product(far_left, far_right)
+
     near_dense = dense(normed_two, normed_two_side, cotangent, cotangent_side)
-    far_dense = dense(
-        after(normed_two_far, near_dense[2]), normed_two_corner, cotangent_far, cotangent_corner
-    )
-
-    def weight_grads(near_left, far_left, near_right, far_right):
-        product = functools.partial(jnp.einsum, "gd,gf->df", preferred_element_type=F32)
-        return product(near_left, near_right) + product(far_left, far_right)
-
     near_two = jnp.concatenate([normed_two, normed_two_side], axis=0)
+    grad_up = product(near_two, near_dense[5])
+    grad_down = product(near_dense[6], near_dense[4])
+    normed_two_far, grad_up, grad_down, own_rows = lax.optimization_barrier(
+        (normed_two_far, grad_up, grad_down, own_rows)
+    )
+    far_rows = from_far(own_rows)
+    far_grads = dispatch(far_slots, after(cotangent_far, own_rows))
+    normed_two_corner = from_side(normed_two_far)
+    far_dense = list(dense(normed_two_far, normed_two_corner, cotangent_far, cotangent_corner))
+    far_rows, far_dense[6], far_dense[5] = lax.optimization_barrier(
+        (far_rows, far_dense[6], far_dense[5])
+    )
     far_two = jnp.concatenate([normed_two_far, normed_two_corner], axis=0)
-    grad_up = weight_grads(near_two, far_two, near_dense[5], far_dense[5])
-    grad_down = weight_grads(near_dense[6], far_dense[6], near_dense[4], far_dense[4])
+    grad_up = grad_up + product(far_two, far_dense[5])
+    grad_down = grad_down + product(far_dense[6], far_dense[4])
     dense_grads = jnp.concatenate([grad_up.astype(BF16), grad_down.astype(BF16)], axis=1)
 
     expert = lax.axis_index("expert").astype(jnp.int32)
@@ -709,29 +719,39 @@
     far_rows, dense_grads = lax.optimization_barrier((far_rows, dense_grads))
     dense_grads = scatter_sum(dense_grads)
     corner_rows = from_side(far_rows)
-    far_expert = routed(far_rows, corner_rows, far_grads, from_side(far_grads))
     side_rows = from_side(own_rows)
-    near_expert = routed(after(own_rows, far_expert[2]), side_rows, own_grads, side_grads)
 
     def chip_sum(parts, place, *others):
         return plus_side(parts[place], after(parts[place + 1], *others))
 
-    def returned(rows):
+    far_expert = routed(far_rows, corner_rows, far_grads, from_side(far_grads))
+    dense_back_far = from_far(chip_sum(far_dense, 2).astype(BF16))
+    dense_out_far = from_far(chip_sum(far_dense, 0).astype(BF16))
+    dense_back, dense_out = chip_sum(near_dense, 2), chip_sum(near_dense, 0)
+    far_back = chip_sum(far_expert, 2).astype(BF16)
+    own_rows, far_back, dense_back_far, dense_out_far = lax.optimization_barrier(
+        (own_rows, far_back, dense_back_far, dense_out_far)
+    )
+    near_expert = routed(own_rows, side_rows, own_grads, side_grads)
+    dense_back = dense_back + dense_back_far.astype(F32)
+    dense_out = dense_out + dense_out_far.astype(F32)
+
+    def send_back(rows):
         rows = rows.astype(BF16).reshape(experts, capacity, width)
-        rows = exchange(rows).reshape(-1, width)
+        return exchange(rows).reshape(-1, width)
+
+    def picked(rows):
         return lax.dot_general(
             own_slots, rows, (((0,), (0,)), ((), ())), preferred_element_type=F32
         )
 
-    dense_back = chip_sum(near_dense, 2) + from_far(chip_sum(far_dense, 2).astype(BF16)).astype(F32)
-    far_back = chip_sum(far_expert, 2).astype(BF16)
     expert_back = chip_sum(near_expert, 2) + from_far(far_back).astype(F32)
-    grad_normed_two = dense_back + returned(expert_back)
-    far_dense_out = chip_sum(far_dense, 0, far_back).astype(BF16)
-    far_expert_out = chip_sum(far_expert, 0, far_back).astype(BF16)
-    dense_out = chip_sum(near_dense, 0, far_back) + from_far(far_dense_out).astype(F32)
+    grad_normed_two, dense_grads = lax.optimization_barrier(
+        (dense_back + picked(send_back(expert_back)), dense_grads)
+    )
+    far_expert_out = chip_sum(far_expert, 0, near_expert[2]).astype(BF16)
     expert_out = chip_sum(near_expert, 0, expert_back) + from_far(far_expert_out).astype(F32)
-    expert_out = returned(after(expert_out, grad_normed_two))
+    expert_out = send_back(after(expert_out, grad_normed_two))
 
     near_tokens = jnp.concatenate([own_rows, side_rows], axis=0)
     far_tokens = jnp.concatenate([far_rows, corner_rows], axis=0)
@@ -755,21 +775,26 @@
         return grads.astype(BF16).reshape(2, tok_dev, heads_width)
 
     near_heads, far_heads = into_heads(near_branch), into_heads(far_branch)
-    near_heads, grad_ex_up, grad_ex_down, small, dense_grads = lax.optimization_barrier(
-        (near_heads, grad_ex_up, grad_ex_down, small, dense_grads)
+    near_heads, grad_ex_up, grad_ex_down, small = lax.optimization_barrier(
+        (near_heads, grad_ex_up, grad_ex_down, small)
     )
     near_result, far_result = attention_backward(
         leaves, near_qkv, far_qkv, near_heads, far_heads, near_out, far_out, logs
     )
-    far_result, expert_out = lax.optimization_barrier((far_result, expert_out))
-    out = (residual + dense_out + expert_out).astype(BF16)
+    near_result, expert_out = lax.optimization_barrier((near_result, expert_out))
 
     def normed_part(grads):
         return jnp.einsum("sgc,sdc->gd", grads, w_qkv, preferred_element_type=F32)
 
-    far_sum = plus_side(normed_part(far_result[:, 0]), normed_part(far_result[:, 1])).astype(BF16)
-    grad_normed_one = plus_side(normed_part(near_result[:, 0]), normed_part(near_result[:, 1]))
-    grad_normed_one = grad_normed_one + from_far(far_sum).astype(F32)
+    corner_part = normed_part(far_result[:, 1])
+    far_result, corner_part = lax.optimization_barrier((far_result, corner_part))
+    far_sum = plus_side(normed_part(far_result[:, 0]), corner_part).astype(BF16)
+    near_result, far_result, near_branch, expert_out, far_sum = lax.optimization_barrier(
+        (near_result, far_result, near_branch, expert_out, far_sum)
+    )
+    near_sum = plus_side(normed_part(near_result[:, 0]), normed_part(near_result[:, 1]))
+    grad_normed_one = near_sum + from_far(far_sum).astype(F32)
+    out = (residual + dense_out + picked(expert_out)).astype(BF16)
 
     near_result = near_result.reshape(3, 2 * tok_dev, heads_width)
     far_result = far_result.reshape(3, 2 * tok_dev, heads_width)
@@ -790,7 +815,8 @@
             axis=1,
         )
     )
-    gain_one = jnp.sum(grad_normed_one * scaled_one, axis=0, keepdims=True)
+    scaled_far = normed_far.astype(F32) / ln_attn
+    gain_one = jnp.sum(near_sum * scaled_one + far_sum.astype(F32) * scaled_far, axis=0, keepdims=True)
     grad_ln_attn = sum_over(sum_over(gain_one, "tensor"), "expert")[0]
     grad_tokens = grad_residual + norm_back(grad_normed_one, ln_attn, scaled_one, inverse_one)
 

time: 716 us -> 673 us (0.940)
  waiting for transfers between devices: 250 us -> 191 us
  matrix products: 118 us -> 128 us
  other arithmetic: 46.6 us -> 55.3 us
    ppermute x11, waiting for transfers between devices: 214 us -> 141 us  [from_far(): return lax.ppermute(values, 'tensor', [(i, i ^ 2) for i in range(4)])]
    unnamed x112 -> x92, local copies, waits for them, and re-layouts: 18.8 us -> 8.91 us
    reduce_scatter x0 -> x2, waiting for transfers between devices: none -> 8.73 us  [scatter_sum(): lax.psum_scatter(strips, 'expert', scatter_dimension=0, tiled=True)]
  transfers between devices with their start and end apart: 49 -> 49, of which waited for: 16 -> 20; matrix products, arithmetic and copies ran while one was open for 23% -> 24% of each run, Pallas kernels for 28% -> 30%
where the time goes in v4:
time: 673 us; the launch traced here: 668 us
  Pallas kernels  203 us (30%)
  waiting for transfers between devices  191 us (28%)
  matrix products  128 us (19%)
  starting transfers between devices  58.6 us (9%)
  other arithmetic  55.3 us (8%)
  local copies, waits for them, and re-layouts  17.3 us (3%)
  between operations  15.1 us (2%)
    ppermute x11, waiting for transfers between devices, from_far(): return lax.ppermute(values, 'tensor', [(i, i ^ 2) for i in range(4)])  141 us
    pallas_call x4, Pallas kernels, feed(): pl.pallas_call(functools.partial(feed_kernel, experts, routed), grid_spec...  136 us
    dot_general x10, matrix products, product(): return jnp.einsum('gd,gf->df', left, right, preferred_element_type=F32)  61.1 us
    pallas_call x1, Pallas kernels, attention_backward(): pl.pallas_call(backward_kernel, grid_spec=pltpu.PrefetchScalarGridSpec(nu...  40.9 us
    all_to_all x5, starting transfers between devices, exchange(): lax.all_to_all(blocks, 'expert', split_axis=0, concat_axis=0, tiled=True)  30.9 us
    pallas_call x1, Pallas kernels, attention_forward(): pl.pallas_call(forward_kernel, grid_spec=pltpu.PrefetchScalarGridSpec(num...  25.6 us
    all_to_all x5, waiting for transfers between devices, exchange(): lax.all_to_all(blocks, 'expert', split_axis=0, concat_axis=0, tiled=True)  19.6 us
    ppermute x24, waiting for transfers between devices, from_side(): return lax.ppermute(values, 'tensor', [(i, i ^ 1) for i in range(4)])  18.1 us
  transfers between devices with their start and end apart: 49, of which 20 were waited for; matrix products, arithmetic and copies ran while one was open for 24% of the time, Pallas kernels for 30%

profile of v4, /device:TPU:0, one launch (start us, length us, event | category | flops | bytes accessed | tf_op | source)
XLA Modules:
  0.0 668.3 jit_solution(11622440887751664982)
XLA Ops:
  20.1 6.3 all-to-all-start
  33.1 11.9 %collective-permute-done = bf16[640,1024]{1,0:T(8,128)(2,1)} collective-permute-done((bf16[640,1024]{1,0:T(8,128)(2,1)}, bf16[640,1024]{1,0:T(8,128)(2,1)}, u32[]{:S(2)}, u32[]{:S(2)}) %collective-permute-start) | collective-permute-done | bytes 1310752 | tf_op jit(solution)/shard_map/ppermute | solution.py:555
  55.4 25.6 %tree_attention.1 = (bf16[2,640,256]{2,1,0:T(8,128)(2,1)}, bf16[2,640,256]{2,1,0:T(8,128)(2,1)}, f32[2,2,1024]{2,1,0:T(2,128)}, f32[2,4,2,384]{3,2,1,0:T(2,128)}) custom-call(s32[9]{0:T(128)} %pad_add_fusion.leaves_ref, bf16[3,2,640,256]{3,2,1,0:T(8,128)(2,1)} %bitcast.155, bf16[3,2,640,256]{3,2,1,0:T(8,128)(2,1)} %bitcast.157), custom_call_target="tpu_custom_call" | custom-call | flops 1241513984 | bytes 1310720 | tf_op jit(solution)/shard_map/tree_attention/pallas_call | solution.py:192
  90.5 28.2 %collective-permute-done.7 = bf16[640,1024]{1,0:T(8,128)(2,1)S(1)} collective-permute-done((bf16[640,1024]{1,0:T(8,128)(2,1)S(1)}, bf16[640,1024]{1,0:T(8,128)(2,1)S(1)}, u32[]{:S(2)}, u32[]{:S(2)}) %collective-permute-start.7) | collective-permute-done | bytes 1310752 | tf_op jit(solution)/shard_map/ppermute | solution.py:555
  123.8 6.2 all-to-all-start.1
  133.5 28.1 %feed_dense.2 = (bf16[640,1024]{1,0:T(8,128)(2,1)}, bf16[640,1024]{1,0:T(8,128)(2,1)}, bf16[640,1024]{1,0:T(8,128)(2,1)}, bf16[640,1024]{1,0:T(8,128)(2,1)}, bf1...) custom-call(s32[1]{0:T(128)} %constant.47.clone.1.expert_ref, ...), custom_call_target="tpu_custom_call" | custom-call | flops 1342177280 | bytes 2490368 | tf_op jit(solution)/shard_map/feed_dense/pallas_call | solution.py:481
  161.6 7.6 %fusion.22 = f32[1024,1024]{1,0:T(8,128)} fusion(bf16[1280,1024]{1,0:T(8,128)(2,1)} %get-tuple-element.106, bf16[640,1024]{1,0:T(8,128)(2,1)} %collective-permute-done.10.side_ref, bf16[640,1024]{1,0:T(8,128)(2,1)} %copy-done.7), kind=kOutput, calls=%fused_computation.39 | convolution fusion | flops 2689597440 | bytes 9437184 | tf_op jit(solution)/shard_map/gd,gf->df/dot_general | solution.py:679
  185.3 28.3 %feed_dense.3 = (bf16[640,1024]{1,0:T(8,128)(2,1)}, bf16[640,1024]{1,0:T(8,128)(2,1)}, bf16[640,1024]{1,0:T(8,128)(2,1)}, bf16[640,1024]{1,0:T(8,128)(2,1)}, bf1...) custom-call(s32[1]{0:T(128)} %constant.47.clone.1.expert_ref, ...), custom_call_target="tpu_custom_call" | custom-call | flops 1342177280 | bytes 2490368 | tf_op jit(solution)/shard_map/feed_dense/pallas_call | solution.py:481
  216.0 7.6 %fusion.26 = f32[1024,1024]{1,0:T(8,128)} fusion(bf16[1280,1024]{1,0:T(8,128)(2,1)} %get-tuple-element.116, bf16[640,1024]{1,0:T(8,128)(2,1)} %collective-permute-done.14.side_ref, bf16[640,1024]{1,0:T(8,128)(2,1)} %collective-permute-done.12.own_ref), kind=kOutput, calls=%fused_computation.43 | convolution fusion | flops 2689597440 | bytes 9437184 | tf_op jit(solution)/shard_map/gd,gf->df/dot_general | solution.py:679
  228.1 7.4 %add_convert_fusion = (bf16[1024,1024]{1,0:T(8,128)(2,1)S(1)}, bf16[1024,1024]{1,0:T(8,128)(2,1)S(1)}) fusion(f32[1024,1024]{1,0:T(8,128)} %fusion.89, f32[1024,1024]{1,0:T(8,128)} %fusion.90, f32[1024,1024]{1,0:T(8,128)} %fusion.22, f32[1024,1024]{1,0:T(8,128)} %fusion.26), kind=kLoop, calls=%fused_computation.3 | loop fusion | flops 4194304 | bytes 20971520 | tf_op jit(solution)/shard_map/convert_element_type | solution.py:701
  244.7 40.2 %feed_routed.2 = (bf16[896,1024]{1,0:T(8,128)(2,1)}, bf16[896,1024]{1,0:T(8,128)(2,1)}, bf16[896,1024]{1,0:T(8,128)(2,1)}, bf16[896,1024]{1,0:T(8,128)(2,1)}, bf...) custom-call(s32[1]{0:T(128)} %bitcast.18.expert_ref, ...), custom_call_target="tpu_custom_call" | custom-call | flops 1879048192 | bytes 3276800 | tf_op jit(solution)/shard_map/feed_routed/pallas_call | solution.py:481
  293.8 25.5 %collective-permute-done.19 = bf16[640,1024]{1,0:T(8,128)(2,1)S(1)} collective-permute-done((bf16[640,1024]{1,0:T(8,128)(2,1)S(1)}, bf16[640,1024]{1,0:T(8,128)(2,1)S(1)}, u32[]{:S(2)}, u32[]{:S(2)}) %collective-permute-start.19) | collective-permute-done | bytes 1310752 | tf_op jit(solution)/shard_map/ppermute | solution.py:555
  319.4 27.3 %collective-permute-done.21 = bf16[640,1024]{1,0:T(8,128)(2,1)S(1)} collective-permute-done((bf16[640,1024]{1,0:T(8,128)(2,1)S(1)}, bf16[640,1024]{1,0:T(8,128)(2,1)S(1)}, u32[]{:S(2)}, u32[]{:S(2)}) %collective-permute-start.21) | collective-permute-done | bytes 1310752 | tf_op jit(solution)/shard_map/ppermute | solution.py:555
  349.1 39.6 %feed_routed.3 = (bf16[896,1024]{1,0:T(8,128)(2,1)}, bf16[896,1024]{1,0:T(8,128)(2,1)}, bf16[896,1024]{1,0:T(8,128)(2,1)}, bf16[896,1024]{1,0:T(8,128)(2,1)}, bf...) custom-call(s32[1]{0:T(128)} %bitcast.18.expert_ref, ...), custom_call_target="tpu_custom_call" | custom-call | flops 1879048192 | bytes 3276800 | tf_op jit(solution)/shard_map/feed_routed/pallas_call | solution.py:481
  397.4 6.3 all-to-all-start.3
  404.3 9.3 %fusion.91 = f32[1024,1024]{1,0:T(8,128)} fusion(bf16[1792,1024]{1,0:T(8,128)(2,1)} %get-tuple-element.143, bf16[1792,1024]{1,0:T(8,128)(2,1)} %get-tuple-element.144), kind=kOutput, calls=%fused_computation.163 | convolution fusion | flops 3758096384 | bytes 11534336 | tf_op jit(solution)/shard_map/gd,gf->df/dot_general | solution.py:679
  413.6 7.8 %fusion.4 = f32[1024,1024]{1,0:T(8,128)} fusion(bf16[1792,1024]{1,0:T(8,128)(2,1)S(1)} %copy-done.28, bf16[896,1024]{1,0:T(8,128)(2,1)} %collective-permute-done.15.side_ref, bf16[896,1024]{1,0:T(8,128)(2,1)} %collective-permute-done.13.own_ref), kind=kOutput, calls=%fused_computation.12 | convolution fusion | flops 3765436416 | bytes 11534336 | tf_op jit(solution)/shard_map/gd,gf->df/dot_general | solution.py:679
  427.1 19.6 %all-to-all-done.3 = bf16[8,112,1024]{2,1,0:T(8,128)(2,1)} async-done(((bf16[8,112,1024]{2,1,0:T(8,128)(2,1)}), bf16[8,112,1024]{2,1,0:T(8,128)(2,1)}, u32[]{:S(2)}, u32[]{:S(2)}) %all-to-all-start.3) | async-done | bytes 1835040 | tf_op jit(solution)/shard_map/all_to_all | solution.py:572
  480.6 15.0 %collective-permute-done.29 = bf16[640,1024]{1,0:T(8,128)(2,1)} collective-permute-done((bf16[640,1024]{1,0:T(8,128)(2,1)}, bf16[640,1024]{1,0:T(8,128)(2,1)}, u32[]{:S(2)}, u32[]{:S(2)}) %collective-permute-start.29) | collective-permute-done | bytes 1310752 | tf_op jit(solution)/shard_map/ppermute | solution.py:555
  495.6 10.4 %add_bitcast_fusion.1 = f32[1,1024,1024]{2,1,0:T(8,128)} fusion(f32[1024,1024]{1,0:T(8,128)} %fusion.4, bf16[1792,1024]{1,0:T(8,128)(2,1)} %get-tuple-element.139, bf16[896,1024]{1,0:T(8,128)(2,1)} %collective-permute-done.23.side_ref, bf16[896,1024]{1,0:T(8,128)(2,1)} %bitcast.17.own_ref), kind=kOutput, calls=%fused_computation.2 | convolution fusion | flops 3766484992 | bytes 15728640 | tf_op jit(solution)/shard_map/gd,gf->df/dot_general | solution.py:679
  513.6 40.9 %tree_attention_back.1 = (bf16[3,2,640,256]{3,2,1,0:T(8,128)(2,1)}, bf16[3,2,640,256]{3,2,1,0:T(8,128)(2,1)}) custom-call(s32[9]{0:T(128)} %pad_add_fusion.leaves_ref, bf16[3,2,640,256]{3,2,1,0:T(8,128)(2,1)} %bitcast.156, bf16[3,2,640,256]{3,2,1,0:T(8,128)(2,1)} %bitcast.158, bf16[2,640,256]{2,1,0:T(8,128)(2,1)} %bitcast.161, ...), custom_call_target="tpu_custom_call" | custom-call | flops 3103784960 | bytes 1310720 | tf_op jit(solution)/shard_map/tree_attention_back/pallas_call | solution.py:336
  589.8 28.2 %collective-permute-done.36 = bf16[640,1024]{1,0:T(8,128)(2,1)S(1)} collective-permute-done((bf16[640,1024]{1,0:T(8,128)(2,1)S(1)}, bf16[640,1024]{1,0:T(8,128)(2,1)S(1)}, u32[]{:S(2)}, u32[]{:S(2)}) %collective-permute-start.36) | collective-permute-done | bytes 1310752 | tf_op jit(solution)/shard_map/ppermute | solution.py:555
  625.5 6.5 add_convert_fusion.5
  645.1 8.7 %reduce-scatter.5.cloned.1.call-done = bf16[128,1152]{1,0:T(8,128)(2,1)} async-done(((bf16[1024,1152]{1,0:T(8,128)(2,1)}), bf16[128,1152]{1,0:T(8,128)(2,1)}) %reduce-scatter.5.cloned.1.call-update) | async-done | bytes 294928 | tf_op jit(solution)/shard_map/reduce_scatter | solution.py:577
  (270 shorter events, 210.5 us)
Async XLA Ops:
  12.7 32.3 %collective-permute-start = (bf16[640,1024]{1,0:T(8,128)(2,1)}, bf16[640,1024]{1,0:T(8,128)(2,1)}, u32[]{:S(2)}, u32[]{:S(2)}) collective-permute-start(bf16[640,1024]{1,0:T(8,128)(2,1)} %fusion.14), channel_id=1, source_target_pairs={{0,2},{1,3},{2,0},{3,1},{4,6},{5,7},{6,4},{7,5},{8,10},{9,11},{10,... | collective-permute-start | bytes 3932168 | tf_op jit(solution)/shard_map/ppermute | solution.py:555
  20.1 61.0 %all-to-all-start = ((bf16[8,112,1024]{2,1,0:T(8,128)(2,1)}), bf16[8,112,1024]{2,1,0:T(8,128)(2,1)}, u32[]{:S(2)}, u32[]{:S(2)}) async-start(bf16[8,112,1024]{2,1,0:T(8,128)(2,1)} %bitcast.144), calls=%async_computation | async-start | bytes 3670016 | tf_op jit(solution)/shard_map/all_to_all | solution.py:572
  45.0 36.1 %collective-permute-start.5 = (bf16[640,1024]{1,0:T(8,128)(2,1)}, bf16[640,1024]{1,0:T(8,128)(2,1)}, u32[]{:S(2)}, u32[]{:S(2)}) collective-permute-start(bf16[640,1024]{1,0:T(8,128)(2,1)} %own_grads_ref.1), channel_id=1, source_target_pairs={{0,1},{1,0},{2,3},{3,2},{4,5},{5,4},{6,7},{7,6},{8,9},{9,8},{10,11... | collective-permute-start | bytes 3932168 | tf_op jit(solution)/shard_map/ppermute | solution.py:551
  45.5 35.6 %collective-permute-start.4 = (bf16[640,1024]{1,0:T(8,128)(2,1)}, bf16[640,1024]{1,0:T(8,128)(2,1)}, u32[]{:S(2)}, u32[]{:S(2)}) collective-permute-start(bf16[640,1024]{1,0:T(8,128)(2,1)} %own_grads_ref.1), channel_id=1, source_target_pairs={{0,2},{1,3},{2,0},{3,1},{4,6},{5,7},{6,4},{7,5},{8,10},{9,11},{10,... | collective-permute-start | bytes 3932168 | tf_op jit(solution)/shard_map/ppermute | solution.py:555
  123.8 49.9 %all-to-all-start.1 = ((bf16[8,112,1024]{2,1,0:T(8,128)(2,1)}), bf16[8,112,1024]{2,1,0:T(8,128)(2,1)}, u32[]{:S(2)}, u32[]{:S(2)}) async-start(bf16[8,112,1024]{2,1,0:T(8,128)(2,1)} %bitcast.146), calls=%async_computation.1 | async-start | bytes 3670016 | tf_op jit(solution)/shard_map/all_to_all | solution.py:572
  130.1 43.5 %collective-permute-start.12 = (bf16[640,1024]{1,0:T(8,128)(2,1)}, bf16[640,1024]{1,0:T(8,128)(2,1)}, u32[]{:S(2)}, u32[]{:S(2)}) collective-permute-start(bf16[640,1024]{1,0:T(8,128)(2,1)} %copy-done.7), channel_id=1, source_target_pairs={{0,2},{1,3},{2,0},{3,1},{4,6},{5,7},{6,4},{7,5},{8,10},{9,11},{10,... | collective-permute-start | bytes 3932168 | tf_op jit(solution)/shard_map/ppermute | solution.py:555
  173.7 42.4 %collective-permute-start.13 = (bf16[896,1024]{1,0:T(8,128)(2,1)}, bf16[896,1024]{1,0:T(8,128)(2,1)}, u32[]{:S(2)}, u32[]{:S(2)}) collective-permute-start(bf16[896,1024]{1,0:T(8,128)(2,1)} %bitcast.17.own_ref), channel_id=1, source_target_pairs={{0,2},{1,3},{2,0},{3,1},{4,6},{5,7},{6,4},{7,5},{8,10},{9,11},{10,... | collective-permute-start | bytes 5505032 | tf_op jit(solution)/shard_map/ppermute | solution.py:555
  179.3 58.7 %all-to-all-start.2 = ((bf16[8,112,1024]{2,1,0:T(8,128)(2,1)}), bf16[8,112,1024]{2,1,0:T(8,128)(2,1)}, u32[]{:S(2)}, u32[]{:S(2)}) async-start(bf16[8,112,1024]{2,1,0:T(8,128)(2,1)} %bitcast.145), calls=%async_computation.2 | async-start | bytes 3670016 | tf_op jit(solution)/shard_map/all_to_all | solution.py:572
  185.3 239.7 %reduce-scatter.3.cloned.1.call-start = ((), (), s32[]{:S(2)}) async-start(), calls=%async_computation.7 | async-start | bytes 4718592 | tf_op jit(solution)/shard_map/reduce_scatter | solution.py:577
  238.4 47.0 %collective-permute-start.18 = (bf16[640,1024]{1,0:T(8,128)(2,1)}, bf16[640,1024]{1,0:T(8,128)(2,1)}, u32[]{:S(2)}, u32[]{:S(2)}) collective-permute-start(bf16[640,1024]{1,0:T(8,128)(2,1)} %get-tuple-element.125), channel_id=1, source_target_pairs={{0,1},{1,0},{2,3},{3,2},{4,5},{5,4},{6,7},{7,6},{8,9},{9,8},{10,11... | collective-permute-start | bytes 3932168 | tf_op jit(solution)/shard_map/ppermute | solution.py:551
  238.4 50.7 %collective-permute-start.20 = (bf16[640,1024]{1,0:T(8,128)(2,1)}, bf16[640,1024]{1,0:T(8,128)(2,1)}, u32[]{:S(2)}, u32[]{:S(2)}) collective-permute-start(bf16[640,1024]{1,0:T(8,128)(2,1)} %get-tuple-element.127), channel_id=1, source_target_pairs={{0,1},{1,0},{2,3},{3,2},{4,5},{5,4},{6,7},{7,6},{8,9},{9,8},{10,11... | collective-permute-start | bytes 3932168 | tf_op jit(solution)/shard_map/ppermute | solution.py:551
  285.1 64.0 %collective-permute-start.23 = (bf16[896,1024]{1,0:T(8,128)(2,1)}, bf16[896,1024]{1,0:T(8,128)(2,1)}, u32[]{:S(2)}, u32[]{:S(2)}) collective-permute-start(bf16[896,1024]{1,0:T(8,128)(2,1)} %bitcast.17.own_ref), channel_id=1, source_target_pairs={{0,1},{1,0},{2,3},{3,2},{4,5},{5,4},{6,7},{7,6},{8,9},{9,8},{10,11... | collective-permute-start | bytes 5505032 | tf_op jit(solution)/shard_map/ppermute | solution.py:551
  287.7 31.7 %collective-permute-start.19 = (bf16[640,1024]{1,0:T(8,128)(2,1)S(1)}, bf16[640,1024]{1,0:T(8,128)(2,1)S(1)}, u32[]{:S(2)}, u32[]{:S(2)}) collective-permute-start(bf16[640,1024]{1,0:T(8,128)(2,1)S(1)} %add_convert_fusion.7), channel_id=1, source_target_pairs={{0,2},{1,3},{2,0},{3,1},{4,6},{5,7},{6,4},{7,5},{8,10},{9,11},{10,... | collective-permute-start | bytes 3932168 | tf_op jit(solution)/shard_map/ppermute | solution.py:555
  291.0 55.6 %collective-permute-start.21 = (bf16[640,1024]{1,0:T(8,128)(2,1)S(1)}, bf16[640,1024]{1,0:T(8,128)(2,1)S(1)}, u32[]{:S(2)}, u32[]{:S(2)}) collective-permute-start(bf16[640,1024]{1,0:T(8,128)(2,1)S(1)} %add_convert_fusion.6), channel_id=1, source_target_pairs={{0,2},{1,3},{2,0},{3,1},{4,6},{5,7},{6,4},{7,5},{8,10},{9,11},{10,... | collective-permute-start | bytes 3932168 | tf_op jit(solution)/shard_map/ppermute | solution.py:555
  347.7 41.5 %collective-permute-start.25 = (bf16[896,1024]{1,0:T(8,128)(2,1)}, bf16[896,1024]{1,0:T(8,128)(2,1)}, u32[]{:S(2)}, u32[]{:S(2)}) collective-permute-start(bf16[896,1024]{1,0:T(8,128)(2,1)} %add_convert_fusion.3), channel_id=1, source_target_pairs={{0,2},{1,3},{2,0},{3,1},{4,6},{5,7},{6,4},{7,5},{8,10},{9,11},{10,... | collective-permute-start | bytes 5505032 | tf_op jit(solution)/shard_map/ppermute | solution.py:555
  397.4 49.3 %all-to-all-start.3 = ((bf16[8,112,1024]{2,1,0:T(8,128)(2,1)}), bf16[8,112,1024]{2,1,0:T(8,128)(2,1)}, u32[]{:S(2)}, u32[]{:S(2)}) async-start(bf16[8,112,1024]{2,1,0:T(8,128)(2,1)} %bitcast.143), calls=%async_computation.3 | async-start | bytes 3670016 | tf_op jit(solution)/shard_map/all_to_all | solution.py:572
  424.3 43.2 %collective-permute-start.33 = (bf16[896,1024]{1,0:T(8,128)(2,1)}, bf16[896,1024]{1,0:T(8,128)(2,1)}, u32[]{:S(2)}, u32[]{:S(2)}) collective-permute-start(bf16[896,1024]{1,0:T(8,128)(2,1)} %add_convert_fusion.2), channel_id=1, source_target_pairs={{0,2},{1,3},{2,0},{3,1},{4,6},{5,7},{6,4},{7,5},{8,10},{9,11},{10,... | collective-permute-start | bytes 5505032 | tf_op jit(solution)/shard_map/ppermute | solution.py:555
  424.9 42.6 %collective-permute-start.31 = (bf16[896,1024]{1,0:T(8,128)(2,1)}, bf16[896,1024]{1,0:T(8,128)(2,1)}, u32[]{:S(2)}, u32[]{:S(2)}) collective-permute-start(bf16[896,1024]{1,0:T(8,128)(2,1)} %get-tuple-element.155), channel_id=1, source_target_pairs={{0,1},{1,0},{2,3},{3,2},{4,5},{5,4},{6,7},{7,6},{8,9},{9,8},{10,11... | collective-permute-start | bytes 5505032 | tf_op jit(solution)/shard_map/ppermute | solution.py:551
  456.4 39.3 %collective-permute-start.29 = (bf16[640,1024]{1,0:T(8,128)(2,1)}, bf16[640,1024]{1,0:T(8,128)(2,1)}, u32[]{:S(2)}, u32[]{:S(2)}) collective-permute-start(bf16[640,1024]{1,0:T(8,128)(2,1)} %get-tuple-element.231), channel_id=1, source_target_pairs={{0,2},{1,3},{2,0},{3,1},{4,6},{5,7},{6,4},{7,5},{8,10},{9,11},{10,... | collective-permute-start | bytes 3932168 | tf_op jit(solution)/shard_map/ppermute | solution.py:555
  463.5 43.2 %collective-permute-start.26 = (bf16[640,1024]{1,0:T(8,128)(2,1)}, bf16[640,1024]{1,0:T(8,128)(2,1)}, u32[]{:S(2)}, u32[]{:S(2)}) collective-permute-start(bf16[640,1024]{1,0:T(8,128)(2,1)} %get-tuple-element.231), channel_id=1, source_target_pairs={{0,1},{1,0},{2,3},{3,2},{4,5},{5,4},{6,7},{7,6},{8,9},{9,8},{10,11... | collective-permute-start | bytes 3932168 | tf_op jit(solution)/shard_map/ppermute | solution.py:551
  472.7 89.4 %all-to-all-start.4 = ((bf16[8,112,1024]{2,1,0:T(8,128)(2,1)}), bf16[8,112,1024]{2,1,0:T(8,128)(2,1)}, u32[]{:S(2)}, u32[]{:S(2)}) async-start(bf16[8,112,1024]{2,1,0:T(8,128)(2,1)} %bitcast.142), calls=%async_computation.5 | async-start | bytes 3670016 | tf_op jit(solution)/shard_map/all_to_all | solution.py:572
  478.7 175.1 %reduce-scatter.5.cloned.1.call-start = ((), (), s32[]{:S(2)}) async-start(), calls=%async_computation.8 | async-start | bytes 2654208 | tf_op jit(solution)/shard_map/reduce_scatter | solution.py:577
  586.7 31.2 %collective-permute-start.36 = (bf16[640,1024]{1,0:T(8,128)(2,1)S(1)}, bf16[640,1024]{1,0:T(8,128)(2,1)S(1)}, u32[]{:S(2)}, u32[]{:S(2)}) collective-permute-start(bf16[640,1024]{1,0:T(8,128)(2,1)S(1)} %copy-done.37), channel_id=1, source_target_pairs={{0,2},{1,3},{2,0},{3,1},{4,6},{5,7},{6,4},{7,5},{8,10},{9,11},{10,... | collective-permute-start | bytes 3932168 | tf_op jit(solution)/shard_map/ppermute | solution.py:555
  587.4 38.1 %collective-permute-start.11 = (bf16[640,1024]{1,0:T(8,128)(2,1)}, bf16[640,1024]{1,0:T(8,128)(2,1)}, u32[]{:S(2)}, u32[]{:S(2)}) collective-permute-start(bf16[640,1024]{1,0:T(8,128)(2,1)} %get-tuple-element.105), channel_id=1, source_target_pairs={{0,1},{1,0},{2,3},{3,2},{4,5},{5,4},{6,7},{7,6},{8,9},{9,8},{10,11... | collective-permute-start | bytes 3932168 | tf_op jit(solution)/shard_map/ppermute | solution.py:551
  (67 other events, 668.0 us)
Sparse Core Ops, SparseCore 0:
  239.1 89.2 reduce-scatter.2
  584.2 69.5 reduce-scatter.4

commit v5 on v4

--- a/solution.py
+++ b/solution.py
@@ -176,12 +176,12 @@
     return pl.BlockSpec((parts, 2, quarter, PAIR), lambda p, leaves: (0, 0, 0, p))
 
 
-def attention_cost(products):
-    visited = (TRUNK * (TRUNK + QROWS) // 2 + BRANCHES * FAMILY * (TRUNK + SEG)) // COVER
+def attention_cost(products, cover):
+    visited = (TRUNK * (TRUNK + QROWS) // 2 + BRANCHES * FAMILY * (TRUNK + SEG)) // cover
     return pl.CostEstimate(
         flops=2 * products * 4 * visited * 2 * PAIR,
         transcendentals=4 * visited,
-        bytes_accessed=8 * TREE_LEN * 4 * HEAD_DIM * 2 // COVER,
+        bytes_accessed=8 * TREE_LEN * 4 * HEAD_DIM * 2 // cover,
     )
 
 
@@ -213,7 +213,7 @@
             jax.ShapeDtypeStruct((pairs, 2, TRUNK), F32),
             jax.ShapeDtypeStruct((pairs, BRANCHES, 2, FAMILY), F32),
         ],
-        cost_estimate=attention_cost(2),
+        cost_estimate=attention_cost(2, COVER),
         name="tree_attention",
     )(leaves, near, far)
 
@@ -360,7 +360,7 @@
             ],
         ),
         out_shape=[jax.ShapeDtypeStruct(near.shape, BF16), jax.ShapeDtypeStruct(far.shape, BF16)],
-        cost_estimate=attention_cost(5),
+        cost_estimate=attention_cost(5, 1),
         name="tree_attention_back",
     )(leaves, near, far, near_grads, far_grads, near_outs, far_outs, *logs)
 
@@ -577,6 +577,12 @@
     return lax.psum_scatter(strips, "expert", scatter_dimension=0, tiled=True).astype(F32)
 
 
+def strips_sum(strips):
+    count = lax.axis_size("expert")
+    strips = strips.reshape(count, -1, strips.shape[1])
+    return jnp.sum(exchange(strips).astype(F32), axis=0)
+
+
 def slots_of(expert_ids, experts, capacity):
     rows = expert_ids.shape[0]
     chosen = expert_ids[:, None] == jnp.arange(experts, dtype=jnp.int32)[None, :]
@@ -626,11 +632,13 @@
 
     own_slots, far_slots = slots_at(0), slots_at(2)
 
-    def dispatch(slots, rows):
-        placed = jnp.dot(slots, rows, preferred_element_type=F32).astype(BF16)
-        return exchange(placed.reshape(experts, capacity, width)).reshape(-1, width)
-
-    own_grads = dispatch(own_slots, cotangent)
+    def placed(slots, rows):
+        return jnp.dot(slots, rows, preferred_element_type=F32).astype(BF16)
+
+    def sent(rows):
+        return exchange(rows.reshape(experts, capacity, width)).reshape(-1, width)
+
+    own_grads = sent(placed(own_slots, cotangent))
     cotangent_side = from_side(cotangent)
 
     def project(rows):
@@ -659,8 +667,9 @@
     branch_far = from_far(far_sum)
     side_grads = from_side(own_grads)
     cotangent_corner = from_side(cotangent_far)
-    branch_far, side_grads, cotangent_corner = lax.optimization_barrier(
-        (branch_far, side_grads, cotangent_corner)
+    far_placed = placed(far_slots, cotangent_far)
+    branch_far, side_grads, cotangent_corner, far_placed = lax.optimization_barrier(
+        (branch_far, side_grads, cotangent_corner, far_placed)
     )
     residual = tokens.astype(F32) + (branch + branch_far.astype(F32))
 
@@ -668,7 +677,7 @@
     normed_two = (scaled_two * ln_mlp).astype(BF16)
     normed_two_far = from_far(normed_two)
     normed_two_side = from_side(normed_two)
-    own_rows = dispatch(own_slots, normed_two)
+    own_rows = sent(placed(own_slots, normed_two))
 
     def dense(own, side, own_cotangent, side_cotangent):
         return feed(
@@ -689,7 +698,7 @@
         (normed_two_far, grad_up, grad_down, own_rows)
     )
     far_rows = from_far(own_rows)
-    far_grads = dispatch(far_slots, after(cotangent_far, own_rows))
+    far_grads = sent(after(far_placed, own_rows))
     normed_two_corner = from_side(normed_two_far)
     far_dense = list(dense(normed_two_far, normed_two_corner, cotangent_far, cotangent_corner))
     far_rows, far_dense[6], far_dense[5] = lax.optimization_barrier(
@@ -716,29 +725,23 @@
             EXPERT_ROWS,
         )
 
-    far_rows, dense_grads = lax.optimization_barrier((far_rows, dense_grads))
+    def chip_sum(parts, place, *others):
+        return plus_side(parts[place], after(parts[place + 1], *others))
+
+    dense_back_far = chip_sum(far_dense, 2).astype(BF16)
+    dense_out_far = chip_sum(far_dense, 0).astype(BF16)
+    far_rows, dense_grads, dense_back_far, dense_out_far = lax.optimization_barrier(
+        (far_rows, dense_grads, dense_back_far, dense_out_far)
+    )
     dense_grads = scatter_sum(dense_grads)
     corner_rows = from_side(far_rows)
     side_rows = from_side(own_rows)
-
-    def chip_sum(parts, place, *others):
-        return plus_side(parts[place], after(parts[place + 1], *others))
-
     far_expert = routed(far_rows, corner_rows, far_grads, from_side(far_grads))
-    dense_back_far = from_far(chip_sum(far_dense, 2).astype(BF16))
-    dense_out_far = from_far(chip_sum(far_dense, 0).astype(BF16))
     dense_back, dense_out = chip_sum(near_dense, 2), chip_sum(near_dense, 0)
     far_back = chip_sum(far_expert, 2).astype(BF16)
-    own_rows, far_back, dense_back_far, dense_out_far = lax.optimization_barrier(
-        (own_rows, far_back, dense_back_far, dense_out_far)
-    )
+    own_rows, far_back = lax.optimization_barrier((own_rows, far_back))
     near_expert = routed(own_rows, side_rows, own_grads, side_grads)
-    dense_back = dense_back + dense_back_far.astype(F32)
-    dense_out = dense_out + dense_out_far.astype(F32)
-
-    def send_back(rows):
-        rows = rows.astype(BF16).reshape(experts, capacity, width)
-        return exchange(rows).reshape(-1, width)
+    dense_back = dense_back + from_far(after(dense_back_far, near_expert[2])).astype(F32)
 
     def picked(rows):
         return lax.dot_general(
@@ -746,12 +749,15 @@
         )
 
     expert_back = chip_sum(near_expert, 2) + from_far(far_back).astype(F32)
+    far_expert_out = chip_sum(far_expert, 0, far_back).astype(BF16)
+    expert_back, far_expert_out = lax.optimization_barrier(
+        (expert_back.astype(BF16), far_expert_out)
+    )
     grad_normed_two, dense_grads = lax.optimization_barrier(
-        (dense_back + picked(send_back(expert_back)), dense_grads)
-    )
-    far_expert_out = chip_sum(far_expert, 0, near_expert[2]).astype(BF16)
+        (dense_back + picked(sent(expert_back)), dense_grads)
+    )
     expert_out = chip_sum(near_expert, 0, expert_back) + from_far(far_expert_out).astype(F32)
-    expert_out = send_back(after(expert_out, grad_normed_two))
+    expert_out = sent(after(expert_out.astype(BF16), grad_normed_two))
 
     near_tokens = jnp.concatenate([own_rows, side_rows], axis=0)
     far_tokens = jnp.concatenate([far_rows, corner_rows], axis=0)
@@ -764,6 +770,9 @@
     )
     grad_branch = grad_residual.astype(BF16)
     grad_branch_far = from_far(grad_branch)
+    grad_branch_far, grad_ex_up, grad_ex_down = lax.optimization_barrier(
+        (grad_branch_far, grad_ex_up, grad_ex_down)
+    )
     near_branch = jnp.concatenate([grad_branch, from_side(grad_branch)], axis=0)
     far_branch = jnp.concatenate([grad_branch_far, from_side(grad_branch_far)], axis=0)
     head_grads = near_dense[7] + far_dense[7] + near_expert[7] + far_expert[7]
@@ -775,65 +784,59 @@
         return grads.astype(BF16).reshape(2, tok_dev, heads_width)
 
     near_heads, far_heads = into_heads(near_branch), into_heads(far_branch)
-    near_heads, grad_ex_up, grad_ex_down, small = lax.optimization_barrier(
-        (near_heads, grad_ex_up, grad_ex_down, small)
-    )
+    flat = (2 * tok_dev, heads_width)
+    small_columns = -(-small.shape[0] // LANES) * LANES
+    small_block = jnp.pad(small, ((0, small_columns - small.shape[0]), (0, 0))).T
+    grad_w_out = weight_grads(near_branch, far_branch, near_out.reshape(flat), far_out.reshape(flat))
+    side_grads = jnp.concatenate([grad_w_out.astype(BF16), small_block.astype(BF16)], axis=1)
+    dense_out_far = from_far(after(dense_out_far, grad_branch_far))
+    near_heads, side_grads = lax.optimization_barrier((near_heads, side_grads))
+    side_grads = scatter_sum(side_grads)
     near_result, far_result = attention_backward(
         leaves, near_qkv, far_qkv, near_heads, far_heads, near_out, far_out, logs
     )
-    near_result, expert_out = lax.optimization_barrier((near_result, expert_out))
+    near_result, far_result, expert_out, dense_out_far = lax.optimization_barrier(
+        (near_result, far_result, expert_out, dense_out_far)
+    )
 
     def normed_part(grads):
         return jnp.einsum("sgc,sdc->gd", grads, w_qkv, preferred_element_type=F32)
 
     corner_part = normed_part(far_result[:, 1])
-    far_result, corner_part = lax.optimization_barrier((far_result, corner_part))
-    far_sum = plus_side(normed_part(far_result[:, 0]), corner_part).astype(BF16)
-    near_result, far_result, near_branch, expert_out, far_sum = lax.optimization_barrier(
-        (near_result, far_result, near_branch, expert_out, far_sum)
+    from_corner = from_side(corner_part.astype(BF16)).astype(F32)
+    far_result, side_grads = lax.optimization_barrier((far_result, corner_part, side_grads))[::2]
+    far_sum = (normed_part(far_result[:, 0]) + from_corner).astype(BF16)
+    near_result, far_result, expert_out, far_sum = lax.optimization_barrier(
+        (near_result, far_result, expert_out, far_sum)
     )
     near_sum = plus_side(normed_part(near_result[:, 0]), normed_part(near_result[:, 1]))
-    grad_normed_one = near_sum + from_far(far_sum).astype(F32)
-    out = (residual + dense_out + picked(expert_out)).astype(BF16)
+    out = (residual + dense_out + dense_out_far.astype(F32) + picked(expert_out)).astype(BF16)
 
     near_result = near_result.reshape(3, 2 * tok_dev, heads_width)
     far_result = far_result.reshape(3, 2 * tok_dev, heads_width)
     grad_w_qkv = jnp.einsum(
         "gd,sgc->dsc", near_one, near_result, preferred_element_type=F32
     ) + jnp.einsum("gd,sgc->dsc", far_one, far_result, preferred_element_type=F32)
-    flat = (2 * tok_dev, heads_width)
-    grad_w_out = weight_grads(near_branch, far_branch, near_out.reshape(flat), far_out.reshape(flat))
-    small_columns = -(-small.shape[0] // LANES) * LANES
-    small_block = jnp.pad(small, ((0, small_columns - small.shape[0]), (0, 0))).T
-    last_grads = scatter_sum(
-        jnp.concatenate(
-            [
-                grad_w_qkv.reshape(width, 3 * heads_width).astype(BF16),
-                grad_w_out.astype(BF16),
-                small_block.astype(BF16),
-            ],
-            axis=1,
-        )
-    )
+    qkv_grads = strips_sum(grad_w_qkv.reshape(width, 3 * heads_width).astype(BF16))
     scaled_far = normed_far.astype(F32) / ln_attn
     gain_one = jnp.sum(near_sum * scaled_one + far_sum.astype(F32) * scaled_far, axis=0, keepdims=True)
-    grad_ln_attn = sum_over(sum_over(gain_one, "tensor"), "expert")[0]
+    gain_one = sum_over(sum_over(gain_one, "tensor"), "expert")
+    far_sum, grad_ln_attn = lax.optimization_barrier((from_far(far_sum), gain_one[0]))
+    grad_normed_one = near_sum + far_sum.astype(F32)
     grad_tokens = grad_residual + norm_back(grad_normed_one, ln_attn, scaled_one, inverse_one)
 
-    strip = last_grads.shape[0]
-    after_qkv = 3 * heads_width
-    after_out = after_qkv + heads_width
+    strip = qkv_grads.shape[0]
     return (
         out,
         grad_tokens,
         grad_ln_attn,
-        last_grads[:, :after_qkv].reshape(strip, 3, heads_width).transpose(1, 0, 2),
-        last_grads[:, after_qkv:after_out].T,
-        last_grads[:, after_out + experts + 2],
+        qkv_grads.reshape(strip, 3, heads_width).transpose(1, 0, 2),
+        side_grads[:, :heads_width].T,
+        side_grads[:, heads_width + experts + 2],
         dense_grads[:, :hidden],
         dense_grads[:, hidden:].T,
-        last_grads[:, after_out : after_out + experts],
-        last_grads[:, after_out + experts : after_out + experts + 2],
+        side_grads[:, heads_width : heads_width + experts],
+        side_grads[:, heads_width + experts : heads_width + experts + 2],
         grad_ex_up,
         grad_ex_down,
     )

time: 673 us -> 671 us (level)
  waiting for transfers between devices: 191 us -> 176 us
  other arithmetic: 55.3 us -> 69.8 us
  matrix products: 128 us -> 119 us
    ppermute x11, waiting for transfers between devices: 141 us -> 90.7 us  [from_far(): return lax.ppermute(values, 'tensor', [(i, i ^ 2) for i in range(4)])]
    ppermute x7, waiting for transfers between devices: 3.33 us -> 25.8 us  [sum_over(): values = values + lax.ppermute(values, axis, pairs)]
    convert_element_type x3 -> x6, other arithmetic: 6.14 us -> 23.9 us  [the longest x1 5.18 us: per_device(): expert_out = sent(after(expert_out.astype(BF16), grad_normed_two))]
    reduce_scatter x2, waiting for transfers between devices: 8.73 us -> 23.1 us  [scatter_sum(): lax.psum_scatter(strips, 'expert', scatter_dimension=0, tiled=True)]
    add x2 -> x1, other arithmetic: 9.68 us -> 2.82 us  [per_device(): dense_back + picked(sent(expert_back))]
    all_to_all x5 -> x6, starting transfers between devices: 30.9 us -> 35.5 us  [exchange(): lax.all_to_all(blocks, 'expert', split_axis=0, concat_axis=0, tiled=True)]
    all_to_all x5 -> x6, waiting for transfers between devices: 19.6 us -> 18.6 us  [exchange(): lax.all_to_all(blocks, 'expert', split_axis=0, concat_axis=0, tiled=True)]
  transfers between devices with their start and end apart: 49 -> 50, of which waited for: 20 -> 15; matrix products, arithmetic and copies ran while one was open for 24% -> 28% of each run, Pallas kernels for 30% -> 30%
where the time goes in v5:
time: 671 us; the launch traced here: 667 us
  Pallas kernels  203 us (30%)
  waiting for transfers between devices  176 us (26%)
  matrix products  119 us (18%)
  other arithmetic  69.8 us (10%)
  starting transfers between devices  62.8 us (9%)
  local copies, waits for them, and re-layouts  21.5 us (3%)
  between operations  15.1 us (2%)
    pallas_call x4, Pallas kernels, feed(): pl.pallas_call(functools.partial(feed_kernel, experts, routed), grid_spec...  136 us
    ppermute x11, waiting for transfers between devices, from_far(): return lax.ppermute(values, 'tensor', [(i, i ^ 2) for i in range(4)])  90.7 us
    dot_general x10, matrix products, product(): return jnp.einsum('gd,gf->df', left, right, preferred_element_type=F32)  55.4 us
    pallas_call x1, Pallas kernels, attention_backward(): pl.pallas_call(backward_kernel, grid_spec=pltpu.PrefetchScalarGridSpec(nu...  41.1 us
    all_to_all x6, starting transfers between devices, exchange(): lax.all_to_all(blocks, 'expert', split_axis=0, concat_axis=0, tiled=True)  35.5 us
    ppermute x7, waiting for transfers between devices, sum_over(): values = values + lax.ppermute(values, axis, pairs)  25.8 us
    pallas_call x1, Pallas kernels, attention_forward(): pl.pallas_call(forward_kernel, grid_spec=pltpu.PrefetchScalarGridSpec(num...  25.4 us
    reduce_scatter x2, waiting for transfers between devices, scatter_sum(): lax.psum_scatter(strips, 'expert', scatter_dimension=0, tiled=True)  23.1 us
  transfers between devices with their start and end apart: 50, of which 15 were waited for; matrix products, arithmetic and copies ran while one was open for 28% of the time, Pallas kernels for 30%

profile of v5, /device:TPU:0, one launch (start us, length us, event | category | flops | bytes accessed | tf_op | source)
XLA Modules:
  0.0 666.6 jit_solution(16082569047758304381)
XLA Ops:
  20.2 6.3 all-to-all-start
  33.0 12.0 %collective-permute-done = bf16[640,1024]{1,0:T(8,128)(2,1)} collective-permute-done((bf16[640,1024]{1,0:T(8,128)(2,1)}, bf16[640,1024]{1,0:T(8,128)(2,1)}, u32[]{:S(2)}, u32[]{:S(2)}) %collective-permute-start) | collective-permute-done | bytes 1310752 | tf_op jit(solution)/shard_map/ppermute | solution.py:555
  55.5 25.4 %tree_attention.1 = (bf16[2,640,256]{2,1,0:T(8,128)(2,1)}, bf16[2,640,256]{2,1,0:T(8,128)(2,1)}, f32[2,2,1024]{2,1,0:T(2,128)}, f32[2,4,2,384]{3,2,1,0:T(2,128)}) custom-call(s32[9]{0:T(128)} %pad_add_fusion.leaves_ref, bf16[3,2,640,256]{3,2,1,0:T(8,128)(2,1)} %bitcast.161, bf16[3,2,640,256]{3,2,1,0:T(8,128)(2,1)} %bitcast.163), custom_call_target="tpu_custom_call" | custom-call | flops 1241513984 | bytes 1310720 | tf_op jit(solution)/shard_map/tree_attention/pallas_call | solution.py:192
  94.8 23.8 %collective-permute-done.7 = bf16[640,1024]{1,0:T(8,128)(2,1)S(1)} collective-permute-done((bf16[640,1024]{1,0:T(8,128)(2,1)S(1)}, bf16[640,1024]{1,0:T(8,128)(2,1)S(1)}, u32[]{:S(2)}, u32[]{:S(2)}) %collective-permute-start.7) | collective-permute-done | bytes 1310752 | tf_op jit(solution)/shard_map/ppermute | solution.py:555
  123.6 6.5 all-to-all-start.1
  133.5 28.1 %feed_dense.2 = (bf16[640,1024]{1,0:T(8,128)(2,1)}, bf16[640,1024]{1,0:T(8,128)(2,1)}, bf16[640,1024]{1,0:T(8,128)(2,1)}, bf16[640,1024]{1,0:T(8,128)(2,1)}, bf1...) custom-call(s32[1]{0:T(128)} %constant.47.clone.1.expert_ref, ...), custom_call_target="tpu_custom_call" | custom-call | flops 1342177280 | bytes 2490368 | tf_op jit(solution)/shard_map/feed_dense/pallas_call | solution.py:481
  161.6 7.7 %fusion.22 = f32[1024,1024]{1,0:T(8,128)} fusion(bf16[1280,1024]{1,0:T(8,128)(2,1)} %get-tuple-element.117, bf16[640,1024]{1,0:T(8,128)(2,1)} %collective-permute-done.10.side_ref, bf16[640,1024]{1,0:T(8,128)(2,1)} %copy-done.7), kind=kOutput, calls=%fused_computation.40 | convolution fusion | flops 2689597440 | bytes 9437184 | tf_op jit(solution)/shard_map/gd,gf->df/dot_general | solution.py:688
  175.5 6.0 all-to-all-start.2
  181.6 28.3 %feed_dense.3 = (bf16[640,1024]{1,0:T(8,128)(2,1)}, bf16[640,1024]{1,0:T(8,128)(2,1)}, bf16[640,1024]{1,0:T(8,128)(2,1)}, bf16[640,1024]{1,0:T(8,128)(2,1)}, bf1...) custom-call(s32[1]{0:T(128)} %constant.47.clone.1.expert_ref, ...), custom_call_target="tpu_custom_call" | custom-call | flops 1342177280 | bytes 2490368 | tf_op jit(solution)/shard_map/feed_dense/pallas_call | solution.py:481
  216.2 7.6 %fusion.94 = f32[1024,1024]{1,0:T(8,128)} fusion(bf16[1280,1024]{1,0:T(8,128)(2,1)} %get-tuple-element.129, bf16[1280,1024]{1,0:T(8,128)(2,1)} %get-tuple-element.130), kind=kOutput, calls=%fused_computation.167 | convolution fusion | flops 2684354560 | bytes 9437184 | tf_op jit(solution)/shard_map/gd,gf->df/dot_general | solution.py:688
  223.8 6.3 fusion.26
  230.1 7.4 %add_convert_fusion = (bf16[1024,1024]{1,0:T(8,128)(2,1)S(1)}, bf16[1024,1024]{1,0:T(8,128)(2,1)S(1)}) fusion(f32[1024,1024]{1,0:T(8,128)} %fusion.93, f32[1024,1024]{1,0:T(8,128)} %fusion.94, f32[1024,1024]{1,0:T(8,128)} %fusion.22, f32[1024,1024]{1,0:T(8,128)} %fusion.26), kind=kLoop, calls=%fused_computation.3 | loop fusion | flops 4194304 | bytes 20971520 | tf_op jit(solution)/shard_map/convert_element_type | solution.py:710
  253.0 40.0 %feed_routed.2 = (bf16[896,1024]{1,0:T(8,128)(2,1)}, bf16[896,1024]{1,0:T(8,128)(2,1)}, bf16[896,1024]{1,0:T(8,128)(2,1)}, bf16[896,1024]{1,0:T(8,128)(2,1)}, bf...) custom-call(s32[1]{0:T(128)} %bitcast.19.expert_ref, ...), custom_call_target="tpu_custom_call" | custom-call | flops 1879048192 | bytes 3276800 | tf_op jit(solution)/shard_map/feed_routed/pallas_call | solution.py:481
  303.8 39.8 %feed_routed.3 = (bf16[896,1024]{1,0:T(8,128)(2,1)}, bf16[896,1024]{1,0:T(8,128)(2,1)}, bf16[896,1024]{1,0:T(8,128)(2,1)}, bf16[896,1024]{1,0:T(8,128)(2,1)}, bf...) custom-call(s32[1]{0:T(128)} %bitcast.19.expert_ref, ...), custom_call_target="tpu_custom_call" | custom-call | flops 1879048192 | bytes 3276800 | tf_op jit(solution)/shard_map/feed_routed/pallas_call | solution.py:481
  352.1 6.3 all-to-all-start.3
  358.6 6.9 %fusion.4 = f32[1024,1024]{1,0:T(8,128)S(1)} fusion(bf16[1792,1024]{1,0:T(8,128)(2,1)} %get-tuple-element.154, bf16[896,1024]{1,0:T(8,128)(2,1)} %collective-permute-done.18.side_ref, bf16[896,1024]{1,0:T(8,128)(2,1)} %collective-permute-done.14.own_ref), kind=kOutput, calls=%fused_computation.12 | convolution fusion | flops 3765436416 | bytes 11534336 | tf_op jit(solution)/shard_map/gd,gf->df/dot_general | solution.py:688
  371.4 7.6 %add_bitcast_fusion.1 = f32[1,1024,1024]{2,1,0:T(8,128)} fusion(f32[1024,1024]{1,0:T(8,128)S(1)} %fusion.4, bf16[1792,1024]{1,0:T(8,128)(2,1)S(1)} %copy-done.35, bf16[896,1024]{1,0:T(8,128)(2,1)} %collective-permute-done.21.side_ref, bf16[896,1024]{1,0:T(8,128)(2,1)} %bitcast.18.own_ref), kind=kOutput, calls=%fused_computation.2 | convolution fusion | flops 3766484992 | bytes 15728640 | tf_op jit(solution)/shard_map/gd,gf->df/dot_general | solution.py:688
  383.1 18.6 %all-to-all-done.3 = bf16[8,112,1024]{2,1,0:T(8,128)(2,1)} async-done(((bf16[8,112,1024]{2,1,0:T(8,128)(2,1)}), bf16[8,112,1024]{2,1,0:T(8,128)(2,1)}, u32[]{:S(2)}, u32[]{:S(2)}) %all-to-all-start.3) | async-done | bytes 1835040 | tf_op jit(solution)/shard_map/all_to_all | solution.py:572
  414.1 5.7 add_bitcast_fusion
  420.8 49.1 %collective-permute-done.27 = bf16[640,1024]{1,0:T(8,128)(2,1)} collective-permute-done((bf16[640,1024]{1,0:T(8,128)(2,1)}, bf16[640,1024]{1,0:T(8,128)(2,1)}, u32[]{:S(2)}, u32[]{:S(2)}) %collective-permute-start.27) | collective-permute-done | bytes 1310752 | tf_op jit(solution)/shard_map/ppermute | solution.py:555
  481.4 6.0 all-to-all-start.4
  506.9 41.1 %tree_attention_back.1 = (bf16[3,2,640,256]{3,2,1,0:T(8,128)(2,1)}, bf16[3,2,640,256]{3,2,1,0:T(8,128)(2,1)}) custom-call(s32[9]{0:T(128)} %pad_add_fusion.leaves_ref, bf16[3,2,640,256]{3,2,1,0:T(8,128)(2,1)} %bitcast.162, bf16[3,2,640,256]{3,2,1,0:T(8,128)(2,1)} %bitcast.164, bf16[2,640,256]{2,1,0:T(8,128)(2,1)} %bitcast.167, ...), custom_call_target="tpu_custom_call" | custom-call | flops 24830279680 | bytes 10485760 | tf_op jit(solution)/shard_map/tree_attention_back/pallas_call | solution.py:336
  551.6 23.1 %reduce-scatter.5.cloned.1.call-done = bf16[128,384]{1,0:T(8,128)(2,1)} async-done(((bf16[1024,384]{1,0:T(8,128)(2,1)}), bf16[128,384]{1,0:T(8,128)(2,1)}) %reduce-scatter.5.cloned.1.call-update) | async-done | bytes 98320 | tf_op jit(solution)/shard_map/reduce_scatter | solution.py:577
  612.9 20.6 %collective-permute-done.38 = f32[1,1024]{1,0:T(1,128)S(1)} collective-permute-done((f32[1,1024]{1,0:T(1,128)S(1)}, f32[1,1024]{1,0:T(1,128)S(1)}, u32[]{:S(2)}, u32[]{:S(2)}) %collective-permute-start.38) | collective-permute-done | bytes 4128 | tf_op jit(solution)/shard_map/ppermute | solution.py:566
  (280 shorter events, 221.3 us)
Async XLA Ops:
  20.2 60.8 %all-to-all-start = ((bf16[8,112,1024]{2,1,0:T(8,128)(2,1)}), bf16[8,112,1024]{2,1,0:T(8,128)(2,1)}, u32[]{:S(2)}, u32[]{:S(2)}) async-start(bf16[8,112,1024]{2,1,0:T(8,128)(2,1)} %bitcast.152), calls=%async_computation | async-start | bytes 3670016 | tf_op jit(solution)/shard_map/all_to_all | solution.py:572
  45.0 35.9 %collective-permute-start.5 = (bf16[640,1024]{1,0:T(8,128)(2,1)}, bf16[640,1024]{1,0:T(8,128)(2,1)}, u32[]{:S(2)}, u32[]{:S(2)}) collective-permute-start(bf16[640,1024]{1,0:T(8,128)(2,1)} %own_grads_ref.1), channel_id=1, source_target_pairs={{0,1},{1,0},{2,3},{3,2},{4,5},{5,4},{6,7},{7,6},{8,9},{9,8},{10,11... | collective-permute-start | bytes 3932168 | tf_op jit(solution)/shard_map/ppermute | solution.py:551
  45.5 35.4 %collective-permute-start.4 = (bf16[640,1024]{1,0:T(8,128)(2,1)}, bf16[640,1024]{1,0:T(8,128)(2,1)}, u32[]{:S(2)}, u32[]{:S(2)}) collective-permute-start(bf16[640,1024]{1,0:T(8,128)(2,1)} %own_grads_ref.1), channel_id=1, source_target_pairs={{0,2},{1,3},{2,0},{3,1},{4,6},{5,7},{6,4},{7,5},{8,10},{9,11},{10,... | collective-permute-start | bytes 3932168 | tf_op jit(solution)/shard_map/ppermute | solution.py:555
  123.6 50.2 %all-to-all-start.1 = ((bf16[8,112,1024]{2,1,0:T(8,128)(2,1)}), bf16[8,112,1024]{2,1,0:T(8,128)(2,1)}, u32[]{:S(2)}, u32[]{:S(2)}) async-start(bf16[8,112,1024]{2,1,0:T(8,128)(2,1)} %bitcast.153), calls=%async_computation.1 | async-start | bytes 3670016 | tf_op jit(solution)/shard_map/all_to_all | solution.py:572
  130.1 43.7 %collective-permute-start.13 = (bf16[640,1024]{1,0:T(8,128)(2,1)}, bf16[640,1024]{1,0:T(8,128)(2,1)}, u32[]{:S(2)}, u32[]{:S(2)}) collective-permute-start(bf16[640,1024]{1,0:T(8,128)(2,1)} %copy-done.7), channel_id=1, source_target_pairs={{0,2},{1,3},{2,0},{3,1},{4,6},{5,7},{6,4},{7,5},{8,10},{9,11},{10,... | collective-permute-start | bytes 3932168 | tf_op jit(solution)/shard_map/ppermute | solution.py:555
  173.8 42.4 %collective-permute-start.14 = (bf16[896,1024]{1,0:T(8,128)(2,1)}, bf16[896,1024]{1,0:T(8,128)(2,1)}, u32[]{:S(2)}, u32[]{:S(2)}) collective-permute-start(bf16[896,1024]{1,0:T(8,128)(2,1)} %bitcast.18.own_ref), channel_id=1, source_target_pairs={{0,2},{1,3},{2,0},{3,1},{4,6},{5,7},{6,4},{7,5},{8,10},{9,11},{10,... | collective-permute-start | bytes 5505032 | tf_op jit(solution)/shard_map/ppermute | solution.py:555
  175.5 70.7 %all-to-all-start.2 = ((bf16[8,112,1024]{2,1,0:T(8,128)(2,1)}), bf16[8,112,1024]{2,1,0:T(8,128)(2,1)}, u32[]{:S(2)}, u32[]{:S(2)}) async-start(bf16[8,112,1024]{2,1,0:T(8,128)(2,1)} %bitcast.151), calls=%async_computation.2 | async-start | bytes 3670016 | tf_op jit(solution)/shard_map/all_to_all | solution.py:572
  181.5 199.4 %reduce-scatter.3.cloned.1.call-start = ((), (), s32[]{:S(2)}) async-start(), calls=%async_computation.8 | async-start | bytes 4718592 | tf_op jit(solution)/shard_map/reduce_scatter | solution.py:577
  210.2 33.1 %collective-permute-start.17 = (bf16[640,1024]{1,0:T(8,128)(2,1)}, bf16[640,1024]{1,0:T(8,128)(2,1)}, u32[]{:S(2)}, u32[]{:S(2)}) collective-permute-start(bf16[640,1024]{1,0:T(8,128)(2,1)} %get-tuple-element.134), channel_id=1, source_target_pairs={{0,1},{1,0},{2,3},{3,2},{4,5},{5,4},{6,7},{7,6},{8,9},{9,8},{10,11... | collective-permute-start | bytes 3932168 | tf_op jit(solution)/shard_map/ppermute | solution.py:551
  301.9 41.9 %collective-permute-start.25 = (bf16[896,1024]{1,0:T(8,128)(2,1)}, bf16[896,1024]{1,0:T(8,128)(2,1)}, u32[]{:S(2)}, u32[]{:S(2)}) collective-permute-start(bf16[896,1024]{1,0:T(8,128)(2,1)} %get-tuple-element.149), channel_id=1, source_target_pairs={{0,1},{1,0},{2,3},{3,2},{4,5},{5,4},{6,7},{7,6},{8,9},{9,8},{10,11... | collective-permute-start | bytes 5505032 | tf_op jit(solution)/shard_map/ppermute | solution.py:551
  302.0 46.1 %collective-permute-start.24 = (bf16[896,1024]{1,0:T(8,128)(2,1)}, bf16[896,1024]{1,0:T(8,128)(2,1)}, u32[]{:S(2)}, u32[]{:S(2)}) collective-permute-start(bf16[896,1024]{1,0:T(8,128)(2,1)} %add_convert_fusion.5), channel_id=1, source_target_pairs={{0,2},{1,3},{2,0},{3,1},{4,6},{5,7},{6,4},{7,5},{8,10},{9,11},{10,... | collective-permute-start | bytes 5505032 | tf_op jit(solution)/shard_map/ppermute | solution.py:555
  352.1 49.5 %all-to-all-start.3 = ((bf16[8,112,1024]{2,1,0:T(8,128)(2,1)}), bf16[8,112,1024]{2,1,0:T(8,128)(2,1)}, u32[]{:S(2)}, u32[]{:S(2)}) async-start(bf16[8,112,1024]{2,1,0:T(8,128)(2,1)} %bitcast.148), calls=%async_computation.3 | async-start | bytes 3670016 | tf_op jit(solution)/shard_map/all_to_all | solution.py:572
  358.4 46.4 %collective-permute-start.12 = (bf16[640,1024]{1,0:T(8,128)(2,1)}, bf16[640,1024]{1,0:T(8,128)(2,1)}, u32[]{:S(2)}, u32[]{:S(2)}) collective-permute-start(bf16[640,1024]{1,0:T(8,128)(2,1)} %get-tuple-element.116), channel_id=1, source_target_pairs={{0,1},{1,0},{2,3},{3,2},{4,5},{5,4},{6,7},{7,6},{8,9},{9,8},{10,11... | collective-permute-start | bytes 3932168 | tf_op jit(solution)/shard_map/ppermute | solution.py:551
  371.1 33.7 %collective-permute-start.22 = (bf16[640,1024]{1,0:T(8,128)(2,1)}, bf16[640,1024]{1,0:T(8,128)(2,1)}, u32[]{:S(2)}, u32[]{:S(2)}) collective-permute-start(bf16[640,1024]{1,0:T(8,128)(2,1)} %add_convert_fusion.9), channel_id=1, source_target_pairs={{0,2},{1,3},{2,0},{3,1},{4,6},{5,7},{6,4},{7,5},{8,10},{9,11},{10,... | collective-permute-start | bytes 3932168 | tf_op jit(solution)/shard_map/ppermute | solution.py:555
  379.0 97.2 %collective-permute-start.31 = (bf16[896,1024]{1,0:T(8,128)(2,1)}, bf16[896,1024]{1,0:T(8,128)(2,1)}, u32[]{:S(2)}, u32[]{:S(2)}) collective-permute-start(bf16[896,1024]{1,0:T(8,128)(2,1)} %get-tuple-element.171), channel_id=1, source_target_pairs={{0,1},{1,0},{2,3},{3,2},{4,5},{5,4},{6,7},{7,6},{8,9},{9,8},{10,11... | collective-permute-start | bytes 5505032 | tf_op jit(solution)/shard_map/ppermute | solution.py:551
  379.2 97.0 %collective-permute-start.32 = (bf16[896,1024]{1,0:T(8,128)(2,1)}, bf16[896,1024]{1,0:T(8,128)(2,1)}, u32[]{:S(2)}, u32[]{:S(2)}) collective-permute-start(bf16[896,1024]{1,0:T(8,128)(2,1)} %add_convert_fusion.3), channel_id=1, source_target_pairs={{0,2},{1,3},{2,0},{3,1},{4,6},{5,7},{6,4},{7,5},{8,10},{9,11},{10,... | collective-permute-start | bytes 5505032 | tf_op jit(solution)/shard_map/ppermute | solution.py:555
  412.5 57.4 %collective-permute-start.27 = (bf16[640,1024]{1,0:T(8,128)(2,1)}, bf16[640,1024]{1,0:T(8,128)(2,1)}, u32[]{:S(2)}, u32[]{:S(2)}) collective-permute-start(bf16[640,1024]{1,0:T(8,128)(2,1)} %get-tuple-element.248), channel_id=1, source_target_pairs={{0,2},{1,3},{2,0},{3,1},{4,6},{5,7},{6,4},{7,5},{8,10},{9,11},{10,... | collective-permute-start | bytes 3932168 | tf_op jit(solution)/shard_map/ppermute | solution.py:555
  419.8 73.5 %collective-permute-start.26 = (bf16[640,1024]{1,0:T(8,128)(2,1)}, bf16[640,1024]{1,0:T(8,128)(2,1)}, u32[]{:S(2)}, u32[]{:S(2)}) collective-permute-start(bf16[640,1024]{1,0:T(8,128)(2,1)} %get-tuple-element.248), channel_id=1, source_target_pairs={{0,1},{1,0},{2,3},{3,2},{4,5},{5,4},{6,7},{7,6},{8,9},{9,8},{10,11... | collective-permute-start | bytes 3932168 | tf_op jit(solution)/shard_map/ppermute | solution.py:551
  481.4 66.6 %all-to-all-start.4 = ((bf16[8,112,1024]{2,1,0:T(8,128)(2,1)}), bf16[8,112,1024]{2,1,0:T(8,128)(2,1)}, u32[]{:S(2)}, u32[]{:S(2)}) async-start(bf16[8,112,1024]{2,1,0:T(8,128)(2,1)} %bitcast.147), calls=%async_computation.5 | async-start | bytes 3670016 | tf_op jit(solution)/shard_map/all_to_all | solution.py:572
  487.4 87.3 %reduce-scatter.5.cloned.1.call-start = ((), (), s32[]{:S(2)}) async-start(), calls=%async_computation.9 | async-start | bytes 884736 | tf_op jit(solution)/shard_map/reduce_scatter | solution.py:577
  491.5 56.5 %collective-permute-start.33 = (bf16[640,1024]{1,0:T(8,128)(2,1)}, bf16[640,1024]{1,0:T(8,128)(2,1)}, u32[]{:S(2)}, u32[]{:S(2)}) collective-permute-start(bf16[640,1024]{1,0:T(8,128)(2,1)} %add_convert_fusion.8), channel_id=1, source_target_pairs={{0,2},{1,3},{2,0},{3,1},{4,6},{5,7},{6,4},{7,5},{8,10},{9,11},{10,... | collective-permute-start | bytes 3932168 | tf_op jit(solution)/shard_map/ppermute | solution.py:555
  582.6 64.2 %collective-permute-start.11 = (bf16[640,1024]{1,0:T(8,128)(2,1)}, bf16[640,1024]{1,0:T(8,128)(2,1)}, u32[]{:S(2)}, u32[]{:S(2)}) collective-permute-start(bf16[640,1024]{1,0:T(8,128)(2,1)} %get-tuple-element.114), channel_id=1, source_target_pairs={{0,1},{1,0},{2,3},{3,2},{4,5},{5,4},{6,7},{7,6},{8,9},{9,8},{10,11... | collective-permute-start | bytes 3932168 | tf_op jit(solution)/shard_map/ppermute | solution.py:551
  597.9 59.1 %all-to-all-start.5 = ((bf16[8,128,768]{1,2,0:T(8,128)(2,1)}), bf16[8,128,768]{1,2,0:T(8,128)(2,1)}, u32[]{:S(2)}, u32[]{:S(2)}) async-start(bf16[8,128,768]{1,2,0:T(8,128)(2,1)} %copy.89), calls=%async_computation.7 | async-start | bytes 3145728 | tf_op jit(solution)/shard_map/all_to_all | solution.py:572
  602.4 49.2 %collective-permute-start.36 = (bf16[640,1024]{1,0:T(8,128)(2,1)}, bf16[640,1024]{1,0:T(8,128)(2,1)}, u32[]{:S(2)}, u32[]{:S(2)}) collective-permute-start(bf16[640,1024]{1,0:T(8,128)(2,1)} %fusion.30), channel_id=1, source_target_pairs={{0,2},{1,3},{2,0},{3,1},{4,6},{5,7},{6,4},{7,5},{8,10},{9,11},{10,... | collective-permute-start | bytes 3932168 | tf_op jit(solution)/shard_map/ppermute | solution.py:555
  (71 other events, 688.6 us)
Sparse Core Ops, SparseCore 0:
  246.9 89.5 reduce-scatter.2
  503.6 71.0 reduce-scatter.4

commit v6 on v5

--- a/solution.py
+++ b/solution.py
@@ -577,10 +577,12 @@
     return lax.psum_scatter(strips, "expert", scatter_dimension=0, tiled=True).astype(F32)
 
 
-def strips_sum(strips):
-    count = lax.axis_size("expert")
-    strips = strips.reshape(count, -1, strips.shape[1])
-    return jnp.sum(exchange(strips).astype(F32), axis=0)
+def strips_sent(grads):
+    return exchange(grads.reshape(lax.axis_size("expert"), -1, grads.shape[1]))
+
+
+def strips_total(strips):
+    return jnp.sum(strips.astype(F32), axis=0)
 
 
 def slots_of(expert_ids, experts, capacity):
@@ -701,13 +703,6 @@
     far_grads = sent(after(far_placed, own_rows))
     normed_two_corner = from_side(normed_two_far)
     far_dense = list(dense(normed_two_far, normed_two_corner, cotangent_far, cotangent_corner))
-    far_rows, far_dense[6], far_dense[5] = lax.optimization_barrier(
-        (far_rows, far_dense[6], far_dense[5])
-    )
-    far_two = jnp.concatenate([normed_two_far, normed_two_corner], axis=0)
-    grad_up = grad_up + product(far_two, far_dense[5])
-    grad_down = grad_down + product(far_dense[6], far_dense[4])
-    dense_grads = jnp.concatenate([grad_up.astype(BF16), grad_down.astype(BF16)], axis=1)
 
     expert = lax.axis_index("expert").astype(jnp.int32)
 
@@ -728,41 +723,56 @@
     def chip_sum(parts, place, *others):
         return plus_side(parts[place], after(parts[place + 1], *others))
 
+    def chip_sum(parts, place, *others):
+        return plus_side(parts[place], after(parts[place + 1], *others))
+
     dense_back_far = chip_sum(far_dense, 2).astype(BF16)
-    dense_out_far = chip_sum(far_dense, 0).astype(BF16)
-    far_rows, dense_grads, dense_back_far, dense_out_far = lax.optimization_barrier(
-        (far_rows, dense_grads, dense_back_far, dense_out_far)
+    far_rows, far_dense[6], far_dense[5] = lax.optimization_barrier(
+        (far_rows, far_dense[6], far_dense[5])
+    )
+    far_two = jnp.concatenate([normed_two_far, normed_two_corner], axis=0)
+    grad_up = (grad_up + product(far_two, far_dense[5])).astype(BF16)
+    grad_down = (grad_down + product(far_dense[6], far_dense[4])).astype(BF16)
+    dense_grads = jnp.concatenate([grad_up, grad_down], axis=1)
+    far_rows, dense_back_far, dense_grads = lax.optimization_barrier(
+        (far_rows, dense_back_far, dense_grads)
     )
     dense_grads = scatter_sum(dense_grads)
+    dense_back_far = from_far(dense_back_far)
     corner_rows = from_side(far_rows)
     side_rows = from_side(own_rows)
     far_expert = routed(far_rows, corner_rows, far_grads, from_side(far_grads))
-    dense_back, dense_out = chip_sum(near_dense, 2), chip_sum(near_dense, 0)
+    *far_expert, dense_back_far = lax.optimization_barrier((*far_expert, dense_back_far))
     far_back = chip_sum(far_expert, 2).astype(BF16)
     own_rows, far_back = lax.optimization_barrier((own_rows, far_back))
     near_expert = routed(own_rows, side_rows, own_grads, side_grads)
-    dense_back = dense_back + from_far(after(dense_back_far, near_expert[2])).astype(F32)
+    *near_expert, dense_grads = lax.optimization_barrier((*near_expert, dense_grads))
 
     def picked(rows):
         return lax.dot_general(
             own_slots, rows, (((0,), (0,)), ((), ())), preferred_element_type=F32
         )
 
-    expert_back = chip_sum(near_expert, 2) + from_far(far_back).astype(F32)
-    far_expert_out = chip_sum(far_expert, 0, far_back).astype(BF16)
-    expert_back, far_expert_out = lax.optimization_barrier(
-        (expert_back.astype(BF16), far_expert_out)
-    )
-    grad_normed_two, dense_grads = lax.optimization_barrier(
-        (dense_back + picked(sent(expert_back)), dense_grads)
-    )
-    expert_out = chip_sum(near_expert, 0, expert_back) + from_far(far_expert_out).astype(F32)
+    expert_back = (chip_sum(near_expert, 2) + from_far(far_back).astype(F32)).astype(BF16)
+    far_expert_out = chip_sum(far_expert, 0, expert_back).astype(BF16)
+    dense_out_far = chip_sum(far_dense, 0, expert_back).astype(BF16)
+    dense_back = chip_sum(near_dense, 2, far_back) + dense_back_far.astype(F32)
+
+    far_out_rows = from_far(far_expert_out)
+    grad_normed_two, far_out_rows = lax.optimization_barrier(
+        (dense_back + picked(sent(expert_back)), far_out_rows)
+    )
+    dense_out = chip_sum(near_dense, 0, expert_back)
+    expert_out = chip_sum(near_expert, 0, expert_back) + far_out_rows.astype(F32)
     expert_out = sent(after(expert_out.astype(BF16), grad_normed_two))
 
     near_tokens = jnp.concatenate([own_rows, side_rows], axis=0)
+    near_tokens, near_active, far_active, far_expert_out = lax.optimization_barrier(
+        (near_tokens, near_expert[4], far_expert[4], far_expert_out)
+    )
     far_tokens = jnp.concatenate([far_rows, corner_rows], axis=0)
     grad_ex_up = weight_grads(near_tokens, far_tokens, near_expert[5], far_expert[5])[None]
-    grad_ex_down = weight_grads(near_expert[4], far_expert[4], near_expert[6], far_expert[6])[None]
+    grad_ex_down = weight_grads(near_active, far_active, near_expert[6], far_expert[6])[None]
 
     gain_two = jnp.sum(grad_normed_two * scaled_two, axis=0)
     grad_residual = cotangent.astype(F32) + norm_back(
@@ -770,28 +780,24 @@
     )
     grad_branch = grad_residual.astype(BF16)
     grad_branch_far = from_far(grad_branch)
-    grad_branch_far, grad_ex_up, grad_ex_down = lax.optimization_barrier(
-        (grad_branch_far, grad_ex_up, grad_ex_down)
-    )
-    near_branch = jnp.concatenate([grad_branch, from_side(grad_branch)], axis=0)
-    far_branch = jnp.concatenate([grad_branch_far, from_side(grad_branch_far)], axis=0)
+    grad_branch_side = from_side(grad_branch)
+
+    def into_heads(*rows):
+        grads = [jnp.einsum("gd,cd->gc", part, w_out, preferred_element_type=F32) for part in rows]
+        return jnp.stack(grads).astype(BF16)
+
+    near_heads = into_heads(grad_branch, grad_branch_side)
+    grad_branch_far, near_heads, grad_ex_up, grad_ex_down = lax.optimization_barrier(
+        (grad_branch_far, near_heads, grad_ex_up, grad_ex_down)
+    )
+    grad_branch_corner = from_side(grad_branch_far)
+    far_heads = into_heads(grad_branch_far, grad_branch_corner)
     head_grads = near_dense[7] + far_dense[7] + near_expert[7] + far_expert[7]
     small = jnp.concatenate([head_grads[: experts + 2], gain_two[None]], axis=0)
     small = sum_over(small, "tensor")
-
-    def into_heads(rows):
-        grads = jnp.einsum("gd,cd->gc", rows, w_out, preferred_element_type=F32)
-        return grads.astype(BF16).reshape(2, tok_dev, heads_width)
-
-    near_heads, far_heads = into_heads(near_branch), into_heads(far_branch)
-    flat = (2 * tok_dev, heads_width)
     small_columns = -(-small.shape[0] // LANES) * LANES
     small_block = jnp.pad(small, ((0, small_columns - small.shape[0]), (0, 0))).T
-    grad_w_out = weight_grads(near_branch, far_branch, near_out.reshape(flat), far_out.reshape(flat))
-    side_grads = jnp.concatenate([grad_w_out.astype(BF16), small_block.astype(BF16)], axis=1)
     dense_out_far = from_far(after(dense_out_far, grad_branch_far))
-    near_heads, side_grads = lax.optimization_barrier((near_heads, side_grads))
-    side_grads = scatter_sum(side_grads)
     near_result, far_result = attention_backward(
         leaves, near_qkv, far_qkv, near_heads, far_heads, near_out, far_out, logs
     )
@@ -802,9 +808,17 @@
     def normed_part(grads):
         return jnp.einsum("sgc,sdc->gd", grads, w_qkv, preferred_element_type=F32)
 
-    corner_part = normed_part(far_result[:, 1])
-    from_corner = from_side(corner_part.astype(BF16)).astype(F32)
-    far_result, side_grads = lax.optimization_barrier((far_result, corner_part, side_grads))[::2]
+    corner_part = normed_part(far_result[:, 1]).astype(BF16)
+    from_corner = from_side(corner_part).astype(F32)
+
+    flat = (2 * tok_dev, heads_width)
+    near_branch = jnp.concatenate([grad_branch, grad_branch_side], axis=0)
+    far_branch = jnp.concatenate([grad_branch_far, grad_branch_corner], axis=0)
+    near_branch = after(near_branch, corner_part)
+    grad_w_out = weight_grads(near_branch, far_branch, near_out.reshape(flat), far_out.reshape(flat))
+    branch_grads = strips_total(strips_sent(
+        jnp.concatenate([grad_w_out.astype(BF16), small_block.astype(BF16)], axis=1)
+    ))
     far_sum = (normed_part(far_result[:, 0]) + from_corner).astype(BF16)
     near_result, far_result, expert_out, far_sum = lax.optimization_barrier(
         (near_result, far_result, expert_out, far_sum)
@@ -812,17 +826,20 @@
     near_sum = plus_side(normed_part(near_result[:, 0]), normed_part(near_result[:, 1]))
     out = (residual + dense_out + dense_out_far.astype(F32) + picked(expert_out)).astype(BF16)
 
-    near_result = near_result.reshape(3, 2 * tok_dev, heads_width)
-    far_result = far_result.reshape(3, 2 * tok_dev, heads_width)
-    grad_w_qkv = jnp.einsum(
-        "gd,sgc->dsc", near_one, near_result, preferred_element_type=F32
-    ) + jnp.einsum("gd,sgc->dsc", far_one, far_result, preferred_element_type=F32)
-    qkv_grads = strips_sum(grad_w_qkv.reshape(width, 3 * heads_width).astype(BF16))
-    scaled_far = normed_far.astype(F32) / ln_attn
-    gain_one = jnp.sum(near_sum * scaled_one + far_sum.astype(F32) * scaled_far, axis=0, keepdims=True)
-    gain_one = sum_over(sum_over(gain_one, "tensor"), "expert")
-    far_sum, grad_ln_attn = lax.optimization_barrier((from_far(far_sum), gain_one[0]))
-    grad_normed_one = near_sum + far_sum.astype(F32)
+    near_result = near_result.reshape(3, *flat)
+    far_result = far_result.reshape(3, *flat)
+    qkv_grads = strips_total(strips_sent(
+        jnp.concatenate(
+            [
+                weight_grads(near_one, far_one, near_result[part], far_result[part]).astype(BF16)
+                for part in range(3)
+            ],
+            axis=1,
+        )
+    ))
+    grad_normed_one = near_sum + from_far(far_sum).astype(F32)
+    gain_one = jnp.sum(grad_normed_one * scaled_one, axis=0, keepdims=True)
+    grad_ln_attn = sum_over(sum_over(gain_one, "tensor"), "expert")[0]
     grad_tokens = grad_residual + norm_back(grad_normed_one, ln_attn, scaled_one, inverse_one)
 
     strip = qkv_grads.shape[0]
@@ -831,12 +848,12 @@
         grad_tokens,
         grad_ln_attn,
         qkv_grads.reshape(strip, 3, heads_width).transpose(1, 0, 2),
-        side_grads[:, :heads_width].T,
-        side_grads[:, heads_width + experts + 2],
+        branch_grads[:, :heads_width].T,
+        branch_grads[:, heads_width + experts + 2],
         dense_grads[:, :hidden],
         dense_grads[:, hidden:].T,
-        side_grads[:, heads_width : heads_width + experts],
-        side_grads[:, heads_width + experts : heads_width + experts + 2],
+        branch_grads[:, heads_width : heads_width + experts],
+        branch_grads[:, heads_width + experts : heads_width + experts + 2],
         grad_ex_up,
         grad_ex_down,
     )

time: 671 us -> 688 us (1.025)
  waiting for transfers between devices: 176 us -> 202 us
  local copies, waits for them, and re-layouts: 21.5 us -> 13.8 us
  starting transfers between devices: 62.8 us -> 69.9 us
    all_to_all x6 -> x7, waiting for transfers between devices: 18.6 us -> 92.3 us  [exchange(): lax.all_to_all(blocks, 'expert', split_axis=0, concat_axis=0, tiled=True)]
    reduce_scatter x2 -> x1, waiting for transfers between devices: 23.1 us -> 0.02 us  [scatter_sum(): lax.psum_scatter(strips, 'expert', scatter_dimension=0, tiled=True)]
    ppermute x11, waiting for transfers between devices: 90.7 us -> 76.1 us  [from_far(): return lax.ppermute(values, 'tensor', [(i, i ^ 2) for i in range(4)])]
    ppermute x7, waiting for transfers between devices: 25.8 us -> 13.5 us  [sum_over(): values = values + lax.ppermute(values, axis, pairs)]
    dot_general x4, matrix products: 15.8 us -> 4.79 us  [into_heads(): jnp.einsum('gd,cd->gc', part, w_out, preferred_element_type=F32)]
    dot_general x10 -> x16, matrix products: 55.4 us -> 63.8 us  [product(): return jnp.einsum('gd,gf->df', left, right, preferred_element_type=F32)]
    all_to_all x6 -> x7, starting transfers between devices: 35.5 us -> 41.2 us  [exchange(): lax.all_to_all(blocks, 'expert', split_axis=0, concat_axis=0, tiled=True)]
  transfers between devices with their start and end apart: 50 -> 50, of which waited for: 15 -> 19; matrix products, arithmetic and copies ran while one was open for 28% -> 25% of each run, Pallas kernels for 30% -> 30%
where the time goes in v6:
time: 688 us; the launch traced here: 684 us
  waiting for transfers between devices  202 us (29%)
  Pallas kernels  202 us (29%)
  matrix products  114 us (17%)
  starting transfers between devices  69.9 us (10%)
  other arithmetic  67.2 us (10%)
  between operations  15.2 us (2%)
  local copies, waits for them, and re-layouts  13.8 us (2%)
    pallas_call x4, Pallas kernels, feed(): pl.pallas_call(functools.partial(feed_kernel, experts, routed), grid_spec...  136 us
    all_to_all x7, waiting for transfers between devices, exchange(): lax.all_to_all(blocks, 'expert', split_axis=0, concat_axis=0, tiled=True)  92.3 us
    ppermute x11, waiting for transfers between devices, from_far(): return lax.ppermute(values, 'tensor', [(i, i ^ 2) for i in range(4)])  76.1 us
    dot_general x16, matrix products, product(): return jnp.einsum('gd,gf->df', left, right, preferred_element_type=F32)  63.8 us
    all_to_all x7, starting transfers between devices, exchange(): lax.all_to_all(blocks, 'expert', split_axis=0, concat_axis=0, tiled=True)  41.2 us
    pallas_call x1, Pallas kernels, attention_backward(): pl.pallas_call(backward_kernel, grid_spec=pltpu.PrefetchScalarGridSpec(nu...  40.7 us
    pallas_call x1, Pallas kernels, attention_forward(): pl.pallas_call(forward_kernel, grid_spec=pltpu.PrefetchScalarGridSpec(num...  25.4 us
    ppermute x24, waiting for transfers between devices, from_side(): return lax.ppermute(values, 'tensor', [(i, i ^ 1) for i in range(4)])  19.8 us
  transfers between devices with their start and end apart: 50, of which 19 were waited for; matrix products, arithmetic and copies ran while one was open for 25% of the time, Pallas kernels for 30%

profile of v6, /device:TPU:0, one launch (start us, length us, event | category | flops | bytes accessed | tf_op | source)
XLA Modules:
  0.0 683.8 jit_solution(12747069222871184633)
XLA Ops:
  20.2 6.3 all-to-all-start
  33.1 12.0 %collective-permute-done = bf16[640,1024]{1,0:T(8,128)(2,1)} collective-permute-done((bf16[640,1024]{1,0:T(8,128)(2,1)}, bf16[640,1024]{1,0:T(8,128)(2,1)}, u32[]{:S(2)}, u32[]{:S(2)}) %collective-permute-start) | collective-permute-done | bytes 1310752 | tf_op jit(solution)/shard_map/ppermute | solution.py:555
  53.7 25.4 %tree_attention.1 = (bf16[2,640,256]{2,1,0:T(8,128)(2,1)}, bf16[2,640,256]{2,1,0:T(8,128)(2,1)}, f32[2,2,1024]{2,1,0:T(2,128)}, f32[2,4,2,384]{3,2,1,0:T(2,128)}) custom-call(s32[9]{0:T(128)} %pad_add_fusion.leaves_ref, bf16[3,2,640,256]{3,2,1,0:T(8,128)(2,1)} %bitcast.191, bf16[3,2,640,256]{3,2,1,0:T(8,128)(2,1)} %bitcast.193), custom_call_target="tpu_custom_call" | custom-call | flops 1241513984 | bytes 1310720 | tf_op jit(solution)/shard_map/tree_attention/pallas_call | solution.py:192
  93.0 23.8 %collective-permute-done.7 = bf16[640,1024]{1,0:T(8,128)(2,1)S(1)} collective-permute-done((bf16[640,1024]{1,0:T(8,128)(2,1)S(1)}, bf16[640,1024]{1,0:T(8,128)(2,1)S(1)}, u32[]{:S(2)}, u32[]{:S(2)}) %collective-permute-start.7) | collective-permute-done | bytes 1310752 | tf_op jit(solution)/shard_map/ppermute | solution.py:555
  121.9 6.1 all-to-all-start.1
  131.4 28.7 %feed_dense.2 = (bf16[640,1024]{1,0:T(8,128)(2,1)}, bf16[640,1024]{1,0:T(8,128)(2,1)}, bf16[640,1024]{1,0:T(8,128)(2,1)}, bf16[640,1024]{1,0:T(8,128)(2,1)}, bf1...) custom-call(s32[1]{0:T(128)} %constant.47.clone.1.expert_ref, ...), custom_call_target="tpu_custom_call" | custom-call | flops 1342177280 | bytes 2490368 | tf_op jit(solution)/shard_map/feed_dense/pallas_call | solution.py:481
  160.2 7.6 %fusion.17 = f32[1024,1024]{1,0:T(8,128)} fusion(bf16[1280,1024]{1,0:T(8,128)(2,1)} %get-tuple-element.131, bf16[640,1024]{1,0:T(8,128)(2,1)} %collective-permute-done.10.side_ref, bf16[640,1024]{1,0:T(8,128)(2,1)} %copy-done.11), kind=kOutput, calls=%fused_computation.34 | convolution fusion | flops 2689597440 | bytes 9437184 | tf_op jit(solution)/shard_map/gd,gf->df/dot_general | solution.py:690
  177.1 28.3 %feed_dense.3 = (bf16[640,1024]{1,0:T(8,128)(2,1)}, bf16[640,1024]{1,0:T(8,128)(2,1)}, bf16[640,1024]{1,0:T(8,128)(2,1)}, bf16[640,1024]{1,0:T(8,128)(2,1)}, bf1...) custom-call(s32[1]{0:T(128)} %constant.47.clone.1.expert_ref, ...), custom_call_target="tpu_custom_call" | custom-call | flops 1342177280 | bytes 2490368 | tf_op jit(solution)/shard_map/feed_dense/pallas_call | solution.py:481
  205.6 8.9 %collective-permute-done.12.own_ref = bf16[896,1024]{1,0:T(8,128)(2,1)} collective-permute-done((bf16[896,1024]{1,0:T(8,128)(2,1)S(1)}, bf16[896,1024]{1,0:T(8,128)(2,1)}, u32[]{:S(2)}, u32[]{:S(2)}) %collective-permute-start.12) | collective-permute-done | bytes 1835040 | tf_op jit(solution)/shard_map/ppermute | solution.py:555
  214.4 7.6 %fusion.93 = f32[1024,1024]{1,0:T(8,128)} fusion(bf16[1280,1024]{1,0:T(8,128)(2,1)} %get-tuple-element.145, bf16[1280,1024]{1,0:T(8,128)(2,1)} %get-tuple-element.146), kind=kOutput, calls=%fused_computation.178 | convolution fusion | flops 2684354560 | bytes 9437184 | tf_op jit(solution)/shard_map/gd,gf->df/dot_general | solution.py:690
  222.1 6.3 fusion.21
  228.4 7.4 %add_convert_fusion = (bf16[1024,1024]{1,0:T(8,128)(2,1)S(1)}, bf16[1024,1024]{1,0:T(8,128)(2,1)S(1)}) fusion(f32[1024,1024]{1,0:T(8,128)} %fusion.92, f32[1024,1024]{1,0:T(8,128)} %fusion.93, f32[1024,1024]{1,0:T(8,128)} %fusion.17, f32[1024,1024]{1,0:T(8,128)} %fusion.21), kind=kLoop, calls=%fused_computation.3 | loop fusion | flops 4194304 | bytes 20971520 | tf_op jit(solution)/shard_map/convert_element_type | solution.py:735
  241.5 6.2 all-to-all-start.2
  247.8 75.8 %all-to-all-done.2 = bf16[8,112,1024]{2,1,0:T(8,128)(2,1)} async-done(((bf16[8,112,1024]{2,1,0:T(8,128)(2,1)}), bf16[8,112,1024]{2,1,0:T(8,128)(2,1)}, u32[]{:S(2)}, u32[]{:S(2)}) %all-to-all-start.2) | async-done | bytes 1835040 | tf_op jit(solution)/shard_map/all_to_all | solution.py:572
  327.7 39.5 %feed_routed.2 = (bf16[896,1024]{1,0:T(8,128)(2,1)}, bf16[896,1024]{1,0:T(8,128)(2,1)}, bf16[896,1024]{1,0:T(8,128)(2,1)}, bf16[896,1024]{1,0:T(8,128)(2,1)}, bf...) custom-call(s32[1]{0:T(128)} %bitcast.16.expert_ref, ...), custom_call_target="tpu_custom_call" | custom-call | flops 1879048192 | bytes 3276800 | tf_op jit(solution)/shard_map/feed_routed/pallas_call | solution.py:481
  377.5 39.8 %feed_routed.3 = (bf16[896,1024]{1,0:T(8,128)(2,1)}, bf16[896,1024]{1,0:T(8,128)(2,1)}, bf16[896,1024]{1,0:T(8,128)(2,1)}, bf16[896,1024]{1,0:T(8,128)(2,1)}, bf...) custom-call(s32[1]{0:T(128)} %bitcast.16.expert_ref, ...), custom_call_target="tpu_custom_call" | custom-call | flops 1879048192 | bytes 3276800 | tf_op jit(solution)/shard_map/feed_routed/pallas_call | solution.py:481
  431.9 6.9 %fusion = f32[1024,1024]{1,0:T(8,128)S(1)} fusion(bf16[1792,1024]{1,0:T(8,128)(2,1)} %get-tuple-element.188, bf16[896,1024]{1,0:T(8,128)(2,1)} %collective-permute-done.15.side_ref, bf16[896,1024]{1,0:T(8,128)(2,1)} %collective-permute-done.12.own_ref), kind=kOutput, calls=%fused_computation.9 | convolution fusion | flops 3765436416 | bytes 11534336 | tf_op jit(solution)/shard_map/gd,gf->df/dot_general | solution.py:690
  458.8 16.5 %all-to-all-done.3 = bf16[8,112,1024]{2,1,0:T(8,128)(2,1)} async-done(((bf16[8,112,1024]{2,1,0:T(8,128)(2,1)}), bf16[8,112,1024]{2,1,0:T(8,128)(2,1)}, u32[]{:S(2)}, u32[]{:S(2)}) %all-to-all-start.3) | async-done | bytes 1835040 | tf_op jit(solution)/shard_map/all_to_all | solution.py:572
  479.9 9.4 %collective-permute-done.25 = bf16[896,1024]{1,0:T(8,128)(2,1)S(1)} collective-permute-done((bf16[896,1024]{1,0:T(8,128)(2,1)}, bf16[896,1024]{1,0:T(8,128)(2,1)S(1)}, u32[]{:S(2)}, u32[]{:S(2)}) %collective-permute-start.25) | collective-permute-done | bytes 1835040 | tf_op jit(solution)/shard_map/ppermute | solution.py:555
  503.5 22.1 %collective-permute-done.26 = bf16[640,1024]{1,0:T(8,128)(2,1)} collective-permute-done((bf16[640,1024]{1,0:T(8,128)(2,1)S(1)}, bf16[640,1024]{1,0:T(8,128)(2,1)}, u32[]{:S(2)}, u32[]{:S(2)}) %collective-permute-start.26) | collective-permute-done | bytes 1310752 | tf_op jit(solution)/shard_map/ppermute | solution.py:555
  534.4 6.0 all-to-all-start.4
  551.3 40.7 %tree_attention_back.1 = (bf16[3,2,640,256]{3,2,1,0:T(8,128)(2,1)}, bf16[3,2,640,256]{3,2,1,0:T(8,128)(2,1)}) custom-call(s32[9]{0:T(128)} %pad_add_fusion.leaves_ref, bf16[3,2,640,256]{3,2,1,0:T(8,128)(2,1)} %bitcast.192, bf16[3,2,640,256]{3,2,1,0:T(8,128)(2,1)} %bitcast.194, bf16[2,640,256]{2,1,0:T(8,128)(2,1)} %pad_maximum_fusion.4.near_grads_ref, ...), custom_call_target="tpu_custom_call" | custom-call | flops 24830279680 | bytes 10485760 | tf_op jit(solution)/shard_map/tree_attention_back/pallas_call | solution.py:336
  601.3 6.0 all-to-all-start.6
  631.6 6.2 all-to-all-start.5
  (295 shorter events, 225.2 us)
Async XLA Ops:
  12.8 32.3 %collective-permute-start = (bf16[640,1024]{1,0:T(8,128)(2,1)}, bf16[640,1024]{1,0:T(8,128)(2,1)}, u32[]{:S(2)}, u32[]{:S(2)}) collective-permute-start(bf16[640,1024]{1,0:T(8,128)(2,1)} %fusion.10), channel_id=1, source_target_pairs={{0,2},{1,3},{2,0},{3,1},{4,6},{5,7},{6,4},{7,5},{8,10},{9,11},{10,... | collective-permute-start | bytes 3932168 | tf_op jit(solution)/shard_map/ppermute | solution.py:555
  20.2 59.0 %all-to-all-start = ((bf16[8,112,1024]{2,1,0:T(8,128)(2,1)}), bf16[8,112,1024]{2,1,0:T(8,128)(2,1)}, u32[]{:S(2)}, u32[]{:S(2)}) async-start(bf16[8,112,1024]{2,1,0:T(8,128)(2,1)} %bitcast.175), calls=%async_computation | async-start | bytes 3670016 | tf_op jit(solution)/shard_map/all_to_all | solution.py:572
  45.1 34.1 %collective-permute-start.5 = (bf16[640,1024]{1,0:T(8,128)(2,1)}, bf16[640,1024]{1,0:T(8,128)(2,1)}, u32[]{:S(2)}, u32[]{:S(2)}) collective-permute-start(bf16[640,1024]{1,0:T(8,128)(2,1)} %own_grads_ref.1), channel_id=1, source_target_pairs={{0,1},{1,0},{2,3},{3,2},{4,5},{5,4},{6,7},{7,6},{8,9},{9,8},{10,11... | collective-permute-start | bytes 3932168 | tf_op jit(solution)/shard_map/ppermute | solution.py:551
  45.8 33.3 %collective-permute-start.4 = (bf16[640,1024]{1,0:T(8,128)(2,1)}, bf16[640,1024]{1,0:T(8,128)(2,1)}, u32[]{:S(2)}, u32[]{:S(2)}) collective-permute-start(bf16[640,1024]{1,0:T(8,128)(2,1)} %own_grads_ref.1), channel_id=1, source_target_pairs={{0,2},{1,3},{2,0},{3,1},{4,6},{5,7},{6,4},{7,5},{8,10},{9,11},{10,... | collective-permute-start | bytes 3932168 | tf_op jit(solution)/shard_map/ppermute | solution.py:555
  121.9 50.3 %all-to-all-start.1 = ((bf16[8,112,1024]{2,1,0:T(8,128)(2,1)}), bf16[8,112,1024]{2,1,0:T(8,128)(2,1)S(1)}, u32[]{:S(2)}, u32[]{:S(2)}) async-start(bf16[8,112,1024]{2,1,0:T(8,128)(2,1)} %bitcast.176), calls=%async_computation.1 | async-start | bytes 3670016 | tf_op jit(solution)/shard_map/all_to_all | solution.py:572
  127.9 289.4 %reduce-scatter.2.cloned.1.call-start = ((), (), s32[]{:S(2)}) async-start(), calls=%async_computation.8 | async-start | bytes 4718592 | tf_op jit(solution)/shard_map/reduce_scatter | solution.py:577
  128.1 44.2 %collective-permute-start.11 = (bf16[640,1024]{1,0:T(8,128)(2,1)}, bf16[640,1024]{1,0:T(8,128)(2,1)}, u32[]{:S(2)}, u32[]{:S(2)}) collective-permute-start(bf16[640,1024]{1,0:T(8,128)(2,1)} %copy-done.11), channel_id=1, source_target_pairs={{0,2},{1,3},{2,0},{3,1},{4,6},{5,7},{6,4},{7,5},{8,10},{9,11},{10,... | collective-permute-start | bytes 3932168 | tf_op jit(solution)/shard_map/ppermute | solution.py:555
  172.2 42.2 %collective-permute-start.12 = (bf16[896,1024]{1,0:T(8,128)(2,1)S(1)}, bf16[896,1024]{1,0:T(8,128)(2,1)}, u32[]{:S(2)}, u32[]{:S(2)}) collective-permute-start(bf16[896,1024]{1,0:T(8,128)(2,1)S(1)} %bitcast.165), channel_id=1, source_target_pairs={{0,2},{1,3},{2,0},{3,1},{4,6},{5,7},{6,4},{7,5},{8,10},{9,11},{10,... | collective-permute-start | bytes 5505032 | tf_op jit(solution)/shard_map/ppermute | solution.py:555
  205.4 32.8 %collective-permute-start.14 = (bf16[640,1024]{1,0:T(8,128)(2,1)}, bf16[640,1024]{1,0:T(8,128)(2,1)}, u32[]{:S(2)}, u32[]{:S(2)}) collective-permute-start(bf16[640,1024]{1,0:T(8,128)(2,1)} %get-tuple-element.141), channel_id=1, source_target_pairs={{0,1},{1,0},{2,3},{3,2},{4,5},{5,4},{6,7},{7,6},{8,9},{9,8},{10,11... | collective-permute-start | bytes 3932168 | tf_op jit(solution)/shard_map/ppermute | solution.py:551
  241.5 82.1 %all-to-all-start.2 = ((bf16[8,112,1024]{2,1,0:T(8,128)(2,1)}), bf16[8,112,1024]{2,1,0:T(8,128)(2,1)}, u32[]{:S(2)}, u32[]{:S(2)}) async-start(bf16[8,112,1024]{2,1,0:T(8,128)(2,1)} %bitcast.174), calls=%async_computation.2 | async-start | bytes 3670016 | tf_op jit(solution)/shard_map/all_to_all | solution.py:572
  247.7 77.3 %collective-permute-start.15 = (bf16[896,1024]{1,0:T(8,128)(2,1)}, bf16[896,1024]{1,0:T(8,128)(2,1)}, u32[]{:S(2)}, u32[]{:S(2)}) collective-permute-start(bf16[896,1024]{1,0:T(8,128)(2,1)} %collective-permute-done.12.own_ref), channel_id=1, source_target_pairs={{0,1},{1,0},{2,3},{3,2},{4,5},{5,4},{6,7},{7,6},{8,9},{9,8},{10,11... | collective-permute-start | bytes 5505032 | tf_op jit(solution)/shard_map/ppermute | solution.py:551
  323.6 43.7 %collective-permute-start.17 = (bf16[640,1024]{1,0:T(8,128)(2,1)}, bf16[640,1024]{1,0:T(8,128)(2,1)}, u32[]{:S(2)}, u32[]{:S(2)}) collective-permute-start(bf16[640,1024]{1,0:T(8,128)(2,1)} %add_convert_fusion.8), channel_id=1, source_target_pairs={{0,2},{1,3},{2,0},{3,1},{4,6},{5,7},{6,4},{7,5},{8,10},{9,11},{10,... | collective-permute-start | bytes 3932168 | tf_op jit(solution)/shard_map/ppermute | solution.py:555
  376.1 42.5 %collective-permute-start.21 = (bf16[896,1024]{1,0:T(8,128)(2,1)}, bf16[896,1024]{1,0:T(8,128)(2,1)}, u32[]{:S(2)}, u32[]{:S(2)}) collective-permute-start(bf16[896,1024]{1,0:T(8,128)(2,1)} %add_convert_fusion.5), channel_id=1, source_target_pairs={{0,2},{1,3},{2,0},{3,1},{4,6},{5,7},{6,4},{7,5},{8,10},{9,11},{10,... | collective-permute-start | bytes 5505032 | tf_op jit(solution)/shard_map/ppermute | solution.py:555
  427.3 47.9 %all-to-all-start.3 = ((bf16[8,112,1024]{2,1,0:T(8,128)(2,1)}), bf16[8,112,1024]{2,1,0:T(8,128)(2,1)}, u32[]{:S(2)}, u32[]{:S(2)}) async-start(bf16[8,112,1024]{2,1,0:T(8,128)(2,1)} %bitcast.24), calls=%async_computation.4 | async-start | bytes 3670016 | tf_op jit(solution)/shard_map/all_to_all | solution.py:572
  442.4 98.0 %collective-permute-start.30 = (bf16[640,1024]{1,0:T(8,128)(2,1)}, bf16[640,1024]{1,0:T(8,128)(2,1)}, u32[]{:S(2)}, u32[]{:S(2)}) collective-permute-start(bf16[640,1024]{1,0:T(8,128)(2,1)} %get-tuple-element.206), channel_id=1, source_target_pairs={{0,1},{1,0},{2,3},{3,2},{4,5},{5,4},{6,7},{7,6},{8,9},{9,8},{10,11... | collective-permute-start | bytes 3932168 | tf_op jit(solution)/shard_map/ppermute | solution.py:551
  442.5 86.7 %collective-permute-start.29 = (bf16[896,1024]{1,0:T(8,128)(2,1)}, bf16[896,1024]{1,0:T(8,128)(2,1)}, u32[]{:S(2)}, u32[]{:S(2)}) collective-permute-start(bf16[896,1024]{1,0:T(8,128)(2,1)} %get-tuple-element.201), channel_id=1, source_target_pairs={{0,1},{1,0},{2,3},{3,2},{4,5},{5,4},{6,7},{7,6},{8,9},{9,8},{10,11... | collective-permute-start | bytes 5505032 | tf_op jit(solution)/shard_map/ppermute | solution.py:551
  447.0 42.3 %collective-permute-start.25 = (bf16[896,1024]{1,0:T(8,128)(2,1)}, bf16[896,1024]{1,0:T(8,128)(2,1)S(1)}, u32[]{:S(2)}, u32[]{:S(2)}) collective-permute-start(bf16[896,1024]{1,0:T(8,128)(2,1)} %add_convert_fusion.3), channel_id=1, source_target_pairs={{0,2},{1,3},{2,0},{3,1},{4,6},{5,7},{6,4},{7,5},{8,10},{9,11},{10,... | collective-permute-start | bytes 5505032 | tf_op jit(solution)/shard_map/ppermute | solution.py:555
  528.6 112.4 %collective-permute-start.22 = (bf16[640,1024]{1,0:T(8,128)(2,1)}, bf16[640,1024]{1,0:T(8,128)(2,1)}, u32[]{:S(2)}, u32[]{:S(2)}) collective-permute-start(bf16[640,1024]{1,0:T(8,128)(2,1)} %get-tuple-element.175), channel_id=1, source_target_pairs={{0,1},{1,0},{2,3},{3,2},{4,5},{5,4},{6,7},{7,6},{8,9},{9,8},{10,11... | collective-permute-start | bytes 3932168 | tf_op jit(solution)/shard_map/ppermute | solution.py:551
  534.4 57.6 %all-to-all-start.4 = ((bf16[8,112,1024]{2,1,0:T(8,128)(2,1)}), bf16[8,112,1024]{2,1,0:T(8,128)(2,1)}, u32[]{:S(2)}, u32[]{:S(2)}) async-start(bf16[8,112,1024]{2,1,0:T(8,128)(2,1)} %bitcast.173), calls=%async_computation.5 | async-start | bytes 3670016 | tf_op jit(solution)/shard_map/all_to_all | solution.py:572
  544.5 51.0 %collective-permute-start.41 = (f32[11,1024]{1,0:T(8,128)S(1)}, f32[11,1024]{1,0:T(8,128)S(1)}, u32[]{:S(2)}, u32[]{:S(2)}) collective-permute-start(f32[11,1024]{1,0:T(8,128)S(1)} %fusion.146), channel_id=1, source_target_pairs={{0,2},{1,3},{2,0},{3,1},{4,6},{5,7},{6,4},{7,5},{8,10},{9,11},{10,... | collective-permute-start | bytes 135176 | tf_op jit(solution)/shard_map/ppermute | solution.py:566
  545.2 46.7 %collective-permute-start.31 = (bf16[640,1024]{1,0:T(8,128)(2,1)}, bf16[640,1024]{1,0:T(8,128)(2,1)}, u32[]{:S(2)}, u32[]{:S(2)}) collective-permute-start(bf16[640,1024]{1,0:T(8,128)(2,1)} %add_convert_fusion.7), channel_id=1, source_target_pairs={{0,2},{1,3},{2,0},{3,1},{4,6},{5,7},{6,4},{7,5},{8,10},{9,11},{10,... | collective-permute-start | bytes 3932168 | tf_op jit(solution)/shard_map/ppermute | solution.py:555
  613.8 31.6 %collective-permute-start.33 = (bf16[640,1024]{1,0:T(8,128)(2,1)}, bf16[640,1024]{1,0:T(8,128)(2,1)}, u32[]{:S(2)}, u32[]{:S(2)}) collective-permute-start(bf16[640,1024]{1,0:T(8,128)(2,1)} %bitcast_convert_fusion), channel_id=1, source_target_pairs={{0,1},{1,0},{2,3},{3,2},{4,5},{5,4},{6,7},{7,6},{8,9},{9,8},{10,11... | collective-permute-start | bytes 3932168 | tf_op jit(solution)/shard_map/ppermute | solution.py:551
  614.0 31.4 %collective-permute-start.34 = (bf16[640,1024]{1,0:T(8,128)(2,1)}, bf16[640,1024]{1,0:T(8,128)(2,1)}, u32[]{:S(2)}, u32[]{:S(2)}) collective-permute-start(bf16[640,1024]{1,0:T(8,128)(2,1)} %fusion.30), channel_id=1, source_target_pairs={{0,2},{1,3},{2,0},{3,1},{4,6},{5,7},{6,4},{7,5},{8,10},{9,11},{10,... | collective-permute-start | bytes 3932168 | tf_op jit(solution)/shard_map/ppermute | solution.py:555
  631.6 44.0 %all-to-all-start.5 = ((bf16[8,128,768]{1,2,0:T(8,128)(2,1)}), bf16[8,128,768]{1,2,0:T(8,128)(2,1)S(1)}, u32[]{:S(2)}, u32[]{:S(2)}) async-start(bf16[8,128,768]{1,2,0:T(8,128)(2,1)} %copy_bitcast_fusion), calls=%async_computation.6 | async-start | bytes 3145728 | tf_op jit(solution)/shard_map/all_to_all | solution.py:572
  (76 other events, 863.8 us)
Sparse Core Ops, SparseCore 0:
  241.6 124.4 reduce-scatter.1

commit v7 on v6

--- a/solution.py
+++ b/solution.py
@@ -360,7 +360,7 @@
             ],
         ),
         out_shape=[jax.ShapeDtypeStruct(near.shape, BF16), jax.ShapeDtypeStruct(far.shape, BF16)],
-        cost_estimate=attention_cost(5, 1),
+        cost_estimate=attention_cost(5, 5),
         name="tree_attention_back",
     )(leaves, near, far, near_grads, far_grads, near_outs, far_outs, *logs)
 
@@ -390,6 +390,16 @@
     probs = raised / jnp.sum(raised, axis=1, keepdims=True)
     gate = jnp.sum(jnp.where(lane == expert, probs, 0.0), axis=1, keepdims=True)
     return lane, first, second, probs, gate
+
+
+def both(own_ref, side_ref):
+    return jnp.concatenate([own_ref[...], side_ref[...]], axis=0)
+
+
+def split_store(own_ref, side_ref, rows):
+    half = rows.shape[0] // 2
+    own_ref[...] = rows[:half]
+    side_ref[...] = rows[half:]
 
 
 def feed_kernel(
@@ -412,26 +422,25 @@
     grad_ref,
     head_grad_ref,
 ):
-    step = pl.program_id(0)
-    early = step < pl.num_programs(0) // 2
-    rows = jnp.where(early, own_ref[...], side_ref[...])
-    grads = jnp.where(early, own_grads_ref[...], side_grads_ref[...]).astype(F32)
+    rows = both(own_ref, side_ref)
+    grads = both(own_grads_ref, side_grads_ref).astype(F32)
+    expert = expert_ref[0] if routed else None
     logits = dot_nn(rows, head_ref[...])
-    expert = expert_ref[0] if routed else None
     lane, first, second, probs, gate = gates(logits, experts, expert)
     coef = second * gate if routed else first
     weighted = (coef * grads).astype(BF16)
-    grad_ref[...] = weighted
     pre = dot_nn(rows, up_ref[...])
     grad_active = dot_nt(weighted, down_ref[...])
     cumulative = 0.5 + 0.5 * lax.erf(pre * 0.7071067811865476)
     slope = cumulative + pre * jnp.exp(-0.5 * pre * pre) * 0.3989422804014327
     active = (pre * cumulative).astype(BF16)
-    active_ref[...] = active
     grad_pre = (grad_active * slope).astype(BF16)
-    pre_ref[...] = grad_pre
+    half = rows.shape[0] // 2
+    for ref, value in ((active_ref, active), (pre_ref, grad_pre), (grad_ref, weighted)):
+        ref[0] = value[:half]
+        ref[1] = value[half:]
     out = dot_nn(active, down_ref[...])
-    out_rows = (coef * out).astype(BF16)
+    split_store(own_out_ref, side_out_ref, (coef * out).astype(BF16))
     inner = jnp.sum(grads * out, axis=1, keepdims=True)
     swing = first * second * inner
     if routed:
@@ -443,63 +452,54 @@
             lane < experts, probs * picked * (second * inner), 0.0
         )
     back = dot_nt(grad_pre, up_ref[...]) + dot_nt(grad_logits.astype(BF16), head_ref[...])
-    back_rows = back.astype(BF16)
-
-    @pl.when(early)
-    def _():
-        own_out_ref[...] = out_rows
-        own_back_ref[...] = back_rows
-
-    @pl.when(jnp.logical_not(early))
-    def _():
-        side_out_ref[...] = out_rows
-        side_back_ref[...] = back_rows
-
-    @pl.when(step == 0)
+    split_store(own_back_ref, side_back_ref, back.astype(BF16))
+    head_grad = dot_nn(grad_logits.T.astype(BF16), rows)
+
+    @pl.when(pl.program_id(0) == 0)
     def _():
         head_grad_ref[...] = jnp.zeros_like(head_grad_ref)
 
-    head_grad_ref[...] += dot_nn(grad_logits.T.astype(BF16), rows)
+    head_grad_ref[...] += head_grad
 
 
 def feed(own, side, own_grads, side_grads, head, up, down, experts, expert, size):
     count = own.shape[0]
     width, hidden = up.shape
-    half = count // size
+    steps = count // size
     lanes = head.shape[1]
     routed = expert is not None
     pick = jnp.reshape(expert, (1,)) if routed else jnp.zeros((1,), jnp.int32)
-    early = pl.BlockSpec((size, width), lambda i, pick: (jnp.minimum(i, half - 1), 0))
-    late = pl.BlockSpec((size, width), lambda i, pick: (jnp.maximum(i - half, 0), 0))
-
-    def held(shape):
+    rows = pl.BlockSpec((size, width), lambda i, pick: (i, 0))
+
+    def whole(shape):
         return pl.BlockSpec(shape, lambda i, pick: (0, 0), pipeline_mode=pl.Buffered(1))
 
-    wide = pl.BlockSpec((size, width), lambda i, pick: (i, 0))
-    deep = pl.BlockSpec((size, hidden), lambda i, pick: (i, 0))
+    def pairs(columns):
+        return pl.BlockSpec((2, size, columns), lambda i, pick: (0, i, 0))
+
     quarter = jax.ShapeDtypeStruct((count, width), BF16)
-    return pl.pallas_call(
+    *sums, active, pre, weighted, head_grad = pl.pallas_call(
         functools.partial(feed_kernel, experts, routed),
         grid_spec=pltpu.PrefetchScalarGridSpec(
             num_scalar_prefetch=1,
-            grid=(2 * half,),
+            grid=(steps,),
             in_specs=[
-                early,
-                late,
-                early,
-                late,
-                held((width, lanes)),
-                held((width, hidden)),
-                held((hidden, width)),
+                rows,
+                rows,
+                rows,
+                rows,
+                whole((width, lanes)),
+                whole((width, hidden)),
+                whole((hidden, width)),
             ],
             out_specs=[
-                early,
-                late,
-                early,
-                late,
-                deep,
-                deep,
-                wide,
+                rows,
+                rows,
+                rows,
+                rows,
+                pairs(hidden),
+                pairs(hidden),
+                pairs(width),
                 pl.BlockSpec((lanes, width), lambda i, pick: (0, 0)),
             ],
         ),
@@ -508,9 +508,9 @@
             quarter,
             quarter,
             quarter,
-            jax.ShapeDtypeStruct((2 * count, hidden), BF16),
-            jax.ShapeDtypeStruct((2 * count, hidden), BF16),
-            jax.ShapeDtypeStruct((2 * count, width), BF16),
+            jax.ShapeDtypeStruct((2, count, hidden), BF16),
+            jax.ShapeDtypeStruct((2, count, hidden), BF16),
+            jax.ShapeDtypeStruct((2, count, width), BF16),
             jax.ShapeDtypeStruct((lanes, width), F32),
         ],
         cost_estimate=pl.CostEstimate(
@@ -521,11 +521,14 @@
         compiler_params=pltpu.CompilerParams(vmem_limit_bytes=60 * 1024 * 1024),
         name="feed_routed" if routed else "feed_dense",
     )(pick, own, side, own_grads, side_grads, head, up, down)
+    flat = [value.reshape(2 * count, value.shape[2]) for value in (active, pre, weighted)]
+    return [*sums, *flat, head_grad]
 
 
 LANES = 128
-DENSE_ROWS = 320
-EXPERT_ROWS = 448
+DIRECT = 8
+EARLY = 4
+QUARTER_ROWS = 128
 
 
 def norm_parts(values):
@@ -579,6 +582,20 @@
 
 def strips_sent(grads):
     return exchange(grads.reshape(lax.axis_size("expert"), -1, grads.shape[1]))
+
+
+def strips_sent_each(grads, before, since):
+    count = lax.axis_size("expert")
+    if count > DIRECT:
+        return [] if before else [strips_total(strips_sent(grads))]
+    here = lax.axis_index("expert")
+    strips = grads.reshape(count, -1, grads.shape[1])
+    parts = []
+    for step in range(since, before or count):
+        strip = lax.dynamic_index_in_dim(strips, (here + step) % count, 0, keepdims=False)
+        pairs = [(i, (i + step) % count) for i in range(count)]
+        parts.append(lax.ppermute(strip, "expert", pairs) if step else strip)
+    return parts
 
 
 def strips_total(strips):
@@ -683,7 +700,7 @@
 
     def dense(own, side, own_cotangent, side_cotangent):
         return feed(
-            own, side, own_cotangent, side_cotangent, head, w_up, w_down, experts, None, DENSE_ROWS
+            own, side, own_cotangent, side_cotangent, head, w_up, w_down, experts, None, QUARTER_ROWS
         )
 
     def product(left, right):
@@ -717,7 +734,7 @@
             ex_down[0],
             experts,
             expert,
-            EXPERT_ROWS,
+            QUARTER_ROWS,
         )
 
     def chip_sum(parts, place, *others):
@@ -733,6 +750,7 @@
     far_two = jnp.concatenate([normed_two_far, normed_two_corner], axis=0)
     grad_up = (grad_up + product(far_two, far_dense[5])).astype(BF16)
     grad_down = (grad_down + product(far_dense[6], far_dense[4])).astype(BF16)
+    grad_up, grad_down, far_grads = lax.optimization_barrier((grad_up, grad_down, far_grads))
     dense_grads = jnp.concatenate([grad_up, grad_down], axis=1)
     far_rows, dense_back_far, dense_grads = lax.optimization_barrier(
         (far_rows, dense_back_far, dense_grads)
@@ -758,20 +776,17 @@
     dense_out_far = chip_sum(far_dense, 0, expert_back).astype(BF16)
     dense_back = chip_sum(near_dense, 2, far_back) + dense_back_far.astype(F32)
 
-    far_out_rows = from_far(far_expert_out)
-    grad_normed_two, far_out_rows = lax.optimization_barrier(
-        (dense_back + picked(sent(expert_back)), far_out_rows)
-    )
+    grad_normed_two = dense_back + picked(sent(expert_back))
     dense_out = chip_sum(near_dense, 0, expert_back)
-    expert_out = chip_sum(near_expert, 0, expert_back) + far_out_rows.astype(F32)
-    expert_out = sent(after(expert_out.astype(BF16), grad_normed_two))
-
+    expert_out = chip_sum(near_expert, 0, expert_back) + from_far(far_expert_out).astype(F32)
+    expert_out = after(expert_out.astype(BF16), grad_normed_two)
+
+    near_active, far_active, near_pre, far_pre, far_expert_out = lax.optimization_barrier(
+        (near_expert[4], far_expert[4], near_expert[5], far_expert[5], far_expert_out)
+    )
     near_tokens = jnp.concatenate([own_rows, side_rows], axis=0)
-    near_tokens, near_active, far_active, far_expert_out = lax.optimization_barrier(
-        (near_tokens, near_expert[4], far_expert[4], far_expert_out)
-    )
     far_tokens = jnp.concatenate([far_rows, corner_rows], axis=0)
-    grad_ex_up = weight_grads(near_tokens, far_tokens, near_expert[5], far_expert[5])[None]
+    grad_ex_up = weight_grads(near_tokens, far_tokens, near_pre, far_pre)[None]
     grad_ex_down = weight_grads(near_active, far_active, near_expert[6], far_expert[6])[None]
 
     gain_two = jnp.sum(grad_normed_two * scaled_two, axis=0)
@@ -787,47 +802,62 @@
         return jnp.stack(grads).astype(BF16)
 
     near_heads = into_heads(grad_branch, grad_branch_side)
-    grad_branch_far, near_heads, grad_ex_up, grad_ex_down = lax.optimization_barrier(
-        (grad_branch_far, near_heads, grad_ex_up, grad_ex_down)
-    )
-    grad_branch_corner = from_side(grad_branch_far)
-    far_heads = into_heads(grad_branch_far, grad_branch_corner)
     head_grads = near_dense[7] + far_dense[7] + near_expert[7] + far_expert[7]
     small = jnp.concatenate([head_grads[: experts + 2], gain_two[None]], axis=0)
     small = sum_over(small, "tensor")
+    out_rows = sent(expert_out)
+    grad_branch_far, small, near_heads, grad_ex_up, grad_ex_down, _, dense_out_far, dense_out = (
+        lax.optimization_barrier(
+            (
+                grad_branch_far,
+                small,
+                near_heads,
+                grad_ex_up,
+                grad_ex_down,
+                expert_out,
+                dense_out_far,
+                dense_out,
+            )
+        )
+    )
+    grad_branch_corner = from_side(grad_branch_far)
+    far_heads = into_heads(grad_branch_far, grad_branch_corner)
     small_columns = -(-small.shape[0] // LANES) * LANES
     small_block = jnp.pad(small, ((0, small_columns - small.shape[0]), (0, 0))).T
-    dense_out_far = from_far(after(dense_out_far, grad_branch_far))
-    near_result, far_result = attention_backward(
-        leaves, near_qkv, far_qkv, near_heads, far_heads, near_out, far_out, logs
-    )
-    near_result, far_result, expert_out, dense_out_far = lax.optimization_barrier(
-        (near_result, far_result, expert_out, dense_out_far)
-    )
-
-    def normed_part(grads):
-        return jnp.einsum("sgc,sdc->gd", grads, w_qkv, preferred_element_type=F32)
-
-    corner_part = normed_part(far_result[:, 1]).astype(BF16)
-    from_corner = from_side(corner_part).astype(F32)
+    dense_out_far = from_far(dense_out_far)
 
     flat = (2 * tok_dev, heads_width)
     near_branch = jnp.concatenate([grad_branch, grad_branch_side], axis=0)
     far_branch = jnp.concatenate([grad_branch_far, grad_branch_corner], axis=0)
-    near_branch = after(near_branch, corner_part)
     grad_w_out = weight_grads(near_branch, far_branch, near_out.reshape(flat), far_out.reshape(flat))
-    branch_grads = strips_total(strips_sent(
-        jnp.concatenate([grad_w_out.astype(BF16), small_block.astype(BF16)], axis=1)
-    ))
+    branch_grads = jnp.concatenate([grad_w_out.astype(BF16), small_block.astype(BF16)], axis=1)
+    branch_early = strips_sent_each(branch_grads, EARLY, 0)
+    near_result, far_result = attention_backward(
+        leaves, near_qkv, far_qkv, near_heads, far_heads, near_out, far_out, logs
+    )
+    near_result, far_result, out_rows, dense_out_far, *branch_early = lax.optimization_barrier(
+        (near_result, far_result, out_rows, dense_out_far, *branch_early)
+    )
+
+    def normed_part(grads):
+        return jnp.einsum("sgc,sdc->gd", grads, w_qkv, preferred_element_type=F32)
+
+    corner_part = normed_part(far_result[:, 1]).astype(BF16)
+    from_corner = from_side(corner_part).astype(F32)
+
     far_sum = (normed_part(far_result[:, 0]) + from_corner).astype(BF16)
-    near_result, far_result, expert_out, far_sum = lax.optimization_barrier(
-        (near_result, far_result, expert_out, far_sum)
-    )
+    near_result, far_result, out_rows, far_sum, branch_grads = lax.optimization_barrier(
+        (near_result, far_result, out_rows, far_sum, branch_grads)
+    )
+    branch_late = strips_sent_each(branch_grads, 0, EARLY)
     near_sum = plus_side(normed_part(near_result[:, 0]), normed_part(near_result[:, 1]))
-    out = (residual + dense_out + dense_out_far.astype(F32) + picked(expert_out)).astype(BF16)
+    out = (residual + dense_out + dense_out_far.astype(F32) + picked(out_rows)).astype(BF16)
 
     near_result = near_result.reshape(3, *flat)
     far_result = far_result.reshape(3, *flat)
+    branch_grads = functools.reduce(
+        jnp.add, [part.astype(F32) for part in branch_early + branch_late]
+    )
     qkv_grads = strips_total(strips_sent(
         jnp.concatenate(
             [

time: 688 us -> 634 us (0.922)
  waiting for transfers between devices: 202 us -> 137 us
  Pallas kernels: 202 us -> 173 us
  starting transfers between devices: 69.9 us -> 84.6 us
  other arithmetic: 67.2 us -> 76.9 us
  local copies, waits for them, and re-layouts: 13.8 us -> 21.1 us
  matrix products: 114 us -> 121 us
    all_to_all x7 -> x6, waiting for transfers between devices: 92.3 us -> 20 us  [exchange(): lax.all_to_all(blocks, 'expert', split_axis=0, concat_axis=0, tiled=True)]
    pallas_call x4, Pallas kernels: 136 us -> 107 us  [feed(): pl.pallas_call(functools.partial(feed_kernel, experts, routed), grid_spec...]
    ppermute x11, waiting for transfers between devices: 76.1 us -> 49.6 us  [from_far(): return lax.ppermute(values, 'tensor', [(i, i ^ 2) for i in range(4)])]
    ppermute x0 -> x7, waiting for transfers between devices: none -> 17.2 us  [strips_sent_each(): parts.append(lax.ppermute(strip, 'expert', pairs) if step else strip)]
    ppermute x0 -> x7, starting transfers between devices: none -> 15.2 us  [strips_sent_each(): parts.append(lax.ppermute(strip, 'expert', pairs) if step else strip)]
    ppermute x7, waiting for transfers between devices: 13.5 us -> 26.5 us  [sum_over(): values = values + lax.ppermute(values, axis, pairs)]
    all_to_all x7 -> x6, starting transfers between devices: 41.2 us -> 30.1 us  [exchange(): lax.all_to_all(blocks, 'expert', split_axis=0, concat_axis=0, tiled=True)]
    ppermute x7, starting transfers between devices: 8.76 us -> 16.9 us  [sum_over(): values = values + lax.ppermute(values, axis, pairs)]
  transfers between devices with their start and end apart: 50 -> 56, of which waited for: 19 -> 20; matrix products, arithmetic and copies ran while one was open for 25% -> 29% of each run, Pallas kernels for 30% -> 28%
where the time goes in v7:
time: 634 us; the launch traced here: 629 us
  Pallas kernels  173 us (27%)
  waiting for transfers between devices  137 us (22%)
  matrix products  121 us (19%)
  starting transfers between devices  84.6 us (13%)
  other arithmetic  76.9 us (12%)
  local copies, waits for them, and re-layouts  21.1 us (3%)
  between operations  15.3 us (2%)
    pallas_call x4, Pallas kernels, feed(): pl.pallas_call(functools.partial(feed_kernel, experts, routed), grid_spec...  107 us
    dot_general x16, matrix products, product(): return jnp.einsum('gd,gf->df', left, right, preferred_element_type=F32)  67.1 us
    ppermute x11, waiting for transfers between devices, from_far(): return lax.ppermute(values, 'tensor', [(i, i ^ 2) for i in range(4)])  49.6 us
    pallas_call x1, Pallas kernels, attention_backward(): pl.pallas_call(backward_kernel, grid_spec=pltpu.PrefetchScalarGridSpec(nu...  40.6 us
    all_to_all x6, starting transfers between devices, exchange(): lax.all_to_all(blocks, 'expert', split_axis=0, concat_axis=0, tiled=True)  30.1 us
    ppermute x7, waiting for transfers between devices, sum_over(): values = values + lax.ppermute(values, axis, pairs)  26.5 us
    pallas_call x1, Pallas kernels, attention_forward(): pl.pallas_call(forward_kernel, grid_spec=pltpu.PrefetchScalarGridSpec(num...  25.3 us
    all_to_all x6, waiting for transfers between devices, exchange(): lax.all_to_all(blocks, 'expert', split_axis=0, concat_axis=0, tiled=True)  20 us
  transfers between devices with their start and end apart: 56, of which 20 were waited for; matrix products, arithmetic and copies ran while one was open for 29% of the time, Pallas kernels for 28%

profile of v7, /device:TPU:0, one launch (start us, length us, event | category | flops | bytes accessed | tf_op | source)
XLA Modules:
  0.0 628.9 jit_solution(13736847039484765505)
XLA Ops:
  20.2 6.2 all-to-all-start
  33.0 12.1 %collective-permute-done = bf16[640,1024]{1,0:T(8,128)(2,1)} collective-permute-done((bf16[640,1024]{1,0:T(8,128)(2,1)}, bf16[640,1024]{1,0:T(8,128)(2,1)}, u32[]{:S(2)}, u32[]{:S(2)}) %collective-permute-start) | collective-permute-done | bytes 1310752 | tf_op jit(solution)/shard_map/ppermute | solution.py:558
  53.7 25.3 %tree_attention.1 = (bf16[2,640,256]{2,1,0:T(8,128)(2,1)}, bf16[2,640,256]{2,1,0:T(8,128)(2,1)}, f32[2,2,1024]{2,1,0:T(2,128)}, f32[2,4,2,384]{3,2,1,0:T(2,128)}) custom-call(s32[9]{0:T(128)} %pad_add_fusion.leaves_ref, bf16[3,2,640,256]{3,2,1,0:T(8,128)(2,1)} %bitcast.221, bf16[3,2,640,256]{3,2,1,0:T(8,128)(2,1)} %bitcast.223), custom_call_target="tpu_custom_call" | custom-call | flops 1241513984 | bytes 1310720 | tf_op jit(solution)/shard_map/tree_attention/pallas_call | solution.py:192
  92.9 23.8 %collective-permute-done.7 = bf16[640,1024]{1,0:T(8,128)(2,1)S(1)} collective-permute-done((bf16[640,1024]{1,0:T(8,128)(2,1)S(1)}, bf16[640,1024]{1,0:T(8,128)(2,1)S(1)}, u32[]{:S(2)}, u32[]{:S(2)}) %collective-permute-start.7) | collective-permute-done | bytes 1310752 | tf_op jit(solution)/shard_map/ppermute | solution.py:558
  121.7 6.3 %all-to-all-start.1 = ((bf16[8,112,1024]{2,1,0:T(8,128)(2,1)}), bf16[8,112,1024]{2,1,0:T(8,128)(2,1)}, u32[]{:S(2)}, u32[]{:S(2)}) async-start(bf16[8,112,1024]{2,1,0:T(8,128)(2,1)} %bitcast.196), calls=%async_computation.1 | async-start | bytes 3670016 | tf_op jit(solution)/shard_map/all_to_all | solution.py:575
  131.5 20.1 %feed_dense.2 = (bf16[640,1024]{1,0:T(8,128)(2,1)}, bf16[640,1024]{1,0:T(8,128)(2,1)}, bf16[640,1024]{1,0:T(8,128)(2,1)}, bf16[640,1024]{1,0:T(8,128)(2,1)}, bf1...) custom-call(s32[1]{0:T(128)} %constant.108.clone.1.expert_ref, ...), custom_call_target="tpu_custom_call" | custom-call | flops 1342177280 | bytes 2490368 | tf_op jit(solution)/shard_map/feed_dense/pallas_call | solution.py:481
  151.6 7.6 %fusion.21 = f32[1024,1024]{1,0:T(8,128)} fusion(bf16[1280,1024]{1,0:T(8,128)(2,1)} %bitcast.220, bf16[640,1024]{1,0:T(8,128)(2,1)} %collective-permute-done.10.side_ref, bf16[640,1024]{1,0:T(8,128)(2,1)} %copy-done.7), kind=kOutput, calls=%fused_computation.37 | convolution fusion | flops 2689597440 | bytes 9437184 | tf_op jit(solution)/shard_map/gd,gf->df/dot_general | solution.py:707
  163.7 6.5 %all-to-all-done.1 = bf16[8,112,1024]{2,1,0:T(8,128)(2,1)} async-done(((bf16[8,112,1024]{2,1,0:T(8,128)(2,1)}), bf16[8,112,1024]{2,1,0:T(8,128)(2,1)}, u32[]{:S(2)}, u32[]{:S(2)}) %all-to-all-start.1) | async-done | bytes 1835040 | tf_op jit(solution)/shard_map/all_to_all | solution.py:575
  176.1 20.5 %feed_dense.3 = (bf16[640,1024]{1,0:T(8,128)(2,1)}, bf16[640,1024]{1,0:T(8,128)(2,1)}, bf16[640,1024]{1,0:T(8,128)(2,1)}, bf16[640,1024]{1,0:T(8,128)(2,1)}, bf1...) custom-call(s32[1]{0:T(128)} %constant.108.clone.1.expert_ref, ...), custom_call_target="tpu_custom_call" | custom-call | flops 1342177280 | bytes 2490368 | tf_op jit(solution)/shard_map/feed_dense/pallas_call | solution.py:481
  197.2 13.3 %collective-permute-done.12.own_ref = bf16[896,1024]{1,0:T(8,128)(2,1)} collective-permute-done((bf16[896,1024]{1,0:T(8,128)(2,1)}, bf16[896,1024]{1,0:T(8,128)(2,1)}, u32[]{:S(2)}, u32[]{:S(2)}) %collective-permute-start.12) | collective-permute-done | bytes 1835040 | tf_op jit(solution)/shard_map/ppermute | solution.py:558
  210.6 7.6 %fusion.112 = f32[1024,1024]{1,0:T(8,128)} fusion(bf16[1280,1024]{1,0:T(8,128)(2,1)} %bitcast.219, bf16[1280,1024]{1,0:T(8,128)(2,1)} %bitcast.218), kind=kOutput, calls=%fused_computation.196 | convolution fusion | flops 2684354560 | bytes 9437184 | tf_op jit(solution)/shard_map/gd,gf->df/dot_general | solution.py:707
  218.2 6.5 %fusion.25 = f32[1024,1024]{1,0:T(8,128)} fusion(bf16[1280,1024]{1,0:T(8,128)(2,1)S(1)} %bitcast.217, bf16[640,1024]{1,0:T(8,128)(2,1)} %collective-permute-done.13.side_ref, bf16[640,1024]{1,0:T(8,128)(2,1)} %collective-permute-done.11.own_ref), kind=kOutput, calls=%fused_computation.41 | convolution fusion | flops 2689597440 | bytes 9437184 | tf_op jit(solution)/shard_map/gd,gf->df/dot_general | solution.py:707
  224.7 8.4 %add_convert_fusion = (bf16[1024,1024]{1,0:T(8,128)(2,1)}, bf16[1024,1024]{1,0:T(8,128)(2,1)}) fusion(f32[1024,1024]{1,0:T(8,128)} %convolution_bitcast_fusion, f32[1024,1024]{1,0:T(8,128)} %fusion.112, f32[1024,1024]{1,0:T(8,128)S(1)} %copy-done.8, f32[1024,1024]{1,0:T(8,128)} %fusion.25), kind=kLoop, calls=%fused_computation.3 | loop fusion | flops 4194304 | bytes 20971520 | tf_op jit(solution)/shard_map/convert_element_type | solution.py:752
  247.6 33.5 %feed_routed.2 = (bf16[896,1024]{1,0:T(8,128)(2,1)}, bf16[896,1024]{1,0:T(8,128)(2,1)}, bf16[896,1024]{1,0:T(8,128)(2,1)}, bf16[896,1024]{1,0:T(8,128)(2,1)}, bf...) custom-call(s32[1]{0:T(128)} %bitcast.20.expert_ref, ...), custom_call_target="tpu_custom_call" | custom-call | flops 1879048192 | bytes 3276800 | tf_op jit(solution)/shard_map/feed_routed/pallas_call | solution.py:481
  291.6 33.0 %feed_routed.3 = (bf16[896,1024]{1,0:T(8,128)(2,1)}, bf16[896,1024]{1,0:T(8,128)(2,1)}, bf16[896,1024]{1,0:T(8,128)(2,1)}, bf16[896,1024]{1,0:T(8,128)(2,1)}, bf...) custom-call(s32[1]{0:T(128)} %bitcast.20.expert_ref, ...), custom_call_target="tpu_custom_call" | custom-call | flops 1879048192 | bytes 3276800 | tf_op jit(solution)/shard_map/feed_routed/pallas_call | solution.py:481
  363.4 7.8 %fusion.4 = f32[1024,1024]{1,0:T(8,128)} fusion(bf16[1792,1024]{1,0:T(8,128)(2,1)S(1)} %bitcast.214, bf16[896,1024]{1,0:T(8,128)(2,1)} %collective-permute-done.15.side_ref, bf16[896,1024]{1,0:T(8,128)(2,1)} %collective-permute-done.12.own_ref), kind=kOutput, calls=%fused_computation.12 | convolution fusion | flops 3765436416 | bytes 11534336 | tf_op jit(solution)/shard_map/gd,gf->df/dot_general | solution.py:707
  371.2 5.5 add_bitcast_fusion
  376.7 13.5 %all-to-all-done.3 = bf16[8,112,1024]{2,1,0:T(8,128)(2,1)} async-done(((bf16[8,112,1024]{2,1,0:T(8,128)(2,1)}), bf16[8,112,1024]{2,1,0:T(8,128)(2,1)}, u32[]{:S(2)}, u32[]{:S(2)}) %all-to-all-start.3) | async-done | bytes 1835040 | tf_op jit(solution)/shard_map/all_to_all | solution.py:575
  390.2 6.2 multiply_reduce_fusion
  402.5 7.6 %add_bitcast_fusion.1 = f32[1,1024,1024]{2,1,0:T(8,128)} fusion(f32[1024,1024]{1,0:T(8,128)S(1)} %copy-done.46, bf16[1792,1024]{1,0:T(8,128)(2,1)S(1)} %bitcast.213, bf16[896,1024]{1,0:T(8,128)(2,1)} %collective-permute-done.20.side_ref, bf16[896,1024]{1,0:T(8,128)(2,1)} %bitcast.19.own_ref), kind=kOutput, calls=%fused_computation.2 | convolution fusion | flops 3766484992 | bytes 15728640 | tf_op jit(solution)/shard_map/gd,gf->df/dot_general | solution.py:707
  413.3 20.2 %collective-permute-done.25 = f32[11,1024]{1,0:T(8,128)S(1)} collective-permute-done((f32[11,1024]{1,0:T(8,128)S(1)}, f32[11,1024]{1,0:T(8,128)S(1)}, u32[]{:S(2)}, u32[]{:S(2)}) %collective-permute-start.25) | collective-permute-done | bytes 45088 | tf_op jit(solution)/shard_map/ppermute | solution.py:569
  469.4 40.6 %tree_attention_back.1 = (bf16[3,2,640,256]{3,2,1,0:T(8,128)(2,1)}, bf16[3,2,640,256]{3,2,1,0:T(8,128)(2,1)}) custom-call(s32[9]{0:T(128)} %pad_add_fusion.leaves_ref, bf16[3,2,640,256]{3,2,1,0:T(8,128)(2,1)} %bitcast.222, bf16[3,2,640,256]{3,2,1,0:T(8,128)(2,1)} %bitcast.224, bf16[2,640,256]{2,1,0:T(8,128)(2,1)} %pad_maximum_fusion.3.near_grads_ref, ...), custom_call_target="tpu_custom_call" | custom-call | flops 4966051840 | bytes 2097152 | tf_op jit(solution)/shard_map/tree_attention_back/pallas_call | solution.py:336
  565.7 17.2 %collective-permute-done.46 = bf16[128,384]{1,0:T(8,128)(2,1)S(1)} collective-permute-done((bf16[128,384]{1,0:T(8,128)(2,1)S(1)}, bf16[128,384]{1,0:T(8,128)(2,1)S(1)}, u32[]{:S(2)}, u32[]{:S(2)}) %collective-permute-start.46) | collective-permute-done | bytes 98336 | tf_op jit(solution)/shard_map/ppermute | solution.py:597
  593.8 13.9 %collective-permute-start.42 = (f32[1,1024]{1,0:T(1,128)S(1)}, f32[1,1024]{1,0:T(1,128)S(1)}, u32[]{:S(2)}, u32[]{:S(2)}) collective-permute-start(f32[1,1024]{1,0:T(1,128)S(1)} %add.326), channel_id=1, source_target_pairs={{0,4},{4,0},{8,12},{12,8},{16,20},{20,16},{24,28},{28,24},{1,5},{5... | collective-permute-start | bytes 12296 | tf_op jit(solution)/shard_map/ppermute | solution.py:569
  (306 shorter events, 250.4 us)
Async XLA Ops:
  20.2 58.9 %all-to-all-start = ((bf16[8,112,1024]{2,1,0:T(8,128)(2,1)}), bf16[8,112,1024]{2,1,0:T(8,128)(2,1)}, u32[]{:S(2)}, u32[]{:S(2)}) async-start(bf16[8,112,1024]{2,1,0:T(8,128)(2,1)} %bitcast.195), calls=%async_computation | async-start | bytes 3670016 | tf_op jit(solution)/shard_map/all_to_all | solution.py:575
  121.7 48.5 %all-to-all-start.1 = ((bf16[8,112,1024]{2,1,0:T(8,128)(2,1)}), bf16[8,112,1024]{2,1,0:T(8,128)(2,1)}, u32[]{:S(2)}, u32[]{:S(2)}) async-start(bf16[8,112,1024]{2,1,0:T(8,128)(2,1)} %bitcast.196), calls=%async_computation.1 | async-start | bytes 3670016 | tf_op jit(solution)/shard_map/all_to_all | solution.py:575
  128.1 35.5 %collective-permute-start.11 = (bf16[640,1024]{1,0:T(8,128)(2,1)}, bf16[640,1024]{1,0:T(8,128)(2,1)}, u32[]{:S(2)}, u32[]{:S(2)}) collective-permute-start(bf16[640,1024]{1,0:T(8,128)(2,1)} %copy-done.7), channel_id=1, source_target_pairs={{0,2},{1,3},{2,0},{3,1},{4,6},{5,7},{6,4},{7,5},{8,10},{9,11},{10,... | collective-permute-start | bytes 3932168 | tf_op jit(solution)/shard_map/ppermute | solution.py:558
  170.2 40.4 %collective-permute-start.12 = (bf16[896,1024]{1,0:T(8,128)(2,1)}, bf16[896,1024]{1,0:T(8,128)(2,1)}, u32[]{:S(2)}, u32[]{:S(2)}) collective-permute-start(bf16[896,1024]{1,0:T(8,128)(2,1)} %bitcast.19.own_ref), channel_id=1, source_target_pairs={{0,2},{1,3},{2,0},{3,1},{4,6},{5,7},{6,4},{7,5},{8,10},{9,11},{10,... | collective-permute-start | bytes 5505032 | tf_op jit(solution)/shard_map/ppermute | solution.py:558
  171.7 64.3 %all-to-all-start.2 = ((bf16[8,112,1024]{2,1,0:T(8,128)(2,1)}), bf16[8,112,1024]{2,1,0:T(8,128)(2,1)}, u32[]{:S(2)}, u32[]{:S(2)}) async-start(bf16[8,112,1024]{2,1,0:T(8,128)(2,1)} %bitcast.194), calls=%async_computation.2 | async-start | bytes 3670016 | tf_op jit(solution)/shard_map/all_to_all | solution.py:575
  176.0 153.8 %reduce-scatter.2.cloned.1.call-start = ((), (), s32[]{:S(2)}) async-start(), calls=%async_computation.7 | async-start | bytes 4718592 | tf_op jit(solution)/shard_map/reduce_scatter | solution.py:580
  196.7 36.4 %collective-permute-start.14 = (bf16[640,1024]{1,0:T(8,128)(2,1)}, bf16[640,1024]{1,0:T(8,128)(2,1)}, u32[]{:S(2)}, u32[]{:S(2)}) collective-permute-start(bf16[640,1024]{1,0:T(8,128)(2,1)} %get-tuple-element.149), channel_id=1, source_target_pairs={{0,1},{1,0},{2,3},{3,2},{4,5},{5,4},{6,7},{7,6},{8,9},{9,8},{10,11... | collective-permute-start | bytes 3932168 | tf_op jit(solution)/shard_map/ppermute | solution.py:554
  241.4 39.7 %collective-permute-start.17 = (bf16[640,1024]{1,0:T(8,128)(2,1)}, bf16[640,1024]{1,0:T(8,128)(2,1)}, u32[]{:S(2)}, u32[]{:S(2)}) collective-permute-start(bf16[640,1024]{1,0:T(8,128)(2,1)} %add_convert_fusion.8), channel_id=1, source_target_pairs={{0,2},{1,3},{2,0},{3,1},{4,6},{5,7},{6,4},{7,5},{8,10},{9,11},{10,... | collective-permute-start | bytes 3932168 | tf_op jit(solution)/shard_map/ppermute | solution.py:558
  290.0 42.4 %collective-permute-start.22 = (bf16[896,1024]{1,0:T(8,128)(2,1)}, bf16[896,1024]{1,0:T(8,128)(2,1)}, u32[]{:S(2)}, u32[]{:S(2)}) collective-permute-start(bf16[896,1024]{1,0:T(8,128)(2,1)} %add_convert_fusion.5), channel_id=1, source_target_pairs={{0,2},{1,3},{2,0},{3,1},{4,6},{5,7},{6,4},{7,5},{8,10},{9,11},{10,... | collective-permute-start | bytes 5505032 | tf_op jit(solution)/shard_map/ppermute | solution.py:558
  341.2 35.6 %collective-permute-start.19 = (bf16[640,1024]{1,0:T(8,128)(2,1)}, bf16[640,1024]{1,0:T(8,128)(2,1)}, u32[]{:S(2)}, u32[]{:S(2)}) collective-permute-start(bf16[640,1024]{1,0:T(8,128)(2,1)} %get-tuple-element.173), channel_id=1, source_target_pairs={{0,1},{1,0},{2,3},{3,2},{4,5},{5,4},{6,7},{7,6},{8,9},{9,8},{10,11... | collective-permute-start | bytes 3932168 | tf_op jit(solution)/shard_map/ppermute | solution.py:554
  342.5 47.7 %all-to-all-start.3 = ((bf16[8,112,1024]{2,1,0:T(8,128)(2,1)}), bf16[8,112,1024]{2,1,0:T(8,128)(2,1)}, u32[]{:S(2)}, u32[]{:S(2)}) async-start(bf16[8,112,1024]{2,1,0:T(8,128)(2,1)} %bitcast.191), calls=%async_computation.4 | async-start | bytes 3670016 | tf_op jit(solution)/shard_map/all_to_all | solution.py:575
  347.1 86.4 %collective-permute-start.28 = (bf16[896,1024]{1,0:T(8,128)(2,1)}, bf16[896,1024]{1,0:T(8,128)(2,1)}, u32[]{:S(2)}, u32[]{:S(2)}) collective-permute-start(bf16[896,1024]{1,0:T(8,128)(2,1)} %get-tuple-element.207), channel_id=1, source_target_pairs={{0,1},{1,0},{2,3},{3,2},{4,5},{5,4},{6,7},{7,6},{8,9},{9,8},{10,11... | collective-permute-start | bytes 5505032 | tf_op jit(solution)/shard_map/ppermute | solution.py:554
  357.8 75.7 %collective-permute-start.29 = (bf16[896,1024]{1,0:T(8,128)(2,1)}, bf16[896,1024]{1,0:T(8,128)(2,1)}, u32[]{:S(2)}, u32[]{:S(2)}) collective-permute-start(bf16[896,1024]{1,0:T(8,128)(2,1)} %add_convert_fusion.3), channel_id=1, source_target_pairs={{0,2},{1,3},{2,0},{3,1},{4,6},{5,7},{6,4},{7,5},{8,10},{9,11},{10,... | collective-permute-start | bytes 5505032 | tf_op jit(solution)/shard_map/ppermute | solution.py:558
  400.7 41.8 %collective-permute-start.26 = (bf16[640,1024]{1,0:T(8,128)(2,1)}, bf16[640,1024]{1,0:T(8,128)(2,1)}, u32[]{:S(2)}, u32[]{:S(2)}) collective-permute-start(bf16[640,1024]{1,0:T(8,128)(2,1)} %get-tuple-element.309), channel_id=1, source_target_pairs={{0,1},{1,0},{2,3},{3,2},{4,5},{5,4},{6,7},{7,6},{8,9},{9,8},{10,11... | collective-permute-start | bytes 3932168 | tf_op jit(solution)/shard_map/ppermute | solution.py:554
  400.7 45.6 %collective-permute-start.23 = (bf16[640,1024]{1,0:T(8,128)(2,1)}, bf16[640,1024]{1,0:T(8,128)(2,1)}, u32[]{:S(2)}, u32[]{:S(2)}) collective-permute-start(bf16[640,1024]{1,0:T(8,128)(2,1)} %get-tuple-element.309), channel_id=1, source_target_pairs={{0,2},{1,3},{2,0},{3,1},{4,6},{5,7},{6,4},{7,5},{8,10},{9,11},{10,... | collective-permute-start | bytes 3932168 | tf_op jit(solution)/shard_map/ppermute | solution.py:558
  438.2 71.9 %all-to-all-start.4 = ((bf16[8,112,1024]{2,1,0:T(8,128)(2,1)}), bf16[8,112,1024]{2,1,0:T(8,128)(2,1)}, u32[]{:S(2)}, u32[]{:S(2)}) async-start(bf16[8,112,1024]{2,1,0:T(8,128)(2,1)} %bitcast.190), calls=%async_computation.5 | async-start | bytes 3670016 | tf_op jit(solution)/shard_map/all_to_all | solution.py:575
  446.3 63.8 %collective-permute-start.33 = (bf16[640,1024]{1,0:T(8,128)(2,1)}, bf16[640,1024]{1,0:T(8,128)(2,1)}, u32[]{:S(2)}, u32[]{:S(2)}) collective-permute-start(bf16[640,1024]{1,0:T(8,128)(2,1)} %add_convert_fusion.7), channel_id=1, source_target_pairs={{0,2},{1,3},{2,0},{3,1},{4,6},{5,7},{6,4},{7,5},{8,10},{9,11},{10,... | collective-permute-start | bytes 3932168 | tf_op jit(solution)/shard_map/ppermute | solution.py:558
  460.9 49.2 %collective-permute-start.36 = (bf16[128,384]{1,0:T(8,128)(2,1)}, bf16[128,384]{1,0:T(8,128)(2,1)}, u32[]{:S(2)}, u32[]{:S(2)}) collective-permute-start(bf16[128,384]{1,0:T(8,128)(2,1)} %get-tuple-element.325), channel_id=1, source_target_pairs={{0,12},{4,16},{8,20},{12,24},{16,28},{20,0},{24,4},{28,8},{1,13},{... | collective-permute-start | bytes 294920 | tf_op jit(solution)/shard_map/ppermute | solution.py:597
  463.7 46.4 %collective-permute-start.35 = (bf16[128,384]{1,0:T(8,128)(2,1)}, bf16[128,384]{1,0:T(8,128)(2,1)}, u32[]{:S(2)}, u32[]{:S(2)}) collective-permute-start(bf16[128,384]{1,0:T(8,128)(2,1)} %get-tuple-element.326), channel_id=1, source_target_pairs={{0,8},{4,12},{8,16},{12,20},{16,24},{20,28},{24,0},{28,4},{1,9},{5... | collective-permute-start | bytes 294920 | tf_op jit(solution)/shard_map/ppermute | solution.py:597
  465.1 44.9 %collective-permute-start.34 = (bf16[128,384]{1,0:T(8,128)(2,1)S(1)}, bf16[128,384]{1,0:T(8,128)(2,1)}, u32[]{:S(2)}, u32[]{:S(2)}) collective-permute-start(bf16[128,384]{1,0:T(8,128)(2,1)S(1)} %get-tuple-element.327), channel_id=1, source_target_pairs={{0,4},{4,8},{8,12},{12,16},{16,20},{20,24},{24,28},{28,0},{1,5},{5... | collective-permute-start | bytes 294920 | tf_op jit(solution)/shard_map/ppermute | solution.py:597
  529.4 36.2 %collective-permute-start.48 = (bf16[128,384]{1,0:T(8,128)(2,1)}, bf16[128,384]{1,0:T(8,128)(2,1)}, u32[]{:S(2)}, u32[]{:S(2)}) collective-permute-start(bf16[128,384]{1,0:T(8,128)(2,1)} %get-tuple-element.322), channel_id=1, source_target_pairs={{0,28},{4,0},{8,4},{12,8},{16,12},{20,16},{24,20},{28,24},{1,29},{... | collective-permute-start | bytes 294920 | tf_op jit(solution)/shard_map/ppermute | solution.py:597
  534.4 49.7 %collective-permute-start.38 = (bf16[640,1024]{1,0:T(8,128)(2,1)}, bf16[640,1024]{1,0:T(8,128)(2,1)}, u32[]{:S(2)}, u32[]{:S(2)}) collective-permute-start(bf16[640,1024]{1,0:T(8,128)(2,1)} %bitcast_convert_fusion), channel_id=1, source_target_pairs={{0,1},{1,0},{2,3},{3,2},{4,5},{5,4},{6,7},{7,6},{8,9},{9,8},{10,11... | collective-permute-start | bytes 3932168 | tf_op jit(solution)/shard_map/ppermute | solution.py:554
  534.4 49.7 %collective-permute-start.39 = (bf16[640,1024]{1,0:T(8,128)(2,1)}, bf16[640,1024]{1,0:T(8,128)(2,1)}, u32[]{:S(2)}, u32[]{:S(2)}) collective-permute-start(bf16[640,1024]{1,0:T(8,128)(2,1)} %fusion.38), channel_id=1, source_target_pairs={{0,2},{1,3},{2,0},{3,1},{4,6},{5,7},{6,4},{7,5},{8,10},{9,11},{10,... | collective-permute-start | bytes 3932168 | tf_op jit(solution)/shard_map/ppermute | solution.py:558
  549.1 70.1 %all-to-all-start.5 = ((bf16[8,128,768]{1,2,0:T(8,128)(2,1)}), bf16[8,128,768]{1,2,0:T(8,128)(2,1)}, u32[]{:S(2)}, u32[]{:S(2)}) async-start(bf16[8,128,768]{1,2,0:T(8,128)(2,1)} %copy_bitcast_fusion), calls=%async_computation.6 | async-start | bytes 3145728 | tf_op jit(solution)/shard_map/all_to_all | solution.py:575
  (79 other events, 853.6 us)
Sparse Core Ops, SparseCore 0:
  240.9 88.8 reduce-scatter.1

commit v8 on v7

--- a/solution.py
+++ b/solution.py
@@ -526,8 +526,6 @@
 
 
 LANES = 128
-DIRECT = 8
-EARLY = 4
 QUARTER_ROWS = 128
 
 
@@ -577,25 +575,11 @@
 
 def scatter_sum(strips):
     strips = with_layout_constraint(strips.astype(BF16), Layout(major_to_minor=(0, 1)))
-    return lax.psum_scatter(strips, "expert", scatter_dimension=0, tiled=True).astype(F32)
+    return lax.psum_scatter(strips, "expert", scatter_dimension=0, tiled=True)
 
 
 def strips_sent(grads):
     return exchange(grads.reshape(lax.axis_size("expert"), -1, grads.shape[1]))
-
-
-def strips_sent_each(grads, before, since):
-    count = lax.axis_size("expert")
-    if count > DIRECT:
-        return [] if before else [strips_total(strips_sent(grads))]
-    here = lax.axis_index("expert")
-    strips = grads.reshape(count, -1, grads.shape[1])
-    parts = []
-    for step in range(since, before or count):
-        strip = lax.dynamic_index_in_dim(strips, (here + step) % count, 0, keepdims=False)
-        pairs = [(i, (i + step) % count) for i in range(count)]
-        parts.append(lax.ppermute(strip, "expert", pairs) if step else strip)
-    return parts
 
 
 def strips_total(strips):
@@ -744,14 +728,11 @@
         return plus_side(parts[place], after(parts[place + 1], *others))
 
     dense_back_far = chip_sum(far_dense, 2).astype(BF16)
-    far_rows, far_dense[6], far_dense[5] = lax.optimization_barrier(
-        (far_rows, far_dense[6], far_dense[5])
-    )
     far_two = jnp.concatenate([normed_two_far, normed_two_corner], axis=0)
+    grad_down = (grad_down + product(far_dense[6], far_dense[4])).astype(BF16)
+    far_two, far_rows, grad_down = lax.optimization_barrier((far_two, far_rows, grad_down))
     grad_up = (grad_up + product(far_two, far_dense[5])).astype(BF16)
-    grad_down = (grad_down + product(far_dense[6], far_dense[4])).astype(BF16)
-    grad_up, grad_down, far_grads = lax.optimization_barrier((grad_up, grad_down, far_grads))
-    dense_grads = jnp.concatenate([grad_up, grad_down], axis=1)
+    dense_grads = after(jnp.concatenate([grad_up, grad_down], axis=1), far_grads)
     far_rows, dense_back_far, dense_grads = lax.optimization_barrier(
         (far_rows, dense_back_far, dense_grads)
     )
@@ -802,16 +783,16 @@
         return jnp.stack(grads).astype(BF16)
 
     near_heads = into_heads(grad_branch, grad_branch_side)
-    head_grads = near_dense[7] + far_dense[7] + near_expert[7] + far_expert[7]
-    small = jnp.concatenate([head_grads[: experts + 2], gain_two[None]], axis=0)
-    small = sum_over(small, "tensor")
     out_rows = sent(expert_out)
-    grad_branch_far, small, near_heads, grad_ex_up, grad_ex_down, _, dense_out_far, dense_out = (
+    flat = (2 * tok_dev, heads_width)
+    near_branch = jnp.concatenate([grad_branch, grad_branch_side], axis=0)
+    grad_w_out = product(near_branch, near_out.reshape(flat))
+    grad_branch_far, near_heads, grad_w_out, grad_ex_up, grad_ex_down, _, dense_out_far, dense_out = (
         lax.optimization_barrier(
             (
                 grad_branch_far,
-                small,
                 near_heads,
+                grad_w_out,
                 grad_ex_up,
                 grad_ex_down,
                 expert_out,
@@ -822,42 +803,45 @@
     )
     grad_branch_corner = from_side(grad_branch_far)
     far_heads = into_heads(grad_branch_far, grad_branch_corner)
+    dense_out_far = from_far(dense_out_far)
+    head_grads = near_dense[7] + far_dense[7] + near_expert[7] + far_expert[7]
+    small = jnp.concatenate([head_grads[: experts + 2], gain_two[None]], axis=0)
+    near_result, far_result = attention_backward(
+        leaves, near_qkv, far_qkv, near_heads, far_heads, near_out, far_out, logs
+    )
+    near_result, far_result, out_rows, dense_out_far, small = lax.optimization_barrier(
+        (near_result, far_result, out_rows, dense_out_far, small)
+    )
+    small = sum_over(small, "tensor")
+
+    def normed_part(grads):
+        return jnp.einsum("sgc,sdc->gd", grads, w_qkv, preferred_element_type=F32)
+
+    corner_part = normed_part(far_result[:, 1]).astype(BF16)
+    from_corner = from_side(corner_part).astype(F32)
+
+    far_branch = jnp.concatenate([grad_branch_far, grad_branch_corner], axis=0)
+    grad_w_out = grad_w_out + product(after(far_branch, corner_part), far_out.reshape(flat))
     small_columns = -(-small.shape[0] // LANES) * LANES
     small_block = jnp.pad(small, ((0, small_columns - small.shape[0]), (0, 0))).T
-    dense_out_far = from_far(dense_out_far)
-
-    flat = (2 * tok_dev, heads_width)
-    near_branch = jnp.concatenate([grad_branch, grad_branch_side], axis=0)
-    far_branch = jnp.concatenate([grad_branch_far, grad_branch_corner], axis=0)
-    grad_w_out = weight_grads(near_branch, far_branch, near_out.reshape(flat), far_out.reshape(flat))
     branch_grads = jnp.concatenate([grad_w_out.astype(BF16), small_block.astype(BF16)], axis=1)
-    branch_early = strips_sent_each(branch_grads, EARLY, 0)
-    near_result, far_result = attention_backward(
-        leaves, near_qkv, far_qkv, near_heads, far_heads, near_out, far_out, logs
-    )
-    near_result, far_result, out_rows, dense_out_far, *branch_early = lax.optimization_barrier(
-        (near_result, far_result, out_rows, dense_out_far, *branch_early)
-    )
-
-    def normed_part(grads):
-        return jnp.einsum("sgc,sdc->gd", grads, w_qkv, preferred_element_type=F32)
-
-    corner_part = normed_part(far_result[:, 1]).astype(BF16)
-    from_corner = from_side(corner_part).astype(F32)
-
+    far_result, branch_grads = lax.optimization_barrier((far_result, branch_grads))
+    branch_grads = strips_total(strips_sent(branch_grads))
     far_sum = (normed_part(far_result[:, 0]) + from_corner).astype(BF16)
-    near_result, far_result, out_rows, far_sum, branch_grads = lax.optimization_barrier(
-        (near_result, far_result, out_rows, far_sum, branch_grads)
-    )
-    branch_late = strips_sent_each(branch_grads, 0, EARLY)
+    near_result, far_result, out_rows, far_sum = lax.optimization_barrier(
+        (near_result, far_result, out_rows, far_sum)
+    )
     near_sum = plus_side(normed_part(near_result[:, 0]), normed_part(near_result[:, 1]))
     out = (residual + dense_out + dense_out_far.astype(F32) + picked(out_rows)).astype(BF16)
 
     near_result = near_result.reshape(3, *flat)
     far_result = far_result.reshape(3, *flat)
-    branch_grads = functools.reduce(
-        jnp.add, [part.astype(F32) for part in branch_early + branch_late]
-    )
+    scaled_far = normed_far.astype(F32) / ln_attn
+    gain_one = jnp.sum(
+        near_sum * scaled_one + far_sum.astype(F32) * scaled_far, axis=0, keepdims=True
+    )
+    gain_one = sum_over(gain_one, "expert")
+    near_result = after(near_result, gain_one)
     qkv_grads = strips_total(strips_sent(
         jnp.concatenate(
             [
@@ -867,9 +851,8 @@
             axis=1,
         )
     ))
-    grad_normed_one = near_sum + from_far(far_sum).astype(F32)
-    gain_one = jnp.sum(grad_normed_one * scaled_one, axis=0, keepdims=True)
-    grad_ln_attn = sum_over(sum_over(gain_one, "tensor"), "expert")[0]
+    grad_normed_one = near_sum + after(from_far(far_sum), gain_one).astype(F32)
+    grad_ln_attn = sum_over(gain_one, "tensor")[0]
     grad_tokens = grad_residual + norm_back(grad_normed_one, ln_attn, scaled_one, inverse_one)
 
     strip = qkv_grads.shape[0]
@@ -880,8 +863,8 @@
         qkv_grads.reshape(strip, 3, heads_width).transpose(1, 0, 2),
         branch_grads[:, :heads_width].T,
         branch_grads[:, heads_width + experts + 2],
-        dense_grads[:, :hidden],
-        dense_grads[:, hidden:].T,
+        dense_grads[:, :hidden].astype(F32),
+        dense_grads[:, hidden:].T.astype(F32),
         branch_grads[:, heads_width : heads_width + experts],
         branch_grads[:, heads_width + experts : heads_width + experts + 2],
         grad_ex_up,

time: 634 us -> 574 us (0.905)
  waiting for transfers between devices: 137 us -> 116 us
  starting transfers between devices: 84.6 us -> 67.3 us
  other arithmetic: 76.9 us -> 68.6 us
  local copies, waits for them, and re-layouts: 21.1 us -> 14 us
    ppermute x11, waiting for transfers between devices: 49.6 us -> 70.3 us  [from_far(): return lax.ppermute(values, 'tensor', [(i, i ^ 2) for i in range(4)])]
    ppermute x7, waiting for transfers between devices: 26.5 us -> 7.95 us  [sum_over(): values = values + lax.ppermute(values, axis, pairs)]
    ppermute x7 -> x0, waiting for transfers between devices: 17.2 us -> none  [strips_sent_each(): parts.append(lax.ppermute(strip, 'expert', pairs) if step else strip)]
    ppermute x7 -> x0, starting transfers between devices: 15.2 us -> none  [strips_sent_each(): parts.append(lax.ppermute(strip, 'expert', pairs) if step else strip)]
    ppermute x7, starting transfers between devices: 16.9 us -> 9.03 us  [sum_over(): values = values + lax.ppermute(values, axis, pairs)]
    convert_element_type x1, other arithmetic: 8.41 us -> 1.07 us  [per_device(): grad_down = (grad_down + product(far_dense[6], far_dense[4])).astype(BF16)]
    dot_general x16, matrix products: 67.1 us -> 60.5 us  [product(): return jnp.einsum('gd,gf->df', left, right, preferred_element_type=F32)]
    all_to_all x6 -> x7, starting transfers between devices: 30.1 us -> 35.4 us  [exchange(): lax.all_to_all(blocks, 'expert', split_axis=0, concat_axis=0, tiled=True)]
  transfers between devices with their start and end apart: 56 -> 50, of which waited for: 20 -> 22; matrix products, arithmetic and copies ran while one was open for 29% -> 29% of each run, Pallas kernels for 28% -> 30%
where the time goes in v8:
time: 574 us; the launch traced here: 570 us
  Pallas kernels  172 us (30%)
  matrix products  116 us (20%)
  waiting for transfers between devices  116 us (20%)
  other arithmetic  68.6 us (12%)
  starting transfers between devices  67.3 us (12%)
  between operations  15.4 us (3%)
  local copies, waits for them, and re-layouts  14 us (2%)
    pallas_call x4, Pallas kernels, feed(): pl.pallas_call(functools.partial(feed_kernel, experts, routed), grid_spec...  106 us
    ppermute x11, waiting for transfers between devices, from_far(): return lax.ppermute(values, 'tensor', [(i, i ^ 2) for i in range(4)])  70.3 us
    dot_general x16, matrix products, product(): return jnp.einsum('gd,gf->df', left, right, preferred_element_type=F32)  60.5 us
    pallas_call x1, Pallas kernels, attention_backward(): pl.pallas_call(backward_kernel, grid_spec=pltpu.PrefetchScalarGridSpec(nu...  40.6 us
    all_to_all x7, starting transfers between devices, exchange(): lax.all_to_all(blocks, 'expert', split_axis=0, concat_axis=0, tiled=True)  35.4 us
    pallas_call x1, Pallas kernels, attention_forward(): pl.pallas_call(forward_kernel, grid_spec=pltpu.PrefetchScalarGridSpec(num...  25.3 us
    all_to_all x7, waiting for transfers between devices, exchange(): lax.all_to_all(blocks, 'expert', split_axis=0, concat_axis=0, tiled=True)  20.1 us
    ppermute x11, starting transfers between devices, from_far(): return lax.ppermute(values, 'tensor', [(i, i ^ 2) for i in range(4)])  18.1 us
  transfers between devices with their start and end apart: 50, of which 22 were waited for; matrix products, arithmetic and copies ran while one was open for 29% of the time, Pallas kernels for 30%

profile of v8, /device:TPU:0, one launch (start us, length us, event | category | flops | bytes accessed | tf_op | source)
XLA Modules:
  0.0 569.6 jit_solution(8134021741736118918)
XLA Ops:
  20.1 6.2 %all-to-all-start = ((bf16[8,112,1024]{2,1,0:T(8,128)(2,1)}), bf16[8,112,1024]{2,1,0:T(8,128)(2,1)}, u32[]{:S(2)}, u32[]{:S(2)}) async-start(bf16[8,112,1024]{2,1,0:T(8,128)(2,1)} %bitcast.191), calls=%async_computation | async-start | bytes 3670016 | tf_op jit(solution)/shard_map/all_to_all | solution.py:573
  27.7 5.3 convolution_convert_fusion.1
  33.0 12.0 %collective-permute-done = bf16[640,1024]{1,0:T(8,128)(2,1)} collective-permute-done((bf16[640,1024]{1,0:T(8,128)(2,1)}, bf16[640,1024]{1,0:T(8,128)(2,1)}, u32[]{:S(2)}, u32[]{:S(2)}) %collective-permute-start) | collective-permute-done | bytes 1310752 | tf_op jit(solution)/shard_map/ppermute | solution.py:556
  53.7 25.3 %tree_attention.1 = (bf16[2,640,256]{2,1,0:T(8,128)(2,1)}, bf16[2,640,256]{2,1,0:T(8,128)(2,1)}, f32[2,2,1024]{2,1,0:T(2,128)}, f32[2,4,2,384]{3,2,1,0:T(2,128)}) custom-call(s32[9]{0:T(128)} %pad_add_fusion.leaves_ref, bf16[3,2,640,256]{3,2,1,0:T(8,128)(2,1)} %bitcast.209, bf16[3,2,640,256]{3,2,1,0:T(8,128)(2,1)} %bitcast.211), custom_call_target="tpu_custom_call" | custom-call | flops 1241513984 | bytes 1310720 | tf_op jit(solution)/shard_map/tree_attention/pallas_call | solution.py:192
  93.0 23.8 %collective-permute-done.7 = bf16[640,1024]{1,0:T(8,128)(2,1)S(1)} collective-permute-done((bf16[640,1024]{1,0:T(8,128)(2,1)S(1)}, bf16[640,1024]{1,0:T(8,128)(2,1)S(1)}, u32[]{:S(2)}, u32[]{:S(2)}) %collective-permute-start.7) | collective-permute-done | bytes 1310752 | tf_op jit(solution)/shard_map/ppermute | solution.py:556
  121.8 6.4 %all-to-all-start.1 = ((bf16[8,112,1024]{2,1,0:T(8,128)(2,1)}), bf16[8,112,1024]{2,1,0:T(8,128)(2,1)}, u32[]{:S(2)}, u32[]{:S(2)}) async-start(bf16[8,112,1024]{2,1,0:T(8,128)(2,1)} %bitcast.192), calls=%async_computation.1 | async-start | bytes 3670016 | tf_op jit(solution)/shard_map/all_to_all | solution.py:573
  131.6 20.1 %feed_dense.2 = (bf16[640,1024]{1,0:T(8,128)(2,1)}, bf16[640,1024]{1,0:T(8,128)(2,1)}, bf16[640,1024]{1,0:T(8,128)(2,1)}, bf16[640,1024]{1,0:T(8,128)(2,1)}, bf1...) custom-call(s32[1]{0:T(128)} %constant.47.clone.1.expert_ref, ...), custom_call_target="tpu_custom_call" | custom-call | flops 1342177280 | bytes 2490368 | tf_op jit(solution)/shard_map/feed_dense/pallas_call | solution.py:481
  151.7 7.6 %fusion.23 = f32[1024,1024]{1,0:T(8,128)} fusion(bf16[1280,1024]{1,0:T(8,128)(2,1)} %bitcast.208, bf16[640,1024]{1,0:T(8,128)(2,1)} %collective-permute-done.10.side_ref, bf16[640,1024]{1,0:T(8,128)(2,1)} %copy-done.8), kind=kOutput, calls=%fused_computation.39 | convolution fusion | flops 2689597440 | bytes 9437184 | tf_op jit(solution)/shard_map/gd,gf->df/dot_general | solution.py:691
  163.8 6.5 %all-to-all-done.1 = bf16[8,112,1024]{2,1,0:T(8,128)(2,1)} async-done(((bf16[8,112,1024]{2,1,0:T(8,128)(2,1)}), bf16[8,112,1024]{2,1,0:T(8,128)(2,1)}, u32[]{:S(2)}, u32[]{:S(2)}) %all-to-all-start.1) | async-done | bytes 1835040 | tf_op jit(solution)/shard_map/all_to_all | solution.py:573
  176.3 20.2 %feed_dense.3 = (bf16[640,1024]{1,0:T(8,128)(2,1)}, bf16[640,1024]{1,0:T(8,128)(2,1)}, bf16[640,1024]{1,0:T(8,128)(2,1)}, bf16[640,1024]{1,0:T(8,128)(2,1)}, bf1...) custom-call(s32[1]{0:T(128)} %constant.47.clone.1.expert_ref, ...), custom_call_target="tpu_custom_call" | custom-call | flops 1342177280 | bytes 2490368 | tf_op jit(solution)/shard_map/feed_dense/pallas_call | solution.py:481
  203.9 9.1 %collective-permute-done.13.own_ref = bf16[896,1024]{1,0:T(8,128)(2,1)} collective-permute-done((bf16[896,1024]{1,0:T(8,128)(2,1)}, bf16[896,1024]{1,0:T(8,128)(2,1)}, u32[]{:S(2)}, u32[]{:S(2)}) %collective-permute-start.13) | collective-permute-done | bytes 1835040 | tf_op jit(solution)/shard_map/ppermute | solution.py:556
  229.7 33.1 %feed_routed.2 = (bf16[896,1024]{1,0:T(8,128)(2,1)}, bf16[896,1024]{1,0:T(8,128)(2,1)}, bf16[896,1024]{1,0:T(8,128)(2,1)}, bf16[896,1024]{1,0:T(8,128)(2,1)}, bf...) custom-call(s32[1]{0:T(128)} %bitcast.20.expert_ref, ...), custom_call_target="tpu_custom_call" | custom-call | flops 1879048192 | bytes 3276800 | tf_op jit(solution)/shard_map/feed_routed/pallas_call | solution.py:481
  263.4 4.7 collective-permute-done.18
  273.4 33.1 %feed_routed.3 = (bf16[896,1024]{1,0:T(8,128)(2,1)}, bf16[896,1024]{1,0:T(8,128)(2,1)}, bf16[896,1024]{1,0:T(8,128)(2,1)}, bf16[896,1024]{1,0:T(8,128)(2,1)}, bf...) custom-call(s32[1]{0:T(128)} %bitcast.20.expert_ref, ...), custom_call_target="tpu_custom_call" | custom-call | flops 1879048192 | bytes 3276800 | tf_op jit(solution)/shard_map/feed_routed/pallas_call | solution.py:481
  319.7 4.8 all-to-all-start.3
  340.9 5.6 add_bitcast_fusion
  346.5 7.6 %fusion.5 = f32[1024,1024]{1,0:T(8,128)} fusion(bf16[1792,1024]{1,0:T(8,128)(2,1)S(1)} %bitcast.204, bf16[896,1024]{1,0:T(8,128)(2,1)} %collective-permute-done.15.side_ref, bf16[896,1024]{1,0:T(8,128)(2,1)} %collective-permute-done.13.own_ref), kind=kOutput, calls=%fused_computation.13 | convolution fusion | flops 3765436416 | bytes 11534336 | tf_op jit(solution)/shard_map/gd,gf->df/dot_general | solution.py:691
  354.1 13.6 %all-to-all-done.3 = bf16[8,112,1024]{2,1,0:T(8,128)(2,1)} async-done(((bf16[8,112,1024]{2,1,0:T(8,128)(2,1)}), bf16[8,112,1024]{2,1,0:T(8,128)(2,1)}, u32[]{:S(2)}, u32[]{:S(2)}) %all-to-all-start.3) | async-done | bytes 1835040 | tf_op jit(solution)/shard_map/all_to_all | solution.py:573
  367.7 6.2 %multiply_reduce_fusion = (f32[1024]{0:T(1024)S(1)}, f32[640]{0:T(1024)S(1)}, f32[640]{0:T(1024)S(1)}, f32[640,1024]{1,0:T(8,128)S(1)}) fusion(f32[640,1024]{1,0:T(8,128)} %copy-done.1, f32[640]{0:T(1024)S(1)} %add_rsqrt_fusion, f32[640]{0:T(1024)S(1)} %broadcast_multiply_fusion.4, f32[1024]{0:T(1024)S(1)} %copy-done.26, bf16[896,1024]{1,0:T(8,128)(2,1)} %bitcast.34, ...), kind=kOutput, calls=%fused_computation.58 | convolution fusion | flops 1184151296 | bytes 11031040 | tf_op jit(solution)/shard_map/dot_general | solution.py:751
  383.8 4.6 all-to-all-start.4
  388.4 10.4 %add_bitcast_fusion.1 = f32[1,1024,1024]{2,1,0:T(8,128)} fusion(f32[1024,1024]{1,0:T(8,128)} %fusion.5, bf16[1792,1024]{1,0:T(8,128)(2,1)} %bitcast.203, bf16[896,1024]{1,0:T(8,128)(2,1)} %collective-permute-done.20.side_ref, bf16[896,1024]{1,0:T(8,128)(2,1)} %bitcast.19.own_ref), kind=kOutput, calls=%fused_computation.4 | convolution fusion | flops 3766484992 | bytes 15728640 | tf_op jit(solution)/shard_map/gd,gf->df/dot_general | solution.py:691
  415.6 40.6 %tree_attention_back.1 = (bf16[3,2,640,256]{3,2,1,0:T(8,128)(2,1)}, bf16[3,2,640,256]{3,2,1,0:T(8,128)(2,1)}) custom-call(s32[9]{0:T(128)} %pad_add_fusion.leaves_ref, bf16[3,2,640,256]{3,2,1,0:T(8,128)(2,1)} %bitcast.210, bf16[3,2,640,256]{3,2,1,0:T(8,128)(2,1)} %bitcast.212, bf16[2,640,256]{2,1,0:T(8,128)(2,1)} %pad_maximum_fusion.5.near_grads_ref, ...), custom_call_target="tpu_custom_call" | custom-call | flops 4966051840 | bytes 2097152 | tf_op jit(solution)/shard_map/tree_attention_back/pallas_call | solution.py:336
  485.3 4.9 fusion.17
  532.3 19.3 %collective-permute-done.36 = bf16[640,1024]{1,0:T(8,128)(2,1)} collective-permute-done((bf16[640,1024]{1,0:T(8,128)(2,1)}, bf16[640,1024]{1,0:T(8,128)(2,1)}, u32[]{:S(2)}, u32[]{:S(2)}) %collective-permute-start.36) | collective-permute-done | bytes 1310752 | tf_op jit(solution)/shard_map/ppermute | solution.py:556
  (284 shorter events, 223.2 us)
Async XLA Ops:
  12.7 32.3 %collective-permute-start = (bf16[640,1024]{1,0:T(8,128)(2,1)}, bf16[640,1024]{1,0:T(8,128)(2,1)}, u32[]{:S(2)}, u32[]{:S(2)}) collective-permute-start(bf16[640,1024]{1,0:T(8,128)(2,1)} %fusion.15), channel_id=1, source_target_pairs={{0,2},{1,3},{2,0},{3,1},{4,6},{5,7},{6,4},{7,5},{8,10},{9,11},{10,... | collective-permute-start | bytes 3932168 | tf_op jit(solution)/shard_map/ppermute | solution.py:556
  20.1 58.9 %all-to-all-start = ((bf16[8,112,1024]{2,1,0:T(8,128)(2,1)}), bf16[8,112,1024]{2,1,0:T(8,128)(2,1)}, u32[]{:S(2)}, u32[]{:S(2)}) async-start(bf16[8,112,1024]{2,1,0:T(8,128)(2,1)} %bitcast.191), calls=%async_computation | async-start | bytes 3670016 | tf_op jit(solution)/shard_map/all_to_all | solution.py:573
  45.0 34.0 %collective-permute-start.5 = (bf16[640,1024]{1,0:T(8,128)(2,1)}, bf16[640,1024]{1,0:T(8,128)(2,1)}, u32[]{:S(2)}, u32[]{:S(2)}) collective-permute-start(bf16[640,1024]{1,0:T(8,128)(2,1)} %own_grads_ref.1), channel_id=1, source_target_pairs={{0,1},{1,0},{2,3},{3,2},{4,5},{5,4},{6,7},{7,6},{8,9},{9,8},{10,11... | collective-permute-start | bytes 3932168 | tf_op jit(solution)/shard_map/ppermute | solution.py:552
  45.8 33.3 %collective-permute-start.4 = (bf16[640,1024]{1,0:T(8,128)(2,1)}, bf16[640,1024]{1,0:T(8,128)(2,1)}, u32[]{:S(2)}, u32[]{:S(2)}) collective-permute-start(bf16[640,1024]{1,0:T(8,128)(2,1)} %own_grads_ref.1), channel_id=1, source_target_pairs={{0,2},{1,3},{2,0},{3,1},{4,6},{5,7},{6,4},{7,5},{8,10},{9,11},{10,... | collective-permute-start | bytes 3932168 | tf_op jit(solution)/shard_map/ppermute | solution.py:556
  85.6 31.2 %collective-permute-start.7 = (bf16[640,1024]{1,0:T(8,128)(2,1)S(1)}, bf16[640,1024]{1,0:T(8,128)(2,1)S(1)}, u32[]{:S(2)}, u32[]{:S(2)}) collective-permute-start(bf16[640,1024]{1,0:T(8,128)(2,1)S(1)} %add_convert_fusion.8), channel_id=1, source_target_pairs={{0,2},{1,3},{2,0},{3,1},{4,6},{5,7},{6,4},{7,5},{8,10},{9,11},{10,... | collective-permute-start | bytes 3932168 | tf_op jit(solution)/shard_map/ppermute | solution.py:556
  88.2 28.6 %collective-permute-start.3 = (bf16[640,1024]{1,0:T(8,128)(2,1)S(1)}, bf16[640,1024]{1,0:T(8,128)(2,1)S(1)}, u32[]{:S(2)}, u32[]{:S(2)}) collective-permute-start(bf16[640,1024]{1,0:T(8,128)(2,1)S(1)} %convolution_convert_fusion.3), channel_id=1, source_target_pairs={{0,1},{1,0},{2,3},{3,2},{4,5},{5,4},{6,7},{7,6},{8,9},{9,8},{10,11... | collective-permute-start | bytes 3932168 | tf_op jit(solution)/shard_map/ppermute | solution.py:552
  121.8 48.5 %all-to-all-start.1 = ((bf16[8,112,1024]{2,1,0:T(8,128)(2,1)}), bf16[8,112,1024]{2,1,0:T(8,128)(2,1)}, u32[]{:S(2)}, u32[]{:S(2)}) async-start(bf16[8,112,1024]{2,1,0:T(8,128)(2,1)} %bitcast.192), calls=%async_computation.1 | async-start | bytes 3670016 | tf_op jit(solution)/shard_map/all_to_all | solution.py:573
  128.2 35.5 %collective-permute-start.11 = (bf16[640,1024]{1,0:T(8,128)(2,1)}, bf16[640,1024]{1,0:T(8,128)(2,1)}, u32[]{:S(2)}, u32[]{:S(2)}) collective-permute-start(bf16[640,1024]{1,0:T(8,128)(2,1)} %copy-done.8), channel_id=1, source_target_pairs={{0,2},{1,3},{2,0},{3,1},{4,6},{5,7},{6,4},{7,5},{8,10},{9,11},{10,... | collective-permute-start | bytes 3932168 | tf_op jit(solution)/shard_map/ppermute | solution.py:556
  170.3 42.7 %collective-permute-start.13 = (bf16[896,1024]{1,0:T(8,128)(2,1)}, bf16[896,1024]{1,0:T(8,128)(2,1)}, u32[]{:S(2)}, u32[]{:S(2)}) collective-permute-start(bf16[896,1024]{1,0:T(8,128)(2,1)} %bitcast.19.own_ref), channel_id=1, source_target_pairs={{0,2},{1,3},{2,0},{3,1},{4,6},{5,7},{6,4},{7,5},{8,10},{9,11},{10,... | collective-permute-start | bytes 5505032 | tf_op jit(solution)/shard_map/ppermute | solution.py:556
  171.9 51.0 %all-to-all-start.2 = ((bf16[8,112,1024]{2,1,0:T(8,128)(2,1)}), bf16[8,112,1024]{2,1,0:T(8,128)(2,1)}, u32[]{:S(2)}, u32[]{:S(2)}) async-start(bf16[8,112,1024]{2,1,0:T(8,128)(2,1)} %bitcast.190), calls=%async_computation.2 | async-start | bytes 3670016 | tf_op jit(solution)/shard_map/all_to_all | solution.py:573
  176.2 133.9 %reduce-scatter.2.cloned.1.call-start = ((), (), s32[]{:S(2)}) async-start(), calls=%async_computation.8 | async-start | bytes 4718592 | tf_op jit(solution)/shard_map/reduce_scatter | solution.py:578
  223.5 39.4 %collective-permute-start.17 = (bf16[640,1024]{1,0:T(8,128)(2,1)}, bf16[640,1024]{1,0:T(8,128)(2,1)}, u32[]{:S(2)}, u32[]{:S(2)}) collective-permute-start(bf16[640,1024]{1,0:T(8,128)(2,1)} %add_convert_fusion.7), channel_id=1, source_target_pairs={{0,2},{1,3},{2,0},{3,1},{4,6},{5,7},{6,4},{7,5},{8,10},{9,11},{10,... | collective-permute-start | bytes 3932168 | tf_op jit(solution)/shard_map/ppermute | solution.py:556
  271.7 42.4 %collective-permute-start.22 = (bf16[896,1024]{1,0:T(8,128)(2,1)}, bf16[896,1024]{1,0:T(8,128)(2,1)}, u32[]{:S(2)}, u32[]{:S(2)}) collective-permute-start(bf16[896,1024]{1,0:T(8,128)(2,1)} %add_convert_fusion.4), channel_id=1, source_target_pairs={{0,2},{1,3},{2,0},{3,1},{4,6},{5,7},{6,4},{7,5},{8,10},{9,11},{10,... | collective-permute-start | bytes 5505032 | tf_op jit(solution)/shard_map/ppermute | solution.py:556
  319.3 34.7 %collective-permute-start.19 = (bf16[640,1024]{1,0:T(8,128)(2,1)}, bf16[640,1024]{1,0:T(8,128)(2,1)}, u32[]{:S(2)}, u32[]{:S(2)}) collective-permute-start(bf16[640,1024]{1,0:T(8,128)(2,1)} %get-tuple-element.170), channel_id=1, source_target_pairs={{0,1},{1,0},{2,3},{3,2},{4,5},{5,4},{6,7},{7,6},{8,9},{9,8},{10,11... | collective-permute-start | bytes 3932168 | tf_op jit(solution)/shard_map/ppermute | solution.py:552
  319.7 47.9 %all-to-all-start.3 = ((bf16[8,112,1024]{2,1,0:T(8,128)(2,1)}), bf16[8,112,1024]{2,1,0:T(8,128)(2,1)}, u32[]{:S(2)}, u32[]{:S(2)}) async-start(bf16[8,112,1024]{2,1,0:T(8,128)(2,1)} %bitcast.186), calls=%async_computation.4 | async-start | bytes 3670016 | tf_op jit(solution)/shard_map/all_to_all | solution.py:573
  324.5 54.7 %collective-permute-start.26 = (bf16[896,1024]{1,0:T(8,128)(2,1)}, bf16[896,1024]{1,0:T(8,128)(2,1)}, u32[]{:S(2)}, u32[]{:S(2)}) collective-permute-start(bf16[896,1024]{1,0:T(8,128)(2,1)} %get-tuple-element.200), channel_id=1, source_target_pairs={{0,1},{1,0},{2,3},{3,2},{4,5},{5,4},{6,7},{7,6},{8,9},{9,8},{10,11... | collective-permute-start | bytes 5505032 | tf_op jit(solution)/shard_map/ppermute | solution.py:552
  335.3 44.0 %collective-permute-start.27 = (bf16[896,1024]{1,0:T(8,128)(2,1)}, bf16[896,1024]{1,0:T(8,128)(2,1)}, u32[]{:S(2)}, u32[]{:S(2)}) collective-permute-start(bf16[896,1024]{1,0:T(8,128)(2,1)} %add_convert_fusion.2), channel_id=1, source_target_pairs={{0,2},{1,3},{2,0},{3,1},{4,6},{5,7},{6,4},{7,5},{8,10},{9,11},{10,... | collective-permute-start | bytes 5505032 | tf_op jit(solution)/shard_map/ppermute | solution.py:556
  377.7 31.5 %collective-permute-start.23 = (bf16[640,1024]{1,0:T(8,128)(2,1)}, bf16[640,1024]{1,0:T(8,128)(2,1)}, u32[]{:S(2)}, u32[]{:S(2)}) collective-permute-start(bf16[640,1024]{1,0:T(8,128)(2,1)} %get-tuple-element.306), channel_id=1, source_target_pairs={{0,2},{1,3},{2,0},{3,1},{4,6},{5,7},{6,4},{7,5},{8,10},{9,11},{10,... | collective-permute-start | bytes 3932168 | tf_op jit(solution)/shard_map/ppermute | solution.py:556
  383.8 72.4 %all-to-all-start.4 = ((bf16[8,112,1024]{2,1,0:T(8,128)(2,1)}), bf16[8,112,1024]{2,1,0:T(8,128)(2,1)}, u32[]{:S(2)}, u32[]{:S(2)}) async-start(bf16[8,112,1024]{2,1,0:T(8,128)(2,1)} %bitcast.185), calls=%async_computation.5 | async-start | bytes 3670016 | tf_op jit(solution)/shard_map/all_to_all | solution.py:573
  409.2 47.0 %collective-permute-start.31 = (bf16[640,1024]{1,0:T(8,128)(2,1)}, bf16[640,1024]{1,0:T(8,128)(2,1)}, u32[]{:S(2)}, u32[]{:S(2)}) collective-permute-start(bf16[640,1024]{1,0:T(8,128)(2,1)} %add_convert_fusion.6), channel_id=1, source_target_pairs={{0,2},{1,3},{2,0},{3,1},{4,6},{5,7},{6,4},{7,5},{8,10},{9,11},{10,... | collective-permute-start | bytes 3932168 | tf_op jit(solution)/shard_map/ppermute | solution.py:556
  478.3 35.0 %all-to-all-start.6 = ((bf16[8,128,384]{2,1,0:T(8,128)(2,1)}), bf16[8,128,384]{2,1,0:T(8,128)(2,1)}, u32[]{:S(2)}, u32[]{:S(2)}) async-start(bf16[8,128,384]{2,1,0:T(8,128)(2,1)} %bitcast.189), calls=%async_computation.7 | async-start | bytes 1572864 | tf_op jit(solution)/shard_map/all_to_all | solution.py:573
  513.3 46.4 %all-to-all-start.5 = ((bf16[8,128,768]{1,2,0:T(8,128)(2,1)}), bf16[8,128,768]{1,2,0:T(8,128)(2,1)}, u32[]{:S(2)}, u32[]{:S(2)}) async-start(bf16[8,128,768]{1,2,0:T(8,128)(2,1)} %copy_bitcast_fusion), calls=%async_computation.6 | async-start | bytes 3145728 | tf_op jit(solution)/shard_map/all_to_all | solution.py:573
  520.8 30.8 %collective-permute-start.36 = (bf16[640,1024]{1,0:T(8,128)(2,1)}, bf16[640,1024]{1,0:T(8,128)(2,1)}, u32[]{:S(2)}, u32[]{:S(2)}) collective-permute-start(bf16[640,1024]{1,0:T(8,128)(2,1)} %fusion.31), channel_id=1, source_target_pairs={{0,2},{1,3},{2,0},{3,1},{4,6},{5,7},{6,4},{7,5},{8,10},{9,11},{10,... | collective-permute-start | bytes 3932168 | tf_op jit(solution)/shard_map/ppermute | solution.py:556
  532.3 23.1 %collective-permute-start.40 = (f32[1,1024]{1,0:T(1,128)S(1)}, f32[1,1024]{1,0:T(1,128)S(1)}, u32[]{:S(2)}, u32[]{:S(2)}) collective-permute-start(f32[1,1024]{1,0:T(1,128)S(1)} %add.226), channel_id=1, source_target_pairs={{0,1},{1,0},{2,3},{3,2},{4,5},{5,4},{6,7},{7,6},{8,9},{9,8},{10,11... | collective-permute-start | bytes 12296 | tf_op jit(solution)/shard_map/ppermute | solution.py:567
  (69 other events, 491.8 us)
Sparse Core Ops, SparseCore 0:
  223.0 87.0 reduce-scatter.1

commit v9 on v8

--- a/solution.py
+++ b/solution.py
@@ -15,6 +15,8 @@
 TREE_LEN = 2560
 BRANCHES = 4
 FAMILY = 3 * SEG
+TEAM = 2 * FAMILY
+TEAMS = BRANCHES // 2
 QROWS = 256
 COVER = 8
 PAIR = 2 * HEAD_DIM
@@ -73,13 +75,19 @@
     return groups + [(first, QROWS, 0, QROWS, "causal")]
 
 
-def family_groups(starts):
-    return [
-        (0, TRUNK, 0, FAMILY, None),
-        (starts[0], SEG, 0, FAMILY, "branch"),
-        (starts[1], SEG, SEG, 2 * SEG, "causal"),
-        (starts[2], SEG, 2 * SEG, FAMILY, "causal"),
-    ]
+def team_rows(leaves_ref, team):
+    return family_rows(leaves_ref, 2 * team) + family_rows(leaves_ref, 2 * team + 1)
+
+
+def team_groups(starts):
+    groups = [(0, TRUNK, 0, TEAM, None)]
+    for first in range(0, TEAM, FAMILY):
+        at = first // SEG
+        groups.append((starts[at], SEG, first, first + FAMILY, "branch"))
+        for leaf in (1, 2):
+            begin = first + leaf * SEG
+            groups.append((starts[at + leaf], SEG, begin, begin + SEG, "causal"))
+    return groups
 
 
 def masked_scores(keys, queries, rule):
@@ -154,16 +162,16 @@
         out_ref[pl.ds(first, QROWS), :] = out
         trunk_log_ref[0, :, pl.ds(first, QROWS)] = logs
 
-    def one_family(branch, carry):
-        starts = family_rows(leaves_ref, branch)
+    def one_team(team, carry):
+        starts = team_rows(leaves_ref, team)
         queries = scaled_queries(qkv_ref, starts, SEG)
-        out, logs = forward_block(qkv_ref, values_t_ref, queries, family_groups(starts))
+        out, logs = forward_block(qkv_ref, values_t_ref, queries, team_groups(starts))
         for place, start in enumerate(starts):
             out_ref[pl.ds(start, SEG), :] = out[place * SEG : (place + 1) * SEG]
-        family_log_ref[0, branch] = logs
+        family_log_ref[0, team] = logs
         return carry
 
-    lax.fori_loop(0, BRANCHES, one_family, 0)
+    lax.fori_loop(0, TEAMS, one_team, 0)
     for offset in range(4):
         half_ref = near_out_ref if offset < 2 else far_out_ref
         half_ref[offset % 2] = out_ref[quarter_rows(leaves_ref, offset), :]
@@ -199,7 +207,7 @@
                 halves_spec(1),
                 halves_spec(1),
                 pl.BlockSpec((1, 2, TRUNK), lambda p, leaves: (p, 0, 0)),
-                pl.BlockSpec((1, BRANCHES, 2, FAMILY), lambda p, leaves: (p, 0, 0, 0)),
+                pl.BlockSpec((1, TEAMS, 2, TEAM), lambda p, leaves: (p, 0, 0, 0)),
             ],
             scratch_shapes=[
                 pltpu.VMEM((3, TREE_LEN, PAIR), BF16),
@@ -211,7 +219,7 @@
             jax.ShapeDtypeStruct((2, quarter, width), BF16),
             jax.ShapeDtypeStruct((2, quarter, width), BF16),
             jax.ShapeDtypeStruct((pairs, 2, TRUNK), F32),
-            jax.ShapeDtypeStruct((pairs, BRANCHES, 2, FAMILY), F32),
+            jax.ShapeDtypeStruct((pairs, TEAMS, 2, TEAM), F32),
         ],
         cost_estimate=attention_cost(2, COVER),
         name="tree_attention",
@@ -302,16 +310,16 @@
             trunk_keys_ref[pl.ds(start, size), :] += key_grad
             trunk_values_ref[pl.ds(start, size), :] += value_grad
 
-    def one_family(branch, carry):
-        starts = family_rows(leaves_ref, branch)
-        groups = family_groups(starts)
+    def one_team(team, carry):
+        starts = team_rows(leaves_ref, team)
+        groups = team_groups(starts)
         grad_query, key_grads, value_grads = backward_block(
             qkv_ref,
             keys_t_ref,
             scaled_queries(qkv_ref, starts, SEG),
             jnp.concatenate([grads_ref[pl.ds(start, SEG), :] for start in starts], axis=0),
             jnp.concatenate([outs_ref[pl.ds(start, SEG), :] for start in starts], axis=0),
-            family_log_ref[0, branch],
+            family_log_ref[0, team],
             groups,
         )
         trunk_keys_ref[...] += key_grads[0]
@@ -323,32 +331,38 @@
             result_ref[2, rows, :] = value_grads[1 + place].astype(BF16)
         return carry
 
-    lax.fori_loop(0, BRANCHES, one_family, 0)
+    lax.fori_loop(0, TEAMS, one_team, 0)
     result_ref[1, pl.ds(0, TRUNK), :] = trunk_keys_ref[...].astype(BF16)
     result_ref[2, pl.ds(0, TRUNK), :] = trunk_values_ref[...].astype(BF16)
     for offset in range(4):
         half_ref = near_result_ref if offset < 2 else far_result_ref
-        half_ref[:, offset % 2] = result_ref[:, quarter_rows(leaves_ref, offset), :]
-
-
-def attention_backward(leaves, near, far, near_grads, far_grads, near_outs, far_outs, logs):
-    pairs = near.shape[3] // PAIR
+        rows = quarter_rows(leaves_ref, offset)
+        for part in range(3):
+            half_ref[offset % 2, :, part * PAIR : (part + 1) * PAIR] = result_ref[part, rows, :]
+
+
+def attention_backward(leaves, pair, near, far, near_grads, far_grads, near_outs, far_outs, logs):
+    quarter = TREE_LEN // 4
+    rows = pl.BlockSpec((2, quarter, PAIR), lambda i, leaves: (0, 0, pair))
+    parts = pl.BlockSpec((3, 2, quarter, PAIR), lambda i, leaves: (0, 0, 0, pair))
+    result = pl.BlockSpec((2, quarter, 3 * PAIR), lambda i, leaves: (0, 0, 0))
+    shape = jax.ShapeDtypeStruct((2, quarter, 3 * PAIR), BF16)
     return pl.pallas_call(
         backward_kernel,
         grid_spec=pltpu.PrefetchScalarGridSpec(
             num_scalar_prefetch=1,
-            grid=(pairs,),
+            grid=(1,),
             in_specs=[
-                halves_spec(3),
-                halves_spec(3),
-                halves_spec(1),
-                halves_spec(1),
-                halves_spec(1),
-                halves_spec(1),
-                pl.BlockSpec((1, 2, TRUNK), lambda p, leaves: (p, 0, 0)),
-                pl.BlockSpec((1, BRANCHES, 2, FAMILY), lambda p, leaves: (p, 0, 0, 0)),
+                parts,
+                parts,
+                rows,
+                rows,
+                rows,
+                rows,
+                pl.BlockSpec((1, 2, TRUNK), lambda i, leaves: (pair, 0, 0)),
+                pl.BlockSpec((1, TEAMS, 2, TEAM), lambda i, leaves: (pair, 0, 0, 0)),
             ],
-            out_specs=[halves_spec(3), halves_spec(3)],
+            out_specs=[result, result],
             scratch_shapes=[
                 pltpu.VMEM((3, TREE_LEN, PAIR), BF16),
                 pltpu.VMEM((TREE_LEN, PAIR), BF16),
@@ -359,8 +373,8 @@
                 pltpu.VMEM((TRUNK, PAIR), F32),
             ],
         ),
-        out_shape=[jax.ShapeDtypeStruct(near.shape, BF16), jax.ShapeDtypeStruct(far.shape, BF16)],
-        cost_estimate=attention_cost(5, 5),
+        out_shape=[shape, shape],
+        cost_estimate=attention_cost(5, 10),
         name="tree_attention_back",
     )(leaves, near, far, near_grads, far_grads, near_outs, far_outs, *logs)
 
@@ -806,53 +820,71 @@
     dense_out_far = from_far(dense_out_far)
     head_grads = near_dense[7] + far_dense[7] + near_expert[7] + far_expert[7]
     small = jnp.concatenate([head_grads[: experts + 2], gain_two[None]], axis=0)
-    near_result, far_result = attention_backward(
-        leaves, near_qkv, far_qkv, near_heads, far_heads, near_out, far_out, logs
-    )
-    near_result, far_result, out_rows, dense_out_far, small = lax.optimization_barrier(
-        (near_result, far_result, out_rows, dense_out_far, small)
-    )
+
+    def pair_back(pair, near_grads, far_grads):
+        return attention_backward(
+            leaves, pair, near_qkv, far_qkv, near_grads, far_grads, near_out, far_out, logs
+        )
+
+    def pair_weights(pair):
+        lanes = slice(pair * PAIR, (pair + 1) * PAIR)
+        return jnp.concatenate([w_qkv[part, :, lanes] for part in range(3)], axis=1)
+
+    def total(values):
+        return functools.reduce(jnp.add, values)
+
+    pairs = heads_width // PAIR
+    near_results, far_results = [None] * pairs, [None] * pairs
+    near_results[0], far_results[0] = pair_back(0, near_heads, far_heads)
+    far_branch = jnp.concatenate([grad_branch_far, grad_branch_corner], axis=0)
+    grad_w_out = grad_w_out + product(far_branch, far_out.reshape(flat))
     small = sum_over(small, "tensor")
-
-    def normed_part(grads):
-        return jnp.einsum("sgc,sdc->gd", grads, w_qkv, preferred_element_type=F32)
-
-    corner_part = normed_part(far_result[:, 1]).astype(BF16)
-    from_corner = from_side(corner_part).astype(F32)
-
-    far_branch = jnp.concatenate([grad_branch_far, grad_branch_corner], axis=0)
-    grad_w_out = grad_w_out + product(after(far_branch, corner_part), far_out.reshape(flat))
     small_columns = -(-small.shape[0] // LANES) * LANES
     small_block = jnp.pad(small, ((0, small_columns - small.shape[0]), (0, 0))).T
     branch_grads = jnp.concatenate([grad_w_out.astype(BF16), small_block.astype(BF16)], axis=1)
-    far_result, branch_grads = lax.optimization_barrier((far_result, branch_grads))
-    branch_grads = strips_total(strips_sent(branch_grads))
-    far_sum = (normed_part(far_result[:, 0]) + from_corner).astype(BF16)
-    near_result, far_result, out_rows, far_sum = lax.optimization_barrier(
-        (near_result, far_result, out_rows, far_sum)
-    )
-    near_sum = plus_side(normed_part(near_result[:, 0]), normed_part(near_result[:, 1]))
+    near_results[0], far_results[0], out_rows, dense_out_far, branch_grads, near_heads = (
+        lax.optimization_barrier(
+            (near_results[0], far_results[0], out_rows, dense_out_far, branch_grads, near_heads)
+        )
+    )
+    branch_grads = strips_sent(branch_grads)
+    for pair in range(1, pairs):
+        near_results[pair], far_results[pair] = pair_back(pair, near_heads, far_heads)
+    near_results, far_results, branch_grads = lax.optimization_barrier(
+        (near_results, far_results, branch_grads)
+    )
+
+    def normed_part(results, quarter):
+        return total([dot_nt(results[pair][quarter], pair_weights(pair)) for pair in range(pairs)])
+
+    def qkv_strips(pair, *others):
+        near_rows = near_results[pair].reshape(2 * tok_dev, 3 * PAIR)
+        far_rows = far_results[pair].reshape(2 * tok_dev, 3 * PAIR)
+        near_rows = after(near_rows, *others)
+        return strips_sent(weight_grads(near_one, far_one, near_rows, far_rows).astype(BF16))
+
+    corner_part = normed_part(far_results, 1).astype(BF16)
+    from_corner = from_side(corner_part).astype(F32)
+    qkv_grads = [qkv_strips(0, corner_part)]
+    far_sum = (normed_part(far_results, 0) + from_corner).astype(BF16)
+    near_results, far_results, out_rows, far_sum = lax.optimization_barrier(
+        (near_results, far_results, out_rows, far_sum)
+    )
+    near_sum = plus_side(normed_part(near_results, 0), normed_part(near_results, 1))
     out = (residual + dense_out + dense_out_far.astype(F32) + picked(out_rows)).astype(BF16)
 
-    near_result = near_result.reshape(3, *flat)
-    far_result = far_result.reshape(3, *flat)
     scaled_far = normed_far.astype(F32) / ln_attn
     gain_one = jnp.sum(
         near_sum * scaled_one + far_sum.astype(F32) * scaled_far, axis=0, keepdims=True
     )
     gain_one = sum_over(gain_one, "expert")
-    near_result = after(near_result, gain_one)
-    qkv_grads = strips_total(strips_sent(
-        jnp.concatenate(
-            [
-                weight_grads(near_one, far_one, near_result[part], far_result[part]).astype(BF16)
-                for part in range(3)
-            ],
-            axis=1,
-        )
-    ))
+    qkv_grads += [qkv_strips(pair, gain_one) for pair in range(1, pairs)]
     grad_normed_one = near_sum + after(from_far(far_sum), gain_one).astype(F32)
     grad_ln_attn = sum_over(gain_one, "tensor")[0]
+    branch_grads = strips_total(branch_grads)
+    qkv_grads = jnp.stack(
+        [strips_total(grads).reshape(-1, 3, PAIR) for grads in qkv_grads], axis=2
+    )
     grad_tokens = grad_residual + norm_back(grad_normed_one, ln_attn, scaled_one, inverse_one)
 
     strip = qkv_grads.shape[0]

time: 574 us -> 578 us (level)
  waiting for transfers between devices: 116 us -> 106 us
  matrix products: 116 us -> 124 us
    ppermute x11, waiting for transfers between devices: 70.3 us -> 54.4 us  [from_far(): return lax.ppermute(values, 'tensor', [(i, i ^ 2) for i in range(4)])]
    all_to_all x7 -> x8, waiting for transfers between devices: 20.1 us -> 27.7 us  [exchange(): lax.all_to_all(blocks, 'expert', split_axis=0, concat_axis=0, tiled=True)]
    all_to_all x7 -> x8, starting transfers between devices: 35.4 us -> 40.8 us  [exchange(): lax.all_to_all(blocks, 'expert', split_axis=0, concat_axis=0, tiled=True)]
    dot_general x4 -> x8, matrix products: 15 us -> 19.8 us  [dot_nt(): lax.dot_general(a, b, (((1,), (1,)), ((), ())), preferred_element_type=F32)]
    pallas_call x1 -> x2, Pallas kernels: 40.6 us -> 44.4 us  [attention_backward(): pl.pallas_call(backward_kernel, grid_spec=pltpu.PrefetchScalarGridSpec(nu...]
    dot_general x16 -> x14, matrix products: 60.5 us -> 62.9 us  [product(): return jnp.einsum('gd,gf->df', left, right, preferred_element_type=F32)]
  transfers between devices with their start and end apart: 50 -> 51, of which waited for: 22 -> 19; matrix products, arithmetic and copies ran while one was open for 29% -> 31% of each run, Pallas kernels for 30% -> 30%
where the time goes in v9:
time: 578 us; the launch traced here: 573 us
  Pallas kernels  173 us (30%)
  matrix products  124 us (21%)
  waiting for transfers between devices  106 us (18%)
  starting transfers between devices  72.6 us (13%)
  other arithmetic  64.1 us (11%)
  local copies, waits for them, and re-layouts  17.8 us (3%)
  between operations  15.5 us (3%)
    pallas_call x4, Pallas kernels, feed(): pl.pallas_call(functools.partial(feed_kernel, experts, routed), grid_spec...  106 us
    dot_general x14, matrix products, product(): return jnp.einsum('gd,gf->df', left, right, preferred_element_type=F32)  62.9 us
    ppermute x11, waiting for transfers between devices, from_far(): return lax.ppermute(values, 'tensor', [(i, i ^ 2) for i in range(4)])  54.4 us
    pallas_call x2, Pallas kernels, attention_backward(): pl.pallas_call(backward_kernel, grid_spec=pltpu.PrefetchScalarGridSpec(nu...  44.4 us
    all_to_all x8, starting transfers between devices, exchange(): lax.all_to_all(blocks, 'expert', split_axis=0, concat_axis=0, tiled=True)  40.8 us
    all_to_all x8, waiting for transfers between devices, exchange(): lax.all_to_all(blocks, 'expert', split_axis=0, concat_axis=0, tiled=True)  27.7 us
    pallas_call x1, Pallas kernels, attention_forward(): pl.pallas_call(forward_kernel, grid_spec=pltpu.PrefetchScalarGridSpec(num...  22.2 us
    dot_general x8, matrix products, dot_nt(): lax.dot_general(a, b, (((1,), (1,)), ((), ())), preferred_element_type=F32)  19.8 us
  transfers between devices with their start and end apart: 51, of which 19 were waited for; matrix products, arithmetic and copies ran while one was open for 31% of the time, Pallas kernels for 30%

profile of v9, /device:TPU:0, one launch (start us, length us, event | category | flops | bytes accessed | tf_op | source)
XLA Modules:
  0.0 572.5 jit_solution(11511944761799260935)
XLA Ops:
  20.1 6.1 %all-to-all-start = ((bf16[8,112,1024]{2,1,0:T(8,128)(2,1)}), bf16[8,112,1024]{2,1,0:T(8,128)(2,1)S(1)}, u32[]{:S(2)}, u32[]{:S(2)}) async-start(bf16[8,112,1024]{2,1,0:T(8,128)(2,1)} %bitcast.189), calls=%async_computation | async-start | bytes 3670016 | tf_op jit(solution)/shard_map/all_to_all | solution.py:587
  27.6 5.8 %convolution_convert_fusion.1 = bf16[1280,3,256]{2,0,1:T(8,128)(2,1)} fusion(bf16[3,1024,256]{2,1,0:T(8,128)(2,1)} %param.19, bf16[640,1024]{1,0:T(8,128)(2,1)} %collective-permute-done.1, bf16[640,1024]{1,0:T(8,128)(2,1)} %fusion.15), kind=kOutput, calls=%fused_computation.22 | convolution fusion | flops 2019491840 | bytes 6160384 | tf_op jit(solution)/shard_map/td,sdc->stc/dot_general | solution.py:662
  33.4 11.6 %collective-permute-done = bf16[640,1024]{1,0:T(8,128)(2,1)} collective-permute-done((bf16[640,1024]{1,0:T(8,128)(2,1)}, bf16[640,1024]{1,0:T(8,128)(2,1)}, u32[]{:S(2)}, u32[]{:S(2)}) %collective-permute-start) | collective-permute-done | bytes 1310752 | tf_op jit(solution)/shard_map/ppermute | solution.py:570
  53.7 22.2 %tree_attention.1 = (bf16[2,640,256]{2,1,0:T(8,128)(2,1)}, bf16[2,640,256]{2,1,0:T(8,128)(2,1)}, f32[2,2,1024]{2,1,0:T(2,128)}, f32[2,2,2,768]{3,2,1,0:T(2,128)}) custom-call(s32[9]{0:T(128)} %pad_add_fusion.leaves_ref, bf16[3,2,640,256]{3,2,1,0:T(8,128)(2,1)} %bitcast.210, bf16[3,2,640,256]{3,2,1,0:T(8,128)(2,1)} %bitcast.213), custom_call_target="tpu_custom_call" | custom-call | flops 1241513984 | bytes 1310720 | tf_op jit(solution)/shard_map/tree_attention/pallas_call | solution.py:200
  91.5 23.7 %collective-permute-done.7 = bf16[640,1024]{1,0:T(8,128)(2,1)S(1)} collective-permute-done((bf16[640,1024]{1,0:T(8,128)(2,1)S(1)}, bf16[640,1024]{1,0:T(8,128)(2,1)S(1)}, u32[]{:S(2)}, u32[]{:S(2)}) %collective-permute-start.7) | collective-permute-done | bytes 1310752 | tf_op jit(solution)/shard_map/ppermute | solution.py:570
  119.9 6.0 %all-to-all-start.1 = ((bf16[8,112,1024]{2,1,0:T(8,128)(2,1)}), bf16[8,112,1024]{2,1,0:T(8,128)(2,1)}, u32[]{:S(2)}, u32[]{:S(2)}) async-start(bf16[8,112,1024]{2,1,0:T(8,128)(2,1)} %bitcast.190), calls=%async_computation.1 | async-start | bytes 3670016 | tf_op jit(solution)/shard_map/all_to_all | solution.py:587
  129.3 20.1 %feed_dense.2 = (bf16[640,1024]{1,0:T(8,128)(2,1)}, bf16[640,1024]{1,0:T(8,128)(2,1)}, bf16[640,1024]{1,0:T(8,128)(2,1)}, bf16[640,1024]{1,0:T(8,128)(2,1)}, bf1...) custom-call(s32[1]{0:T(128)} %constant.47.clone.1.expert_ref, ...), custom_call_target="tpu_custom_call" | custom-call | flops 1342177280 | bytes 2490368 | tf_op jit(solution)/shard_map/feed_dense/pallas_call | solution.py:495
  149.3 7.6 %fusion.23 = f32[1024,1024]{1,0:T(8,128)} fusion(bf16[1280,1024]{1,0:T(8,128)(2,1)} %bitcast.209, bf16[640,1024]{1,0:T(8,128)(2,1)} %collective-permute-done.10.side_ref, bf16[640,1024]{1,0:T(8,128)(2,1)} %copy-done.11), kind=kOutput, calls=%fused_computation.38 | convolution fusion | flops 2689597440 | bytes 9437184 | tf_op jit(solution)/shard_map/gd,gf->df/dot_general | solution.py:705
  161.4 6.7 %all-to-all-done.1 = bf16[8,112,1024]{2,1,0:T(8,128)(2,1)} async-done(((bf16[8,112,1024]{2,1,0:T(8,128)(2,1)}), bf16[8,112,1024]{2,1,0:T(8,128)(2,1)}, u32[]{:S(2)}, u32[]{:S(2)}) %all-to-all-start.1) | async-done | bytes 1835040 | tf_op jit(solution)/shard_map/all_to_all | solution.py:587
  174.0 20.2 %feed_dense.3 = (bf16[640,1024]{1,0:T(8,128)(2,1)}, bf16[640,1024]{1,0:T(8,128)(2,1)}, bf16[640,1024]{1,0:T(8,128)(2,1)}, bf16[640,1024]{1,0:T(8,128)(2,1)}, bf1...) custom-call(s32[1]{0:T(128)} %constant.47.clone.1.expert_ref, ...), custom_call_target="tpu_custom_call" | custom-call | flops 1342177280 | bytes 2490368 | tf_op jit(solution)/shard_map/feed_dense/pallas_call | solution.py:495
  201.6 9.2 %collective-permute-done.13.own_ref = bf16[896,1024]{1,0:T(8,128)(2,1)} collective-permute-done((bf16[896,1024]{1,0:T(8,128)(2,1)}, bf16[896,1024]{1,0:T(8,128)(2,1)}, u32[]{:S(2)}, u32[]{:S(2)}) %collective-permute-start.13) | collective-permute-done | bytes 1835040 | tf_op jit(solution)/shard_map/ppermute | solution.py:570
  227.5 33.1 %feed_routed.2 = (bf16[896,1024]{1,0:T(8,128)(2,1)}, bf16[896,1024]{1,0:T(8,128)(2,1)}, bf16[896,1024]{1,0:T(8,128)(2,1)}, bf16[896,1024]{1,0:T(8,128)(2,1)}, bf...) custom-call(s32[1]{0:T(128)} %bitcast.20.expert_ref, ...), custom_call_target="tpu_custom_call" | custom-call | flops 1879048192 | bytes 3276800 | tf_op jit(solution)/shard_map/feed_routed/pallas_call | solution.py:495
  271.1 33.1 %feed_routed.3 = (bf16[896,1024]{1,0:T(8,128)(2,1)}, bf16[896,1024]{1,0:T(8,128)(2,1)}, bf16[896,1024]{1,0:T(8,128)(2,1)}, bf16[896,1024]{1,0:T(8,128)(2,1)}, bf...) custom-call(s32[1]{0:T(128)} %bitcast.20.expert_ref, ...), custom_call_target="tpu_custom_call" | custom-call | flops 1879048192 | bytes 3276800 | tf_op jit(solution)/shard_map/feed_routed/pallas_call | solution.py:495
  338.5 7.8 %fusion.5 = f32[1024,1024]{1,0:T(8,128)} fusion(bf16[1792,1024]{1,0:T(8,128)(2,1)S(1)} %bitcast.205, bf16[896,1024]{1,0:T(8,128)(2,1)} %collective-permute-done.15.side_ref, bf16[896,1024]{1,0:T(8,128)(2,1)} %collective-permute-done.13.own_ref), kind=kOutput, calls=%fused_computation.13 | convolution fusion | flops 3765436416 | bytes 11534336 | tf_op jit(solution)/shard_map/gd,gf->df/dot_general | solution.py:705
  346.3 5.6 add_bitcast_fusion
  351.9 13.4 %all-to-all-done.3 = bf16[8,112,1024]{2,1,0:T(8,128)(2,1)} async-done(((bf16[8,112,1024]{2,1,0:T(8,128)(2,1)}), bf16[8,112,1024]{2,1,0:T(8,128)(2,1)}, u32[]{:S(2)}, u32[]{:S(2)}) %all-to-all-start.3) | async-done | bytes 1835040 | tf_op jit(solution)/shard_map/all_to_all | solution.py:587
  365.3 5.3 multiply_reduce_fusion
  376.1 7.7 %add_bitcast_fusion.1 = f32[1,1024,1024]{2,1,0:T(8,128)} fusion(f32[1024,1024]{1,0:T(8,128)S(1)} %copy-done.63, bf16[1792,1024]{1,0:T(8,128)(2,1)S(1)} %bitcast.204, bf16[896,1024]{1,0:T(8,128)(2,1)} %collective-permute-done.20.side_ref, bf16[896,1024]{1,0:T(8,128)(2,1)} %bitcast.19.own_ref), kind=kOutput, calls=%fused_computation.4 | convolution fusion | flops 3766484992 | bytes 15728640 | tf_op jit(solution)/shard_map/gd,gf->df/dot_general | solution.py:705
  401.2 4.9 collective-permute-done.23
  425.3 22.2 %tree_attention_back.2 = (bf16[2,640,384]{2,1,0:T(8,128)(2,1)}, bf16[2,640,384]{2,1,0:T(8,128)(2,1)}) custom-call(s32[9]{0:T(128)} %pad_add_fusion.leaves_ref, bf16[3,2,640,256]{3,2,1,0:T(8,128)(2,1)} %bitcast.211, bf16[3,2,640,256]{3,2,1,0:T(8,128)(2,1)} %bitcast.214, bf16[2,640,256]{2,1,0:T(8,128)(2,1)} %pad_maximum_fusion.9.near_grads_ref, ...), custom_call_target="tpu_custom_call" | custom-call | flops 2483025920 | bytes 1048576 | tf_op jit(solution)/shard_map/tree_attention_back/pallas_call | solution.py:350
  454.6 22.2 %tree_attention_back.3 = (bf16[2,640,384]{2,1,0:T(8,128)(2,1)}, bf16[2,640,384]{2,1,0:T(8,128)(2,1)}) custom-call(s32[9]{0:T(128)} %pad_add_fusion.leaves_ref, bf16[3,2,640,256]{3,2,1,0:T(8,128)(2,1)} %bitcast.212, bf16[3,2,640,256]{3,2,1,0:T(8,128)(2,1)} %bitcast.215, bf16[2,640,256]{2,1,0:T(8,128)(2,1)} %pad_maximum_fusion.9.near_grads_ref, ...), custom_call_target="tpu_custom_call" | custom-call | flops 2483025920 | bytes 1048576 | tf_op jit(solution)/shard_map/tree_attention_back/pallas_call | solution.py:350
  507.7 6.3 %all-to-all-start.6 = ((bf16[8,128,384]{2,1,0:T(8,128)(2,1)}), bf16[8,128,384]{2,1,0:T(8,128)(2,1)}, u32[]{:S(2)}, u32[]{:S(2)}) async-start(bf16[8,128,384]{2,1,0:T(8,128)(2,1)} %bitcast.193), calls=%async_computation.7 | async-start | bytes 1572864 | tf_op jit(solution)/shard_map/all_to_all | solution.py:587
  518.5 4.8 fusion.17
  556.6 7.6 %all-to-all-done.7 = bf16[8,128,384]{2,1,0:T(8,128)(2,1)S(1)} async-done(((bf16[8,128,384]{2,1,0:T(8,128)(2,1)}), bf16[8,128,384]{2,1,0:T(8,128)(2,1)S(1)}, u32[]{:S(2)}, u32[]{:S(2)}) %all-to-all-start.7) | async-done | bytes 786464 | tf_op jit(solution)/shard_map/all_to_all | solution.py:587
  (334 shorter events, 243.9 us)
Async XLA Ops:
  12.7 32.3 %collective-permute-start = (bf16[640,1024]{1,0:T(8,128)(2,1)}, bf16[640,1024]{1,0:T(8,128)(2,1)}, u32[]{:S(2)}, u32[]{:S(2)}) collective-permute-start(bf16[640,1024]{1,0:T(8,128)(2,1)} %fusion.15), channel_id=1, source_target_pairs={{0,2},{1,3},{2,0},{3,1},{4,6},{5,7},{6,4},{7,5},{8,10},{9,11},{10,... | collective-permute-start | bytes 3932168 | tf_op jit(solution)/shard_map/ppermute | solution.py:570
  20.1 56.7 %all-to-all-start = ((bf16[8,112,1024]{2,1,0:T(8,128)(2,1)}), bf16[8,112,1024]{2,1,0:T(8,128)(2,1)S(1)}, u32[]{:S(2)}, u32[]{:S(2)}) async-start(bf16[8,112,1024]{2,1,0:T(8,128)(2,1)} %bitcast.189), calls=%async_computation | async-start | bytes 3670016 | tf_op jit(solution)/shard_map/all_to_all | solution.py:587
  45.0 30.9 %collective-permute-start.5 = (bf16[640,1024]{1,0:T(8,128)(2,1)}, bf16[640,1024]{1,0:T(8,128)(2,1)}, u32[]{:S(2)}, u32[]{:S(2)}) collective-permute-start(bf16[640,1024]{1,0:T(8,128)(2,1)} %own_grads_ref.1), channel_id=1, source_target_pairs={{0,1},{1,0},{2,3},{3,2},{4,5},{5,4},{6,7},{7,6},{8,9},{9,8},{10,11... | collective-permute-start | bytes 3932168 | tf_op jit(solution)/shard_map/ppermute | solution.py:566
  45.8 31.1 %collective-permute-start.4 = (bf16[640,1024]{1,0:T(8,128)(2,1)}, bf16[640,1024]{1,0:T(8,128)(2,1)}, u32[]{:S(2)}, u32[]{:S(2)}) collective-permute-start(bf16[640,1024]{1,0:T(8,128)(2,1)} %own_grads_ref.1), channel_id=1, source_target_pairs={{0,2},{1,3},{2,0},{3,1},{4,6},{5,7},{6,4},{7,5},{8,10},{9,11},{10,... | collective-permute-start | bytes 3932168 | tf_op jit(solution)/shard_map/ppermute | solution.py:570
  84.4 30.9 %collective-permute-start.7 = (bf16[640,1024]{1,0:T(8,128)(2,1)S(1)}, bf16[640,1024]{1,0:T(8,128)(2,1)S(1)}, u32[]{:S(2)}, u32[]{:S(2)}) collective-permute-start(bf16[640,1024]{1,0:T(8,128)(2,1)S(1)} %add_convert_fusion.11), channel_id=1, source_target_pairs={{0,2},{1,3},{2,0},{3,1},{4,6},{5,7},{6,4},{7,5},{8,10},{9,11},{10,... | collective-permute-start | bytes 3932168 | tf_op jit(solution)/shard_map/ppermute | solution.py:570
  86.7 28.6 %collective-permute-start.3 = (bf16[640,1024]{1,0:T(8,128)(2,1)S(1)}, bf16[640,1024]{1,0:T(8,128)(2,1)S(1)}, u32[]{:S(2)}, u32[]{:S(2)}) collective-permute-start(bf16[640,1024]{1,0:T(8,128)(2,1)S(1)} %convolution_convert_fusion.3), channel_id=1, source_target_pairs={{0,1},{1,0},{2,3},{3,2},{4,5},{5,4},{6,7},{7,6},{8,9},{9,8},{10,11... | collective-permute-start | bytes 3932168 | tf_op jit(solution)/shard_map/ppermute | solution.py:566
  119.9 48.2 %all-to-all-start.1 = ((bf16[8,112,1024]{2,1,0:T(8,128)(2,1)}), bf16[8,112,1024]{2,1,0:T(8,128)(2,1)}, u32[]{:S(2)}, u32[]{:S(2)}) async-start(bf16[8,112,1024]{2,1,0:T(8,128)(2,1)} %bitcast.190), calls=%async_computation.1 | async-start | bytes 3670016 | tf_op jit(solution)/shard_map/all_to_all | solution.py:587
  125.9 35.5 %collective-permute-start.11 = (bf16[640,1024]{1,0:T(8,128)(2,1)}, bf16[640,1024]{1,0:T(8,128)(2,1)}, u32[]{:S(2)}, u32[]{:S(2)}) collective-permute-start(bf16[640,1024]{1,0:T(8,128)(2,1)} %copy-done.11), channel_id=1, source_target_pairs={{0,2},{1,3},{2,0},{3,1},{4,6},{5,7},{6,4},{7,5},{8,10},{9,11},{10,... | collective-permute-start | bytes 3932168 | tf_op jit(solution)/shard_map/ppermute | solution.py:570
  168.1 42.7 %collective-permute-start.13 = (bf16[896,1024]{1,0:T(8,128)(2,1)}, bf16[896,1024]{1,0:T(8,128)(2,1)}, u32[]{:S(2)}, u32[]{:S(2)}) collective-permute-start(bf16[896,1024]{1,0:T(8,128)(2,1)} %bitcast.19.own_ref), channel_id=1, source_target_pairs={{0,2},{1,3},{2,0},{3,1},{4,6},{5,7},{6,4},{7,5},{8,10},{9,11},{10,... | collective-permute-start | bytes 5505032 | tf_op jit(solution)/shard_map/ppermute | solution.py:570
  169.6 51.0 %all-to-all-start.2 = ((bf16[8,112,1024]{2,1,0:T(8,128)(2,1)}), bf16[8,112,1024]{2,1,0:T(8,128)(2,1)}, u32[]{:S(2)}, u32[]{:S(2)}) async-start(bf16[8,112,1024]{2,1,0:T(8,128)(2,1)} %bitcast.188), calls=%async_computation.2 | async-start | bytes 3670016 | tf_op jit(solution)/shard_map/all_to_all | solution.py:587
  173.9 133.9 %reduce-scatter.2.cloned.1.call-start = ((), (), s32[]{:S(2)}) async-start(), calls=%async_computation.9 | async-start | bytes 4718592 | tf_op jit(solution)/shard_map/reduce_scatter | solution.py:592
  221.2 39.4 %collective-permute-start.17 = (bf16[640,1024]{1,0:T(8,128)(2,1)}, bf16[640,1024]{1,0:T(8,128)(2,1)}, u32[]{:S(2)}, u32[]{:S(2)}) collective-permute-start(bf16[640,1024]{1,0:T(8,128)(2,1)} %add_convert_fusion.10), channel_id=1, source_target_pairs={{0,2},{1,3},{2,0},{3,1},{4,6},{5,7},{6,4},{7,5},{8,10},{9,11},{10,... | collective-permute-start | bytes 3932168 | tf_op jit(solution)/shard_map/ppermute | solution.py:570
  269.4 42.4 %collective-permute-start.22 = (bf16[896,1024]{1,0:T(8,128)(2,1)}, bf16[896,1024]{1,0:T(8,128)(2,1)}, u32[]{:S(2)}, u32[]{:S(2)}) collective-permute-start(bf16[896,1024]{1,0:T(8,128)(2,1)} %add_convert_fusion.4), channel_id=1, source_target_pairs={{0,2},{1,3},{2,0},{3,1},{4,6},{5,7},{6,4},{7,5},{8,10},{9,11},{10,... | collective-permute-start | bytes 5505032 | tf_op jit(solution)/shard_map/ppermute | solution.py:570
  317.0 34.9 %collective-permute-start.19 = (bf16[640,1024]{1,0:T(8,128)(2,1)}, bf16[640,1024]{1,0:T(8,128)(2,1)}, u32[]{:S(2)}, u32[]{:S(2)}) collective-permute-start(bf16[640,1024]{1,0:T(8,128)(2,1)} %get-tuple-element.177), channel_id=1, source_target_pairs={{0,1},{1,0},{2,3},{3,2},{4,5},{5,4},{6,7},{7,6},{8,9},{9,8},{10,11... | collective-permute-start | bytes 3932168 | tf_op jit(solution)/shard_map/ppermute | solution.py:566
  317.4 47.9 %all-to-all-start.3 = ((bf16[8,112,1024]{2,1,0:T(8,128)(2,1)}), bf16[8,112,1024]{2,1,0:T(8,128)(2,1)}, u32[]{:S(2)}, u32[]{:S(2)}) async-start(bf16[8,112,1024]{2,1,0:T(8,128)(2,1)} %bitcast.180), calls=%async_computation.4 | async-start | bytes 3670016 | tf_op jit(solution)/shard_map/all_to_all | solution.py:587
  322.2 63.5 %collective-permute-start.26 = (bf16[896,1024]{1,0:T(8,128)(2,1)}, bf16[896,1024]{1,0:T(8,128)(2,1)}, u32[]{:S(2)}, u32[]{:S(2)}) collective-permute-start(bf16[896,1024]{1,0:T(8,128)(2,1)} %get-tuple-element.207), channel_id=1, source_target_pairs={{0,1},{1,0},{2,3},{3,2},{4,5},{5,4},{6,7},{7,6},{8,9},{9,8},{10,11... | collective-permute-start | bytes 5505032 | tf_op jit(solution)/shard_map/ppermute | solution.py:566
  332.9 52.8 %collective-permute-start.27 = (bf16[896,1024]{1,0:T(8,128)(2,1)}, bf16[896,1024]{1,0:T(8,128)(2,1)}, u32[]{:S(2)}, u32[]{:S(2)}) collective-permute-start(bf16[896,1024]{1,0:T(8,128)(2,1)} %add_convert_fusion.2), channel_id=1, source_target_pairs={{0,2},{1,3},{2,0},{3,1},{4,6},{5,7},{6,4},{7,5},{8,10},{9,11},{10,... | collective-permute-start | bytes 5505032 | tf_op jit(solution)/shard_map/ppermute | solution.py:570
  374.6 31.5 %collective-permute-start.23 = (bf16[640,1024]{1,0:T(8,128)(2,1)}, bf16[640,1024]{1,0:T(8,128)(2,1)}, u32[]{:S(2)}, u32[]{:S(2)}) collective-permute-start(bf16[640,1024]{1,0:T(8,128)(2,1)} %get-tuple-element.331), channel_id=1, source_target_pairs={{0,2},{1,3},{2,0},{3,1},{4,6},{5,7},{6,4},{7,5},{8,10},{9,11},{10,... | collective-permute-start | bytes 3932168 | tf_op jit(solution)/shard_map/ppermute | solution.py:570
  390.3 57.2 %all-to-all-start.4 = ((bf16[8,112,1024]{2,1,0:T(8,128)(2,1)}), bf16[8,112,1024]{2,1,0:T(8,128)(2,1)}, u32[]{:S(2)}, u32[]{:S(2)}) async-start(bf16[8,112,1024]{2,1,0:T(8,128)(2,1)} %bitcast.179), calls=%async_computation.5 | async-start | bytes 3670016 | tf_op jit(solution)/shard_map/all_to_all | solution.py:587
  414.5 33.0 %collective-permute-start.31 = (bf16[640,1024]{1,0:T(8,128)(2,1)}, bf16[640,1024]{1,0:T(8,128)(2,1)}, u32[]{:S(2)}, u32[]{:S(2)}) collective-permute-start(bf16[640,1024]{1,0:T(8,128)(2,1)} %add_convert_fusion.9), channel_id=1, source_target_pairs={{0,2},{1,3},{2,0},{3,1},{4,6},{5,7},{6,4},{7,5},{8,10},{9,11},{10,... | collective-permute-start | bytes 3932168 | tf_op jit(solution)/shard_map/ppermute | solution.py:570
  447.5 29.2 %all-to-all-start.5 = ((bf16[8,128,384]{2,1,0:T(8,128)(2,1)}), bf16[8,128,384]{2,1,0:T(8,128)(2,1)}, u32[]{:S(2)}, u32[]{:S(2)}) async-start(bf16[8,128,384]{2,1,0:T(8,128)(2,1)} %bitcast.185), calls=%async_computation.6 | async-start | bytes 1572864 | tf_op jit(solution)/shard_map/all_to_all | solution.py:587
  494.3 24.1 %collective-permute-start.35 = (bf16[640,1024]{1,0:T(8,128)(2,1)}, bf16[640,1024]{1,0:T(8,128)(2,1)}, u32[]{:S(2)}, u32[]{:S(2)}) collective-permute-start(bf16[640,1024]{1,0:T(8,128)(2,1)} %add_convert_fusion.5), channel_id=1, source_target_pairs={{0,1},{1,0},{2,3},{3,2},{4,5},{5,4},{6,7},{7,6},{8,9},{9,8},{10,11... | collective-permute-start | bytes 3932168 | tf_op jit(solution)/shard_map/ppermute | solution.py:566
  507.7 34.6 %all-to-all-start.6 = ((bf16[8,128,384]{2,1,0:T(8,128)(2,1)}), bf16[8,128,384]{2,1,0:T(8,128)(2,1)}, u32[]{:S(2)}, u32[]{:S(2)}) async-start(bf16[8,128,384]{2,1,0:T(8,128)(2,1)} %bitcast.193), calls=%async_computation.7 | async-start | bytes 1572864 | tf_op jit(solution)/shard_map/all_to_all | solution.py:587
  515.5 32.6 %collective-permute-start.36 = (bf16[640,1024]{1,0:T(8,128)(2,1)}, bf16[640,1024]{1,0:T(8,128)(2,1)}, u32[]{:S(2)}, u32[]{:S(2)}) collective-permute-start(bf16[640,1024]{1,0:T(8,128)(2,1)} %add_convert_fusion.7), channel_id=1, source_target_pairs={{0,2},{1,3},{2,0},{3,1},{4,6},{5,7},{6,4},{7,5},{8,10},{9,11},{10,... | collective-permute-start | bytes 3932168 | tf_op jit(solution)/shard_map/ppermute | solution.py:570
  (91 other events, 650.9 us)
Sparse Core Ops, SparseCore 0:
  220.8 86.9 reduce-scatter.1

commit v10 on v9

--- a/solution.py
+++ b/solution.py
@@ -540,6 +540,8 @@
 
 
 LANES = 128
+DIRECT = 8
+EARLY = 5
 QUARTER_ROWS = 128
 
 
@@ -587,6 +589,22 @@
     return lax.all_to_all(blocks, "expert", split_axis=0, concat_axis=0, tiled=True)
 
 
+def steps_sent(blocks):
+    count = lax.axis_size("expert")
+    parts = [blocks[0]]
+    for step in range(1, count):
+        pairs = [(i, (i + step) % count) for i in range(count)]
+        parts.append(lax.ppermute(blocks[step], "expert", pairs))
+    return parts
+
+
+def in_order(parts):
+    count = len(parts)
+    onward = jnp.stack([parts[-step % count] for step in range(count)] * 2)
+    start = count - lax.axis_index("expert")
+    return lax.dynamic_slice_in_dim(onward, start, count, 0)
+
+
 def scatter_sum(strips):
     strips = with_layout_constraint(strips.astype(BF16), Layout(major_to_minor=(0, 1)))
     return lax.psum_scatter(strips, "expert", scatter_dimension=0, tiled=True)
@@ -600,14 +618,15 @@
     return jnp.sum(strips.astype(F32), axis=0)
 
 
-def slots_of(expert_ids, experts, capacity):
+def slots_of(expert_ids, experts, capacity, relative):
     rows = expert_ids.shape[0]
     chosen = expert_ids[:, None] == jnp.arange(experts, dtype=jnp.int32)[None, :]
     at = jnp.arange(rows, dtype=jnp.int32)
     before = (at[None, :] < at[:, None]).astype(BF16)
     earlier = jnp.dot(before, chosen.astype(BF16), preferred_element_type=F32)
     slot = jnp.sum(jnp.where(chosen, earlier, 0.0), axis=1).astype(jnp.int32)
-    place = expert_ids * capacity + slot
+    block = (expert_ids - lax.axis_index("expert")) % experts if relative else expert_ids
+    place = block * capacity + slot
     places = jnp.arange(experts * capacity, dtype=jnp.int32)
     return (places[:, None] == place[None, :]).astype(BF16)
 
@@ -643,11 +662,12 @@
 
     quarter_ids = routes[:, 0].reshape(4, tok_dev)
 
-    def slots_at(offset):
+    def slots_at(offset, relative):
         ids = lax.dynamic_index_in_dim(quarter_ids, mine ^ offset, 0, keepdims=False)
-        return slots_of(ids, experts, capacity)
-
-    own_slots, far_slots = slots_at(0), slots_at(2)
+        return slots_of(ids, experts, capacity, relative)
+
+    direct = experts <= DIRECT
+    own_slots, far_slots = slots_at(0, False), slots_at(2, direct)
 
     def placed(slots, rows):
         return jnp.dot(slots, rows, preferred_element_type=F32).astype(BF16)
@@ -685,8 +705,11 @@
     side_grads = from_side(own_grads)
     cotangent_corner = from_side(cotangent_far)
     far_placed = placed(far_slots, cotangent_far)
-    branch_far, side_grads, cotangent_corner, far_placed = lax.optimization_barrier(
-        (branch_far, side_grads, cotangent_corner, far_placed)
+    far_parts = steps_sent(far_placed.reshape(experts, capacity, width)) if direct else []
+    branch_far, side_grads, cotangent_corner, far_placed, *far_parts[:EARLY] = (
+        lax.optimization_barrier(
+            (branch_far, side_grads, cotangent_corner, far_placed, *far_parts[:EARLY])
+        )
     )
     residual = tokens.astype(F32) + (branch + branch_far.astype(F32))
 
@@ -715,7 +738,11 @@
         (normed_two_far, grad_up, grad_down, own_rows)
     )
     far_rows = from_far(own_rows)
-    far_grads = sent(after(far_placed, own_rows))
+    if direct:
+        normed_two_far, *far_parts = lax.optimization_barrier((normed_two_far, *far_parts))
+        far_grads = in_order(far_parts).reshape(-1, width)
+    else:
+        far_grads = sent(after(far_placed, own_rows))
     normed_two_corner = from_side(normed_two_far)
     far_dense = list(dense(normed_two_far, normed_two_corner, cotangent_far, cotangent_corner))
 
@@ -744,9 +771,9 @@
     dense_back_far = chip_sum(far_dense, 2).astype(BF16)
     far_two = jnp.concatenate([normed_two_far, normed_two_corner], axis=0)
     grad_down = (grad_down + product(far_dense[6], far_dense[4])).astype(BF16)
-    far_two, far_rows, grad_down = lax.optimization_barrier((far_two, far_rows, grad_down))
+    far_two, grad_down = lax.optimization_barrier((far_two, grad_down))
     grad_up = (grad_up + product(far_two, far_dense[5])).astype(BF16)
-    dense_grads = after(jnp.concatenate([grad_up, grad_down], axis=1), far_grads)
+    dense_grads = jnp.concatenate([grad_up, grad_down], axis=1)
     far_rows, dense_back_far, dense_grads = lax.optimization_barrier(
         (far_rows, dense_back_far, dense_grads)
     )
@@ -838,7 +865,6 @@
     near_results[0], far_results[0] = pair_back(0, near_heads, far_heads)
     far_branch = jnp.concatenate([grad_branch_far, grad_branch_corner], axis=0)
     grad_w_out = grad_w_out + product(far_branch, far_out.reshape(flat))
-    small = sum_over(small, "tensor")
     small_columns = -(-small.shape[0] // LANES) * LANES
     small_block = jnp.pad(small, ((0, small_columns - small.shape[0]), (0, 0))).T
     branch_grads = jnp.concatenate([grad_w_out.astype(BF16), small_block.astype(BF16)], axis=1)
@@ -857,15 +883,17 @@
     def normed_part(results, quarter):
         return total([dot_nt(results[pair][quarter], pair_weights(pair)) for pair in range(pairs)])
 
-    def qkv_strips(pair, *others):
+    def qkv_weights(pair, *others):
         near_rows = near_results[pair].reshape(2 * tok_dev, 3 * PAIR)
         far_rows = far_results[pair].reshape(2 * tok_dev, 3 * PAIR)
         near_rows = after(near_rows, *others)
-        return strips_sent(weight_grads(near_one, far_one, near_rows, far_rows).astype(BF16))
+        return weight_grads(near_one, far_one, near_rows, far_rows).astype(BF16)
 
     corner_part = normed_part(far_results, 1).astype(BF16)
     from_corner = from_side(corner_part).astype(F32)
-    qkv_grads = [qkv_strips(0, corner_part)]
+    first_grads = qkv_weights(0, corner_part)
+    far_results, first_grads = lax.optimization_barrier((far_results, first_grads))
+    qkv_grads = [strips_sent(first_grads)]
     far_sum = (normed_part(far_results, 0) + from_corner).astype(BF16)
     near_results, far_results, out_rows, far_sum = lax.optimization_barrier(
         (near_results, far_results, out_rows, far_sum)
@@ -878,10 +906,11 @@
         near_sum * scaled_one + far_sum.astype(F32) * scaled_far, axis=0, keepdims=True
     )
     gain_one = sum_over(gain_one, "expert")
-    qkv_grads += [qkv_strips(pair, gain_one) for pair in range(1, pairs)]
+    qkv_grads += [strips_sent(qkv_weights(pair, gain_one)) for pair in range(1, pairs)]
     grad_normed_one = near_sum + after(from_far(far_sum), gain_one).astype(F32)
     grad_ln_attn = sum_over(gain_one, "tensor")[0]
-    branch_grads = strips_total(branch_grads)
+    branch_grads = strips_total(after(branch_grads, gain_one))
+    small = sum_over(branch_grads[:, heads_width:], "tensor")
     qkv_grads = jnp.stack(
         [strips_total(grads).reshape(-1, 3, PAIR) for grads in qkv_grads], axis=2
     )
@@ -894,11 +923,11 @@
         grad_ln_attn,
         qkv_grads.reshape(strip, 3, heads_width).transpose(1, 0, 2),
         branch_grads[:, :heads_width].T,
-        branch_grads[:, heads_width + experts + 2],
+        small[:, experts + 2],
         dense_grads[:, :hidden].astype(F32),
         dense_grads[:, hidden:].T.astype(F32),
-        branch_grads[:, heads_width : heads_width + experts],
-        branch_grads[:, heads_width + experts : heads_width + experts + 2],
+        small[:, :experts],
+        small[:, experts : experts + 2],
         grad_ex_up,
         grad_ex_down,
     )

time: 578 us -> 604 us (1.045)
  local copies, waits for them, and re-layouts: 17.8 us -> 27.8 us
  waiting for transfers between devices: 106 us -> 116 us
  starting transfers between devices: 72.6 us -> 79.1 us
    ppermute x0 -> x7, waiting for transfers between devices: none -> 43.2 us  [steps_sent(): parts.append(lax.ppermute(blocks[step], 'expert', pairs))]
    ppermute x11, waiting for transfers between devices: 54.4 us -> 28.3 us  [from_far(): return lax.ppermute(values, 'tensor', [(i, i ^ 2) for i in range(4)])]
    unnamed x136 -> x161, local copies, waits for them, and re-layouts: 11.1 us -> 22.2 us
    ppermute x0 -> x7, starting transfers between devices: none -> 9.31 us  [steps_sent(): parts.append(lax.ppermute(blocks[step], 'expert', pairs))]
    all_to_all x8 -> x7, starting transfers between devices: 40.8 us -> 44.3 us  [exchange(): lax.all_to_all(blocks, 'expert', split_axis=0, concat_axis=0, tiled=True)]
    all_to_all x8 -> x7, waiting for transfers between devices: 27.7 us -> 25.4 us  [exchange(): lax.all_to_all(blocks, 'expert', split_axis=0, concat_axis=0, tiled=True)]
  transfers between devices with their start and end apart: 51 -> 57, of which waited for: 19 -> 22; matrix products, arithmetic and copies ran while one was open for 31% -> 31% of each run, Pallas kernels for 30% -> 29%
where the time goes in v10:
time: 604 us; the launch traced here: 599 us
  Pallas kernels  174 us (29%)
  matrix products  122 us (20%)
  waiting for transfers between devices  116 us (19%)
  starting transfers between devices  79.1 us (13%)
  other arithmetic  65.3 us (11%)
  local copies, waits for them, and re-layouts  27.8 us (5%)
  between operations  15.6 us (3%)
    pallas_call x4, Pallas kernels, feed(): pl.pallas_call(functools.partial(feed_kernel, experts, routed), grid_spec...  107 us
    dot_general x14, matrix products, product(): return jnp.einsum('gd,gf->df', left, right, preferred_element_type=F32)  65.9 us
    pallas_call x2, Pallas kernels, attention_backward(): pl.pallas_call(backward_kernel, grid_spec=pltpu.PrefetchScalarGridSpec(nu...  44.7 us
    all_to_all x7, starting transfers between devices, exchange(): lax.all_to_all(blocks, 'expert', split_axis=0, concat_axis=0, tiled=True)  44.3 us
    ppermute x7, waiting for transfers between devices, steps_sent(): parts.append(lax.ppermute(blocks[step], 'expert', pairs))  43.2 us
    ppermute x11, waiting for transfers between devices, from_far(): return lax.ppermute(values, 'tensor', [(i, i ^ 2) for i in range(4)])  28.3 us
    all_to_all x7, waiting for transfers between devices, exchange(): lax.all_to_all(blocks, 'expert', split_axis=0, concat_axis=0, tiled=True)  25.4 us
    unnamed x161, local copies, waits for them, and re-layouts  22.2 us
  transfers between devices with their start and end apart: 57, of which 22 were waited for; matrix products, arithmetic and copies ran while one was open for 31% of the time, Pallas kernels for 29%

profile of v10, /device:TPU:0, one launch (start us, length us, event | category | flops | bytes accessed | tf_op | source)
XLA Modules:
  0.0 599.3 jit_solution(12150212080726628358)
XLA Ops:
  20.2 6.1 %all-to-all-start = ((bf16[8,112,1024]{2,1,0:T(8,128)(2,1)}), bf16[8,112,1024]{2,1,0:T(8,128)(2,1)S(1)}, u32[]{:S(2)}, u32[]{:S(2)}) async-start(bf16[8,112,1024]{2,1,0:T(8,128)(2,1)} %bitcast.213), calls=%async_computation | async-start | bytes 3670016 | tf_op jit(solution)/shard_map/all_to_all | solution.py:589
  27.7 5.8 convolution_convert_fusion.1
  33.4 11.6 %collective-permute-done = bf16[640,1024]{1,0:T(8,128)(2,1)} collective-permute-done((bf16[640,1024]{1,0:T(8,128)(2,1)}, bf16[640,1024]{1,0:T(8,128)(2,1)}, u32[]{:S(2)}, u32[]{:S(2)}) %collective-permute-start) | collective-permute-done | bytes 1310752 | tf_op jit(solution)/shard_map/ppermute | solution.py:572
  53.7 22.0 %tree_attention.1 = (bf16[2,640,256]{2,1,0:T(8,128)(2,1)}, bf16[2,640,256]{2,1,0:T(8,128)(2,1)}, f32[2,2,1024]{2,1,0:T(2,128)}, f32[2,2,2,768]{3,2,1,0:T(2,128)}) custom-call(s32[9]{0:T(128)} %pad_add_fusion.leaves_ref, bf16[3,2,640,256]{3,2,1,0:T(8,128)(2,1)} %bitcast.233, bf16[3,2,640,256]{3,2,1,0:T(8,128)(2,1)} %bitcast.236), custom_call_target="tpu_custom_call" | custom-call | flops 1241513984 | bytes 1310720 | tf_op jit(solution)/shard_map/tree_attention/pallas_call | solution.py:200
  90.5 10.6 %collective-permute-done.13 = bf16[112,1024]{1,0:T(8,128)(2,1)S(1)} collective-permute-done((bf16[112,1024]{1,0:T(8,128)(2,1)S(1)}, bf16[112,1024]{1,0:T(8,128)(2,1)S(1)}, u32[]{:S(2)}, u32[]{:S(2)}) %collective-permute-start.13) | collective-permute-done | bytes 229408 | tf_op jit(solution)/shard_map/ppermute | solution.py:597
  102.6 16.5 %collective-permute-done.12 = bf16[112,1024]{1,0:T(8,128)(2,1)S(1)} collective-permute-done((bf16[112,1024]{1,0:T(8,128)(2,1)S(1)}, bf16[112,1024]{1,0:T(8,128)(2,1)S(1)}, u32[]{:S(2)}, u32[]{:S(2)}) %collective-permute-start.12) | collective-permute-done | bytes 229408 | tf_op jit(solution)/shard_map/ppermute | solution.py:597
  119.2 7.8 %collective-permute-done.11 = bf16[112,1024]{1,0:T(8,128)(2,1)S(1)} collective-permute-done((bf16[112,1024]{1,0:T(8,128)(2,1)S(1)}, bf16[112,1024]{1,0:T(8,128)(2,1)S(1)}, u32[]{:S(2)}, u32[]{:S(2)}) %collective-permute-start.11) | collective-permute-done | bytes 229408 | tf_op jit(solution)/shard_map/ppermute | solution.py:597
  127.5 8.2 %collective-permute-done.10 = bf16[112,1024]{1,0:T(8,128)(2,1)S(1)} collective-permute-done((bf16[112,1024]{1,0:T(8,128)(2,1)S(1)}, bf16[112,1024]{1,0:T(8,128)(2,1)S(1)}, u32[]{:S(2)}, u32[]{:S(2)}) %collective-permute-start.10) | collective-permute-done | bytes 229408 | tf_op jit(solution)/shard_map/ppermute | solution.py:597
  152.3 20.4 %feed_dense.2 = (bf16[640,1024]{1,0:T(8,128)(2,1)}, bf16[640,1024]{1,0:T(8,128)(2,1)}, bf16[640,1024]{1,0:T(8,128)(2,1)}, bf16[640,1024]{1,0:T(8,128)(2,1)}, bf1...) custom-call(s32[1]{0:T(128)} %constant.65.clone.1.expert_ref, ...), custom_call_target="tpu_custom_call" | custom-call | flops 1342177280 | bytes 2490368 | tf_op jit(solution)/shard_map/feed_dense/pallas_call | solution.py:495
  172.8 7.6 %convolution_bitcast_fusion = f32[1024,1024]{1,0:T(8,128)} fusion(bf16[2,640,1024]{2,1,0:T(8,128)(2,1)} %get-tuple-element.160, bf16[2,640,1024]{2,1,0:T(8,128)(2,1)} %get-tuple-element.161), kind=kOutput, calls=%fused_computation.78 | convolution fusion | flops 2684354560 | bytes 9437184 | tf_op jit(solution)/shard_map/gd,gf->df/dot_general | solution.py:728
  180.4 5.8 fusion.23
  186.2 5.6 all-to-all-done.1
  195.3 20.3 %feed_dense.3 = (bf16[640,1024]{1,0:T(8,128)(2,1)}, bf16[640,1024]{1,0:T(8,128)(2,1)}, bf16[640,1024]{1,0:T(8,128)(2,1)}, bf16[640,1024]{1,0:T(8,128)(2,1)}, bf1...) custom-call(s32[1]{0:T(128)} %constant.65.clone.1.expert_ref, ...), custom_call_target="tpu_custom_call" | custom-call | flops 1342177280 | bytes 2490368 | tf_op jit(solution)/shard_map/feed_dense/pallas_call | solution.py:495
  251.0 33.1 %feed_routed.2 = (bf16[896,1024]{1,0:T(8,128)(2,1)}, bf16[896,1024]{1,0:T(8,128)(2,1)}, bf16[896,1024]{1,0:T(8,128)(2,1)}, bf16[896,1024]{1,0:T(8,128)(2,1)}, bf...) custom-call(s32[1]{0:T(128)} %bitcast.20.expert_ref, ...), custom_call_target="tpu_custom_call" | custom-call | flops 1879048192 | bytes 3276800 | tf_op jit(solution)/shard_map/feed_routed/pallas_call | solution.py:495
  293.6 33.1 %feed_routed.3 = (bf16[896,1024]{1,0:T(8,128)(2,1)}, bf16[896,1024]{1,0:T(8,128)(2,1)}, bf16[896,1024]{1,0:T(8,128)(2,1)}, bf16[896,1024]{1,0:T(8,128)(2,1)}, bf...) custom-call(s32[1]{0:T(128)} %bitcast.20.expert_ref, ...), custom_call_target="tpu_custom_call" | custom-call | flops 1879048192 | bytes 3276800 | tf_op jit(solution)/shard_map/feed_routed/pallas_call | solution.py:495
  341.3 13.3 %all-to-all-start.2 = ((bf16[8,112,1024]{2,1,0:T(8,128)(2,1)}), bf16[8,112,1024]{2,1,0:T(8,128)(2,1)}, u32[]{:S(2)}, u32[]{:S(2)}) async-start(bf16[8,112,1024]{2,1,0:T(8,128)(2,1)} %bitcast.203), calls=%async_computation.3 | async-start | bytes 3670016 | tf_op jit(solution)/shard_map/all_to_all | solution.py:589
  370.1 7.8 %fusion.5 = f32[1024,1024]{1,0:T(8,128)} fusion(bf16[1792,1024]{1,0:T(8,128)(2,1)S(1)} %bitcast.228, bf16[896,1024]{1,0:T(8,128)(2,1)} %collective-permute-done.22.side_ref, bf16[896,1024]{1,0:T(8,128)(2,1)} %collective-permute-done.16.own_ref), kind=kOutput, calls=%fused_computation.13 | convolution fusion | flops 3765436416 | bytes 11534336 | tf_op jit(solution)/shard_map/gd,gf->df/dot_general | solution.py:728
  383.4 14.0 %all-to-all-done.2 = bf16[8,112,1024]{2,1,0:T(8,128)(2,1)} async-done(((bf16[8,112,1024]{2,1,0:T(8,128)(2,1)}), bf16[8,112,1024]{2,1,0:T(8,128)(2,1)}, u32[]{:S(2)}, u32[]{:S(2)}) %all-to-all-start.2) | async-done | bytes 1835040 | tf_op jit(solution)/shard_map/all_to_all | solution.py:589
  407.9 7.6 %add_bitcast_fusion.1 = f32[1,1024,1024]{2,1,0:T(8,128)} fusion(f32[1024,1024]{1,0:T(8,128)S(1)} %copy-done.67, bf16[1792,1024]{1,0:T(8,128)(2,1)S(1)} %bitcast.227, bf16[896,1024]{1,0:T(8,128)(2,1)} %collective-permute-done.27.side_ref, bf16[896,1024]{1,0:T(8,128)(2,1)} %bitcast.19.own_ref), kind=kOutput, calls=%fused_computation.4 | convolution fusion | flops 3766484992 | bytes 15728640 | tf_op jit(solution)/shard_map/gd,gf->df/dot_general | solution.py:728
  450.1 22.2 %tree_attention_back.2 = (bf16[2,640,384]{2,1,0:T(8,128)(2,1)}, bf16[2,640,384]{2,1,0:T(8,128)(2,1)}) custom-call(s32[9]{0:T(128)} %pad_add_fusion.leaves_ref, bf16[3,2,640,256]{3,2,1,0:T(8,128)(2,1)} %bitcast.234, bf16[3,2,640,256]{3,2,1,0:T(8,128)(2,1)} %bitcast.237, bf16[2,640,256]{2,1,0:T(8,128)(2,1)} %pad_maximum_fusion.9.near_grads_ref, ...), custom_call_target="tpu_custom_call" | custom-call | flops 2483025920 | bytes 1048576 | tf_op jit(solution)/shard_map/tree_attention_back/pallas_call | solution.py:350
  479.2 22.5 %tree_attention_back.3 = (bf16[2,640,384]{2,1,0:T(8,128)(2,1)}, bf16[2,640,384]{2,1,0:T(8,128)(2,1)}) custom-call(s32[9]{0:T(128)} %pad_add_fusion.leaves_ref, bf16[3,2,640,256]{3,2,1,0:T(8,128)(2,1)} %bitcast.235, bf16[3,2,640,256]{3,2,1,0:T(8,128)(2,1)} %bitcast.238, bf16[2,640,256]{2,1,0:T(8,128)(2,1)} %pad_maximum_fusion.9.near_grads_ref, ...), custom_call_target="tpu_custom_call" | custom-call | flops 2483025920 | bytes 1048576 | tf_op jit(solution)/shard_map/tree_attention_back/pallas_call | solution.py:350
  521.1 6.0 all-to-all-start.5
  565.8 5.7 all-to-all-start.6
  585.2 5.8 all-to-all-done.6
  (374 shorter events, 264.2 us)
Async XLA Ops:
  12.7 32.3 %collective-permute-start = (bf16[640,1024]{1,0:T(8,128)(2,1)}, bf16[640,1024]{1,0:T(8,128)(2,1)}, u32[]{:S(2)}, u32[]{:S(2)}) collective-permute-start(bf16[640,1024]{1,0:T(8,128)(2,1)} %fusion.15), channel_id=1, source_target_pairs={{0,2},{1,3},{2,0},{3,1},{4,6},{5,7},{6,4},{7,5},{8,10},{9,11},{10,... | collective-permute-start | bytes 3932168 | tf_op jit(solution)/shard_map/ppermute | solution.py:572
  20.2 56.7 %all-to-all-start = ((bf16[8,112,1024]{2,1,0:T(8,128)(2,1)}), bf16[8,112,1024]{2,1,0:T(8,128)(2,1)S(1)}, u32[]{:S(2)}, u32[]{:S(2)}) async-start(bf16[8,112,1024]{2,1,0:T(8,128)(2,1)} %bitcast.213), calls=%async_computation | async-start | bytes 3670016 | tf_op jit(solution)/shard_map/all_to_all | solution.py:589
  45.8 31.1 %collective-permute-start.4 = (bf16[640,1024]{1,0:T(8,128)(2,1)}, bf16[640,1024]{1,0:T(8,128)(2,1)}, u32[]{:S(2)}, u32[]{:S(2)}) collective-permute-start(bf16[640,1024]{1,0:T(8,128)(2,1)} %own_grads_ref.1), channel_id=1, source_target_pairs={{0,2},{1,3},{2,0},{3,1},{4,6},{5,7},{6,4},{7,5},{8,10},{9,11},{10,... | collective-permute-start | bytes 3932168 | tf_op jit(solution)/shard_map/ppermute | solution.py:572
  80.1 57.3 %collective-permute-start.3 = (bf16[640,1024]{1,0:T(8,128)(2,1)S(1)}, bf16[640,1024]{1,0:T(8,128)(2,1)S(1)}, u32[]{:S(2)}, u32[]{:S(2)}) collective-permute-start(bf16[640,1024]{1,0:T(8,128)(2,1)S(1)} %convolution_convert_fusion.3), channel_id=1, source_target_pairs={{0,1},{1,0},{2,3},{3,2},{4,5},{5,4},{6,7},{7,6},{8,9},{9,8},{10,11... | collective-permute-start | bytes 3932168 | tf_op jit(solution)/shard_map/ppermute | solution.py:568
  80.7 55.0 %collective-permute-start.9 = (bf16[640,1024]{1,0:T(8,128)(2,1)}, bf16[640,1024]{1,0:T(8,128)(2,1)S(1)}, u32[]{:S(2)}, u32[]{:S(2)}) collective-permute-start(bf16[640,1024]{1,0:T(8,128)(2,1)} %collective-permute-done.4.own_grads_ref), channel_id=1, source_target_pairs={{0,1},{1,0},{2,3},{3,2},{4,5},{5,4},{6,7},{7,6},{8,9},{9,8},{10,11... | collective-permute-start | bytes 3932168 | tf_op jit(solution)/shard_map/ppermute | solution.py:568
  80.8 55.0 %collective-permute-start.8 = (bf16[896,1024]{1,0:T(8,128)(2,1)S(1)}, bf16[896,1024]{1,0:T(8,128)(2,1)S(1)}, u32[]{:S(2)}, u32[]{:S(2)}) collective-permute-start(bf16[896,1024]{1,0:T(8,128)(2,1)S(1)} %bitcast.204), channel_id=1, source_target_pairs={{0,1},{1,0},{2,3},{3,2},{4,5},{5,4},{6,7},{7,6},{8,9},{9,8},{10,11... | collective-permute-start | bytes 5505032 | tf_op jit(solution)/shard_map/ppermute | solution.py:568
  82.2 53.5 %collective-permute-start.7 = (bf16[640,1024]{1,0:T(8,128)(2,1)S(1)}, bf16[640,1024]{1,0:T(8,128)(2,1)S(1)}, u32[]{:S(2)}, u32[]{:S(2)}) collective-permute-start(bf16[640,1024]{1,0:T(8,128)(2,1)S(1)} %add_convert_fusion.11), channel_id=1, source_target_pairs={{0,2},{1,3},{2,0},{3,1},{4,6},{5,7},{6,4},{7,5},{8,10},{9,11},{10,... | collective-permute-start | bytes 3932168 | tf_op jit(solution)/shard_map/ppermute | solution.py:572
  142.1 49.7 %all-to-all-start.1 = ((bf16[8,112,1024]{2,1,0:T(8,128)(2,1)}), bf16[8,112,1024]{2,1,0:T(8,128)(2,1)}, u32[]{:S(2)}, u32[]{:S(2)}) async-start(bf16[8,112,1024]{2,1,0:T(8,128)(2,1)} %bitcast.214), calls=%async_computation.1 | async-start | bytes 3670016 | tf_op jit(solution)/shard_map/all_to_all | solution.py:589
  146.4 184.1 %reduce-scatter.2.cloned.1.call-start = ((), (), s32[]{:S(2)}) async-start(), calls=%async_computation.8 | async-start | bytes 4718592 | tf_op jit(solution)/shard_map/reduce_scatter | solution.py:610
  146.6 45.3 %collective-permute-start.19 = (bf16[112,1024]{1,0:T(8,128)(2,1)}, bf16[112,1024]{1,0:T(8,128)(2,1)}, u32[]{:S(2)}, u32[]{:S(2)}) collective-permute-start(bf16[112,1024]{1,0:T(8,128)(2,1)} %get-tuple-element.363), channel_id=1, source_target_pairs={{0,28},{4,0},{8,4},{12,8},{16,12},{20,16},{24,20},{28,24},{1,29},{... | collective-permute-start | bytes 688136 | tf_op jit(solution)/shard_map/ppermute | solution.py:597
  151.1 40.7 %collective-permute-start.18 = (bf16[112,1024]{1,0:T(8,128)(2,1)}, bf16[112,1024]{1,0:T(8,128)(2,1)}, u32[]{:S(2)}, u32[]{:S(2)}) collective-permute-start(bf16[112,1024]{1,0:T(8,128)(2,1)} %get-tuple-element.364), channel_id=1, source_target_pairs={{0,24},{4,28},{8,0},{12,4},{16,8},{20,12},{24,16},{28,20},{1,25},{... | collective-permute-start | bytes 688136 | tf_op jit(solution)/shard_map/ppermute | solution.py:597
  151.7 40.2 %collective-permute-start.17 = (bf16[112,1024]{1,0:T(8,128)(2,1)}, bf16[112,1024]{1,0:T(8,128)(2,1)}, u32[]{:S(2)}, u32[]{:S(2)}) collective-permute-start(bf16[112,1024]{1,0:T(8,128)(2,1)} %get-tuple-element.365), channel_id=1, source_target_pairs={{0,20},{4,24},{8,28},{12,0},{16,4},{20,8},{24,12},{28,16},{1,21},{... | collective-permute-start | bytes 688136 | tf_op jit(solution)/shard_map/ppermute | solution.py:597
  151.7 34.5 %collective-permute-start.15 = (bf16[640,1024]{1,0:T(8,128)(2,1)}, bf16[640,1024]{1,0:T(8,128)(2,1)}, u32[]{:S(2)}, u32[]{:S(2)}) collective-permute-start(bf16[640,1024]{1,0:T(8,128)(2,1)} %copy-done.10), channel_id=1, source_target_pairs={{0,2},{1,3},{2,0},{3,1},{4,6},{5,7},{6,4},{7,5},{8,10},{9,11},{10,... | collective-permute-start | bytes 3932168 | tf_op jit(solution)/shard_map/ppermute | solution.py:572
  191.9 42.9 %collective-permute-start.16 = (bf16[896,1024]{1,0:T(8,128)(2,1)}, bf16[896,1024]{1,0:T(8,128)(2,1)}, u32[]{:S(2)}, u32[]{:S(2)}) collective-permute-start(bf16[896,1024]{1,0:T(8,128)(2,1)} %bitcast.19.own_ref), channel_id=1, source_target_pairs={{0,2},{1,3},{2,0},{3,1},{4,6},{5,7},{6,4},{7,5},{8,10},{9,11},{10,... | collective-permute-start | bytes 5505032 | tf_op jit(solution)/shard_map/ppermute | solution.py:572
  244.8 39.4 %collective-permute-start.24 = (bf16[640,1024]{1,0:T(8,128)(2,1)}, bf16[640,1024]{1,0:T(8,128)(2,1)}, u32[]{:S(2)}, u32[]{:S(2)}) collective-permute-start(bf16[640,1024]{1,0:T(8,128)(2,1)} %add_convert_fusion.10), channel_id=1, source_target_pairs={{0,2},{1,3},{2,0},{3,1},{4,6},{5,7},{6,4},{7,5},{8,10},{9,11},{10,... | collective-permute-start | bytes 3932168 | tf_op jit(solution)/shard_map/ppermute | solution.py:572
  293.1 42.6 %collective-permute-start.29 = (bf16[896,1024]{1,0:T(8,128)(2,1)}, bf16[896,1024]{1,0:T(8,128)(2,1)}, u32[]{:S(2)}, u32[]{:S(2)}) collective-permute-start(bf16[896,1024]{1,0:T(8,128)(2,1)} %add_convert_fusion.4), channel_id=1, source_target_pairs={{0,2},{1,3},{2,0},{3,1},{4,6},{5,7},{6,4},{7,5},{8,10},{9,11},{10,... | collective-permute-start | bytes 5505032 | tf_op jit(solution)/shard_map/ppermute | solution.py:572
  340.8 42.7 %collective-permute-start.26 = (bf16[640,1024]{1,0:T(8,128)(2,1)}, bf16[640,1024]{1,0:T(8,128)(2,1)}, u32[]{:S(2)}, u32[]{:S(2)}) collective-permute-start(bf16[640,1024]{1,0:T(8,128)(2,1)} %get-tuple-element.201), channel_id=1, source_target_pairs={{0,1},{1,0},{2,3},{3,2},{4,5},{5,4},{6,7},{7,6},{8,9},{9,8},{10,11... | collective-permute-start | bytes 3932168 | tf_op jit(solution)/shard_map/ppermute | solution.py:568
  341.3 56.2 %all-to-all-start.2 = ((bf16[8,112,1024]{2,1,0:T(8,128)(2,1)}), bf16[8,112,1024]{2,1,0:T(8,128)(2,1)}, u32[]{:S(2)}, u32[]{:S(2)}) async-start(bf16[8,112,1024]{2,1,0:T(8,128)(2,1)} %bitcast.203), calls=%async_computation.3 | async-start | bytes 3670016 | tf_op jit(solution)/shard_map/all_to_all | solution.py:589
  354.6 62.9 %collective-permute-start.33 = (bf16[896,1024]{1,0:T(8,128)(2,1)}, bf16[896,1024]{1,0:T(8,128)(2,1)}, u32[]{:S(2)}, u32[]{:S(2)}) collective-permute-start(bf16[896,1024]{1,0:T(8,128)(2,1)} %get-tuple-element.231), channel_id=1, source_target_pairs={{0,1},{1,0},{2,3},{3,2},{4,5},{5,4},{6,7},{7,6},{8,9},{9,8},{10,11... | collective-permute-start | bytes 5505032 | tf_op jit(solution)/shard_map/ppermute | solution.py:568
  365.3 52.2 %collective-permute-start.34 = (bf16[896,1024]{1,0:T(8,128)(2,1)}, bf16[896,1024]{1,0:T(8,128)(2,1)}, u32[]{:S(2)}, u32[]{:S(2)}) collective-permute-start(bf16[896,1024]{1,0:T(8,128)(2,1)} %add_convert_fusion.2), channel_id=1, source_target_pairs={{0,2},{1,3},{2,0},{3,1},{4,6},{5,7},{6,4},{7,5},{8,10},{9,11},{10,... | collective-permute-start | bytes 5505032 | tf_op jit(solution)/shard_map/ppermute | solution.py:572
  406.8 31.5 %collective-permute-start.30 = (bf16[640,1024]{1,0:T(8,128)(2,1)}, bf16[640,1024]{1,0:T(8,128)(2,1)}, u32[]{:S(2)}, u32[]{:S(2)}) collective-permute-start(bf16[640,1024]{1,0:T(8,128)(2,1)} %get-tuple-element.359), channel_id=1, source_target_pairs={{0,2},{1,3},{2,0},{3,1},{4,6},{5,7},{6,4},{7,5},{8,10},{9,11},{10,... | collective-permute-start | bytes 3932168 | tf_op jit(solution)/shard_map/ppermute | solution.py:572
  422.1 50.2 %all-to-all-start.3 = ((bf16[8,112,1024]{2,1,0:T(8,128)(2,1)}), bf16[8,112,1024]{2,1,0:T(8,128)(2,1)}, u32[]{:S(2)}, u32[]{:S(2)}) async-start(bf16[8,112,1024]{2,1,0:T(8,128)(2,1)} %bitcast.202), calls=%async_computation.4 | async-start | bytes 3670016 | tf_op jit(solution)/shard_map/all_to_all | solution.py:589
  440.1 32.2 %collective-permute-start.38 = (bf16[640,1024]{1,0:T(8,128)(2,1)}, bf16[640,1024]{1,0:T(8,128)(2,1)}, u32[]{:S(2)}, u32[]{:S(2)}) collective-permute-start(bf16[640,1024]{1,0:T(8,128)(2,1)} %add_convert_fusion.9), channel_id=1, source_target_pairs={{0,2},{1,3},{2,0},{3,1},{4,6},{5,7},{6,4},{7,5},{8,10},{9,11},{10,... | collective-permute-start | bytes 3932168 | tf_op jit(solution)/shard_map/ppermute | solution.py:572
  527.1 31.3 %collective-permute-start.41 = (bf16[640,1024]{1,0:T(8,128)(2,1)}, bf16[640,1024]{1,0:T(8,128)(2,1)}, u32[]{:S(2)}, u32[]{:S(2)}) collective-permute-start(bf16[640,1024]{1,0:T(8,128)(2,1)} %add_convert_fusion.7), channel_id=1, source_target_pairs={{0,2},{1,3},{2,0},{3,1},{4,6},{5,7},{6,4},{7,5},{8,10},{9,11},{10,... | collective-permute-start | bytes 3932168 | tf_op jit(solution)/shard_map/ppermute | solution.py:572
  (102 other events, 887.7 us)
Sparse Core Ops, SparseCore 0:
  234.9 95.5 reduce-scatter.1

commit v11 on v9

--- a/solution.py
+++ b/solution.py
@@ -838,7 +838,6 @@
     near_results[0], far_results[0] = pair_back(0, near_heads, far_heads)
     far_branch = jnp.concatenate([grad_branch_far, grad_branch_corner], axis=0)
     grad_w_out = grad_w_out + product(far_branch, far_out.reshape(flat))
-    small = sum_over(small, "tensor")
     small_columns = -(-small.shape[0] // LANES) * LANES
     small_block = jnp.pad(small, ((0, small_columns - small.shape[0]), (0, 0))).T
     branch_grads = jnp.concatenate([grad_w_out.astype(BF16), small_block.astype(BF16)], axis=1)
@@ -857,15 +856,17 @@
     def normed_part(results, quarter):
         return total([dot_nt(results[pair][quarter], pair_weights(pair)) for pair in range(pairs)])
 
-    def qkv_strips(pair, *others):
+    def qkv_weights(pair, *others):
         near_rows = near_results[pair].reshape(2 * tok_dev, 3 * PAIR)
         far_rows = far_results[pair].reshape(2 * tok_dev, 3 * PAIR)
         near_rows = after(near_rows, *others)
-        return strips_sent(weight_grads(near_one, far_one, near_rows, far_rows).astype(BF16))
+        return weight_grads(near_one, far_one, near_rows, far_rows).astype(BF16)
 
     corner_part = normed_part(far_results, 1).astype(BF16)
     from_corner = from_side(corner_part).astype(F32)
-    qkv_grads = [qkv_strips(0, corner_part)]
+    first_grads = qkv_weights(0, corner_part)
+    far_results, first_grads = lax.optimization_barrier((far_results, first_grads))
+    qkv_grads = [strips_sent(first_grads)]
     far_sum = (normed_part(far_results, 0) + from_corner).astype(BF16)
     near_results, far_results, out_rows, far_sum = lax.optimization_barrier(
         (near_results, far_results, out_rows, far_sum)
@@ -878,10 +879,15 @@
         near_sum * scaled_one + far_sum.astype(F32) * scaled_far, axis=0, keepdims=True
     )
     gain_one = sum_over(gain_one, "expert")
-    qkv_grads += [qkv_strips(pair, gain_one) for pair in range(1, pairs)]
-    grad_normed_one = near_sum + after(from_far(far_sum), gain_one).astype(F32)
+    last_grads = [qkv_weights(pair, far_sum) for pair in range(1, pairs)]
+    qkv_grads += [strips_sent(grads) for grads in last_grads]
+    far_arrived, gain_one, dense_grads, *_ = lax.optimization_barrier(
+        (from_far(far_sum), gain_one, dense_grads, *last_grads)
+    )
+    grad_normed_one = near_sum + far_arrived.astype(F32)
     grad_ln_attn = sum_over(gain_one, "tensor")[0]
-    branch_grads = strips_total(branch_grads)
+    branch_grads = strips_total(after(branch_grads, gain_one))
+    small = sum_over(branch_grads[:, heads_width:], "tensor")
     qkv_grads = jnp.stack(
         [strips_total(grads).reshape(-1, 3, PAIR) for grads in qkv_grads], axis=2
     )
@@ -894,11 +900,11 @@
         grad_ln_attn,
         qkv_grads.reshape(strip, 3, heads_width).transpose(1, 0, 2),
         branch_grads[:, :heads_width].T,
-        branch_grads[:, heads_width + experts + 2],
+        small[:, experts + 2],
         dense_grads[:, :hidden].astype(F32),
         dense_grads[:, hidden:].T.astype(F32),
-        branch_grads[:, heads_width : heads_width + experts],
-        branch_grads[:, heads_width + experts : heads_width + experts + 2],
+        small[:, :experts],
+        small[:, experts : experts + 2],
         grad_ex_up,
         grad_ex_down,
     )

time: 578 us -> 561 us (0.971)
  waiting for transfers between devices: 106 us -> 98.3 us
  matrix products: 124 us -> 118 us
  transfers between devices with their start and end apart: 51 -> 51, of which waited for: 19 -> 18; matrix products, arithmetic and copies ran while one was open for 31% -> 30% of each run, Pallas kernels for 30% -> 31%
where the time goes in v11:
time: 561 us; the launch traced here: 556 us
  Pallas kernels  173 us (31%)
  matrix products  118 us (21%)
  waiting for transfers between devices  98.3 us (18%)
  starting transfers between devices  72.5 us (13%)
  other arithmetic  64.1 us (11%)
  between operations  15.4 us (3%)
  local copies, waits for them, and re-layouts  14.2 us (3%)
    pallas_call x4, Pallas kernels, feed(): pl.pallas_call(functools.partial(feed_kernel, experts, routed), grid_spec...  106 us
    dot_general x14, matrix products, product(): return jnp.einsum('gd,gf->df', left, right, preferred_element_type=F32)  60.8 us
    ppermute x11, waiting for transfers between devices, from_far(): return lax.ppermute(values, 'tensor', [(i, i ^ 2) for i in range(4)])  54.3 us
    pallas_call x2, Pallas kernels, attention_backward(): pl.pallas_call(backward_kernel, grid_spec=pltpu.PrefetchScalarGridSpec(nu...  44.7 us
    all_to_all x8, starting transfers between devices, exchange(): lax.all_to_all(blocks, 'expert', split_axis=0, concat_axis=0, tiled=True)  39.6 us
    all_to_all x8, waiting for transfers between devices, exchange(): lax.all_to_all(blocks, 'expert', split_axis=0, concat_axis=0, tiled=True)  23.4 us
    pallas_call x1, Pallas kernels, attention_forward(): pl.pallas_call(forward_kernel, grid_spec=pltpu.PrefetchScalarGridSpec(num...  22.2 us
    ppermute x11, starting transfers between devices, from_far(): return lax.ppermute(values, 'tensor', [(i, i ^ 2) for i in range(4)])  17.7 us
  transfers between devices with their start and end apart: 51, of which 18 were waited for; matrix products, arithmetic and copies ran while one was open for 30% of the time, Pallas kernels for 31%

profile of v11, /device:TPU:0, one launch (start us, length us, event | category | flops | bytes accessed | tf_op | source)
XLA Modules:
  0.0 556.0 jit_solution(2846889586597938721)
XLA Ops:
  20.2 6.1 %all-to-all-start = ((bf16[8,112,1024]{2,1,0:T(8,128)(2,1)}), bf16[8,112,1024]{2,1,0:T(8,128)(2,1)S(1)}, u32[]{:S(2)}, u32[]{:S(2)}) async-start(bf16[8,112,1024]{2,1,0:T(8,128)(2,1)} %bitcast.189), calls=%async_computation | async-start | bytes 3670016 | tf_op jit(solution)/shard_map/all_to_all | solution.py:587
  27.7 5.8 %convolution_convert_fusion.1 = bf16[1280,3,256]{2,0,1:T(8,128)(2,1)} fusion(bf16[3,1024,256]{2,1,0:T(8,128)(2,1)} %param.19, bf16[640,1024]{1,0:T(8,128)(2,1)} %collective-permute-done.1, bf16[640,1024]{1,0:T(8,128)(2,1)} %fusion.15), kind=kOutput, calls=%fused_computation.22 | convolution fusion | flops 2019491840 | bytes 6160384 | tf_op jit(solution)/shard_map/td,sdc->stc/dot_general | solution.py:662
  33.4 11.6 %collective-permute-done = bf16[640,1024]{1,0:T(8,128)(2,1)} collective-permute-done((bf16[640,1024]{1,0:T(8,128)(2,1)}, bf16[640,1024]{1,0:T(8,128)(2,1)}, u32[]{:S(2)}, u32[]{:S(2)}) %collective-permute-start) | collective-permute-done | bytes 1310752 | tf_op jit(solution)/shard_map/ppermute | solution.py:570
  53.7 22.2 %tree_attention.1 = (bf16[2,640,256]{2,1,0:T(8,128)(2,1)}, bf16[2,640,256]{2,1,0:T(8,128)(2,1)}, f32[2,2,1024]{2,1,0:T(2,128)}, f32[2,2,2,768]{3,2,1,0:T(2,128)}) custom-call(s32[9]{0:T(128)} %pad_add_fusion.leaves_ref, bf16[3,2,640,256]{3,2,1,0:T(8,128)(2,1)} %bitcast.209, bf16[3,2,640,256]{3,2,1,0:T(8,128)(2,1)} %bitcast.212), custom_call_target="tpu_custom_call" | custom-call | flops 1241513984 | bytes 1310720 | tf_op jit(solution)/shard_map/tree_attention/pallas_call | solution.py:200
  91.5 23.7 %collective-permute-done.7 = bf16[640,1024]{1,0:T(8,128)(2,1)S(1)} collective-permute-done((bf16[640,1024]{1,0:T(8,128)(2,1)S(1)}, bf16[640,1024]{1,0:T(8,128)(2,1)S(1)}, u32[]{:S(2)}, u32[]{:S(2)}) %collective-permute-start.7) | collective-permute-done | bytes 1310752 | tf_op jit(solution)/shard_map/ppermute | solution.py:570
  119.9 6.0 %all-to-all-start.1 = ((bf16[8,112,1024]{2,1,0:T(8,128)(2,1)}), bf16[8,112,1024]{2,1,0:T(8,128)(2,1)}, u32[]{:S(2)}, u32[]{:S(2)}) async-start(bf16[8,112,1024]{2,1,0:T(8,128)(2,1)} %bitcast.190), calls=%async_computation.1 | async-start | bytes 3670016 | tf_op jit(solution)/shard_map/all_to_all | solution.py:587
  129.3 20.1 %feed_dense.2 = (bf16[640,1024]{1,0:T(8,128)(2,1)}, bf16[640,1024]{1,0:T(8,128)(2,1)}, bf16[640,1024]{1,0:T(8,128)(2,1)}, bf16[640,1024]{1,0:T(8,128)(2,1)}, bf1...) custom-call(s32[1]{0:T(128)} %constant.47.clone.1.expert_ref, ...), custom_call_target="tpu_custom_call" | custom-call | flops 1342177280 | bytes 2490368 | tf_op jit(solution)/shard_map/feed_dense/pallas_call | solution.py:495
  149.4 7.6 %fusion.23 = f32[1024,1024]{1,0:T(8,128)} fusion(bf16[1280,1024]{1,0:T(8,128)(2,1)} %bitcast.208, bf16[640,1024]{1,0:T(8,128)(2,1)} %collective-permute-done.10.side_ref, bf16[640,1024]{1,0:T(8,128)(2,1)} %copy-done.11), kind=kOutput, calls=%fused_computation.38 | convolution fusion | flops 2689597440 | bytes 9437184 | tf_op jit(solution)/shard_map/gd,gf->df/dot_general | solution.py:705
  161.4 6.7 %all-to-all-done.1 = bf16[8,112,1024]{2,1,0:T(8,128)(2,1)} async-done(((bf16[8,112,1024]{2,1,0:T(8,128)(2,1)}), bf16[8,112,1024]{2,1,0:T(8,128)(2,1)}, u32[]{:S(2)}, u32[]{:S(2)}) %all-to-all-start.1) | async-done | bytes 1835040 | tf_op jit(solution)/shard_map/all_to_all | solution.py:587
  174.0 20.2 %feed_dense.3 = (bf16[640,1024]{1,0:T(8,128)(2,1)}, bf16[640,1024]{1,0:T(8,128)(2,1)}, bf16[640,1024]{1,0:T(8,128)(2,1)}, bf16[640,1024]{1,0:T(8,128)(2,1)}, bf1...) custom-call(s32[1]{0:T(128)} %constant.47.clone.1.expert_ref, ...), custom_call_target="tpu_custom_call" | custom-call | flops 1342177280 | bytes 2490368 | tf_op jit(solution)/shard_map/feed_dense/pallas_call | solution.py:495
  201.6 9.2 %collective-permute-done.13.own_ref = bf16[896,1024]{1,0:T(8,128)(2,1)} collective-permute-done((bf16[896,1024]{1,0:T(8,128)(2,1)}, bf16[896,1024]{1,0:T(8,128)(2,1)}, u32[]{:S(2)}, u32[]{:S(2)}) %collective-permute-start.13) | collective-permute-done | bytes 1835040 | tf_op jit(solution)/shard_map/ppermute | solution.py:570
  227.5 33.1 %feed_routed.2 = (bf16[896,1024]{1,0:T(8,128)(2,1)}, bf16[896,1024]{1,0:T(8,128)(2,1)}, bf16[896,1024]{1,0:T(8,128)(2,1)}, bf16[896,1024]{1,0:T(8,128)(2,1)}, bf...) custom-call(s32[1]{0:T(128)} %bitcast.20.expert_ref, ...), custom_call_target="tpu_custom_call" | custom-call | flops 1879048192 | bytes 3276800 | tf_op jit(solution)/shard_map/feed_routed/pallas_call | solution.py:495
  271.1 33.1 %feed_routed.3 = (bf16[896,1024]{1,0:T(8,128)(2,1)}, bf16[896,1024]{1,0:T(8,128)(2,1)}, bf16[896,1024]{1,0:T(8,128)(2,1)}, bf16[896,1024]{1,0:T(8,128)(2,1)}, bf...) custom-call(s32[1]{0:T(128)} %bitcast.20.expert_ref, ...), custom_call_target="tpu_custom_call" | custom-call | flops 1879048192 | bytes 3276800 | tf_op jit(solution)/shard_map/feed_routed/pallas_call | solution.py:495
  317.4 4.8 all-to-all-start.3
  338.6 7.8 %fusion.5 = f32[1024,1024]{1,0:T(8,128)} fusion(bf16[1792,1024]{1,0:T(8,128)(2,1)S(1)} %bitcast.204, bf16[896,1024]{1,0:T(8,128)(2,1)} %collective-permute-done.15.side_ref, bf16[896,1024]{1,0:T(8,128)(2,1)} %collective-permute-done.13.own_ref), kind=kOutput, calls=%fused_computation.13 | convolution fusion | flops 3765436416 | bytes 11534336 | tf_op jit(solution)/shard_map/gd,gf->df/dot_general | solution.py:705
  346.4 5.6 add_bitcast_fusion
  352.0 13.4 %all-to-all-done.3 = bf16[8,112,1024]{2,1,0:T(8,128)(2,1)} async-done(((bf16[8,112,1024]{2,1,0:T(8,128)(2,1)}), bf16[8,112,1024]{2,1,0:T(8,128)(2,1)}, u32[]{:S(2)}, u32[]{:S(2)}) %all-to-all-start.3) | async-done | bytes 1835040 | tf_op jit(solution)/shard_map/all_to_all | solution.py:587
  365.3 5.3 multiply_reduce_fusion
  376.2 7.6 %add_bitcast_fusion.1 = f32[1,1024,1024]{2,1,0:T(8,128)} fusion(f32[1024,1024]{1,0:T(8,128)S(1)} %copy-done.59, bf16[1792,1024]{1,0:T(8,128)(2,1)S(1)} %bitcast.203, bf16[896,1024]{1,0:T(8,128)(2,1)} %collective-permute-done.20.side_ref, bf16[896,1024]{1,0:T(8,128)(2,1)} %bitcast.19.own_ref), kind=kOutput, calls=%fused_computation.4 | convolution fusion | flops 3766484992 | bytes 15728640 | tf_op jit(solution)/shard_map/gd,gf->df/dot_general | solution.py:705
  401.2 4.9 collective-permute-done.23
  418.8 22.3 %tree_attention_back.2 = (bf16[2,640,384]{2,1,0:T(8,128)(2,1)}, bf16[2,640,384]{2,1,0:T(8,128)(2,1)}) custom-call(s32[9]{0:T(128)} %pad_add_fusion.leaves_ref, bf16[3,2,640,256]{3,2,1,0:T(8,128)(2,1)} %bitcast.210, bf16[3,2,640,256]{3,2,1,0:T(8,128)(2,1)} %bitcast.213, bf16[2,640,256]{2,1,0:T(8,128)(2,1)} %pad_maximum_fusion.9.near_grads_ref, ...), custom_call_target="tpu_custom_call" | custom-call | flops 2483025920 | bytes 1048576 | tf_op jit(solution)/shard_map/tree_attention_back/pallas_call | solution.py:350
  448.0 22.5 %tree_attention_back.3 = (bf16[2,640,384]{2,1,0:T(8,128)(2,1)}, bf16[2,640,384]{2,1,0:T(8,128)(2,1)}) custom-call(s32[9]{0:T(128)} %pad_add_fusion.leaves_ref, bf16[3,2,640,256]{3,2,1,0:T(8,128)(2,1)} %bitcast.211, bf16[3,2,640,256]{3,2,1,0:T(8,128)(2,1)} %bitcast.214, bf16[2,640,256]{2,1,0:T(8,128)(2,1)} %pad_maximum_fusion.9.near_grads_ref, ...), custom_call_target="tpu_custom_call" | custom-call | flops 2483025920 | bytes 1048576 | tf_op jit(solution)/shard_map/tree_attention_back/pallas_call | solution.py:350
  486.9 6.0 %all-to-all-start.6 = ((bf16[8,128,384]{2,1,0:T(8,128)(2,1)}), bf16[8,128,384]{2,1,0:T(8,128)(2,1)}, u32[]{:S(2)}, u32[]{:S(2)}) async-start(bf16[8,128,384]{2,1,0:T(8,128)(2,1)} %bitcast.194), calls=%async_computation.7 | async-start | bytes 1572864 | tf_op jit(solution)/shard_map/all_to_all | solution.py:587
  502.5 4.9 fusion.17
  (326 shorter events, 230.2 us)
Async XLA Ops:
  12.8 32.3 %collective-permute-start = (bf16[640,1024]{1,0:T(8,128)(2,1)}, bf16[640,1024]{1,0:T(8,128)(2,1)}, u32[]{:S(2)}, u32[]{:S(2)}) collective-permute-start(bf16[640,1024]{1,0:T(8,128)(2,1)} %fusion.15), channel_id=1, source_target_pairs={{0,2},{1,3},{2,0},{3,1},{4,6},{5,7},{6,4},{7,5},{8,10},{9,11},{10,... | collective-permute-start | bytes 3932168 | tf_op jit(solution)/shard_map/ppermute | solution.py:570
  20.2 56.7 %all-to-all-start = ((bf16[8,112,1024]{2,1,0:T(8,128)(2,1)}), bf16[8,112,1024]{2,1,0:T(8,128)(2,1)S(1)}, u32[]{:S(2)}, u32[]{:S(2)}) async-start(bf16[8,112,1024]{2,1,0:T(8,128)(2,1)} %bitcast.189), calls=%async_computation | async-start | bytes 3670016 | tf_op jit(solution)/shard_map/all_to_all | solution.py:587
  45.0 30.9 %collective-permute-start.5 = (bf16[640,1024]{1,0:T(8,128)(2,1)}, bf16[640,1024]{1,0:T(8,128)(2,1)}, u32[]{:S(2)}, u32[]{:S(2)}) collective-permute-start(bf16[640,1024]{1,0:T(8,128)(2,1)} %own_grads_ref.1), channel_id=1, source_target_pairs={{0,1},{1,0},{2,3},{3,2},{4,5},{5,4},{6,7},{7,6},{8,9},{9,8},{10,11... | collective-permute-start | bytes 3932168 | tf_op jit(solution)/shard_map/ppermute | solution.py:566
  45.8 31.1 %collective-permute-start.4 = (bf16[640,1024]{1,0:T(8,128)(2,1)}, bf16[640,1024]{1,0:T(8,128)(2,1)}, u32[]{:S(2)}, u32[]{:S(2)}) collective-permute-start(bf16[640,1024]{1,0:T(8,128)(2,1)} %own_grads_ref.1), channel_id=1, source_target_pairs={{0,2},{1,3},{2,0},{3,1},{4,6},{5,7},{6,4},{7,5},{8,10},{9,11},{10,... | collective-permute-start | bytes 3932168 | tf_op jit(solution)/shard_map/ppermute | solution.py:570
  84.4 30.9 %collective-permute-start.7 = (bf16[640,1024]{1,0:T(8,128)(2,1)S(1)}, bf16[640,1024]{1,0:T(8,128)(2,1)S(1)}, u32[]{:S(2)}, u32[]{:S(2)}) collective-permute-start(bf16[640,1024]{1,0:T(8,128)(2,1)S(1)} %add_convert_fusion.11), channel_id=1, source_target_pairs={{0,2},{1,3},{2,0},{3,1},{4,6},{5,7},{6,4},{7,5},{8,10},{9,11},{10,... | collective-permute-start | bytes 3932168 | tf_op jit(solution)/shard_map/ppermute | solution.py:570
  86.7 28.6 %collective-permute-start.3 = (bf16[640,1024]{1,0:T(8,128)(2,1)S(1)}, bf16[640,1024]{1,0:T(8,128)(2,1)S(1)}, u32[]{:S(2)}, u32[]{:S(2)}) collective-permute-start(bf16[640,1024]{1,0:T(8,128)(2,1)S(1)} %convolution_convert_fusion.3), channel_id=1, source_target_pairs={{0,1},{1,0},{2,3},{3,2},{4,5},{5,4},{6,7},{7,6},{8,9},{9,8},{10,11... | collective-permute-start | bytes 3932168 | tf_op jit(solution)/shard_map/ppermute | solution.py:566
  119.9 48.2 %all-to-all-start.1 = ((bf16[8,112,1024]{2,1,0:T(8,128)(2,1)}), bf16[8,112,1024]{2,1,0:T(8,128)(2,1)}, u32[]{:S(2)}, u32[]{:S(2)}) async-start(bf16[8,112,1024]{2,1,0:T(8,128)(2,1)} %bitcast.190), calls=%async_computation.1 | async-start | bytes 3670016 | tf_op jit(solution)/shard_map/all_to_all | solution.py:587
  125.9 35.5 %collective-permute-start.11 = (bf16[640,1024]{1,0:T(8,128)(2,1)}, bf16[640,1024]{1,0:T(8,128)(2,1)}, u32[]{:S(2)}, u32[]{:S(2)}) collective-permute-start(bf16[640,1024]{1,0:T(8,128)(2,1)} %copy-done.11), channel_id=1, source_target_pairs={{0,2},{1,3},{2,0},{3,1},{4,6},{5,7},{6,4},{7,5},{8,10},{9,11},{10,... | collective-permute-start | bytes 3932168 | tf_op jit(solution)/shard_map/ppermute | solution.py:570
  168.1 42.7 %collective-permute-start.13 = (bf16[896,1024]{1,0:T(8,128)(2,1)}, bf16[896,1024]{1,0:T(8,128)(2,1)}, u32[]{:S(2)}, u32[]{:S(2)}) collective-permute-start(bf16[896,1024]{1,0:T(8,128)(2,1)} %bitcast.19.own_ref), channel_id=1, source_target_pairs={{0,2},{1,3},{2,0},{3,1},{4,6},{5,7},{6,4},{7,5},{8,10},{9,11},{10,... | collective-permute-start | bytes 5505032 | tf_op jit(solution)/shard_map/ppermute | solution.py:570
  169.6 51.0 %all-to-all-start.2 = ((bf16[8,112,1024]{2,1,0:T(8,128)(2,1)}), bf16[8,112,1024]{2,1,0:T(8,128)(2,1)}, u32[]{:S(2)}, u32[]{:S(2)}) async-start(bf16[8,112,1024]{2,1,0:T(8,128)(2,1)} %bitcast.188), calls=%async_computation.2 | async-start | bytes 3670016 | tf_op jit(solution)/shard_map/all_to_all | solution.py:587
  174.0 133.9 %reduce-scatter.2.cloned.1.call-start = ((), (), s32[]{:S(2)}) async-start(), calls=%async_computation.9 | async-start | bytes 4718592 | tf_op jit(solution)/shard_map/reduce_scatter | solution.py:592
  194.3 23.1 %collective-permute-start.14 = (bf16[640,1024]{1,0:T(8,128)(2,1)}, bf16[640,1024]{1,0:T(8,128)(2,1)}, u32[]{:S(2)}, u32[]{:S(2)}) collective-permute-start(bf16[640,1024]{1,0:T(8,128)(2,1)} %get-tuple-element.162), channel_id=1, source_target_pairs={{0,1},{1,0},{2,3},{3,2},{4,5},{5,4},{6,7},{7,6},{8,9},{9,8},{10,11... | collective-permute-start | bytes 3932168 | tf_op jit(solution)/shard_map/ppermute | solution.py:566
  221.2 39.4 %collective-permute-start.17 = (bf16[640,1024]{1,0:T(8,128)(2,1)}, bf16[640,1024]{1,0:T(8,128)(2,1)}, u32[]{:S(2)}, u32[]{:S(2)}) collective-permute-start(bf16[640,1024]{1,0:T(8,128)(2,1)} %add_convert_fusion.10), channel_id=1, source_target_pairs={{0,2},{1,3},{2,0},{3,1},{4,6},{5,7},{6,4},{7,5},{8,10},{9,11},{10,... | collective-permute-start | bytes 3932168 | tf_op jit(solution)/shard_map/ppermute | solution.py:570
  269.4 42.4 %collective-permute-start.22 = (bf16[896,1024]{1,0:T(8,128)(2,1)}, bf16[896,1024]{1,0:T(8,128)(2,1)}, u32[]{:S(2)}, u32[]{:S(2)}) collective-permute-start(bf16[896,1024]{1,0:T(8,128)(2,1)} %add_convert_fusion.4), channel_id=1, source_target_pairs={{0,2},{1,3},{2,0},{3,1},{4,6},{5,7},{6,4},{7,5},{8,10},{9,11},{10,... | collective-permute-start | bytes 5505032 | tf_op jit(solution)/shard_map/ppermute | solution.py:570
  317.0 34.9 %collective-permute-start.19 = (bf16[640,1024]{1,0:T(8,128)(2,1)}, bf16[640,1024]{1,0:T(8,128)(2,1)}, u32[]{:S(2)}, u32[]{:S(2)}) collective-permute-start(bf16[640,1024]{1,0:T(8,128)(2,1)} %get-tuple-element.183), channel_id=1, source_target_pairs={{0,1},{1,0},{2,3},{3,2},{4,5},{5,4},{6,7},{7,6},{8,9},{9,8},{10,11... | collective-permute-start | bytes 3932168 | tf_op jit(solution)/shard_map/ppermute | solution.py:566
  317.4 47.9 %all-to-all-start.3 = ((bf16[8,112,1024]{2,1,0:T(8,128)(2,1)}), bf16[8,112,1024]{2,1,0:T(8,128)(2,1)}, u32[]{:S(2)}, u32[]{:S(2)}) async-start(bf16[8,112,1024]{2,1,0:T(8,128)(2,1)} %bitcast.180), calls=%async_computation.4 | async-start | bytes 3670016 | tf_op jit(solution)/shard_map/all_to_all | solution.py:587
  322.2 63.6 %collective-permute-start.26 = (bf16[896,1024]{1,0:T(8,128)(2,1)}, bf16[896,1024]{1,0:T(8,128)(2,1)}, u32[]{:S(2)}, u32[]{:S(2)}) collective-permute-start(bf16[896,1024]{1,0:T(8,128)(2,1)} %get-tuple-element.213), channel_id=1, source_target_pairs={{0,1},{1,0},{2,3},{3,2},{4,5},{5,4},{6,7},{7,6},{8,9},{9,8},{10,11... | collective-permute-start | bytes 5505032 | tf_op jit(solution)/shard_map/ppermute | solution.py:566
  333.0 52.9 %collective-permute-start.27 = (bf16[896,1024]{1,0:T(8,128)(2,1)}, bf16[896,1024]{1,0:T(8,128)(2,1)}, u32[]{:S(2)}, u32[]{:S(2)}) collective-permute-start(bf16[896,1024]{1,0:T(8,128)(2,1)} %add_convert_fusion.2), channel_id=1, source_target_pairs={{0,2},{1,3},{2,0},{3,1},{4,6},{5,7},{6,4},{7,5},{8,10},{9,11},{10,... | collective-permute-start | bytes 5505032 | tf_op jit(solution)/shard_map/ppermute | solution.py:570
  374.6 31.5 %collective-permute-start.23 = (bf16[640,1024]{1,0:T(8,128)(2,1)}, bf16[640,1024]{1,0:T(8,128)(2,1)}, u32[]{:S(2)}, u32[]{:S(2)}) collective-permute-start(bf16[640,1024]{1,0:T(8,128)(2,1)} %get-tuple-element.343), channel_id=1, source_target_pairs={{0,2},{1,3},{2,0},{3,1},{4,6},{5,7},{6,4},{7,5},{8,10},{9,11},{10,... | collective-permute-start | bytes 3932168 | tf_op jit(solution)/shard_map/ppermute | solution.py:570
  390.4 50.7 %all-to-all-start.4 = ((bf16[8,112,1024]{2,1,0:T(8,128)(2,1)}), bf16[8,112,1024]{2,1,0:T(8,128)(2,1)}, u32[]{:S(2)}, u32[]{:S(2)}) async-start(bf16[8,112,1024]{2,1,0:T(8,128)(2,1)} %bitcast.179), calls=%async_computation.5 | async-start | bytes 3670016 | tf_op jit(solution)/shard_map/all_to_all | solution.py:587
  408.0 33.1 %collective-permute-start.31 = (bf16[640,1024]{1,0:T(8,128)(2,1)}, bf16[640,1024]{1,0:T(8,128)(2,1)}, u32[]{:S(2)}, u32[]{:S(2)}) collective-permute-start(bf16[640,1024]{1,0:T(8,128)(2,1)} %add_convert_fusion.9), channel_id=1, source_target_pairs={{0,2},{1,3},{2,0},{3,1},{4,6},{5,7},{6,4},{7,5},{8,10},{9,11},{10,... | collective-permute-start | bytes 3932168 | tf_op jit(solution)/shard_map/ppermute | solution.py:570
  441.1 29.4 %all-to-all-start.5 = ((bf16[8,128,384]{2,1,0:T(8,128)(2,1)}), bf16[8,128,384]{2,1,0:T(8,128)(2,1)}, u32[]{:S(2)}, u32[]{:S(2)}) async-start(bf16[8,128,384]{2,1,0:T(8,128)(2,1)} %bitcast.185), calls=%async_computation.6 | async-start | bytes 1572864 | tf_op jit(solution)/shard_map/all_to_all | solution.py:587
  486.9 32.8 %all-to-all-start.6 = ((bf16[8,128,384]{2,1,0:T(8,128)(2,1)}), bf16[8,128,384]{2,1,0:T(8,128)(2,1)}, u32[]{:S(2)}, u32[]{:S(2)}) async-start(bf16[8,128,384]{2,1,0:T(8,128)(2,1)} %bitcast.194), calls=%async_computation.7 | async-start | bytes 1572864 | tf_op jit(solution)/shard_map/all_to_all | solution.py:587
  492.9 31.8 %collective-permute-start.34 = (bf16[640,1024]{1,0:T(8,128)(2,1)}, bf16[640,1024]{1,0:T(8,128)(2,1)}, u32[]{:S(2)}, u32[]{:S(2)}) collective-permute-start(bf16[640,1024]{1,0:T(8,128)(2,1)} %add_convert_fusion.7), channel_id=1, source_target_pairs={{0,2},{1,3},{2,0},{3,1},{4,6},{5,7},{6,4},{7,5},{8,10},{9,11},{10,... | collective-permute-start | bytes 3932168 | tf_op jit(solution)/shard_map/ppermute | solution.py:570
  (87 other events, 644.6 us)
Sparse Core Ops, SparseCore 0:
  220.8 86.9 reduce-scatter.1

commit v12 on v11

--- a/solution.py
+++ b/solution.py
@@ -143,6 +143,7 @@
     leaves_ref,
     near_ref,
     far_ref,
+    corner_ref,
     near_out_ref,
     far_out_ref,
     trunk_log_ref,
@@ -152,8 +153,8 @@
     values_t_ref,
 ):
     for offset in range(4):
-        half_ref = near_ref if offset < 2 else far_ref
-        qkv_ref[:, quarter_rows(leaves_ref, offset), :] = half_ref[:, offset % 2]
+        part = near_ref[:, offset] if offset < 2 else (far_ref, corner_ref)[offset - 2][...]
+        qkv_ref[:, quarter_rows(leaves_ref, offset), :] = part
     transpose_into(values_t_ref, qkv_ref, 2)
     for block in range(TRUNK // QROWS):
         first = block * QROWS
@@ -177,11 +178,9 @@
         half_ref[offset % 2] = out_ref[quarter_rows(leaves_ref, offset), :]
 
 
-def halves_spec(parts):
+def lanes_spec(parts):
     quarter = TREE_LEN // 4
-    if parts == 1:
-        return pl.BlockSpec((2, quarter, PAIR), lambda p, leaves: (0, 0, p))
-    return pl.BlockSpec((parts, 2, quarter, PAIR), lambda p, leaves: (0, 0, 0, p))
+    return pl.BlockSpec((parts, quarter, PAIR), lambda p, leaves: (0, 0, p))
 
 
 def attention_cost(products, cover):
@@ -193,7 +192,7 @@
     )
 
 
-def attention_forward(leaves, near, far):
+def attention_forward(leaves, near, far, corner):
     width = near.shape[3]
     quarter = TREE_LEN // 4
     pairs = width // PAIR
@@ -202,10 +201,14 @@
         grid_spec=pltpu.PrefetchScalarGridSpec(
             num_scalar_prefetch=1,
             grid=(pairs,),
-            in_specs=[halves_spec(3), halves_spec(3)],
+            in_specs=[
+                pl.BlockSpec((3, 2, quarter, PAIR), lambda p, leaves: (0, 0, 0, p)),
+                lanes_spec(3),
+                lanes_spec(3),
+            ],
             out_specs=[
-                halves_spec(1),
-                halves_spec(1),
+                lanes_spec(2),
+                lanes_spec(2),
                 pl.BlockSpec((1, 2, TRUNK), lambda p, leaves: (p, 0, 0)),
                 pl.BlockSpec((1, TEAMS, 2, TEAM), lambda p, leaves: (p, 0, 0, 0)),
             ],
@@ -223,7 +226,7 @@
         ],
         cost_estimate=attention_cost(2, COVER),
         name="tree_attention",
-    )(leaves, near, far)
+    )(leaves, near, far, corner)
 
 
 def backward_block(qkv_ref, keys_t_ref, queries, grads, outs, logs, groups):
@@ -267,6 +270,7 @@
     leaves_ref,
     near_ref,
     far_ref,
+    corner_ref,
     near_grads_ref,
     far_grads_ref,
     near_outs_ref,
@@ -286,7 +290,8 @@
     for offset in range(4):
         rows = quarter_rows(leaves_ref, offset)
         at = offset % 2
-        qkv_ref[:, rows, :] = (near_ref if offset < 2 else far_ref)[:, at]
+        part = near_ref[:, at] if offset < 2 else (far_ref, corner_ref)[at][...]
+        qkv_ref[:, rows, :] = part
         grads_ref[rows, :] = (near_grads_ref if offset < 2 else far_grads_ref)[at]
         outs_ref[rows, :] = (near_outs_ref if offset < 2 else far_outs_ref)[at]
     transpose_into(keys_t_ref, qkv_ref, 1)
@@ -341,10 +346,10 @@
             half_ref[offset % 2, :, part * PAIR : (part + 1) * PAIR] = result_ref[part, rows, :]
 
 
-def attention_backward(leaves, pair, near, far, near_grads, far_grads, near_outs, far_outs, logs):
+def attention_backward(leaves, pair, qkv, near_grads, far_grads, near_outs, far_outs, logs):
     quarter = TREE_LEN // 4
     rows = pl.BlockSpec((2, quarter, PAIR), lambda i, leaves: (0, 0, pair))
-    parts = pl.BlockSpec((3, 2, quarter, PAIR), lambda i, leaves: (0, 0, 0, pair))
+    parts = pl.BlockSpec((3, quarter, PAIR), lambda i, leaves: (0, 0, pair))
     result = pl.BlockSpec((2, quarter, 3 * PAIR), lambda i, leaves: (0, 0, 0))
     shape = jax.ShapeDtypeStruct((2, quarter, 3 * PAIR), BF16)
     return pl.pallas_call(
@@ -353,6 +358,7 @@
             num_scalar_prefetch=1,
             grid=(1,),
             in_specs=[
+                pl.BlockSpec((3, 2, quarter, PAIR), lambda i, leaves: (0, 0, 0, pair)),
                 parts,
                 parts,
                 rows,
@@ -376,7 +382,7 @@
         out_shape=[shape, shape],
         cost_estimate=attention_cost(5, 10),
         name="tree_attention_back",
-    )(leaves, near, far, near_grads, far_grads, near_outs, far_outs, *logs)
+    )(leaves, *qkv, near_grads, far_grads, near_outs, far_outs, *logs)
 
 
 def leaf_order(parents_row):
@@ -659,19 +665,19 @@
     cotangent_side = from_side(cotangent)
 
     def project(rows):
-        qkv = jnp.einsum("td,sdc->stc", rows, w_qkv, preferred_element_type=F32)
-        return qkv.astype(BF16).reshape(3, 2, tok_dev, heads_width)
+        return jnp.einsum("td,sdc->stc", rows, w_qkv, preferred_element_type=F32).astype(BF16)
 
     lanes = -(-(experts + 2) // LANES) * LANES
     head = jnp.concatenate(
         [w_router, w_mix, jnp.zeros((width, lanes - experts - 2), BF16)], axis=1
     )
-    near_qkv = project(near_one)
+    near_qkv = project(near_one).reshape(3, 2, tok_dev, heads_width)
     cotangent_far = from_far(after(cotangent, normed_far))
     normed_far, near_qkv, head = lax.optimization_barrier((normed_far, near_qkv, head))
-    far_one = jnp.concatenate([normed_far, from_side(normed_far)], axis=0)
-    far_qkv = project(far_one)
-    near_out, far_out, *logs = attention_forward(leaves, near_qkv, far_qkv)
+    normed_corner = from_side(normed_far)
+    qkv = near_qkv, project(normed_far), project(normed_corner)
+    near_out, far_out, *logs = attention_forward(leaves, *qkv)
+    far_one = jnp.concatenate([normed_far, normed_corner], axis=0)
     far_out, own_grads, cotangent_far, cotangent_side = lax.optimization_barrier(
         (far_out, own_grads, cotangent_far, cotangent_side)
     )
@@ -744,7 +750,7 @@
     dense_back_far = chip_sum(far_dense, 2).astype(BF16)
     far_two = jnp.concatenate([normed_two_far, normed_two_corner], axis=0)
     grad_down = (grad_down + product(far_dense[6], far_dense[4])).astype(BF16)
-    far_two, far_rows, grad_down = lax.optimization_barrier((far_two, far_rows, grad_down))
+    far_two, grad_down = lax.optimization_barrier((far_two, grad_down))
     grad_up = (grad_up + product(far_two, far_dense[5])).astype(BF16)
     dense_grads = after(jnp.concatenate([grad_up, grad_down], axis=1), far_grads)
     far_rows, dense_back_far, dense_grads = lax.optimization_barrier(
@@ -823,7 +829,7 @@
 
     def pair_back(pair, near_grads, far_grads):
         return attention_backward(
-            leaves, pair, near_qkv, far_qkv, near_grads, far_grads, near_out, far_out, logs
+            leaves, pair, qkv, near_grads, far_grads, near_out, far_out, logs
         )
 
     def pair_weights(pair):
@@ -868,9 +874,12 @@
     far_results, first_grads = lax.optimization_barrier((far_results, first_grads))
     qkv_grads = [strips_sent(first_grads)]
     far_sum = (normed_part(far_results, 0) + from_corner).astype(BF16)
-    near_results, far_results, out_rows, far_sum = lax.optimization_barrier(
-        (near_results, far_results, out_rows, far_sum)
-    )
+    near_results, far_results, far_sum = lax.optimization_barrier(
+        (near_results, far_results, far_sum)
+    )
+    last_grads = [qkv_weights(pair, far_sum) for pair in range(1, pairs)]
+    out_rows, *last_grads = lax.optimization_barrier((out_rows, *last_grads))
+    qkv_grads += [strips_sent(grads) for grads in last_grads]
     near_sum = plus_side(normed_part(near_results, 0), normed_part(near_results, 1))
     out = (residual + dense_out + dense_out_far.astype(F32) + picked(out_rows)).astype(BF16)
 
@@ -879,8 +888,6 @@
         near_sum * scaled_one + far_sum.astype(F32) * scaled_far, axis=0, keepdims=True
     )
     gain_one = sum_over(gain_one, "expert")
-    last_grads = [qkv_weights(pair, far_sum) for pair in range(1, pairs)]
-    qkv_grads += [strips_sent(grads) for grads in last_grads]
     far_arrived, gain_one, dense_grads, *_ = lax.optimization_barrier(
         (from_far(far_sum), gain_one, dense_grads, *last_grads)
     )

time: 561 us -> 571 us (1.018)
  waiting for transfers between devices: 98.3 us -> 109 us
  starting transfers between devices: 72.5 us -> 66.7 us
    unnamed x128 -> x142, local copies, waits for them, and re-layouts: 9.65 us -> 12.9 us
    dot_general x2 -> x3, matrix products: 9.26 us -> 11.4 us  [project(): jnp.einsum('td,sdc->stc', rows, w_qkv, preferred_element_type=F32)]
  transfers between devices with their start and end apart: 51 -> 51, of which waited for: 18 -> 16; matrix products, arithmetic and copies ran while one was open for 30% -> 30% of each run, Pallas kernels for 31% -> 31%
where the time goes in v12:
time: 571 us; the launch traced here: 567 us
  Pallas kernels  173 us (30%)
  matrix products  121 us (21%)
  waiting for transfers between devices  109 us (19%)
  starting transfers between devices  66.7 us (12%)
  other arithmetic  63.9 us (11%)
  local copies, waits for them, and re-layouts  17.5 us (3%)
  between operations  15.5 us (3%)
    pallas_call x4, Pallas kernels, feed(): pl.pallas_call(functools.partial(feed_kernel, experts, routed), grid_spec...  107 us
    dot_general x14, matrix products, product(): return jnp.einsum('gd,gf->df', left, right, preferred_element_type=F32)  63 us
    ppermute x11, waiting for transfers between devices, from_far(): return lax.ppermute(values, 'tensor', [(i, i ^ 2) for i in range(4)])  56.8 us
    pallas_call x2, Pallas kernels, attention_backward(): pl.pallas_call(backward_kernel, grid_spec=pltpu.PrefetchScalarGridSpec(nu...  44.7 us
    all_to_all x8, starting transfers between devices, exchange(): lax.all_to_all(blocks, 'expert', split_axis=0, concat_axis=0, tiled=True)  40.5 us
    all_to_all x8, waiting for transfers between devices, exchange(): lax.all_to_all(blocks, 'expert', split_axis=0, concat_axis=0, tiled=True)  29 us
    pallas_call x1, Pallas kernels, attention_forward(): pl.pallas_call(forward_kernel, grid_spec=pltpu.PrefetchScalarGridSpec(num...  22.2 us
    ppermute x24, waiting for transfers between devices, from_side(): return lax.ppermute(values, 'tensor', [(i, i ^ 1) for i in range(4)])  15.9 us
  transfers between devices with their start and end apart: 51, of which 16 were waited for; matrix products, arithmetic and copies ran while one was open for 30% of the time, Pallas kernels for 31%

profile of v12, /device:TPU:0, one launch (start us, length us, event | category | flops | bytes accessed | tf_op | source)
XLA Modules:
  0.0 566.5 jit_solution(161617835368203332)
XLA Ops:
  17.6 7.2 %all-to-all-start = ((bf16[8,112,1024]{2,1,0:T(8,128)(2,1)}), bf16[8,112,1024]{2,1,0:T(8,128)(2,1)S(1)}, u32[]{:S(2)}, u32[]{:S(2)}) async-start(bf16[8,112,1024]{2,1,0:T(8,128)(2,1)} %bitcast.194), calls=%async_computation | async-start | bytes 3670016 | tf_op jit(solution)/shard_map/all_to_all | solution.py:593
  27.7 5.8 %convolution_convert_fusion = bf16[1280,3,256]{2,0,1:T(8,128)(2,1)} fusion(bf16[3,1024,256]{2,1,0:T(8,128)(2,1)} %param.19, bf16[640,1024]{1,0:T(8,128)(2,1)} %collective-permute-done.1, bf16[640,1024]{1,0:T(8,128)(2,1)} %fusion.15), kind=kOutput, calls=%fused_computation.21 | convolution fusion | flops 2019491840 | bytes 6160384 | tf_op jit(solution)/shard_map/td,sdc->stc/dot_general | solution.py:668
  33.5 22.5 %collective-permute-done = bf16[640,1024]{1,0:T(8,128)(2,1)} collective-permute-done((bf16[640,1024]{1,0:T(8,128)(2,1)}, bf16[640,1024]{1,0:T(8,128)(2,1)}, u32[]{:S(2)}, u32[]{:S(2)}) %collective-permute-start) | collective-permute-done | bytes 1310752 | tf_op jit(solution)/shard_map/ppermute | solution.py:576
  65.9 22.2 %tree_attention.1 = (bf16[2,640,256]{2,1,0:T(8,128)(2,1)}, bf16[2,640,256]{2,1,0:T(8,128)(2,1)}, f32[2,2,1024]{2,1,0:T(2,128)}, f32[2,2,2,768]{3,2,1,0:T(2,128)}) custom-call(s32[9]{0:T(128)} %pad_add_fusion.leaves_ref, bf16[3,2,640,256]{3,2,1,0:T(8,128)(2,1)} %bitcast.215, bf16[3,640,256]{2,1,0:T(8,128)(2,1)} %fusion.48.far_ref, ...), custom_call_target="tpu_custom_call" | custom-call | flops 1241513984 | bytes 1310720 | tf_op jit(solution)/shard_map/tree_attention/pallas_call | solution.py:199
  102.1 24.4 %collective-permute-done.7 = bf16[640,1024]{1,0:T(8,128)(2,1)S(1)} collective-permute-done((bf16[640,1024]{1,0:T(8,128)(2,1)S(1)}, bf16[640,1024]{1,0:T(8,128)(2,1)S(1)}, u32[]{:S(2)}, u32[]{:S(2)}) %collective-permute-start.7) | collective-permute-done | bytes 1310752 | tf_op jit(solution)/shard_map/ppermute | solution.py:576
  131.1 5.7 %all-to-all-start.1 = ((bf16[8,112,1024]{2,1,0:T(8,128)(2,1)}), bf16[8,112,1024]{2,1,0:T(8,128)(2,1)}, u32[]{:S(2)}, u32[]{:S(2)}) async-start(bf16[8,112,1024]{2,1,0:T(8,128)(2,1)} %bitcast.195), calls=%async_computation.1 | async-start | bytes 3670016 | tf_op jit(solution)/shard_map/all_to_all | solution.py:593
  140.2 20.1 %feed_dense.2 = (bf16[640,1024]{1,0:T(8,128)(2,1)}, bf16[640,1024]{1,0:T(8,128)(2,1)}, bf16[640,1024]{1,0:T(8,128)(2,1)}, bf16[640,1024]{1,0:T(8,128)(2,1)}, bf1...) custom-call(s32[1]{0:T(128)} %constant.47.clone.1.expert_ref, ...), custom_call_target="tpu_custom_call" | custom-call | flops 1342177280 | bytes 2490368 | tf_op jit(solution)/shard_map/feed_dense/pallas_call | solution.py:501
  160.3 7.6 %fusion.23 = f32[1024,1024]{1,0:T(8,128)} fusion(bf16[1280,1024]{1,0:T(8,128)(2,1)} %bitcast.214, bf16[640,1024]{1,0:T(8,128)(2,1)} %collective-permute-done.10.side_ref, bf16[640,1024]{1,0:T(8,128)(2,1)} %copy-done.13), kind=kOutput, calls=%fused_computation.37 | convolution fusion | flops 2689597440 | bytes 9437184 | tf_op jit(solution)/shard_map/gd,gf->df/dot_general | solution.py:711
  172.4 6.6 %all-to-all-done.1 = bf16[8,112,1024]{2,1,0:T(8,128)(2,1)} async-done(((bf16[8,112,1024]{2,1,0:T(8,128)(2,1)}), bf16[8,112,1024]{2,1,0:T(8,128)(2,1)}, u32[]{:S(2)}, u32[]{:S(2)}) %all-to-all-start.1) | async-done | bytes 1835040 | tf_op jit(solution)/shard_map/all_to_all | solution.py:593
  184.5 20.2 %feed_dense.3 = (bf16[640,1024]{1,0:T(8,128)(2,1)}, bf16[640,1024]{1,0:T(8,128)(2,1)}, bf16[640,1024]{1,0:T(8,128)(2,1)}, bf16[640,1024]{1,0:T(8,128)(2,1)}, bf1...) custom-call(s32[1]{0:T(128)} %constant.47.clone.1.expert_ref, ...), custom_call_target="tpu_custom_call" | custom-call | flops 1342177280 | bytes 2490368 | tf_op jit(solution)/shard_map/feed_dense/pallas_call | solution.py:501
  222.6 5.1 all-to-all-done.2
  234.6 33.1 %feed_routed.2 = (bf16[896,1024]{1,0:T(8,128)(2,1)}, bf16[896,1024]{1,0:T(8,128)(2,1)}, bf16[896,1024]{1,0:T(8,128)(2,1)}, bf16[896,1024]{1,0:T(8,128)(2,1)}, bf...) custom-call(s32[1]{0:T(128)} %bitcast.21.expert_ref, ...), custom_call_target="tpu_custom_call" | custom-call | flops 1879048192 | bytes 3276800 | tf_op jit(solution)/shard_map/feed_routed/pallas_call | solution.py:501
  268.3 4.8 collective-permute-done.18
  277.5 33.1 %feed_routed.3 = (bf16[896,1024]{1,0:T(8,128)(2,1)}, bf16[896,1024]{1,0:T(8,128)(2,1)}, bf16[896,1024]{1,0:T(8,128)(2,1)}, bf16[896,1024]{1,0:T(8,128)(2,1)}, bf...) custom-call(s32[1]{0:T(128)} %bitcast.21.expert_ref, ...), custom_call_target="tpu_custom_call" | custom-call | flops 1879048192 | bytes 3276800 | tf_op jit(solution)/shard_map/feed_routed/pallas_call | solution.py:501
  345.1 7.8 %fusion.5 = f32[1024,1024]{1,0:T(8,128)} fusion(bf16[1792,1024]{1,0:T(8,128)(2,1)S(1)} %bitcast.210, bf16[896,1024]{1,0:T(8,128)(2,1)} %collective-permute-done.15.side_ref, bf16[896,1024]{1,0:T(8,128)(2,1)} %collective-permute-done.12.own_ref), kind=kOutput, calls=%fused_computation.13 | convolution fusion | flops 3765436416 | bytes 11534336 | tf_op jit(solution)/shard_map/gd,gf->df/dot_general | solution.py:711
  352.9 5.6 add_bitcast_fusion
  358.5 13.9 %all-to-all-done.3 = bf16[8,112,1024]{2,1,0:T(8,128)(2,1)} async-done(((bf16[8,112,1024]{2,1,0:T(8,128)(2,1)}), bf16[8,112,1024]{2,1,0:T(8,128)(2,1)}, u32[]{:S(2)}, u32[]{:S(2)}) %all-to-all-start.3) | async-done | bytes 1835040 | tf_op jit(solution)/shard_map/all_to_all | solution.py:593
  372.4 5.3 multiply_reduce_fusion
  382.8 7.6 %add_bitcast_fusion.1 = f32[1,1024,1024]{2,1,0:T(8,128)} fusion(f32[1024,1024]{1,0:T(8,128)S(1)} %copy-done.66, bf16[1792,1024]{1,0:T(8,128)(2,1)S(1)} %bitcast.209, bf16[896,1024]{1,0:T(8,128)(2,1)} %collective-permute-done.20.side_ref, bf16[896,1024]{1,0:T(8,128)(2,1)} %bitcast.20.own_ref), kind=kOutput, calls=%fused_computation.4 | convolution fusion | flops 3766484992 | bytes 15728640 | tf_op jit(solution)/shard_map/gd,gf->df/dot_general | solution.py:711
  407.8 5.4 collective-permute-done.23
  425.4 22.2 %tree_attention_back.2 = (bf16[2,640,384]{2,1,0:T(8,128)(2,1)}, bf16[2,640,384]{2,1,0:T(8,128)(2,1)}) custom-call(s32[9]{0:T(128)} %pad_add_fusion.leaves_ref, bf16[3,2,640,256]{3,2,1,0:T(8,128)(2,1)} %bitcast.216, bf16[3,640,256]{2,1,0:T(8,128)(2,1)} %fusion.48.far_ref, bf16[3,640,256]{2,1,0:T(8,128)(2,1)} %fusion.49.corner_ref, ...), custom_call_target="tpu_custom_call" | custom-call | flops 2483025920 | bytes 1048576 | tf_op jit(solution)/shard_map/tree_attention_back/pallas_call | solution.py:355
  454.5 22.5 %tree_attention_back.3 = (bf16[2,640,384]{2,1,0:T(8,128)(2,1)}, bf16[2,640,384]{2,1,0:T(8,128)(2,1)}) custom-call(s32[9]{0:T(128)} %pad_add_fusion.leaves_ref, bf16[3,2,640,256]{3,2,1,0:T(8,128)(2,1)} %bitcast.217, bf16[3,640,256]{2,1,0:T(8,128)(2,1)} %fusion.48.far_ref, bf16[3,640,256]{2,1,0:T(8,128)(2,1)} %fusion.49.corner_ref, ...), custom_call_target="tpu_custom_call" | custom-call | flops 2483025920 | bytes 1048576 | tf_op jit(solution)/shard_map/tree_attention_back/pallas_call | solution.py:355
  495.6 6.2 %all-to-all-start.6 = ((bf16[8,128,384]{2,1,0:T(8,128)(2,1)}), bf16[8,128,384]{2,1,0:T(8,128)(2,1)}, u32[]{:S(2)}, u32[]{:S(2)}) async-start(bf16[8,128,384]{2,1,0:T(8,128)(2,1)} %bitcast.200), calls=%async_computation.7 | async-start | bytes 1572864 | tf_op jit(solution)/shard_map/all_to_all | solution.py:593
  512.8 4.8 fusion.17
  (341 shorter events, 231.4 us)
Async XLA Ops:
  17.6 70.5 %all-to-all-start = ((bf16[8,112,1024]{2,1,0:T(8,128)(2,1)}), bf16[8,112,1024]{2,1,0:T(8,128)(2,1)S(1)}, u32[]{:S(2)}, u32[]{:S(2)}) async-start(bf16[8,112,1024]{2,1,0:T(8,128)(2,1)} %bitcast.194), calls=%async_computation | async-start | bytes 3670016 | tf_op jit(solution)/shard_map/all_to_all | solution.py:593
  24.8 31.3 %collective-permute-start = (bf16[640,1024]{1,0:T(8,128)(2,1)}, bf16[640,1024]{1,0:T(8,128)(2,1)}, u32[]{:S(2)}, u32[]{:S(2)}) collective-permute-start(bf16[640,1024]{1,0:T(8,128)(2,1)} %fusion.15), channel_id=1, source_target_pairs={{0,2},{1,3},{2,0},{3,1},{4,6},{5,7},{6,4},{7,5},{8,10},{9,11},{10,... | collective-permute-start | bytes 3932168 | tf_op jit(solution)/shard_map/ppermute | solution.py:576
  56.1 32.0 %collective-permute-start.5 = (bf16[640,1024]{1,0:T(8,128)(2,1)}, bf16[640,1024]{1,0:T(8,128)(2,1)}, u32[]{:S(2)}, u32[]{:S(2)}) collective-permute-start(bf16[640,1024]{1,0:T(8,128)(2,1)} %own_grads_ref.1), channel_id=1, source_target_pairs={{0,1},{1,0},{2,3},{3,2},{4,5},{5,4},{6,7},{7,6},{8,9},{9,8},{10,11... | collective-permute-start | bytes 3932168 | tf_op jit(solution)/shard_map/ppermute | solution.py:572
  56.7 31.4 %collective-permute-start.4 = (bf16[640,1024]{1,0:T(8,128)(2,1)}, bf16[640,1024]{1,0:T(8,128)(2,1)}, u32[]{:S(2)}, u32[]{:S(2)}) collective-permute-start(bf16[640,1024]{1,0:T(8,128)(2,1)} %own_grads_ref.1), channel_id=1, source_target_pairs={{0,2},{1,3},{2,0},{3,1},{4,6},{5,7},{6,4},{7,5},{8,10},{9,11},{10,... | collective-permute-start | bytes 3932168 | tf_op jit(solution)/shard_map/ppermute | solution.py:576
  95.6 30.9 %collective-permute-start.7 = (bf16[640,1024]{1,0:T(8,128)(2,1)S(1)}, bf16[640,1024]{1,0:T(8,128)(2,1)S(1)}, u32[]{:S(2)}, u32[]{:S(2)}) collective-permute-start(bf16[640,1024]{1,0:T(8,128)(2,1)S(1)} %add_convert_fusion.11), channel_id=1, source_target_pairs={{0,2},{1,3},{2,0},{3,1},{4,6},{5,7},{6,4},{7,5},{8,10},{9,11},{10,... | collective-permute-start | bytes 3932168 | tf_op jit(solution)/shard_map/ppermute | solution.py:576
  97.3 29.2 %collective-permute-start.3 = (bf16[640,1024]{1,0:T(8,128)(2,1)S(1)}, bf16[640,1024]{1,0:T(8,128)(2,1)S(1)}, u32[]{:S(2)}, u32[]{:S(2)}) collective-permute-start(bf16[640,1024]{1,0:T(8,128)(2,1)S(1)} %convolution_convert_fusion.2), channel_id=1, source_target_pairs={{0,1},{1,0},{2,3},{3,2},{4,5},{5,4},{6,7},{7,6},{8,9},{9,8},{10,11... | collective-permute-start | bytes 3932168 | tf_op jit(solution)/shard_map/ppermute | solution.py:572
  131.1 47.9 %all-to-all-start.1 = ((bf16[8,112,1024]{2,1,0:T(8,128)(2,1)}), bf16[8,112,1024]{2,1,0:T(8,128)(2,1)}, u32[]{:S(2)}, u32[]{:S(2)}) async-start(bf16[8,112,1024]{2,1,0:T(8,128)(2,1)} %bitcast.195), calls=%async_computation.1 | async-start | bytes 3670016 | tf_op jit(solution)/shard_map/all_to_all | solution.py:593
  136.9 35.5 %collective-permute-start.11 = (bf16[640,1024]{1,0:T(8,128)(2,1)}, bf16[640,1024]{1,0:T(8,128)(2,1)}, u32[]{:S(2)}, u32[]{:S(2)}) collective-permute-start(bf16[640,1024]{1,0:T(8,128)(2,1)} %copy-done.13), channel_id=1, source_target_pairs={{0,2},{1,3},{2,0},{3,1},{4,6},{5,7},{6,4},{7,5},{8,10},{9,11},{10,... | collective-permute-start | bytes 3932168 | tf_op jit(solution)/shard_map/ppermute | solution.py:576
  179.1 48.7 %collective-permute-start.12 = (bf16[896,1024]{1,0:T(8,128)(2,1)}, bf16[896,1024]{1,0:T(8,128)(2,1)}, u32[]{:S(2)}, u32[]{:S(2)}) collective-permute-start(bf16[896,1024]{1,0:T(8,128)(2,1)} %bitcast.20.own_ref), channel_id=1, source_target_pairs={{0,2},{1,3},{2,0},{3,1},{4,6},{5,7},{6,4},{7,5},{8,10},{9,11},{10,... | collective-permute-start | bytes 5505032 | tf_op jit(solution)/shard_map/ppermute | solution.py:576
  180.1 47.6 %all-to-all-start.2 = ((bf16[8,112,1024]{2,1,0:T(8,128)(2,1)}), bf16[8,112,1024]{2,1,0:T(8,128)(2,1)}, u32[]{:S(2)}, u32[]{:S(2)}) async-start(bf16[8,112,1024]{2,1,0:T(8,128)(2,1)} %bitcast.193), calls=%async_computation.2 | async-start | bytes 3670016 | tf_op jit(solution)/shard_map/all_to_all | solution.py:593
  184.4 130.1 %reduce-scatter.2.cloned.1.call-start = ((), (), s32[]{:S(2)}) async-start(), calls=%async_computation.9 | async-start | bytes 4718592 | tf_op jit(solution)/shard_map/reduce_scatter | solution.py:598
  228.3 39.4 %collective-permute-start.17 = (bf16[640,1024]{1,0:T(8,128)(2,1)}, bf16[640,1024]{1,0:T(8,128)(2,1)}, u32[]{:S(2)}, u32[]{:S(2)}) collective-permute-start(bf16[640,1024]{1,0:T(8,128)(2,1)} %add_convert_fusion.10), channel_id=1, source_target_pairs={{0,2},{1,3},{2,0},{3,1},{4,6},{5,7},{6,4},{7,5},{8,10},{9,11},{10,... | collective-permute-start | bytes 3932168 | tf_op jit(solution)/shard_map/ppermute | solution.py:576
  276.7 42.4 %collective-permute-start.22 = (bf16[896,1024]{1,0:T(8,128)(2,1)}, bf16[896,1024]{1,0:T(8,128)(2,1)}, u32[]{:S(2)}, u32[]{:S(2)}) collective-permute-start(bf16[896,1024]{1,0:T(8,128)(2,1)} %add_convert_fusion.4), channel_id=1, source_target_pairs={{0,2},{1,3},{2,0},{3,1},{4,6},{5,7},{6,4},{7,5},{8,10},{9,11},{10,... | collective-permute-start | bytes 5505032 | tf_op jit(solution)/shard_map/ppermute | solution.py:576
  324.1 34.4 %collective-permute-start.19 = (bf16[640,1024]{1,0:T(8,128)(2,1)}, bf16[640,1024]{1,0:T(8,128)(2,1)}, u32[]{:S(2)}, u32[]{:S(2)}) collective-permute-start(bf16[640,1024]{1,0:T(8,128)(2,1)} %get-tuple-element.182), channel_id=1, source_target_pairs={{0,1},{1,0},{2,3},{3,2},{4,5},{5,4},{6,7},{7,6},{8,9},{9,8},{10,11... | collective-permute-start | bytes 3932168 | tf_op jit(solution)/shard_map/ppermute | solution.py:572
  324.6 47.8 %all-to-all-start.3 = ((bf16[8,112,1024]{2,1,0:T(8,128)(2,1)}), bf16[8,112,1024]{2,1,0:T(8,128)(2,1)}, u32[]{:S(2)}, u32[]{:S(2)}) async-start(bf16[8,112,1024]{2,1,0:T(8,128)(2,1)} %bitcast.185), calls=%async_computation.4 | async-start | bytes 3670016 | tf_op jit(solution)/shard_map/all_to_all | solution.py:593
  329.4 63.1 %collective-permute-start.26 = (bf16[896,1024]{1,0:T(8,128)(2,1)}, bf16[896,1024]{1,0:T(8,128)(2,1)}, u32[]{:S(2)}, u32[]{:S(2)}) collective-permute-start(bf16[896,1024]{1,0:T(8,128)(2,1)} %get-tuple-element.212), channel_id=1, source_target_pairs={{0,1},{1,0},{2,3},{3,2},{4,5},{5,4},{6,7},{7,6},{8,9},{9,8},{10,11... | collective-permute-start | bytes 5505032 | tf_op jit(solution)/shard_map/ppermute | solution.py:572
  340.0 52.4 %collective-permute-start.27 = (bf16[896,1024]{1,0:T(8,128)(2,1)}, bf16[896,1024]{1,0:T(8,128)(2,1)}, u32[]{:S(2)}, u32[]{:S(2)}) collective-permute-start(bf16[896,1024]{1,0:T(8,128)(2,1)} %add_convert_fusion.2), channel_id=1, source_target_pairs={{0,2},{1,3},{2,0},{3,1},{4,6},{5,7},{6,4},{7,5},{8,10},{9,11},{10,... | collective-permute-start | bytes 5505032 | tf_op jit(solution)/shard_map/ppermute | solution.py:576
  381.7 31.5 %collective-permute-start.23 = (bf16[640,1024]{1,0:T(8,128)(2,1)}, bf16[640,1024]{1,0:T(8,128)(2,1)}, u32[]{:S(2)}, u32[]{:S(2)}) collective-permute-start(bf16[640,1024]{1,0:T(8,128)(2,1)} %get-tuple-element.343), channel_id=1, source_target_pairs={{0,2},{1,3},{2,0},{3,1},{4,6},{5,7},{6,4},{7,5},{8,10},{9,11},{10,... | collective-permute-start | bytes 3932168 | tf_op jit(solution)/shard_map/ppermute | solution.py:576
  397.1 50.6 %all-to-all-start.4 = ((bf16[8,112,1024]{2,1,0:T(8,128)(2,1)}), bf16[8,112,1024]{2,1,0:T(8,128)(2,1)}, u32[]{:S(2)}, u32[]{:S(2)}) async-start(bf16[8,112,1024]{2,1,0:T(8,128)(2,1)} %bitcast.184), calls=%async_computation.5 | async-start | bytes 3670016 | tf_op jit(solution)/shard_map/all_to_all | solution.py:593
  415.0 32.6 %collective-permute-start.31 = (bf16[640,1024]{1,0:T(8,128)(2,1)}, bf16[640,1024]{1,0:T(8,128)(2,1)}, u32[]{:S(2)}, u32[]{:S(2)}) collective-permute-start(bf16[640,1024]{1,0:T(8,128)(2,1)} %add_convert_fusion.9), channel_id=1, source_target_pairs={{0,2},{1,3},{2,0},{3,1},{4,6},{5,7},{6,4},{7,5},{8,10},{9,11},{10,... | collective-permute-start | bytes 3932168 | tf_op jit(solution)/shard_map/ppermute | solution.py:576
  447.6 29.4 %all-to-all-start.5 = ((bf16[8,128,384]{2,1,0:T(8,128)(2,1)}), bf16[8,128,384]{2,1,0:T(8,128)(2,1)}, u32[]{:S(2)}, u32[]{:S(2)}) async-start(bf16[8,128,384]{2,1,0:T(8,128)(2,1)} %bitcast.190), calls=%async_computation.6 | async-start | bytes 1572864 | tf_op jit(solution)/shard_map/all_to_all | solution.py:593
  495.6 34.6 %all-to-all-start.6 = ((bf16[8,128,384]{2,1,0:T(8,128)(2,1)}), bf16[8,128,384]{2,1,0:T(8,128)(2,1)}, u32[]{:S(2)}, u32[]{:S(2)}) async-start(bf16[8,128,384]{2,1,0:T(8,128)(2,1)} %bitcast.200), calls=%async_computation.7 | async-start | bytes 1572864 | tf_op jit(solution)/shard_map/all_to_all | solution.py:593
  501.9 33.4 %collective-permute-start.34 = (bf16[640,1024]{1,0:T(8,128)(2,1)}, bf16[640,1024]{1,0:T(8,128)(2,1)}, u32[]{:S(2)}, u32[]{:S(2)}) collective-permute-start(bf16[640,1024]{1,0:T(8,128)(2,1)} %add_convert_fusion.7), channel_id=1, source_target_pairs={{0,2},{1,3},{2,0},{3,1},{4,6},{5,7},{6,4},{7,5},{8,10},{9,11},{10,... | collective-permute-start | bytes 3932168 | tf_op jit(solution)/shard_map/ppermute | solution.py:576
  530.2 22.6 %all-to-all-start.7 = ((bf16[8,128,384]{2,1,0:T(8,128)(2,1)}), bf16[8,128,384]{2,1,0:T(8,128)(2,1)S(1)}, u32[]{:S(2)}, u32[]{:S(2)}) async-start(bf16[8,128,384]{2,1,0:T(8,128)(2,1)} %bitcast.199), calls=%async_computation.8 | async-start | bytes 1572864 | tf_op jit(solution)/shard_map/all_to_all | solution.py:593
  (94 other events, 686.7 us)
Sparse Core Ops, SparseCore 0:
  227.9 86.5 reduce-scatter.1

commit v13 on v11

--- a/solution.py
+++ b/solution.py
@@ -744,7 +744,7 @@
     dense_back_far = chip_sum(far_dense, 2).astype(BF16)
     far_two = jnp.concatenate([normed_two_far, normed_two_corner], axis=0)
     grad_down = (grad_down + product(far_dense[6], far_dense[4])).astype(BF16)
-    far_two, far_rows, grad_down = lax.optimization_barrier((far_two, far_rows, grad_down))
+    far_two, grad_down = lax.optimization_barrier((far_two, grad_down))
     grad_up = (grad_up + product(far_two, far_dense[5])).astype(BF16)
     dense_grads = after(jnp.concatenate([grad_up, grad_down], axis=1), far_grads)
     far_rows, dense_back_far, dense_grads = lax.optimization_barrier(
@@ -872,13 +872,14 @@
         (near_results, far_results, out_rows, far_sum)
     )
     near_sum = plus_side(normed_part(near_results, 0), normed_part(near_results, 1))
-    out = (residual + dense_out + dense_out_far.astype(F32) + picked(out_rows)).astype(BF16)
 
     scaled_far = normed_far.astype(F32) / ln_attn
     gain_one = jnp.sum(
         near_sum * scaled_one + far_sum.astype(F32) * scaled_far, axis=0, keepdims=True
     )
     gain_one = sum_over(gain_one, "expert")
+    out_rows = after(out_rows, gain_one)
+    out = (residual + dense_out + dense_out_far.astype(F32) + picked(out_rows)).astype(BF16)
     last_grads = [qkv_weights(pair, far_sum) for pair in range(1, pairs)]
     qkv_grads += [strips_sent(grads) for grads in last_grads]
     far_arrived, gain_one, dense_grads, *_ = lax.optimization_barrier(

time: 561 us -> 555 us (0.989)
    unnamed x128 -> x120, local copies, waits for them, and re-layouts: 9.65 us -> 13.9 us
  transfers between devices with their start and end apart: 51 -> 51, of which waited for: 18 -> 21; matrix products, arithmetic and copies ran while one was open for 30% -> 29% of each run, Pallas kernels for 31% -> 31%
where the time goes in v13:
time: 555 us; the launch traced here: 550 us
  Pallas kernels  173 us (31%)
  matrix products  117 us (21%)
  waiting for transfers between devices  99.6 us (18%)
  starting transfers between devices  68.8 us (12%)
  other arithmetic  59 us (11%)
  local copies, waits for them, and re-layouts  16.8 us (3%)
  between operations  15.3 us (3%)
    pallas_call x4, Pallas kernels, feed(): pl.pallas_call(functools.partial(feed_kernel, experts, routed), grid_spec...  107 us
    dot_general x14, matrix products, product(): return jnp.einsum('gd,gf->df', left, right, preferred_element_type=F32)  59.8 us
    ppermute x11, waiting for transfers between devices, from_far(): return lax.ppermute(values, 'tensor', [(i, i ^ 2) for i in range(4)])  50.2 us
    pallas_call x2, Pallas kernels, attention_backward(): pl.pallas_call(backward_kernel, grid_spec=pltpu.PrefetchScalarGridSpec(nu...  44.4 us
    all_to_all x8, starting transfers between devices, exchange(): lax.all_to_all(blocks, 'expert', split_axis=0, concat_axis=0, tiled=True)  39.8 us
    all_to_all x8, waiting for transfers between devices, exchange(): lax.all_to_all(blocks, 'expert', split_axis=0, concat_axis=0, tiled=True)  27.2 us
    pallas_call x1, Pallas kernels, attention_forward(): pl.pallas_call(forward_kernel, grid_spec=pltpu.PrefetchScalarGridSpec(num...  22.2 us
    ppermute x11, starting transfers between devices, from_far(): return lax.ppermute(values, 'tensor', [(i, i ^ 2) for i in range(4)])  15.6 us
  transfers between devices with their start and end apart: 51, of which 21 were waited for; matrix products, arithmetic and copies ran while one was open for 29% of the time, Pallas kernels for 31%

profile of v13, /device:TPU:0, one launch (start us, length us, event | category | flops | bytes accessed | tf_op | source)
XLA Modules:
  0.0 549.8 jit_solution(10210578625764964599)
XLA Ops:
  18.9 6.2 %all-to-all-start = ((bf16[8,112,1024]{2,1,0:T(8,128)(2,1)}), bf16[8,112,1024]{2,1,0:T(8,128)(2,1)}, u32[]{:S(2)}, u32[]{:S(2)}) async-start(bf16[8,112,1024]{2,1,0:T(8,128)(2,1)} %bitcast.186), calls=%async_computation | async-start | bytes 3670016 | tf_op jit(solution)/shard_map/all_to_all | solution.py:587
  28.1 5.7 %convolution_convert_fusion.1 = bf16[1280,3,256]{2,0,1:T(8,128)(2,1)} fusion(bf16[3,1024,256]{2,1,0:T(8,128)(2,1)} %param.19, bf16[640,1024]{1,0:T(8,128)(2,1)} %collective-permute-done.1, bf16[640,1024]{1,0:T(8,128)(2,1)} %fusion.15), kind=kOutput, calls=%fused_computation.22 | convolution fusion | flops 2019491840 | bytes 6160384 | tf_op jit(solution)/shard_map/td,sdc->stc/dot_general | solution.py:662
  33.8 11.3 %collective-permute-done = bf16[640,1024]{1,0:T(8,128)(2,1)} collective-permute-done((bf16[640,1024]{1,0:T(8,128)(2,1)}, bf16[640,1024]{1,0:T(8,128)(2,1)}, u32[]{:S(2)}, u32[]{:S(2)}) %collective-permute-start) | collective-permute-done | bytes 1310752 | tf_op jit(solution)/shard_map/ppermute | solution.py:570
  53.8 22.2 %tree_attention.1 = (bf16[2,640,256]{2,1,0:T(8,128)(2,1)}, bf16[2,640,256]{2,1,0:T(8,128)(2,1)}, f32[2,2,1024]{2,1,0:T(2,128)}, f32[2,2,2,768]{3,2,1,0:T(2,128)}) custom-call(s32[9]{0:T(128)} %pad_add_fusion.leaves_ref, bf16[3,2,640,256]{3,2,1,0:T(8,128)(2,1)} %bitcast.206, bf16[3,2,640,256]{3,2,1,0:T(8,128)(2,1)} %bitcast.209), custom_call_target="tpu_custom_call" | custom-call | flops 1241513984 | bytes 1310720 | tf_op jit(solution)/shard_map/tree_attention/pallas_call | solution.py:200
  91.1 23.8 %collective-permute-done.7 = bf16[640,1024]{1,0:T(8,128)(2,1)S(1)} collective-permute-done((bf16[640,1024]{1,0:T(8,128)(2,1)S(1)}, bf16[640,1024]{1,0:T(8,128)(2,1)S(1)}, u32[]{:S(2)}, u32[]{:S(2)}) %collective-permute-start.7) | collective-permute-done | bytes 1310752 | tf_op jit(solution)/shard_map/ppermute | solution.py:570
  121.9 6.0 %all-to-all-start.1 = ((bf16[8,112,1024]{2,1,0:T(8,128)(2,1)}), bf16[8,112,1024]{2,1,0:T(8,128)(2,1)}, u32[]{:S(2)}, u32[]{:S(2)}) async-start(bf16[8,112,1024]{2,1,0:T(8,128)(2,1)} %bitcast.187), calls=%async_computation.1 | async-start | bytes 3670016 | tf_op jit(solution)/shard_map/all_to_all | solution.py:587
  131.3 20.0 %feed_dense.2 = (bf16[640,1024]{1,0:T(8,128)(2,1)}, bf16[640,1024]{1,0:T(8,128)(2,1)}, bf16[640,1024]{1,0:T(8,128)(2,1)}, bf16[640,1024]{1,0:T(8,128)(2,1)}, bf1...) custom-call(s32[1]{0:T(128)} %constant.47.clone.1.expert_ref, ...), custom_call_target="tpu_custom_call" | custom-call | flops 1342177280 | bytes 2490368 | tf_op jit(solution)/shard_map/feed_dense/pallas_call | solution.py:495
  151.4 7.6 %fusion.23 = f32[1024,1024]{1,0:T(8,128)} fusion(bf16[1280,1024]{1,0:T(8,128)(2,1)} %bitcast.205, bf16[640,1024]{1,0:T(8,128)(2,1)} %collective-permute-done.10.side_ref, bf16[640,1024]{1,0:T(8,128)(2,1)} %multiply_convert_fusion.own_ref), kind=kOutput, calls=%fused_computation.38 | convolution fusion | flops 2689597440 | bytes 9437184 | tf_op jit(solution)/shard_map/gd,gf->df/dot_general | solution.py:705
  163.5 6.7 %all-to-all-done.1 = bf16[8,112,1024]{2,1,0:T(8,128)(2,1)} async-done(((bf16[8,112,1024]{2,1,0:T(8,128)(2,1)}), bf16[8,112,1024]{2,1,0:T(8,128)(2,1)}, u32[]{:S(2)}, u32[]{:S(2)}) %all-to-all-start.1) | async-done | bytes 1835040 | tf_op jit(solution)/shard_map/all_to_all | solution.py:587
  176.0 20.2 %feed_dense.3 = (bf16[640,1024]{1,0:T(8,128)(2,1)}, bf16[640,1024]{1,0:T(8,128)(2,1)}, bf16[640,1024]{1,0:T(8,128)(2,1)}, bf16[640,1024]{1,0:T(8,128)(2,1)}, bf1...) custom-call(s32[1]{0:T(128)} %constant.47.clone.1.expert_ref, ...), custom_call_target="tpu_custom_call" | custom-call | flops 1342177280 | bytes 2490368 | tf_op jit(solution)/shard_map/feed_dense/pallas_call | solution.py:495
  214.1 5.1 all-to-all-done.2
  226.1 33.2 %feed_routed.2 = (bf16[896,1024]{1,0:T(8,128)(2,1)}, bf16[896,1024]{1,0:T(8,128)(2,1)}, bf16[896,1024]{1,0:T(8,128)(2,1)}, bf16[896,1024]{1,0:T(8,128)(2,1)}, bf...) custom-call(s32[1]{0:T(128)} %bitcast.20.expert_ref, ...), custom_call_target="tpu_custom_call" | custom-call | flops 1879048192 | bytes 3276800 | tf_op jit(solution)/shard_map/feed_routed/pallas_call | solution.py:495
  268.7 33.1 %feed_routed.3 = (bf16[896,1024]{1,0:T(8,128)(2,1)}, bf16[896,1024]{1,0:T(8,128)(2,1)}, bf16[896,1024]{1,0:T(8,128)(2,1)}, bf16[896,1024]{1,0:T(8,128)(2,1)}, bf...) custom-call(s32[1]{0:T(128)} %bitcast.20.expert_ref, ...), custom_call_target="tpu_custom_call" | custom-call | flops 1879048192 | bytes 3276800 | tf_op jit(solution)/shard_map/feed_routed/pallas_call | solution.py:495
  335.1 7.8 %fusion.5 = f32[1024,1024]{1,0:T(8,128)} fusion(bf16[1792,1024]{1,0:T(8,128)(2,1)S(1)} %bitcast.201, bf16[896,1024]{1,0:T(8,128)(2,1)} %collective-permute-done.15.side_ref, bf16[896,1024]{1,0:T(8,128)(2,1)} %collective-permute-done.12.own_ref), kind=kOutput, calls=%fused_computation.13 | convolution fusion | flops 3765436416 | bytes 11534336 | tf_op jit(solution)/shard_map/gd,gf->df/dot_general | solution.py:705
  342.9 5.6 %add_bitcast_fusion = f32[1,1024,1024]{2,1,0:T(8,128)} fusion(f32[1024,1024]{1,0:T(8,128)S(1)} %fusion.115, bf16[1792,1024]{1,0:T(8,128)(2,1)S(1)} %bitcast.181, bf16[1792,1024]{1,0:T(8,128)(2,1)S(1)} %bitcast.182), kind=kOutput, calls=%fused_computation.3 | convolution fusion | flops 3759144960 | bytes 15728640 | tf_op jit(solution)/shard_map/gd,gf->df/dot_general | solution.py:705
  348.5 14.4 %all-to-all-done.3 = bf16[8,112,1024]{2,1,0:T(8,128)(2,1)} async-done(((bf16[8,112,1024]{2,1,0:T(8,128)(2,1)}), bf16[8,112,1024]{2,1,0:T(8,128)(2,1)}, u32[]{:S(2)}, u32[]{:S(2)}) %all-to-all-start.3) | async-done | bytes 1835040 | tf_op jit(solution)/shard_map/all_to_all | solution.py:587
  362.9 5.8 %multiply_reduce_fusion = (bf16[1024]{0:T(1024)(128)(2,1)S(1)}, f32[640]{0:T(1024)S(1)}, f32[640]{0:T(1024)S(1)}, f32[640,1024]{1,0:T(8,128)S(1)}) fusion(f32[640,1024]{1,0:T(8,128)} %copy-done.2, f32[640]{0:T(1024)S(1)} %add_rsqrt_fusion, f32[640]{0:T(1024)S(1)} %broadcast_multiply_fusion.4, f32[1024]{0:T(1024)S(1)} %copy-done.40, ...), kind=kOutput, calls=%fused_computation.59 | convolution fusion | flops 1184151296 | bytes 11028992 | tf_op jit(solution)/shard_map/dot_general | solution.py:765
  373.6 7.1 %add_bitcast_fusion.1 = f32[1,1024,1024]{2,1,0:T(8,128)} fusion(f32[1024,1024]{1,0:T(8,128)S(1)} %copy-done.55, bf16[1792,1024]{1,0:T(8,128)(2,1)S(1)} %bitcast.200, bf16[896,1024]{1,0:T(8,128)(2,1)S(1)} %copy-done.20, bf16[896,1024]{1,0:T(8,128)(2,1)} %bitcast.19.own_ref), kind=kOutput, calls=%fused_computation.4 | convolution fusion | flops 3766484992 | bytes 15728640 | tf_op jit(solution)/shard_map/gd,gf->df/dot_general | solution.py:705
  397.1 5.4 collective-permute-done.23
  413.7 22.2 %tree_attention_back.2 = (bf16[2,640,384]{2,1,0:T(8,128)(2,1)}, bf16[2,640,384]{2,1,0:T(8,128)(2,1)}) custom-call(s32[9]{0:T(128)} %pad_add_fusion.leaves_ref, bf16[3,2,640,256]{3,2,1,0:T(8,128)(2,1)} %bitcast.207, bf16[3,2,640,256]{3,2,1,0:T(8,128)(2,1)} %bitcast.210, bf16[2,640,256]{2,1,0:T(8,128)(2,1)} %pad_maximum_fusion.9.near_grads_ref, ...), custom_call_target="tpu_custom_call" | custom-call | flops 2483025920 | bytes 1048576 | tf_op jit(solution)/shard_map/tree_attention_back/pallas_call | solution.py:350
  442.0 22.2 %tree_attention_back.3 = (bf16[2,640,384]{2,1,0:T(8,128)(2,1)}, bf16[2,640,384]{2,1,0:T(8,128)(2,1)}) custom-call(s32[9]{0:T(128)} %pad_add_fusion.leaves_ref, bf16[3,2,640,256]{3,2,1,0:T(8,128)(2,1)} %bitcast.208, bf16[3,2,640,256]{3,2,1,0:T(8,128)(2,1)} %bitcast.211, bf16[2,640,256]{2,1,0:T(8,128)(2,1)} %pad_maximum_fusion.9.near_grads_ref, ...), custom_call_target="tpu_custom_call" | custom-call | flops 2483025920 | bytes 1048576 | tf_op jit(solution)/shard_map/tree_attention_back/pallas_call | solution.py:350
  480.3 5.8 %all-to-all-start.6 = ((bf16[8,128,384]{2,1,0:T(8,128)(2,1)}), bf16[8,128,384]{2,1,0:T(8,128)(2,1)}, u32[]{:S(2)}, u32[]{:S(2)}) async-start(bf16[8,128,384]{2,1,0:T(8,128)(2,1)} %bitcast.191), calls=%async_computation.7 | async-start | bytes 1572864 | tf_op jit(solution)/shard_map/all_to_all | solution.py:587
  488.9 5.0 fusion.17
  512.3 5.1 collective-permute-done.37
  (317 shorter events, 227.0 us)
Async XLA Ops:
  12.8 32.3 %collective-permute-start = (bf16[640,1024]{1,0:T(8,128)(2,1)}, bf16[640,1024]{1,0:T(8,128)(2,1)}, u32[]{:S(2)}, u32[]{:S(2)}) collective-permute-start(bf16[640,1024]{1,0:T(8,128)(2,1)} %fusion.15), channel_id=1, source_target_pairs={{0,2},{1,3},{2,0},{3,1},{4,6},{5,7},{6,4},{7,5},{8,10},{9,11},{10,... | collective-permute-start | bytes 3932168 | tf_op jit(solution)/shard_map/ppermute | solution.py:570
  18.9 57.8 %all-to-all-start = ((bf16[8,112,1024]{2,1,0:T(8,128)(2,1)}), bf16[8,112,1024]{2,1,0:T(8,128)(2,1)}, u32[]{:S(2)}, u32[]{:S(2)}) async-start(bf16[8,112,1024]{2,1,0:T(8,128)(2,1)} %bitcast.186), calls=%async_computation | async-start | bytes 3670016 | tf_op jit(solution)/shard_map/all_to_all | solution.py:587
  45.1 31.0 %collective-permute-start.5 = (bf16[640,1024]{1,0:T(8,128)(2,1)S(1)}, bf16[640,1024]{1,0:T(8,128)(2,1)}, u32[]{:S(2)}, u32[]{:S(2)}) collective-permute-start(bf16[640,1024]{1,0:T(8,128)(2,1)S(1)} %copy-done.7), channel_id=1, source_target_pairs={{0,1},{1,0},{2,3},{3,2},{4,5},{5,4},{6,7},{7,6},{8,9},{9,8},{10,11... | collective-permute-start | bytes 3932168 | tf_op jit(solution)/shard_map/ppermute | solution.py:566
  45.9 30.9 %collective-permute-start.4 = (bf16[640,1024]{1,0:T(8,128)(2,1)S(1)}, bf16[640,1024]{1,0:T(8,128)(2,1)}, u32[]{:S(2)}, u32[]{:S(2)}) collective-permute-start(bf16[640,1024]{1,0:T(8,128)(2,1)S(1)} %copy-done.7), channel_id=1, source_target_pairs={{0,2},{1,3},{2,0},{3,1},{4,6},{5,7},{6,4},{7,5},{8,10},{9,11},{10,... | collective-permute-start | bytes 3932168 | tf_op jit(solution)/shard_map/ppermute | solution.py:570
  84.0 30.9 %collective-permute-start.7 = (bf16[640,1024]{1,0:T(8,128)(2,1)S(1)}, bf16[640,1024]{1,0:T(8,128)(2,1)S(1)}, u32[]{:S(2)}, u32[]{:S(2)}) collective-permute-start(bf16[640,1024]{1,0:T(8,128)(2,1)S(1)} %add_convert_fusion.11), channel_id=1, source_target_pairs={{0,2},{1,3},{2,0},{3,1},{4,6},{5,7},{6,4},{7,5},{8,10},{9,11},{10,... | collective-permute-start | bytes 3932168 | tf_op jit(solution)/shard_map/ppermute | solution.py:570
  86.3 28.6 %collective-permute-start.3 = (bf16[640,1024]{1,0:T(8,128)(2,1)S(1)}, bf16[640,1024]{1,0:T(8,128)(2,1)S(1)}, u32[]{:S(2)}, u32[]{:S(2)}) collective-permute-start(bf16[640,1024]{1,0:T(8,128)(2,1)S(1)} %convolution_convert_fusion.3), channel_id=1, source_target_pairs={{0,1},{1,0},{2,3},{3,2},{4,5},{5,4},{6,7},{7,6},{8,9},{9,8},{10,11... | collective-permute-start | bytes 3932168 | tf_op jit(solution)/shard_map/ppermute | solution.py:566
  121.9 48.2 %all-to-all-start.1 = ((bf16[8,112,1024]{2,1,0:T(8,128)(2,1)}), bf16[8,112,1024]{2,1,0:T(8,128)(2,1)}, u32[]{:S(2)}, u32[]{:S(2)}) async-start(bf16[8,112,1024]{2,1,0:T(8,128)(2,1)} %bitcast.187), calls=%async_computation.1 | async-start | bytes 3670016 | tf_op jit(solution)/shard_map/all_to_all | solution.py:587
  127.9 35.5 %collective-permute-start.11 = (bf16[640,1024]{1,0:T(8,128)(2,1)}, bf16[640,1024]{1,0:T(8,128)(2,1)S(1)}, u32[]{:S(2)}, u32[]{:S(2)}) collective-permute-start(bf16[640,1024]{1,0:T(8,128)(2,1)} %multiply_convert_fusion.own_ref), channel_id=1, source_target_pairs={{0,2},{1,3},{2,0},{3,1},{4,6},{5,7},{6,4},{7,5},{8,10},{9,11},{10,... | collective-permute-start | bytes 3932168 | tf_op jit(solution)/shard_map/ppermute | solution.py:570
  170.1 49.1 %collective-permute-start.12 = (bf16[896,1024]{1,0:T(8,128)(2,1)}, bf16[896,1024]{1,0:T(8,128)(2,1)}, u32[]{:S(2)}, u32[]{:S(2)}) collective-permute-start(bf16[896,1024]{1,0:T(8,128)(2,1)} %bitcast.19.own_ref), channel_id=1, source_target_pairs={{0,2},{1,3},{2,0},{3,1},{4,6},{5,7},{6,4},{7,5},{8,10},{9,11},{10,... | collective-permute-start | bytes 5505032 | tf_op jit(solution)/shard_map/ppermute | solution.py:570
  171.6 47.6 %all-to-all-start.2 = ((bf16[8,112,1024]{2,1,0:T(8,128)(2,1)}), bf16[8,112,1024]{2,1,0:T(8,128)(2,1)}, u32[]{:S(2)}, u32[]{:S(2)}) async-start(bf16[8,112,1024]{2,1,0:T(8,128)(2,1)} %bitcast.185), calls=%async_computation.2 | async-start | bytes 3670016 | tf_op jit(solution)/shard_map/all_to_all | solution.py:587
  176.0 129.5 %reduce-scatter.2.cloned.1.call-start = ((), (), s32[]{:S(2)}) async-start(), calls=%async_computation.9 | async-start | bytes 4718592 | tf_op jit(solution)/shard_map/reduce_scatter | solution.py:592
  219.9 39.5 %collective-permute-start.17 = (bf16[640,1024]{1,0:T(8,128)(2,1)S(1)}, bf16[640,1024]{1,0:T(8,128)(2,1)}, u32[]{:S(2)}, u32[]{:S(2)}) collective-permute-start(bf16[640,1024]{1,0:T(8,128)(2,1)S(1)} %add_convert_fusion.10), channel_id=1, source_target_pairs={{0,2},{1,3},{2,0},{3,1},{4,6},{5,7},{6,4},{7,5},{8,10},{9,11},{10,... | collective-permute-start | bytes 3932168 | tf_op jit(solution)/shard_map/ppermute | solution.py:570
  267.0 42.4 %collective-permute-start.22 = (bf16[896,1024]{1,0:T(8,128)(2,1)}, bf16[896,1024]{1,0:T(8,128)(2,1)}, u32[]{:S(2)}, u32[]{:S(2)}) collective-permute-start(bf16[896,1024]{1,0:T(8,128)(2,1)} %add_convert_fusion.4), channel_id=1, source_target_pairs={{0,2},{1,3},{2,0},{3,1},{4,6},{5,7},{6,4},{7,5},{8,10},{9,11},{10,... | collective-permute-start | bytes 5505032 | tf_op jit(solution)/shard_map/ppermute | solution.py:570
  314.6 33.8 %collective-permute-start.19 = (bf16[640,1024]{1,0:T(8,128)(2,1)}, bf16[640,1024]{1,0:T(8,128)(2,1)}, u32[]{:S(2)}, u32[]{:S(2)}) collective-permute-start(bf16[640,1024]{1,0:T(8,128)(2,1)} %get-tuple-element.182), channel_id=1, source_target_pairs={{0,1},{1,0},{2,3},{3,2},{4,5},{5,4},{6,7},{7,6},{8,9},{9,8},{10,11... | collective-permute-start | bytes 3932168 | tf_op jit(solution)/shard_map/ppermute | solution.py:566
  315.0 47.9 %all-to-all-start.3 = ((bf16[8,112,1024]{2,1,0:T(8,128)(2,1)}), bf16[8,112,1024]{2,1,0:T(8,128)(2,1)}, u32[]{:S(2)}, u32[]{:S(2)}) async-start(bf16[8,112,1024]{2,1,0:T(8,128)(2,1)} %bitcast.180), calls=%async_computation.4 | async-start | bytes 3670016 | tf_op jit(solution)/shard_map/all_to_all | solution.py:587
  319.9 61.3 %collective-permute-start.26 = (bf16[896,1024]{1,0:T(8,128)(2,1)}, bf16[896,1024]{1,0:T(8,128)(2,1)}, u32[]{:S(2)}, u32[]{:S(2)}) collective-permute-start(bf16[896,1024]{1,0:T(8,128)(2,1)} %get-tuple-element.212), channel_id=1, source_target_pairs={{0,1},{1,0},{2,3},{3,2},{4,5},{5,4},{6,7},{7,6},{8,9},{9,8},{10,11... | collective-permute-start | bytes 5505032 | tf_op jit(solution)/shard_map/ppermute | solution.py:566
  329.6 51.6 %collective-permute-start.27 = (bf16[896,1024]{1,0:T(8,128)(2,1)}, bf16[896,1024]{1,0:T(8,128)(2,1)}, u32[]{:S(2)}, u32[]{:S(2)}) collective-permute-start(bf16[896,1024]{1,0:T(8,128)(2,1)} %add_convert_fusion.2), channel_id=1, source_target_pairs={{0,2},{1,3},{2,0},{3,1},{4,6},{5,7},{6,4},{7,5},{8,10},{9,11},{10,... | collective-permute-start | bytes 5505032 | tf_op jit(solution)/shard_map/ppermute | solution.py:570
  371.2 31.3 %collective-permute-start.23 = (bf16[640,1024]{1,0:T(8,128)(2,1)S(1)}, bf16[640,1024]{1,0:T(8,128)(2,1)}, u32[]{:S(2)}, u32[]{:S(2)}) collective-permute-start(bf16[640,1024]{1,0:T(8,128)(2,1)S(1)} %get-tuple-element.343), channel_id=1, source_target_pairs={{0,2},{1,3},{2,0},{3,1},{4,6},{5,7},{6,4},{7,5},{8,10},{9,11},{10,... | collective-permute-start | bytes 3932168 | tf_op jit(solution)/shard_map/ppermute | solution.py:570
  386.7 49.2 %all-to-all-start.4 = ((bf16[8,112,1024]{2,1,0:T(8,128)(2,1)}), bf16[8,112,1024]{2,1,0:T(8,128)(2,1)}, u32[]{:S(2)}, u32[]{:S(2)}) async-start(bf16[8,112,1024]{2,1,0:T(8,128)(2,1)} %bitcast.179), calls=%async_computation.5 | async-start | bytes 3670016 | tf_op jit(solution)/shard_map/all_to_all | solution.py:587
  403.7 32.2 %collective-permute-start.31 = (bf16[640,1024]{1,0:T(8,128)(2,1)}, bf16[640,1024]{1,0:T(8,128)(2,1)}, u32[]{:S(2)}, u32[]{:S(2)}) collective-permute-start(bf16[640,1024]{1,0:T(8,128)(2,1)} %add_convert_fusion.9), channel_id=1, source_target_pairs={{0,2},{1,3},{2,0},{3,1},{4,6},{5,7},{6,4},{7,5},{8,10},{9,11},{10,... | collective-permute-start | bytes 3932168 | tf_op jit(solution)/shard_map/ppermute | solution.py:570
  435.9 28.3 %all-to-all-start.5 = ((bf16[8,128,384]{2,1,0:T(8,128)(2,1)}), bf16[8,128,384]{2,1,0:T(8,128)(2,1)}, u32[]{:S(2)}, u32[]{:S(2)}) async-start(bf16[8,128,384]{2,1,0:T(8,128)(2,1)} %bitcast.47), calls=%async_computation.6 | async-start | bytes 1572864 | tf_op jit(solution)/shard_map/all_to_all | solution.py:587
  480.3 26.8 %all-to-all-start.6 = ((bf16[8,128,384]{2,1,0:T(8,128)(2,1)}), bf16[8,128,384]{2,1,0:T(8,128)(2,1)}, u32[]{:S(2)}, u32[]{:S(2)}) async-start(bf16[8,128,384]{2,1,0:T(8,128)(2,1)} %bitcast.191), calls=%async_computation.7 | async-start | bytes 1572864 | tf_op jit(solution)/shard_map/all_to_all | solution.py:587
  486.1 31.3 %collective-permute-start.37 = (bf16[640,1024]{1,0:T(8,128)(2,1)}, bf16[640,1024]{1,0:T(8,128)(2,1)}, u32[]{:S(2)}, u32[]{:S(2)}) collective-permute-start(bf16[640,1024]{1,0:T(8,128)(2,1)} %add_convert_fusion.7), channel_id=1, source_target_pairs={{0,2},{1,3},{2,0},{3,1},{4,6},{5,7},{6,4},{7,5},{8,10},{9,11},{10,... | collective-permute-start | bytes 3932168 | tf_op jit(solution)/shard_map/ppermute | solution.py:570
  507.1 28.9 %all-to-all-start.7 = ((bf16[8,128,384]{2,1,0:T(8,128)(2,1)}), bf16[8,128,384]{2,1,0:T(8,128)(2,1)S(1)}, u32[]{:S(2)}, u32[]{:S(2)}) async-start(bf16[8,128,384]{2,1,0:T(8,128)(2,1)} %bitcast.70), calls=%async_computation.8 | async-start | bytes 1572864 | tf_op jit(solution)/shard_map/all_to_all | solution.py:587
  (83 other events, 598.1 us)
Sparse Core Ops, SparseCore 0:
  219.4 85.9 reduce-scatter.1

commit v14 on v13

--- a/solution.py
+++ b/solution.py
@@ -747,12 +747,12 @@
     far_two, grad_down = lax.optimization_barrier((far_two, grad_down))
     grad_up = (grad_up + product(far_two, far_dense[5])).astype(BF16)
     dense_grads = after(jnp.concatenate([grad_up, grad_down], axis=1), far_grads)
+    corner_rows = from_side(far_rows)
     far_rows, dense_back_far, dense_grads = lax.optimization_barrier(
         (far_rows, dense_back_far, dense_grads)
     )
     dense_grads = scatter_sum(dense_grads)
     dense_back_far = from_far(dense_back_far)
-    corner_rows = from_side(far_rows)
     side_rows = from_side(own_rows)
     far_expert = routed(far_rows, corner_rows, far_grads, from_side(far_grads))
     *far_expert, dense_back_far = lax.optimization_barrier((*far_expert, dense_back_far))
@@ -868,8 +868,8 @@
     far_results, first_grads = lax.optimization_barrier((far_results, first_grads))
     qkv_grads = [strips_sent(first_grads)]
     far_sum = (normed_part(far_results, 0) + from_corner).astype(BF16)
-    near_results, far_results, out_rows, far_sum = lax.optimization_barrier(
-        (near_results, far_results, out_rows, far_sum)
+    near_results, far_results, out_rows, far_sum, branch_grads = lax.optimization_barrier(
+        (near_results, far_results, out_rows, far_sum, branch_grads)
     )
     near_sum = plus_side(normed_part(near_results, 0), normed_part(near_results, 1))
 
@@ -882,13 +882,13 @@
     out = (residual + dense_out + dense_out_far.astype(F32) + picked(out_rows)).astype(BF16)
     last_grads = [qkv_weights(pair, far_sum) for pair in range(1, pairs)]
     qkv_grads += [strips_sent(grads) for grads in last_grads]
-    far_arrived, gain_one, dense_grads, *_ = lax.optimization_barrier(
-        (from_far(far_sum), gain_one, dense_grads, *last_grads)
+    branch_grads = strips_total(branch_grads)
+    small = sum_over(branch_grads[:, heads_width:], "tensor")
+    far_arrived, gain_one, dense_grads, small, *_ = lax.optimization_barrier(
+        (from_far(far_sum), gain_one, dense_grads, small, *last_grads)
     )
     grad_normed_one = near_sum + far_arrived.astype(F32)
     grad_ln_attn = sum_over(gain_one, "tensor")[0]
-    branch_grads = strips_total(after(branch_grads, gain_one))
-    small = sum_over(branch_grads[:, heads_width:], "tensor")
     qkv_grads = jnp.stack(
         [strips_total(grads).reshape(-1, 3, PAIR) for grads in qkv_grads], axis=2
     )

time: 555 us -> 554 us (level)
  waiting for transfers between devices: 99.6 us -> 92.3 us
  transfers between devices with their start and end apart: 51 -> 51, of which waited for: 21 -> 18; matrix products, arithmetic and copies ran while one was open for 29% -> 29% of each run, Pallas kernels for 31% -> 32%
where the time goes in v14:
time: 554 us; the launch traced here: 545 us
  Pallas kernels  173 us (31%)
  matrix products  118 us (21%)
  waiting for transfers between devices  92.3 us (17%)
  starting transfers between devices  68.7 us (12%)
  other arithmetic  59.8 us (11%)
  local copies, waits for them, and re-layouts  17.2 us (3%)
  between operations  15.3 us (3%)
    pallas_call x4, Pallas kernels, feed(): pl.pallas_call(functools.partial(feed_kernel, experts, routed), grid_spec...  107 us
    dot_general x14, matrix products, product(): return jnp.einsum('gd,gf->df', left, right, preferred_element_type=F32)  61.9 us
    ppermute x11, waiting for transfers between devices, from_far(): return lax.ppermute(values, 'tensor', [(i, i ^ 2) for i in range(4)])  45 us
    pallas_call x2, Pallas kernels, attention_backward(): pl.pallas_call(backward_kernel, grid_spec=pltpu.PrefetchScalarGridSpec(nu...  44.7 us
    all_to_all x8, starting transfers between devices, exchange(): lax.all_to_all(blocks, 'expert', split_axis=0, concat_axis=0, tiled=True)  39.6 us
    all_to_all x8, waiting for transfers between devices, exchange(): lax.all_to_all(blocks, 'expert', split_axis=0, concat_axis=0, tiled=True)  26.9 us
    pallas_call x1, Pallas kernels, attention_forward(): pl.pallas_call(forward_kernel, grid_spec=pltpu.PrefetchScalarGridSpec(num...  22.2 us
    ppermute x11, starting transfers between devices, from_far(): return lax.ppermute(values, 'tensor', [(i, i ^ 2) for i in range(4)])  15.5 us
  transfers between devices with their start and end apart: 51, of which 18 were waited for; matrix products, arithmetic and copies ran while one was open for 29% of the time, Pallas kernels for 32%

profile of v14, /device:TPU:0, one launch (start us, length us, event | category | flops | bytes accessed | tf_op | source)
XLA Modules:
  0.0 544.7 jit_solution(10709796304324039740)
XLA Ops:
  18.9 6.2 %all-to-all-start = ((bf16[8,112,1024]{2,1,0:T(8,128)(2,1)}), bf16[8,112,1024]{2,1,0:T(8,128)(2,1)}, u32[]{:S(2)}, u32[]{:S(2)}) async-start(bf16[8,112,1024]{2,1,0:T(8,128)(2,1)} %bitcast.186), calls=%async_computation | async-start | bytes 3670016 | tf_op jit(solution)/shard_map/all_to_all | solution.py:587
  28.1 5.7 %convolution_convert_fusion.1 = bf16[1280,3,256]{2,0,1:T(8,128)(2,1)} fusion(bf16[3,1024,256]{2,1,0:T(8,128)(2,1)} %param.19, bf16[640,1024]{1,0:T(8,128)(2,1)} %collective-permute-done.1, bf16[640,1024]{1,0:T(8,128)(2,1)} %fusion.15), kind=kOutput, calls=%fused_computation.22 | convolution fusion | flops 2019491840 | bytes 6160384 | tf_op jit(solution)/shard_map/td,sdc->stc/dot_general | solution.py:662
  33.8 11.3 %collective-permute-done = bf16[640,1024]{1,0:T(8,128)(2,1)} collective-permute-done((bf16[640,1024]{1,0:T(8,128)(2,1)}, bf16[640,1024]{1,0:T(8,128)(2,1)}, u32[]{:S(2)}, u32[]{:S(2)}) %collective-permute-start) | collective-permute-done | bytes 1310752 | tf_op jit(solution)/shard_map/ppermute | solution.py:570
  53.8 22.2 %tree_attention.1 = (bf16[2,640,256]{2,1,0:T(8,128)(2,1)}, bf16[2,640,256]{2,1,0:T(8,128)(2,1)}, f32[2,2,1024]{2,1,0:T(2,128)}, f32[2,2,2,768]{3,2,1,0:T(2,128)}) custom-call(s32[9]{0:T(128)} %pad_add_fusion.leaves_ref, bf16[3,2,640,256]{3,2,1,0:T(8,128)(2,1)} %bitcast.207, bf16[3,2,640,256]{3,2,1,0:T(8,128)(2,1)} %bitcast.210), custom_call_target="tpu_custom_call" | custom-call | flops 1241513984 | bytes 1310720 | tf_op jit(solution)/shard_map/tree_attention/pallas_call | solution.py:200
  91.1 23.8 %collective-permute-done.7 = bf16[640,1024]{1,0:T(8,128)(2,1)S(1)} collective-permute-done((bf16[640,1024]{1,0:T(8,128)(2,1)S(1)}, bf16[640,1024]{1,0:T(8,128)(2,1)S(1)}, u32[]{:S(2)}, u32[]{:S(2)}) %collective-permute-start.7) | collective-permute-done | bytes 1310752 | tf_op jit(solution)/shard_map/ppermute | solution.py:570
  121.9 6.0 %all-to-all-start.1 = ((bf16[8,112,1024]{2,1,0:T(8,128)(2,1)}), bf16[8,112,1024]{2,1,0:T(8,128)(2,1)}, u32[]{:S(2)}, u32[]{:S(2)}) async-start(bf16[8,112,1024]{2,1,0:T(8,128)(2,1)} %bitcast.187), calls=%async_computation.1 | async-start | bytes 3670016 | tf_op jit(solution)/shard_map/all_to_all | solution.py:587
  131.3 20.0 %feed_dense.2 = (bf16[640,1024]{1,0:T(8,128)(2,1)}, bf16[640,1024]{1,0:T(8,128)(2,1)}, bf16[640,1024]{1,0:T(8,128)(2,1)}, bf16[640,1024]{1,0:T(8,128)(2,1)}, bf1...) custom-call(s32[1]{0:T(128)} %constant.47.clone.1.expert_ref, ...), custom_call_target="tpu_custom_call" | custom-call | flops 1342177280 | bytes 2490368 | tf_op jit(solution)/shard_map/feed_dense/pallas_call | solution.py:495
  151.4 7.6 %fusion.23 = f32[1024,1024]{1,0:T(8,128)} fusion(bf16[1280,1024]{1,0:T(8,128)(2,1)} %bitcast.206, bf16[640,1024]{1,0:T(8,128)(2,1)} %collective-permute-done.10.side_ref, bf16[640,1024]{1,0:T(8,128)(2,1)} %multiply_convert_fusion.own_ref), kind=kOutput, calls=%fused_computation.38 | convolution fusion | flops 2689597440 | bytes 9437184 | tf_op jit(solution)/shard_map/gd,gf->df/dot_general | solution.py:705
  163.4 6.7 %all-to-all-done.1 = bf16[8,112,1024]{2,1,0:T(8,128)(2,1)} async-done(((bf16[8,112,1024]{2,1,0:T(8,128)(2,1)}), bf16[8,112,1024]{2,1,0:T(8,128)(2,1)}, u32[]{:S(2)}, u32[]{:S(2)}) %all-to-all-start.1) | async-done | bytes 1835040 | tf_op jit(solution)/shard_map/all_to_all | solution.py:587
  176.0 20.2 %feed_dense.3 = (bf16[640,1024]{1,0:T(8,128)(2,1)}, bf16[640,1024]{1,0:T(8,128)(2,1)}, bf16[640,1024]{1,0:T(8,128)(2,1)}, bf16[640,1024]{1,0:T(8,128)(2,1)}, bf1...) custom-call(s32[1]{0:T(128)} %constant.47.clone.1.expert_ref, ...), custom_call_target="tpu_custom_call" | custom-call | flops 1342177280 | bytes 2490368 | tf_op jit(solution)/shard_map/feed_dense/pallas_call | solution.py:495
  214.1 5.1 all-to-all-done.2
  226.1 33.2 %feed_routed.2 = (bf16[896,1024]{1,0:T(8,128)(2,1)}, bf16[896,1024]{1,0:T(8,128)(2,1)}, bf16[896,1024]{1,0:T(8,128)(2,1)}, bf16[896,1024]{1,0:T(8,128)(2,1)}, bf...) custom-call(s32[1]{0:T(128)} %bitcast.20.expert_ref, ...), custom_call_target="tpu_custom_call" | custom-call | flops 1879048192 | bytes 3276800 | tf_op jit(solution)/shard_map/feed_routed/pallas_call | solution.py:495
  268.8 33.0 %feed_routed.3 = (bf16[896,1024]{1,0:T(8,128)(2,1)}, bf16[896,1024]{1,0:T(8,128)(2,1)}, bf16[896,1024]{1,0:T(8,128)(2,1)}, bf16[896,1024]{1,0:T(8,128)(2,1)}, bf...) custom-call(s32[1]{0:T(128)} %bitcast.20.expert_ref, ...), custom_call_target="tpu_custom_call" | custom-call | flops 1879048192 | bytes 3276800 | tf_op jit(solution)/shard_map/feed_routed/pallas_call | solution.py:495
  315.0 4.8 all-to-all-start.3
  335.1 7.2 %fusion.1 = f32[1024,1024]{1,0:T(8,128)} fusion(bf16[1792,1024]{1,0:T(8,128)(2,1)S(1)} %bitcast.204, bf16[896,1024]{1,0:T(8,128)(2,1)S(1)} %copy-done.22, bf16[896,1024]{1,0:T(8,128)(2,1)} %bitcast.19.own_ref), kind=kOutput, calls=%fused_computation.9 | convolution fusion | flops 3765436416 | bytes 11534336 | tf_op jit(solution)/shard_map/gd,gf->df/dot_general | solution.py:705
  342.3 5.6 %add_bitcast_fusion = f32[1,1024,1024]{2,1,0:T(8,128)} fusion(f32[1024,1024]{1,0:T(8,128)S(1)} %fusion.115, bf16[1792,1024]{1,0:T(8,128)(2,1)S(1)} %bitcast.181, bf16[1792,1024]{1,0:T(8,128)(2,1)S(1)} %bitcast.182), kind=kOutput, calls=%fused_computation.3 | convolution fusion | flops 3759144960 | bytes 15728640 | tf_op jit(solution)/shard_map/gd,gf->df/dot_general | solution.py:705
  347.9 15.1 %all-to-all-done.3 = bf16[8,112,1024]{2,1,0:T(8,128)(2,1)} async-done(((bf16[8,112,1024]{2,1,0:T(8,128)(2,1)}), bf16[8,112,1024]{2,1,0:T(8,128)(2,1)}, u32[]{:S(2)}, u32[]{:S(2)}) %all-to-all-start.3) | async-done | bytes 1835040 | tf_op jit(solution)/shard_map/all_to_all | solution.py:587
  362.9 5.8 %multiply_reduce_fusion = (bf16[1024]{0:T(1024)(128)(2,1)S(1)}, f32[640]{0:T(1024)S(1)}, f32[640]{0:T(1024)S(1)}, f32[640,1024]{1,0:T(8,128)S(1)}) fusion(f32[640,1024]{1,0:T(8,128)} %copy-done.2, f32[640]{0:T(1024)S(1)} %add_rsqrt_fusion, f32[640]{0:T(1024)S(1)} %broadcast_multiply_fusion.4, f32[1024]{0:T(1024)S(1)} %copy-done.40, ...), kind=kOutput, calls=%fused_computation.59 | convolution fusion | flops 1184151296 | bytes 11028992 | tf_op jit(solution)/shard_map/dot_general | solution.py:765
  373.0 7.7 %add_bitcast_fusion.1 = f32[1,1024,1024]{2,1,0:T(8,128)} fusion(f32[1024,1024]{1,0:T(8,128)S(1)} %copy-done.55, bf16[1792,1024]{1,0:T(8,128)(2,1)S(1)} %bitcast.201, bf16[896,1024]{1,0:T(8,128)(2,1)} %collective-permute-done.15.side_ref, bf16[896,1024]{1,0:T(8,128)(2,1)} %collective-permute-done.12.own_ref), kind=kOutput, calls=%fused_computation.4 | convolution fusion | flops 3766484992 | bytes 15728640 | tf_op jit(solution)/shard_map/gd,gf->df/dot_general | solution.py:705
  397.1 5.3 collective-permute-done.23
  413.7 22.2 %tree_attention_back.2 = (bf16[2,640,384]{2,1,0:T(8,128)(2,1)}, bf16[2,640,384]{2,1,0:T(8,128)(2,1)}) custom-call(s32[9]{0:T(128)} %pad_add_fusion.leaves_ref, bf16[3,2,640,256]{3,2,1,0:T(8,128)(2,1)} %bitcast.208, bf16[3,2,640,256]{3,2,1,0:T(8,128)(2,1)} %bitcast.211, bf16[2,640,256]{2,1,0:T(8,128)(2,1)} %pad_maximum_fusion.9.near_grads_ref, ...), custom_call_target="tpu_custom_call" | custom-call | flops 2483025920 | bytes 1048576 | tf_op jit(solution)/shard_map/tree_attention_back/pallas_call | solution.py:350
  441.9 22.4 %tree_attention_back.3 = (bf16[2,640,384]{2,1,0:T(8,128)(2,1)}, bf16[2,640,384]{2,1,0:T(8,128)(2,1)}) custom-call(s32[9]{0:T(128)} %pad_add_fusion.leaves_ref, bf16[3,2,640,256]{3,2,1,0:T(8,128)(2,1)} %bitcast.209, bf16[3,2,640,256]{3,2,1,0:T(8,128)(2,1)} %bitcast.212, bf16[2,640,256]{2,1,0:T(8,128)(2,1)} %pad_maximum_fusion.9.near_grads_ref, ...), custom_call_target="tpu_custom_call" | custom-call | flops 2483025920 | bytes 1048576 | tf_op jit(solution)/shard_map/tree_attention_back/pallas_call | solution.py:350
  480.5 6.0 %all-to-all-start.6 = ((bf16[8,128,384]{2,1,0:T(8,128)(2,1)}), bf16[8,128,384]{2,1,0:T(8,128)(2,1)}, u32[]{:S(2)}, u32[]{:S(2)}) async-start(bf16[8,128,384]{2,1,0:T(8,128)(2,1)} %bitcast.192), calls=%async_computation.7 | async-start | bytes 1572864 | tf_op jit(solution)/shard_map/all_to_all | solution.py:587
  526.3 4.8 add_convert_fusion.5
  (317 shorter events, 221.4 us)
Async XLA Ops:
  12.8 32.3 %collective-permute-start = (bf16[640,1024]{1,0:T(8,128)(2,1)}, bf16[640,1024]{1,0:T(8,128)(2,1)}, u32[]{:S(2)}, u32[]{:S(2)}) collective-permute-start(bf16[640,1024]{1,0:T(8,128)(2,1)} %fusion.15), channel_id=1, source_target_pairs={{0,2},{1,3},{2,0},{3,1},{4,6},{5,7},{6,4},{7,5},{8,10},{9,11},{10,... | collective-permute-start | bytes 3932168 | tf_op jit(solution)/shard_map/ppermute | solution.py:570
  18.9 57.8 %all-to-all-start = ((bf16[8,112,1024]{2,1,0:T(8,128)(2,1)}), bf16[8,112,1024]{2,1,0:T(8,128)(2,1)}, u32[]{:S(2)}, u32[]{:S(2)}) async-start(bf16[8,112,1024]{2,1,0:T(8,128)(2,1)} %bitcast.186), calls=%async_computation | async-start | bytes 3670016 | tf_op jit(solution)/shard_map/all_to_all | solution.py:587
  45.1 31.0 %collective-permute-start.5 = (bf16[640,1024]{1,0:T(8,128)(2,1)S(1)}, bf16[640,1024]{1,0:T(8,128)(2,1)}, u32[]{:S(2)}, u32[]{:S(2)}) collective-permute-start(bf16[640,1024]{1,0:T(8,128)(2,1)S(1)} %copy-done.7), channel_id=1, source_target_pairs={{0,1},{1,0},{2,3},{3,2},{4,5},{5,4},{6,7},{7,6},{8,9},{9,8},{10,11... | collective-permute-start | bytes 3932168 | tf_op jit(solution)/shard_map/ppermute | solution.py:566
  45.9 30.9 %collective-permute-start.4 = (bf16[640,1024]{1,0:T(8,128)(2,1)S(1)}, bf16[640,1024]{1,0:T(8,128)(2,1)}, u32[]{:S(2)}, u32[]{:S(2)}) collective-permute-start(bf16[640,1024]{1,0:T(8,128)(2,1)S(1)} %copy-done.7), channel_id=1, source_target_pairs={{0,2},{1,3},{2,0},{3,1},{4,6},{5,7},{6,4},{7,5},{8,10},{9,11},{10,... | collective-permute-start | bytes 3932168 | tf_op jit(solution)/shard_map/ppermute | solution.py:570
  84.0 30.9 %collective-permute-start.7 = (bf16[640,1024]{1,0:T(8,128)(2,1)S(1)}, bf16[640,1024]{1,0:T(8,128)(2,1)S(1)}, u32[]{:S(2)}, u32[]{:S(2)}) collective-permute-start(bf16[640,1024]{1,0:T(8,128)(2,1)S(1)} %add_convert_fusion.11), channel_id=1, source_target_pairs={{0,2},{1,3},{2,0},{3,1},{4,6},{5,7},{6,4},{7,5},{8,10},{9,11},{10,... | collective-permute-start | bytes 3932168 | tf_op jit(solution)/shard_map/ppermute | solution.py:570
  86.3 28.6 %collective-permute-start.3 = (bf16[640,1024]{1,0:T(8,128)(2,1)S(1)}, bf16[640,1024]{1,0:T(8,128)(2,1)S(1)}, u32[]{:S(2)}, u32[]{:S(2)}) collective-permute-start(bf16[640,1024]{1,0:T(8,128)(2,1)S(1)} %convolution_convert_fusion.3), channel_id=1, source_target_pairs={{0,1},{1,0},{2,3},{3,2},{4,5},{5,4},{6,7},{7,6},{8,9},{9,8},{10,11... | collective-permute-start | bytes 3932168 | tf_op jit(solution)/shard_map/ppermute | solution.py:566
  121.9 48.2 %all-to-all-start.1 = ((bf16[8,112,1024]{2,1,0:T(8,128)(2,1)}), bf16[8,112,1024]{2,1,0:T(8,128)(2,1)}, u32[]{:S(2)}, u32[]{:S(2)}) async-start(bf16[8,112,1024]{2,1,0:T(8,128)(2,1)} %bitcast.187), calls=%async_computation.1 | async-start | bytes 3670016 | tf_op jit(solution)/shard_map/all_to_all | solution.py:587
  127.9 35.5 %collective-permute-start.11 = (bf16[640,1024]{1,0:T(8,128)(2,1)}, bf16[640,1024]{1,0:T(8,128)(2,1)S(1)}, u32[]{:S(2)}, u32[]{:S(2)}) collective-permute-start(bf16[640,1024]{1,0:T(8,128)(2,1)} %multiply_convert_fusion.own_ref), channel_id=1, source_target_pairs={{0,2},{1,3},{2,0},{3,1},{4,6},{5,7},{6,4},{7,5},{8,10},{9,11},{10,... | collective-permute-start | bytes 3932168 | tf_op jit(solution)/shard_map/ppermute | solution.py:570
  170.1 49.1 %collective-permute-start.12 = (bf16[896,1024]{1,0:T(8,128)(2,1)}, bf16[896,1024]{1,0:T(8,128)(2,1)}, u32[]{:S(2)}, u32[]{:S(2)}) collective-permute-start(bf16[896,1024]{1,0:T(8,128)(2,1)} %bitcast.19.own_ref), channel_id=1, source_target_pairs={{0,2},{1,3},{2,0},{3,1},{4,6},{5,7},{6,4},{7,5},{8,10},{9,11},{10,... | collective-permute-start | bytes 5505032 | tf_op jit(solution)/shard_map/ppermute | solution.py:570
  171.6 47.6 %all-to-all-start.2 = ((bf16[8,112,1024]{2,1,0:T(8,128)(2,1)}), bf16[8,112,1024]{2,1,0:T(8,128)(2,1)}, u32[]{:S(2)}, u32[]{:S(2)}) async-start(bf16[8,112,1024]{2,1,0:T(8,128)(2,1)} %bitcast.185), calls=%async_computation.2 | async-start | bytes 3670016 | tf_op jit(solution)/shard_map/all_to_all | solution.py:587
  176.0 129.5 %reduce-scatter.2.cloned.1.call-start = ((), (), s32[]{:S(2)}) async-start(), calls=%async_computation.9 | async-start | bytes 4718592 | tf_op jit(solution)/shard_map/reduce_scatter | solution.py:592
  219.9 39.5 %collective-permute-start.17 = (bf16[640,1024]{1,0:T(8,128)(2,1)S(1)}, bf16[640,1024]{1,0:T(8,128)(2,1)}, u32[]{:S(2)}, u32[]{:S(2)}) collective-permute-start(bf16[640,1024]{1,0:T(8,128)(2,1)S(1)} %add_convert_fusion.10), channel_id=1, source_target_pairs={{0,2},{1,3},{2,0},{3,1},{4,6},{5,7},{6,4},{7,5},{8,10},{9,11},{10,... | collective-permute-start | bytes 3932168 | tf_op jit(solution)/shard_map/ppermute | solution.py:570
  267.0 42.4 %collective-permute-start.22 = (bf16[896,1024]{1,0:T(8,128)(2,1)}, bf16[896,1024]{1,0:T(8,128)(2,1)}, u32[]{:S(2)}, u32[]{:S(2)}) collective-permute-start(bf16[896,1024]{1,0:T(8,128)(2,1)} %add_convert_fusion.4), channel_id=1, source_target_pairs={{0,2},{1,3},{2,0},{3,1},{4,6},{5,7},{6,4},{7,5},{8,10},{9,11},{10,... | collective-permute-start | bytes 5505032 | tf_op jit(solution)/shard_map/ppermute | solution.py:570
  314.6 33.2 %collective-permute-start.19 = (bf16[640,1024]{1,0:T(8,128)(2,1)}, bf16[640,1024]{1,0:T(8,128)(2,1)}, u32[]{:S(2)}, u32[]{:S(2)}) collective-permute-start(bf16[640,1024]{1,0:T(8,128)(2,1)} %get-tuple-element.183), channel_id=1, source_target_pairs={{0,1},{1,0},{2,3},{3,2},{4,5},{5,4},{6,7},{7,6},{8,9},{9,8},{10,11... | collective-permute-start | bytes 3932168 | tf_op jit(solution)/shard_map/ppermute | solution.py:566
  315.0 47.9 %all-to-all-start.3 = ((bf16[8,112,1024]{2,1,0:T(8,128)(2,1)}), bf16[8,112,1024]{2,1,0:T(8,128)(2,1)}, u32[]{:S(2)}, u32[]{:S(2)}) async-start(bf16[8,112,1024]{2,1,0:T(8,128)(2,1)} %bitcast.180), calls=%async_computation.4 | async-start | bytes 3670016 | tf_op jit(solution)/shard_map/all_to_all | solution.py:587
  319.8 61.4 %collective-permute-start.26 = (bf16[896,1024]{1,0:T(8,128)(2,1)}, bf16[896,1024]{1,0:T(8,128)(2,1)}, u32[]{:S(2)}, u32[]{:S(2)}) collective-permute-start(bf16[896,1024]{1,0:T(8,128)(2,1)} %get-tuple-element.213), channel_id=1, source_target_pairs={{0,1},{1,0},{2,3},{3,2},{4,5},{5,4},{6,7},{7,6},{8,9},{9,8},{10,11... | collective-permute-start | bytes 5505032 | tf_op jit(solution)/shard_map/ppermute | solution.py:566
  329.5 51.7 %collective-permute-start.27 = (bf16[896,1024]{1,0:T(8,128)(2,1)}, bf16[896,1024]{1,0:T(8,128)(2,1)}, u32[]{:S(2)}, u32[]{:S(2)}) collective-permute-start(bf16[896,1024]{1,0:T(8,128)(2,1)} %add_convert_fusion.2), channel_id=1, source_target_pairs={{0,2},{1,3},{2,0},{3,1},{4,6},{5,7},{6,4},{7,5},{8,10},{9,11},{10,... | collective-permute-start | bytes 5505032 | tf_op jit(solution)/shard_map/ppermute | solution.py:570
  371.2 31.3 %collective-permute-start.23 = (bf16[640,1024]{1,0:T(8,128)(2,1)S(1)}, bf16[640,1024]{1,0:T(8,128)(2,1)}, u32[]{:S(2)}, u32[]{:S(2)}) collective-permute-start(bf16[640,1024]{1,0:T(8,128)(2,1)S(1)} %get-tuple-element.345), channel_id=1, source_target_pairs={{0,2},{1,3},{2,0},{3,1},{4,6},{5,7},{6,4},{7,5},{8,10},{9,11},{10,... | collective-permute-start | bytes 3932168 | tf_op jit(solution)/shard_map/ppermute | solution.py:570
  386.7 49.2 %all-to-all-start.4 = ((bf16[8,112,1024]{2,1,0:T(8,128)(2,1)}), bf16[8,112,1024]{2,1,0:T(8,128)(2,1)}, u32[]{:S(2)}, u32[]{:S(2)}) async-start(bf16[8,112,1024]{2,1,0:T(8,128)(2,1)} %bitcast.179), calls=%async_computation.5 | async-start | bytes 3670016 | tf_op jit(solution)/shard_map/all_to_all | solution.py:587
  403.7 32.3 %collective-permute-start.31 = (bf16[640,1024]{1,0:T(8,128)(2,1)}, bf16[640,1024]{1,0:T(8,128)(2,1)}, u32[]{:S(2)}, u32[]{:S(2)}) collective-permute-start(bf16[640,1024]{1,0:T(8,128)(2,1)} %add_convert_fusion.9), channel_id=1, source_target_pairs={{0,2},{1,3},{2,0},{3,1},{4,6},{5,7},{6,4},{7,5},{8,10},{9,11},{10,... | collective-permute-start | bytes 3932168 | tf_op jit(solution)/shard_map/ppermute | solution.py:570
  436.0 28.4 %all-to-all-start.5 = ((bf16[8,128,384]{2,1,0:T(8,128)(2,1)}), bf16[8,128,384]{2,1,0:T(8,128)(2,1)}, u32[]{:S(2)}, u32[]{:S(2)}) async-start(bf16[8,128,384]{2,1,0:T(8,128)(2,1)} %bitcast.47), calls=%async_computation.6 | async-start | bytes 1572864 | tf_op jit(solution)/shard_map/all_to_all | solution.py:587
  480.5 32.5 %all-to-all-start.6 = ((bf16[8,128,384]{2,1,0:T(8,128)(2,1)}), bf16[8,128,384]{2,1,0:T(8,128)(2,1)}, u32[]{:S(2)}, u32[]{:S(2)}) async-start(bf16[8,128,384]{2,1,0:T(8,128)(2,1)} %bitcast.192), calls=%async_computation.7 | async-start | bytes 1572864 | tf_op jit(solution)/shard_map/all_to_all | solution.py:587
  486.4 32.6 %collective-permute-start.37 = (bf16[640,1024]{1,0:T(8,128)(2,1)}, bf16[640,1024]{1,0:T(8,128)(2,1)}, u32[]{:S(2)}, u32[]{:S(2)}) collective-permute-start(bf16[640,1024]{1,0:T(8,128)(2,1)} %add_convert_fusion.7), channel_id=1, source_target_pairs={{0,2},{1,3},{2,0},{3,1},{4,6},{5,7},{6,4},{7,5},{8,10},{9,11},{10,... | collective-permute-start | bytes 3932168 | tf_op jit(solution)/shard_map/ppermute | solution.py:570
  512.9 23.6 %all-to-all-start.7 = ((bf16[8,128,384]{2,1,0:T(8,128)(2,1)}), bf16[8,128,384]{2,1,0:T(8,128)(2,1)S(1)}, u32[]{:S(2)}, u32[]{:S(2)}) async-start(bf16[8,128,384]{2,1,0:T(8,128)(2,1)} %bitcast.191), calls=%async_computation.8 | async-start | bytes 1572864 | tf_op jit(solution)/shard_map/all_to_all | solution.py:587
  (83 other events, 616.9 us)
Sparse Core Ops, SparseCore 0:
  219.4 85.9 reduce-scatter.1

commit v15 on v13

--- a/solution.py
+++ b/solution.py
@@ -551,6 +551,24 @@
     return (centred * inverse, inverse)
 
 
+def norm_kernel(rows_ref, gain_ref, out_ref):
+    scaled, _ = norm_parts(rows_ref[...].astype(F32))
+    out_ref[...] = (scaled * gain_ref[...]).astype(BF16)
+
+
+def normed_rows(rows, gain_vec):
+    count, width = rows.shape
+    block = pl.BlockSpec((QUARTER_ROWS, width), lambda i: (i, 0))
+    return pl.pallas_call(
+        norm_kernel,
+        grid=(count // QUARTER_ROWS,),
+        in_specs=[block, pl.BlockSpec((1, width), lambda i: (0, 0))],
+        out_specs=block,
+        out_shape=jax.ShapeDtypeStruct((count, width), BF16),
+        name="row_norm",
+    )(rows, gain_vec[None])
+
+
 def norm_back(grad_normed, gain_vec, scaled, inverse):
     grad_scaled = grad_normed * gain_vec
     first_mean = jnp.mean(grad_scaled, axis=-1, keepdims=True)
@@ -637,7 +655,7 @@
     leaves = jnp.concatenate([leaf_order(parents[0]), mine.astype(jnp.int32)[None]])
 
     scaled_one, inverse_one = norm_parts(tokens.astype(F32))
-    normed_own = (scaled_one * ln_attn).astype(BF16)
+    normed_own = normed_rows(tokens, ln_attn)
     normed_far = from_far(normed_own)
     near_one = jnp.concatenate([normed_own, from_side(normed_own)], axis=0)
 

time: 555 us -> 560 us (level)
    unnamed x120 -> x132, local copies, waits for them, and re-layouts: 13.9 us -> 10.4 us
  transfers between devices with their start and end apart: 51 -> 51, of which waited for: 21 -> 18; matrix products, arithmetic and copies ran while one was open for 29% -> 30% of each run, Pallas kernels for 31% -> 31%
where the time goes in v15:
time: 560 us; the launch traced here: 555 us
  Pallas kernels  178 us (32%)
  matrix products  119 us (21%)
  waiting for transfers between devices  98.7 us (18%)
  starting transfers between devices  69.4 us (12%)
  other arithmetic  59.6 us (11%)
  local copies, waits for them, and re-layouts  15.7 us (3%)
  between operations  15.4 us (3%)
    pallas_call x4, Pallas kernels, feed(): pl.pallas_call(functools.partial(feed_kernel, experts, routed), grid_spec...  107 us
    dot_general x14, matrix products, product(): return jnp.einsum('gd,gf->df', left, right, preferred_element_type=F32)  60 us
    ppermute x11, waiting for transfers between devices, from_far(): return lax.ppermute(values, 'tensor', [(i, i ^ 2) for i in range(4)])  50.6 us
    pallas_call x2, Pallas kernels, attention_backward(): pl.pallas_call(backward_kernel, grid_spec=pltpu.PrefetchScalarGridSpec(nu...  44.8 us
    all_to_all x8, starting transfers between devices, exchange(): lax.all_to_all(blocks, 'expert', split_axis=0, concat_axis=0, tiled=True)  40.7 us
    all_to_all x8, waiting for transfers between devices, exchange(): lax.all_to_all(blocks, 'expert', split_axis=0, concat_axis=0, tiled=True)  26.1 us
    pallas_call x1, Pallas kernels, attention_forward(): pl.pallas_call(forward_kernel, grid_spec=pltpu.PrefetchScalarGridSpec(num...  22 us
    ppermute x24, waiting for transfers between devices, from_side(): return lax.ppermute(values, 'tensor', [(i, i ^ 1) for i in range(4)])  16 us
  transfers between devices with their start and end apart: 51, of which 18 were waited for; matrix products, arithmetic and copies ran while one was open for 30% of the time, Pallas kernels for 31%

profile of v15, /device:TPU:0, one launch (start us, length us, event | category | flops | bytes accessed | tf_op | source)
XLA Modules:
  0.0 555.4 jit_solution(3158883978883934069)
XLA Ops:
  19.7 6.1 %all-to-all-start = ((bf16[8,112,1024]{2,1,0:T(8,128)(2,1)}), bf16[8,112,1024]{2,1,0:T(8,128)(2,1)S(1)}, u32[]{:S(2)}, u32[]{:S(2)}) async-start(bf16[8,112,1024]{2,1,0:T(8,128)(2,1)} %bitcast.190), calls=%async_computation | async-start | bytes 3670016 | tf_op jit(solution)/shard_map/all_to_all | solution.py:605
  27.2 5.7 %convolution_convert_fusion.1 = bf16[1280,3,256]{2,0,1:T(8,128)(2,1)} fusion(bf16[3,1024,256]{2,1,0:T(8,128)(2,1)} %param.19, bf16[640,1024]{1,0:T(8,128)(2,1)} %collective-permute-done.1, bf16[640,1024]{1,0:T(8,128)(2,1)} %row_norm.1), kind=kOutput, calls=%fused_computation.22 | convolution fusion | flops 2019491840 | bytes 6160384 | tf_op jit(solution)/shard_map/td,sdc->stc/dot_general | solution.py:680
  32.9 11.6 %collective-permute-done = bf16[640,1024]{1,0:T(8,128)(2,1)} collective-permute-done((bf16[640,1024]{1,0:T(8,128)(2,1)}, bf16[640,1024]{1,0:T(8,128)(2,1)}, u32[]{:S(2)}, u32[]{:S(2)}) %collective-permute-start) | collective-permute-done | bytes 1310752 | tf_op jit(solution)/shard_map/ppermute | solution.py:588
  53.3 22.0 %tree_attention.1 = (bf16[2,640,256]{2,1,0:T(8,128)(2,1)}, bf16[2,640,256]{2,1,0:T(8,128)(2,1)}, f32[2,2,1024]{2,1,0:T(2,128)}, f32[2,2,2,768]{3,2,1,0:T(2,128)}) custom-call(s32[9]{0:T(128)} %pad_add_fusion.leaves_ref, bf16[3,2,640,256]{3,2,1,0:T(8,128)(2,1)} %bitcast.212, bf16[3,2,640,256]{3,2,1,0:T(8,128)(2,1)} %bitcast.215), custom_call_target="tpu_custom_call" | custom-call | flops 1241513984 | bytes 1310720 | tf_op jit(solution)/shard_map/tree_attention/pallas_call | solution.py:200
  91.3 23.5 %collective-permute-done.7 = bf16[640,1024]{1,0:T(8,128)(2,1)S(1)} collective-permute-done((bf16[640,1024]{1,0:T(8,128)(2,1)S(1)}, bf16[640,1024]{1,0:T(8,128)(2,1)S(1)}, u32[]{:S(2)}, u32[]{:S(2)}) %collective-permute-start.7) | collective-permute-done | bytes 1310752 | tf_op jit(solution)/shard_map/ppermute | solution.py:588
  119.9 6.5 %all-to-all-start.1 = ((bf16[8,112,1024]{2,1,0:T(8,128)(2,1)}), bf16[8,112,1024]{2,1,0:T(8,128)(2,1)}, u32[]{:S(2)}, u32[]{:S(2)}) async-start(bf16[8,112,1024]{2,1,0:T(8,128)(2,1)} %bitcast.191), calls=%async_computation.1 | async-start | bytes 3670016 | tf_op jit(solution)/shard_map/all_to_all | solution.py:605
  129.8 20.0 %feed_dense.2 = (bf16[640,1024]{1,0:T(8,128)(2,1)}, bf16[640,1024]{1,0:T(8,128)(2,1)}, bf16[640,1024]{1,0:T(8,128)(2,1)}, bf16[640,1024]{1,0:T(8,128)(2,1)}, bf1...) custom-call(s32[1]{0:T(128)} %constant.47.clone.1.expert_ref, ...), custom_call_target="tpu_custom_call" | custom-call | flops 1342177280 | bytes 2490368 | tf_op jit(solution)/shard_map/feed_dense/pallas_call | solution.py:495
  149.9 7.6 %fusion.21 = f32[1024,1024]{1,0:T(8,128)} fusion(bf16[1280,1024]{1,0:T(8,128)(2,1)} %bitcast.211, bf16[640,1024]{1,0:T(8,128)(2,1)} %collective-permute-done.10.side_ref, bf16[640,1024]{1,0:T(8,128)(2,1)} %copy-done.8), kind=kOutput, calls=%fused_computation.36 | convolution fusion | flops 2689597440 | bytes 9437184 | tf_op jit(solution)/shard_map/gd,gf->df/dot_general | solution.py:723
  162.0 6.5 %all-to-all-done.1 = bf16[8,112,1024]{2,1,0:T(8,128)(2,1)} async-done(((bf16[8,112,1024]{2,1,0:T(8,128)(2,1)}), bf16[8,112,1024]{2,1,0:T(8,128)(2,1)}, u32[]{:S(2)}, u32[]{:S(2)}) %all-to-all-start.1) | async-done | bytes 1835040 | tf_op jit(solution)/shard_map/all_to_all | solution.py:605
  174.4 20.2 %feed_dense.3 = (bf16[640,1024]{1,0:T(8,128)(2,1)}, bf16[640,1024]{1,0:T(8,128)(2,1)}, bf16[640,1024]{1,0:T(8,128)(2,1)}, bf16[640,1024]{1,0:T(8,128)(2,1)}, bf1...) custom-call(s32[1]{0:T(128)} %constant.47.clone.1.expert_ref, ...), custom_call_target="tpu_custom_call" | custom-call | flops 1342177280 | bytes 2490368 | tf_op jit(solution)/shard_map/feed_dense/pallas_call | solution.py:495
  212.5 5.1 all-to-all-done.2
  224.5 33.1 %feed_routed.2 = (bf16[896,1024]{1,0:T(8,128)(2,1)}, bf16[896,1024]{1,0:T(8,128)(2,1)}, bf16[896,1024]{1,0:T(8,128)(2,1)}, bf16[896,1024]{1,0:T(8,128)(2,1)}, bf...) custom-call(s32[1]{0:T(128)} %bitcast.21.expert_ref, ...), custom_call_target="tpu_custom_call" | custom-call | flops 1879048192 | bytes 3276800 | tf_op jit(solution)/shard_map/feed_routed/pallas_call | solution.py:495
  267.1 33.1 %feed_routed.3 = (bf16[896,1024]{1,0:T(8,128)(2,1)}, bf16[896,1024]{1,0:T(8,128)(2,1)}, bf16[896,1024]{1,0:T(8,128)(2,1)}, bf16[896,1024]{1,0:T(8,128)(2,1)}, bf...) custom-call(s32[1]{0:T(128)} %bitcast.21.expert_ref, ...), custom_call_target="tpu_custom_call" | custom-call | flops 1879048192 | bytes 3276800 | tf_op jit(solution)/shard_map/feed_routed/pallas_call | solution.py:495
  303.9 5.0 collective-permute-done.22
  334.5 7.8 %fusion.5 = f32[1024,1024]{1,0:T(8,128)} fusion(bf16[1792,1024]{1,0:T(8,128)(2,1)S(1)} %bitcast.207, bf16[896,1024]{1,0:T(8,128)(2,1)} %collective-permute-done.15.side_ref, bf16[896,1024]{1,0:T(8,128)(2,1)} %collective-permute-done.12.own_ref), kind=kOutput, calls=%fused_computation.13 | convolution fusion | flops 3765436416 | bytes 11534336 | tf_op jit(solution)/shard_map/gd,gf->df/dot_general | solution.py:723
  342.3 5.6 add_bitcast_fusion
  347.8 14.4 %all-to-all-done.3 = bf16[8,112,1024]{2,1,0:T(8,128)(2,1)} async-done(((bf16[8,112,1024]{2,1,0:T(8,128)(2,1)}), bf16[8,112,1024]{2,1,0:T(8,128)(2,1)}, u32[]{:S(2)}, u32[]{:S(2)}) %all-to-all-start.3) | async-done | bytes 1835040 | tf_op jit(solution)/shard_map/all_to_all | solution.py:605
  362.3 5.3 multiply_reduce_fusion
  372.7 7.6 %add_bitcast_fusion.1 = f32[1,1024,1024]{2,1,0:T(8,128)} fusion(f32[1024,1024]{1,0:T(8,128)S(1)} %copy-done.61, bf16[1792,1024]{1,0:T(8,128)(2,1)S(1)} %bitcast.206, bf16[896,1024]{1,0:T(8,128)(2,1)} %collective-permute-done.20.side_ref, bf16[896,1024]{1,0:T(8,128)(2,1)} %bitcast.20.own_ref), kind=kOutput, calls=%fused_computation.4 | convolution fusion | flops 3766484992 | bytes 15728640 | tf_op jit(solution)/shard_map/gd,gf->df/dot_general | solution.py:723
  397.6 5.4 collective-permute-done.23
  414.7 22.3 %tree_attention_back.2 = (bf16[2,640,384]{2,1,0:T(8,128)(2,1)}, bf16[2,640,384]{2,1,0:T(8,128)(2,1)}) custom-call(s32[9]{0:T(128)} %pad_add_fusion.leaves_ref, bf16[3,2,640,256]{3,2,1,0:T(8,128)(2,1)} %bitcast.213, bf16[3,2,640,256]{3,2,1,0:T(8,128)(2,1)} %bitcast.216, bf16[2,640,256]{2,1,0:T(8,128)(2,1)} %pad_maximum_fusion.9.near_grads_ref, ...), custom_call_target="tpu_custom_call" | custom-call | flops 2483025920 | bytes 1048576 | tf_op jit(solution)/shard_map/tree_attention_back/pallas_call | solution.py:350
  444.0 22.5 %tree_attention_back.3 = (bf16[2,640,384]{2,1,0:T(8,128)(2,1)}, bf16[2,640,384]{2,1,0:T(8,128)(2,1)}) custom-call(s32[9]{0:T(128)} %pad_add_fusion.leaves_ref, bf16[3,2,640,256]{3,2,1,0:T(8,128)(2,1)} %bitcast.214, bf16[3,2,640,256]{3,2,1,0:T(8,128)(2,1)} %bitcast.217, bf16[2,640,256]{2,1,0:T(8,128)(2,1)} %pad_maximum_fusion.9.near_grads_ref, ...), custom_call_target="tpu_custom_call" | custom-call | flops 2483025920 | bytes 1048576 | tf_op jit(solution)/shard_map/tree_attention_back/pallas_call | solution.py:350
  482.6 6.0 %all-to-all-start.6 = ((bf16[8,128,384]{2,1,0:T(8,128)(2,1)}), bf16[8,128,384]{2,1,0:T(8,128)(2,1)}, u32[]{:S(2)}, u32[]{:S(2)}) async-start(bf16[8,128,384]{2,1,0:T(8,128)(2,1)} %bitcast.196), calls=%async_computation.7 | async-start | bytes 1572864 | tf_op jit(solution)/shard_map/all_to_all | solution.py:605
  492.3 5.0 fusion.15
  (328 shorter events, 231.9 us)
Async XLA Ops:
  12.3 32.3 %collective-permute-start = (bf16[640,1024]{1,0:T(8,128)(2,1)}, bf16[640,1024]{1,0:T(8,128)(2,1)}, u32[]{:S(2)}, u32[]{:S(2)}) collective-permute-start(bf16[640,1024]{1,0:T(8,128)(2,1)} %row_norm.1), channel_id=1, source_target_pairs={{0,2},{1,3},{2,0},{3,1},{4,6},{5,7},{6,4},{7,5},{8,10},{9,11},{10,... | collective-permute-start | bytes 3932168 | tf_op jit(solution)/shard_map/ppermute | solution.py:588
  19.7 56.7 %all-to-all-start = ((bf16[8,112,1024]{2,1,0:T(8,128)(2,1)}), bf16[8,112,1024]{2,1,0:T(8,128)(2,1)S(1)}, u32[]{:S(2)}, u32[]{:S(2)}) async-start(bf16[8,112,1024]{2,1,0:T(8,128)(2,1)} %bitcast.190), calls=%async_computation | async-start | bytes 3670016 | tf_op jit(solution)/shard_map/all_to_all | solution.py:605
  44.6 30.8 %collective-permute-start.5 = (bf16[640,1024]{1,0:T(8,128)(2,1)}, bf16[640,1024]{1,0:T(8,128)(2,1)}, u32[]{:S(2)}, u32[]{:S(2)}) collective-permute-start(bf16[640,1024]{1,0:T(8,128)(2,1)} %own_grads_ref.1), channel_id=1, source_target_pairs={{0,1},{1,0},{2,3},{3,2},{4,5},{5,4},{6,7},{7,6},{8,9},{9,8},{10,11... | collective-permute-start | bytes 3932168 | tf_op jit(solution)/shard_map/ppermute | solution.py:584
  45.3 31.1 %collective-permute-start.4 = (bf16[640,1024]{1,0:T(8,128)(2,1)}, bf16[640,1024]{1,0:T(8,128)(2,1)}, u32[]{:S(2)}, u32[]{:S(2)}) collective-permute-start(bf16[640,1024]{1,0:T(8,128)(2,1)} %own_grads_ref.1), channel_id=1, source_target_pairs={{0,2},{1,3},{2,0},{3,1},{4,6},{5,7},{6,4},{7,5},{8,10},{9,11},{10,... | collective-permute-start | bytes 3932168 | tf_op jit(solution)/shard_map/ppermute | solution.py:588
  83.9 30.9 %collective-permute-start.7 = (bf16[640,1024]{1,0:T(8,128)(2,1)S(1)}, bf16[640,1024]{1,0:T(8,128)(2,1)S(1)}, u32[]{:S(2)}, u32[]{:S(2)}) collective-permute-start(bf16[640,1024]{1,0:T(8,128)(2,1)S(1)} %add_convert_fusion.11), channel_id=1, source_target_pairs={{0,2},{1,3},{2,0},{3,1},{4,6},{5,7},{6,4},{7,5},{8,10},{9,11},{10,... | collective-permute-start | bytes 3932168 | tf_op jit(solution)/shard_map/ppermute | solution.py:588
  86.2 28.6 %collective-permute-start.3 = (bf16[640,1024]{1,0:T(8,128)(2,1)S(1)}, bf16[640,1024]{1,0:T(8,128)(2,1)S(1)}, u32[]{:S(2)}, u32[]{:S(2)}) collective-permute-start(bf16[640,1024]{1,0:T(8,128)(2,1)S(1)} %convolution_convert_fusion.3), channel_id=1, source_target_pairs={{0,1},{1,0},{2,3},{3,2},{4,5},{5,4},{6,7},{7,6},{8,9},{9,8},{10,11... | collective-permute-start | bytes 3932168 | tf_op jit(solution)/shard_map/ppermute | solution.py:584
  119.9 48.6 %all-to-all-start.1 = ((bf16[8,112,1024]{2,1,0:T(8,128)(2,1)}), bf16[8,112,1024]{2,1,0:T(8,128)(2,1)}, u32[]{:S(2)}, u32[]{:S(2)}) async-start(bf16[8,112,1024]{2,1,0:T(8,128)(2,1)} %bitcast.191), calls=%async_computation.1 | async-start | bytes 3670016 | tf_op jit(solution)/shard_map/all_to_all | solution.py:605
  126.5 35.5 %collective-permute-start.11 = (bf16[640,1024]{1,0:T(8,128)(2,1)}, bf16[640,1024]{1,0:T(8,128)(2,1)}, u32[]{:S(2)}, u32[]{:S(2)}) collective-permute-start(bf16[640,1024]{1,0:T(8,128)(2,1)} %copy-done.8), channel_id=1, source_target_pairs={{0,2},{1,3},{2,0},{3,1},{4,6},{5,7},{6,4},{7,5},{8,10},{9,11},{10,... | collective-permute-start | bytes 3932168 | tf_op jit(solution)/shard_map/ppermute | solution.py:588
  168.5 49.1 %collective-permute-start.12 = (bf16[896,1024]{1,0:T(8,128)(2,1)}, bf16[896,1024]{1,0:T(8,128)(2,1)}, u32[]{:S(2)}, u32[]{:S(2)}) collective-permute-start(bf16[896,1024]{1,0:T(8,128)(2,1)} %bitcast.20.own_ref), channel_id=1, source_target_pairs={{0,2},{1,3},{2,0},{3,1},{4,6},{5,7},{6,4},{7,5},{8,10},{9,11},{10,... | collective-permute-start | bytes 5505032 | tf_op jit(solution)/shard_map/ppermute | solution.py:588
  170.0 47.6 %all-to-all-start.2 = ((bf16[8,112,1024]{2,1,0:T(8,128)(2,1)}), bf16[8,112,1024]{2,1,0:T(8,128)(2,1)}, u32[]{:S(2)}, u32[]{:S(2)}) async-start(bf16[8,112,1024]{2,1,0:T(8,128)(2,1)} %bitcast.189), calls=%async_computation.2 | async-start | bytes 3670016 | tf_op jit(solution)/shard_map/all_to_all | solution.py:605
  174.4 129.5 %reduce-scatter.2.cloned.1.call-start = ((), (), s32[]{:S(2)}) async-start(), calls=%async_computation.9 | async-start | bytes 4718592 | tf_op jit(solution)/shard_map/reduce_scatter | solution.py:610
  218.3 39.4 %collective-permute-start.17 = (bf16[640,1024]{1,0:T(8,128)(2,1)}, bf16[640,1024]{1,0:T(8,128)(2,1)}, u32[]{:S(2)}, u32[]{:S(2)}) collective-permute-start(bf16[640,1024]{1,0:T(8,128)(2,1)} %add_convert_fusion.10), channel_id=1, source_target_pairs={{0,2},{1,3},{2,0},{3,1},{4,6},{5,7},{6,4},{7,5},{8,10},{9,11},{10,... | collective-permute-start | bytes 3932168 | tf_op jit(solution)/shard_map/ppermute | solution.py:588
  266.5 42.4 %collective-permute-start.22 = (bf16[896,1024]{1,0:T(8,128)(2,1)}, bf16[896,1024]{1,0:T(8,128)(2,1)}, u32[]{:S(2)}, u32[]{:S(2)}) collective-permute-start(bf16[896,1024]{1,0:T(8,128)(2,1)} %add_convert_fusion.4), channel_id=1, source_target_pairs={{0,2},{1,3},{2,0},{3,1},{4,6},{5,7},{6,4},{7,5},{8,10},{9,11},{10,... | collective-permute-start | bytes 5505032 | tf_op jit(solution)/shard_map/ppermute | solution.py:588
  314.0 33.8 %collective-permute-start.19 = (bf16[640,1024]{1,0:T(8,128)(2,1)}, bf16[640,1024]{1,0:T(8,128)(2,1)}, u32[]{:S(2)}, u32[]{:S(2)}) collective-permute-start(bf16[640,1024]{1,0:T(8,128)(2,1)} %get-tuple-element.182), channel_id=1, source_target_pairs={{0,1},{1,0},{2,3},{3,2},{4,5},{5,4},{6,7},{7,6},{8,9},{9,8},{10,11... | collective-permute-start | bytes 3932168 | tf_op jit(solution)/shard_map/ppermute | solution.py:584
  314.5 47.8 %all-to-all-start.3 = ((bf16[8,112,1024]{2,1,0:T(8,128)(2,1)}), bf16[8,112,1024]{2,1,0:T(8,128)(2,1)}, u32[]{:S(2)}, u32[]{:S(2)}) async-start(bf16[8,112,1024]{2,1,0:T(8,128)(2,1)} %bitcast.181), calls=%async_computation.4 | async-start | bytes 3670016 | tf_op jit(solution)/shard_map/all_to_all | solution.py:605
  319.2 63.1 %collective-permute-start.26 = (bf16[896,1024]{1,0:T(8,128)(2,1)}, bf16[896,1024]{1,0:T(8,128)(2,1)}, u32[]{:S(2)}, u32[]{:S(2)}) collective-permute-start(bf16[896,1024]{1,0:T(8,128)(2,1)} %get-tuple-element.212), channel_id=1, source_target_pairs={{0,1},{1,0},{2,3},{3,2},{4,5},{5,4},{6,7},{7,6},{8,9},{9,8},{10,11... | collective-permute-start | bytes 5505032 | tf_op jit(solution)/shard_map/ppermute | solution.py:584
  329.9 52.5 %collective-permute-start.27 = (bf16[896,1024]{1,0:T(8,128)(2,1)}, bf16[896,1024]{1,0:T(8,128)(2,1)}, u32[]{:S(2)}, u32[]{:S(2)}) collective-permute-start(bf16[896,1024]{1,0:T(8,128)(2,1)} %add_convert_fusion.2), channel_id=1, source_target_pairs={{0,2},{1,3},{2,0},{3,1},{4,6},{5,7},{6,4},{7,5},{8,10},{9,11},{10,... | collective-permute-start | bytes 5505032 | tf_op jit(solution)/shard_map/ppermute | solution.py:588
  371.6 31.5 %collective-permute-start.23 = (bf16[640,1024]{1,0:T(8,128)(2,1)}, bf16[640,1024]{1,0:T(8,128)(2,1)}, u32[]{:S(2)}, u32[]{:S(2)}) collective-permute-start(bf16[640,1024]{1,0:T(8,128)(2,1)} %get-tuple-element.343), channel_id=1, source_target_pairs={{0,2},{1,3},{2,0},{3,1},{4,6},{5,7},{6,4},{7,5},{8,10},{9,11},{10,... | collective-permute-start | bytes 3932168 | tf_op jit(solution)/shard_map/ppermute | solution.py:588
  386.9 50.2 %all-to-all-start.4 = ((bf16[8,112,1024]{2,1,0:T(8,128)(2,1)}), bf16[8,112,1024]{2,1,0:T(8,128)(2,1)}, u32[]{:S(2)}, u32[]{:S(2)}) async-start(bf16[8,112,1024]{2,1,0:T(8,128)(2,1)} %bitcast.180), calls=%async_computation.5 | async-start | bytes 3670016 | tf_op jit(solution)/shard_map/all_to_all | solution.py:605
  404.9 32.1 %collective-permute-start.31 = (bf16[640,1024]{1,0:T(8,128)(2,1)}, bf16[640,1024]{1,0:T(8,128)(2,1)}, u32[]{:S(2)}, u32[]{:S(2)}) collective-permute-start(bf16[640,1024]{1,0:T(8,128)(2,1)} %add_convert_fusion.9), channel_id=1, source_target_pairs={{0,2},{1,3},{2,0},{3,1},{4,6},{5,7},{6,4},{7,5},{8,10},{9,11},{10,... | collective-permute-start | bytes 3932168 | tf_op jit(solution)/shard_map/ppermute | solution.py:588
  437.1 29.4 %all-to-all-start.5 = ((bf16[8,128,384]{2,1,0:T(8,128)(2,1)}), bf16[8,128,384]{2,1,0:T(8,128)(2,1)}, u32[]{:S(2)}, u32[]{:S(2)}) async-start(bf16[8,128,384]{2,1,0:T(8,128)(2,1)} %bitcast.186), calls=%async_computation.6 | async-start | bytes 1572864 | tf_op jit(solution)/shard_map/all_to_all | solution.py:605
  482.6 27.0 %all-to-all-start.6 = ((bf16[8,128,384]{2,1,0:T(8,128)(2,1)}), bf16[8,128,384]{2,1,0:T(8,128)(2,1)}, u32[]{:S(2)}, u32[]{:S(2)}) async-start(bf16[8,128,384]{2,1,0:T(8,128)(2,1)} %bitcast.196), calls=%async_computation.7 | async-start | bytes 1572864 | tf_op jit(solution)/shard_map/all_to_all | solution.py:605
  488.6 31.3 %collective-permute-start.37 = (bf16[640,1024]{1,0:T(8,128)(2,1)}, bf16[640,1024]{1,0:T(8,128)(2,1)}, u32[]{:S(2)}, u32[]{:S(2)}) collective-permute-start(bf16[640,1024]{1,0:T(8,128)(2,1)} %add_convert_fusion.7), channel_id=1, source_target_pairs={{0,2},{1,3},{2,0},{3,1},{4,6},{5,7},{6,4},{7,5},{8,10},{9,11},{10,... | collective-permute-start | bytes 3932168 | tf_op jit(solution)/shard_map/ppermute | solution.py:588
  509.6 30.2 %all-to-all-start.7 = ((bf16[8,128,384]{2,1,0:T(8,128)(2,1)}), bf16[8,128,384]{2,1,0:T(8,128)(2,1)}, u32[]{:S(2)}, u32[]{:S(2)}) async-start(bf16[8,128,384]{2,1,0:T(8,128)(2,1)} %bitcast.195), calls=%async_computation.8 | async-start | bytes 1572864 | tf_op jit(solution)/shard_map/all_to_all | solution.py:605
  (89 other events, 946.9 us)
Sparse Core Ops, SparseCore 0:
  217.8 86.0 reduce-scatter.1
